TPU v7x, 256 devices: a whole 4x4x8 slice. The times are simulated.
256 devices in a mesh: grp: 16 (over y_lo, z), row: 16 (over y_hi, x, core).
Axes of the slice: x: 4, y: 4 (y_hi: 2, y_lo: 2; y = y_hi * 2 + y_lo), z: 8, core: 2. Of those that a mesh axis runs over, the one named last changes fastest.
Arguments:
- view_a: float32 [16384, 8192], P('row', 'grp'), may hold values from -40 to 40
- view_b: float32 [16384, 8192], P('row', 'grp'), may hold values from -40 to 40
Outputs:
- grad_a: float32 [16384, 8192], P('row', 'grp')
- grad_b: float32 [16384, 8192], P('row', 'grp')
All inputs are finite; a program needn't handle non-finite values.
Results may differ from a plain program's by a relative error of at most 0.00025.
Values sent between devices are 32-bit elements; how exact they have to be, the bound alone decides.
No kernel may reach another device: no remote copies, remote signals or barrier semaphores. Data moves between devices by JAX's collectives and lax.ppermute only.
A program may use at most 64 MiB of HBM per device.

v0:
```python
import jax
import jax.numpy as jnp
from jax import lax
from jax.sharding import PartitionSpec as P

epsilon = 1e-05
off_weight = 0.0051


def with_halo(block, sides, width):
    for axis, dim in sides:
        count = lax.axis_size(axis)
        forward = [(i, i + 1) for i in range(count - 1)]
        forward.append((count - 1, 0))
        backward = [(target, source) for source, target in forward]
        low = lax.ppermute(
            lax.slice_in_dim(block, block.shape[dim] - width, None, axis=dim), axis, forward
        )
        high = lax.ppermute(lax.slice_in_dim(block, 0, width, axis=dim), axis, backward)
        block = jnp.concatenate([low, block, high], axis=dim)
    return block


def shifted(block, axis, distance):
    devices = range(lax.axis_size(axis))
    route = [((i - distance) % len(devices), i) for i in devices]
    return lax.ppermute(block, axis, route)


def penalty_of(corr, panel_width):
    row_index = lax.iota(jnp.int32, corr.shape[0])[:, None]
    column = lax.iota(jnp.int32, corr.shape[1])[None, :]
    on_diagonal = column == row_index + panel_width
    return jnp.where(on_diagonal, -2.0 * (1.0 - corr), 2.0 * off_weight * corr)


def per_device(view_a, view_b):
    highest = lax.Precision.HIGHEST
    local_rows, panel_width = view_a.shape
    row_devices = lax.axis_size("row")
    batch_rows = local_rows * row_devices
    totals = lax.psum(
        (
            jnp.sum(view_a, axis=0),
            jnp.sum(view_a * view_a, axis=0),
            jnp.sum(view_b, axis=0),
            jnp.sum(view_b * view_b, axis=0),
        ),
        "row",
    )
    mean_a = totals[0] / batch_rows
    scale_a = jnp.sqrt(totals[1] / batch_rows - mean_a * mean_a + epsilon)
    mean_b = totals[2] / batch_rows
    scale_b = jnp.sqrt(totals[3] / batch_rows - mean_b * mean_b + epsilon)
    norm_a = (view_a - mean_a) / scale_a
    norm_b = (view_b - mean_b) / scale_b
    neighbours = with_halo(norm_b, (("grp", 1),), panel_width)
    partial_corr = (
        jnp.einsum(
            "rp,rq->pq", norm_a, neighbours, precision=highest, preferred_element_type=jnp.float32
        )
        / batch_rows
    )
    corr = lax.psum(partial_corr, "row")
    penalty = penalty_of(corr, panel_width)
    contrib = jnp.dot(norm_a, penalty, precision=highest, preferred_element_type=jnp.float32)
    from_next = shifted(contrib[:, :panel_width], "grp", -1)
    from_prev = shifted(contrib[:, 2 * panel_width :], "grp", 1)
    grad_own = jnp.einsum(
        "rq,pq->rp", neighbours, penalty, precision=highest, preferred_element_type=jnp.float32
    )
    grad_other = contrib[:, panel_width : 2 * panel_width] + from_next + from_prev
    sums_back = lax.psum(
        (
            jnp.sum(grad_own, axis=0),
            jnp.sum(grad_own * norm_a, axis=0),
            jnp.sum(grad_other, axis=0),
            jnp.sum(grad_other * norm_b, axis=0),
        ),
        "row",
    )
    grad_a = (grad_own - sums_back[0] / batch_rows - norm_a * (sums_back[1] / batch_rows)) / scale_a
    grad_b = (
        grad_other - sums_back[2] / batch_rows - norm_b * (sums_back[3] / batch_rows)
    ) / scale_b
    return (grad_a, grad_b)


def solution(mesh):
    placed = (P("row", "grp"), P("row", "grp"))
    return jax.shard_map(
        per_device,
        mesh=mesh,
        in_specs=placed,
        out_specs=(P("row", "grp"), P("row", "grp")),
        check_vma=False,
    )
```

profile of v0, /device:TPU:1, one launch (start us, length us, event | category | flops | bytes accessed | tf_op | source)
XLA Modules:
  0.0 376.2 jit_solution(16167914780696294608)
XLA Ops:
  7.2 0.0 copy-start
  7.2 0.0 all-reduce.4.cloned.1.call-start
  7.2 2.9 fusion.23
  10.1 36.2 %all-reduce.1 = (f32[512]{0:T(512)S(1)}, f32[512]{0:T(512)S(1)}, f32[512]{0:T(512)S(1)}, f32[512]{0:T(512)S(1)}) all-reduce(f32[512]{0:T(512)S(1)} %get-tuple-element.26, f32[512]{0:T(512)S(1)} %get-tuple-element.27, f32[512]{0:T(512)S(1)} %get-tuple-element.7, f32[512]{0:T(512)S(1)} %get-tuple-element.6), channel_id=1, replica_groups=mesh['grp'=16,'row'=16] {'row'}, use_global_device_ids=true, to_apply=%region_3.0 | all-reduce | flops 2048 | bytes 16384 | tf_op jit(solution)/shard_map/psum | solution.py:42
  46.4 0.0 copy-done
  46.4 0.0 copy-start.1
  46.4 0.3 subtract_divide_fusion.3
  46.7 0.0 copy-start.4
  46.7 4.9 %collective-permute-start.1 = (f32[1024,512]{1,0:T(8,128)S(1)}, f32[1024,512]{1,0:T(8,128)S(1)}, u32[]{:S(2)}, u32[]{:S(2)}) collective-permute-start(f32[1024,512]{1,0:T(8,128)S(1)} %subtract_divide_fusion.3), channel_id=1, source_target_pairs={{16,0},{32,16},{48,32},{64,48},{80,64},{96,80},{112,96},{128,112},... | collective-permute-start | bytes 6291464 | tf_op jit(solution)/shard_map/ppermute | solution.py:19
  51.6 0.0 collective-permute-start
  51.6 40.3 %collective-permute-done.1 = f32[1024,512]{1,0:T(8,128)S(1)} collective-permute-done((f32[1024,512]{1,0:T(8,128)S(1)}, f32[1024,512]{1,0:T(8,128)S(1)}, u32[]{:S(2)}, u32[]{:S(2)}) %collective-permute-start.1) | collective-permute-done | bytes 2097184 | tf_op jit(solution)/shard_map/ppermute | solution.py:19
  91.9 0.0 copy-start.7
  91.9 4.0 %collective-permute-done = f32[1024,512]{1,0:T(8,128)S(1)} collective-permute-done((f32[1024,512]{1,0:T(8,128)S(1)}, f32[1024,512]{1,0:T(8,128)S(1)}, u32[]{:S(2)}, u32[]{:S(2)}) %collective-permute-start) | collective-permute-done | bytes 2097184 | tf_op jit(solution)/shard_map/ppermute | solution.py:16
  96.0 0.0 copy-start.9
  96.0 0.0 copy-done.4
  96.0 0.0 copy-done.7
  96.0 1.3 copy-done.9
  97.3 0.0 copy-done.1
  97.3 12.0 %fusion.2 = f32[512,1536]{1,0:T(8,128)} fusion(f32[1024,512]{1,0:T(8,128)S(1)} %collective-permute-done.1, f32[1024,512]{1,0:T(8,128)S(1)} %subtract_divide_fusion.3, f32[1024,512]{1,0:T(8,128)S(1)} %collective-permute-done, f32[1024,512]{1,0:T(8,128)S(1)} %copy-done.1, f32[512]{0:T(512)S(1)} %get-tuple-element.22, f32[512]{0:T(512)S(1)} %get-tuple-element.21), kind=kOutput, calls=%fused_computation.3 | convolution fusion | flops 9668657152 | bytes 11538432 | tf_op jit(solution)/shard_map/rp,rq->pq/dot_general | solution.py:59
  109.3 0.0 all-reduce.4.cloned.1.call-update
  109.4 150.8 %all-reduce.4.cloned.1.call-done = f32[512,1536]{1,0:T(8,128)} async-done(((f32[512,1536]{1,0:T(8,128)}), f32[512,1536]{1,0:T(8,128)}) %all-reduce.4.cloned.1.call-update) | async-done | bytes 3145744 | tf_op jit(solution)/shard_map/psum | solution.py:64
  260.2 0.0 copy-start.8
  260.2 0.0 copy-start.10
  260.2 13.9 %fusion.3 = f32[1024,1536]{1,0:T(8,128)S(1)} fusion(f32[512,1536]{1,0:T(8,128)} %all-reduce.4.cloned.1.call-done, s32[512]{0:T(512)S(1)} %iota_add_fusion, f32[1024,512]{1,0:T(8,128)} %param.2, f32[512]{0:T(512)S(1)} %get-tuple-element.22, f32[512]{0:T(512)S(1)} %get-tuple-element.21), kind=kOutput, calls=%fused_computation.6 | convolution fusion | flops 9668657152 | bytes 11540480 | tf_op jit(solution)/shard_map/dot_general | solution.py:66
  274.1 0.0 copy-start.2
  274.1 0.0 copy-start.5
  274.1 0.0 copy-start.6
  274.1 0.4 fusion.26
  274.6 3.1 collective-permute-start.2
  277.7 0.0 collective-permute-start.3
  277.7 0.0 copy-done.8
  277.7 0.0 copy-done.10
  277.7 0.0 copy-done.2
  277.7 0.0 copy-done.5
  277.8 0.0 copy-done.6
  277.8 12.2 %fusion.22 = (f32[512]{0:T(512)S(1)}, f32[512]{0:T(512)S(1)}, f32[1024,512]{1,0:T(8,128)}) fusion(f32[512]{0:T(512)S(1)} %get-tuple-element.22, f32[1024,512]{1,0:T(8,128)S(1)} %copy-done.2, f32[512]{0:T(512)S(1)} %get-tuple-element.21, f32[512,1536]{1,0:T(8,128)S(1)} %copy-done.6, s32[512]{0:T(512)S(1)} %iota_add_fusion, f32[1024,512]{1,0:T(8,128)S(1)} %copy-done.8, ...), kind=kOutput, calls=%fused_computation.43 | convolution fusion | flops 9673374720 | bytes 13641728 | tf_op jit(solution)/shard_map/rq,pq->rp/dot_general | solution.py:69
  289.9 31.3 %collective-permute-done.2 = f32[1024,512]{1,0:T(8,128)S(1)} collective-permute-done((f32[1024,512]{1,0:T(8,128)S(1)}, f32[1024,512]{1,0:T(8,128)S(1)}, u32[]{:S(2)}, u32[]{:S(2)}) %collective-permute-start.2) | collective-permute-done | bytes 2097184 | tf_op jit(solution)/shard_map/ppermute | solution.py:27
  321.3 4.0 %collective-permute-done.3 = f32[1024,512]{1,0:T(8,128)S(1)} collective-permute-done((f32[1024,512]{1,0:T(8,128)S(1)}, f32[1024,512]{1,0:T(8,128)S(1)}, u32[]{:S(2)}, u32[]{:S(2)}) %collective-permute-start.3) | collective-permute-done | bytes 2097184 | tf_op jit(solution)/shard_map/ppermute | solution.py:27
  325.3 2.4 fusion.21
  327.7 35.5 %all-reduce = (f32[512]{0:T(512)S(1)}, f32[512]{0:T(512)S(1)}, f32[512]{0:T(512)S(1)}, f32[512]{0:T(512)S(1)}) all-reduce(f32[512]{0:T(512)S(1)} %get-tuple-element.5, f32[512]{0:T(512)S(1)} %get-tuple-element.4, f32[512]{0:T(512)S(1)} %get-tuple-element.3, f32[512]{0:T(512)S(1)} %get-tuple-element.2), channel_id=1, replica_groups=mesh['grp'=16,'row'=16] {'row'}, use_global_device_ids=true, to_apply=%region_12.13 | all-reduce | flops 2048 | bytes 16384 | tf_op jit(solution)/shard_map/psum | solution.py:73
  363.3 0.0 copy-start.3
  363.3 4.2 %subtract_divide_fusion.1 = f32[1024,512]{1,0:T(8,128)} fusion(f32[1024,512]{1,0:T(8,128)} %get-tuple-element.25, f32[512]{0:T(512)S(1)} %broadcast_multiply_fusion.2, f32[512]{0:T(512)S(1)} %broadcast_multiply_fusion.3, f32[512]{0:T(512)S(1)} %get-tuple-element.22, f32[1024,512]{1,0:T(8,128)} %param.2, f32[512]{0:T(512)S(1)} %get-tuple-element.21), kind=kLoop, calls=%fused_computation.11 | loop fusion | flops 3145728 | bytes 6299648 | tf_op jit(solution)/shard_map/div | solution.py:82
  367.5 0.0 copy-done.3
  367.5 1.9 subtract_divide_fusion
  (7 shorter events, 0.0 us)
Async XLA Ops:
  7.2 39.2 %copy-start = (f32[1024,512]{1,0:T(8,128)S(1)}, f32[1024,512]{1,0:T(8,128)}, u32[]{:S(2)}) copy-start(f32[1024,512]{1,0:T(8,128)} %param.3) | copy-start | bytes 6291460
  7.2 253.0 %all-reduce.4.cloned.1.call-start = ((), (), s32[]{:S(2)}) async-start(), calls=%async_computation | async-start | bytes 6291456 | tf_op jit(solution)/shard_map/psum | solution.py:64
  46.4 50.9 %copy-start.1 = (f32[1024,512]{1,0:T(8,128)S(1)}, f32[1024,512]{1,0:T(8,128)}, u32[]{:S(2)}) copy-start(f32[1024,512]{1,0:T(8,128)} %param.2) | copy-start | bytes 6291460
  46.7 49.3 %copy-start.4 = (f32[1024,512]{1,0:T(8,128)}, f32[1024,512]{1,0:T(8,128)S(1)}, u32[]{:S(2)}) copy-start(f32[1024,512]{1,0:T(8,128)S(1)} %subtract_divide_fusion.3) | copy-start | bytes 6291460
  46.7 45.2 %collective-permute-start.1 = (f32[1024,512]{1,0:T(8,128)S(1)}, f32[1024,512]{1,0:T(8,128)S(1)}, u32[]{:S(2)}, u32[]{:S(2)}) collective-permute-start(f32[1024,512]{1,0:T(8,128)S(1)} %subtract_divide_fusion.3), channel_id=1, source_target_pairs={{16,0},{32,16},{48,32},{64,48},{80,64},{96,80},{112,96},{128,112},... | collective-permute-start | bytes 6291464 | tf_op jit(solution)/shard_map/ppermute | solution.py:19
  51.6 44.3 %collective-permute-start = (f32[1024,512]{1,0:T(8,128)S(1)}, f32[1024,512]{1,0:T(8,128)S(1)}, u32[]{:S(2)}, u32[]{:S(2)}) collective-permute-start(f32[1024,512]{1,0:T(8,128)S(1)} %subtract_divide_fusion.3), channel_id=1, source_target_pairs={{0,16},{16,32},{32,48},{48,64},{64,80},{80,96},{96,112},{112,128},... | collective-permute-start | bytes 6291464 | tf_op jit(solution)/shard_map/ppermute | solution.py:16
  91.9 4.0 %copy-start.7 = (f32[1024,512]{1,0:T(8,128)}, f32[1024,512]{1,0:T(8,128)S(1)}, u32[]{:S(2)}) copy-start(f32[1024,512]{1,0:T(8,128)S(1)} %collective-permute-done.1) | copy-start | bytes 6291460
  96.0 1.3 copy-start.9
  260.2 17.6 %copy-start.8 = (f32[1024,512]{1,0:T(8,128)S(1)}, f32[1024,512]{1,0:T(8,128)}, u32[]{:S(2)}) copy-start(f32[1024,512]{1,0:T(8,128)} %copy-done.7) | copy-start | bytes 6291460
  260.2 17.6 %copy-start.10 = (f32[1024,512]{1,0:T(8,128)S(1)}, f32[1024,512]{1,0:T(8,128)}, u32[]{:S(2)}) copy-start(f32[1024,512]{1,0:T(8,128)} %copy-done.9) | copy-start | bytes 6291460
  274.1 3.6 copy-start.2
  274.1 3.6 copy-start.5
  274.1 3.6 copy-start.6
  274.6 46.7 %collective-permute-start.2 = (f32[1024,512]{1,0:T(8,128)S(1)}, f32[1024,512]{1,0:T(8,128)S(1)}, u32[]{:S(2)}, u32[]{:S(2)}) collective-permute-start(f32[1024,512]{1,0:T(8,128)S(1)} %get-tuple-element.19), channel_id=1, source_target_pairs={{16,0},{32,16},{48,32},{64,48},{80,64},{96,80},{112,96},{128,112},... | collective-permute-start | bytes 6291464 | tf_op jit(solution)/shard_map/ppermute | solution.py:27
  277.7 47.6 %collective-permute-start.3 = (f32[1024,512]{1,0:T(8,128)S(1)}, f32[1024,512]{1,0:T(8,128)S(1)}, u32[]{:S(2)}, u32[]{:S(2)}) collective-permute-start(f32[1024,512]{1,0:T(8,128)S(1)} %get-tuple-element.20), channel_id=1, source_target_pairs={{240,0},{0,16},{16,32},{32,48},{48,64},{64,80},{80,96},{96,112},{1... | collective-permute-start | bytes 6291464 | tf_op jit(solution)/shard_map/ppermute | solution.py:27
  363.3 4.2 %copy-start.3 = (f32[1024,512]{1,0:T(8,128)S(1)}, f32[1024,512]{1,0:T(8,128)}, u32[]{:S(2)}) copy-start(f32[1024,512]{1,0:T(8,128)} %get-tuple-element.18) | copy-start | bytes 6291460
Sparse Core Ops, SparseCore 0:
  109.5 150.6 all-reduce.3
where the time goes:
time: 377 us; the launch traced here: 376 us
  waiting for transfers between devices  230 us (61%)
  blocking collectives  71.7 us (19%)
  matrix products  38.1 us (10%)
  between operations  14.2 us (4%)
  other arithmetic  11.7 us (3%)
  starting transfers between devices  8.1 us (2%)
    psum x1, waiting for transfers between devices, per_device(): corr = lax.psum(partial_corr, 'row')  151 us
    ppermute x1, waiting for transfers between devices, with_halo(): lax.ppermute(lax.slice_in_dim(block, 0, width, axis=dim), axis, backward)  40.3 us
    psum x1, blocking collectives, per_device(): lax.psum((jnp.sum(view_a, axis=0), jnp.sum(view_a * view_a, axis=0), jnp....  36.2 us
    psum x1, blocking collectives, per_device(): lax.psum((jnp.sum(grad_own, axis=0), jnp.sum(grad_own * norm_a, axis=0),...  35.5 us
    ppermute x2, waiting for transfers between devices, shifted(): return lax.ppermute(block, axis, route)  35.4 us
    dot_general x1, matrix products, per_device(): jnp.dot(norm_a, penalty, precision=highest, preferred_element_type=jnp.fl...  13.9 us
    dot_general x1, matrix products, per_device(): jnp.einsum('rq,pq->rp', neighbours, penalty, precision=highest, preferred...  12.2 us
    dot_general x1, matrix products, per_device(): jnp.einsum('rp,rq->pq', norm_a, neighbours, precision=highest, preferred_...  12 us
  transfers between devices with their start and end apart: 5, of which 5 were waited for; matrix products, arithmetic and copies ran while one was open for 3% of the time, Pallas kernels for 0%

commit v1 on v0

v1 whole, which is shorter than its diff:
```python
import functools

import jax
import jax.numpy as jnp
from jax import lax
from jax.experimental import pallas as pl
from jax.experimental.pallas import tpu as pltpu
from jax.sharding import PartitionSpec as P

epsilon = 1e-05
off_weight = 0.0051
f32 = jnp.float32
bf16 = jnp.bfloat16


any_spec = pl.BlockSpec(memory_space=pl.ANY)
smem_spec = pl.BlockSpec(memory_space=pltpu.SMEM)
vmem_spec = pl.BlockSpec(memory_space=pltpu.VMEM)
params = pltpu.CompilerParams(vmem_limit_bytes=48 * 1024 * 1024)


def shape(*dims):
    return jax.ShapeDtypeStruct(dims, f32)


def across(block, shift):
    count = lax.axis_size("grp")
    return lax.ppermute(block, "grp", [(i, (i + shift) % count) for i in range(count)])


def to_core(block):
    return lax.ppermute(block, "row", [(i, i ^ 1) for i in range(16)])


def to_y(block):
    return lax.ppermute(block, "row", [(i, i ^ 8) for i in range(16)])


def to_x(block, shift):
    pairs = [(i, (i & 9) | ((((i >> 1) + shift) & 3) << 1)) for i in range(16)]
    return lax.ppermute(block, "row", pairs)


def split(value):
    high = value.astype(bf16)
    return high, (value - high.astype(f32)).astype(bf16)


def mm(a, b):
    return lax.dot_general(a, b, (((1,), (0,)), ((), ())), preferred_element_type=f32)


def gram(a, b):
    a_high, a_low = split(a.T)
    b_high, b_low = split(b)
    return mm(
        jnp.concatenate([a_high, a_high, a_low], axis=1),
        jnp.concatenate([b_high, b_low, b_high], axis=0),
    )


def thrice(value):
    high, low = split(value)
    return jnp.concatenate([high, high, low], axis=1)


def sums_kernel(a_ref, b_ref, out_ref):
    @pl.when(pl.program_id(0) == 0)
    def _():
        out_ref[...] = jnp.zeros_like(out_ref)

    a, b = a_ref[...], b_ref[...]
    for row, value in enumerate((a, a * a, b, b * b)):
        out_ref[row : row + 1, :] += jnp.sum(value, axis=0, keepdims=True)


def sums_of(a, b):
    rows, width = a.shape
    tile = rows // 4
    spec = pl.BlockSpec((tile, width), lambda i: (i, 0))
    return pl.pallas_call(
        sums_kernel,
        grid=(4,),
        in_specs=[spec, spec],
        out_specs=pl.BlockSpec((8, width), lambda i: (0, 0)),
        out_shape=shape(8, width),
        name="sums",
    )(a, b)


def put_slots(at_ref, acc, keep_ref, send_ref, first, rows):
    core, x = at_ref[0], at_ref[1]
    for slot in range(4):
        chunk = (x + slot) & 3
        mine = pl.multiple_of((core * 4 + chunk) * rows, rows)
        theirs = pl.multiple_of(((1 - core) * 4 + chunk) * rows, rows)
        keep_ref[slot, first : first + rows, :] = acc[pl.ds(mine, rows), :]
        send_ref[slot, first : first + rows, :] = acc[pl.ds(theirs, rows), :]


def own_corr_kernel(batch, steps, at_ref, a_ref, b_ref, *refs):
    parts, (top_ref, facts_ref, keep_ref, send_ref, acc_ref) = refs[:4], refs[4:]
    step = pl.program_id(0)

    @pl.when(step == 0)
    def _():
        total = parts[0][...] + parts[1][...] + parts[2][...] + parts[3][...]
        total = total / batch
        rows = []
        for first in (0, 2):
            mean, square = total[first : first + 1], total[first + 1 : first + 2]
            rows += [mean, 1.0 / jnp.sqrt(square - mean * mean + epsilon)]
        facts_ref[0:1, :] = rows[0]
        facts_ref[1:2, :] = rows[1]
        facts_ref[2:3, :] = rows[2]
        facts_ref[3:4, :] = rows[3]
        facts_ref[4:5, :] = (total[0:1] - rows[0]) * rows[1]
        facts_ref[5:6, :] = (total[2:3] - rows[2]) * rows[3]
        facts_ref[6:8, :] = jnp.zeros((2, total.shape[1]), f32)
        acc_ref[...] = jnp.zeros_like(acc_ref)

    norm_a = (a_ref[...] - facts_ref[0:1, :]) * facts_ref[1:2, :]
    norm_b = (b_ref[...] - facts_ref[2:3, :]) * facts_ref[3:4, :]
    top_ref[...] = norm_a
    acc_ref[...] += gram(norm_a, norm_b)

    @pl.when(step == steps - 1)
    def _():
        acc_ref[...] = acc_ref[...] / batch
        put_slots(at_ref, acc_ref, keep_ref, send_ref, 0, keep_ref.shape[1])


def own_corr(at, a, b, parts, batch):
    rows, width = a.shape
    steps = 4
    tile = rows // steps
    spec = pl.BlockSpec((tile, width), lambda i: (i, 0))
    whole = pl.BlockSpec((8, width), lambda i: (0, 0))
    slots = pl.BlockSpec((4, width // 8, width), lambda i: (0, 0, 0))
    return pl.pallas_call(
        functools.partial(own_corr_kernel, batch, steps),
        grid=(steps,),
        in_specs=[smem_spec, spec, spec] + [whole] * 4,
        out_specs=[spec, whole, slots, slots],
        out_shape=[shape(rows, width), shape(8, width)] + [shape(4, width // 8, width)] * 2,
        scratch_shapes=[pltpu.VMEM((width, width), f32)],
        compiler_params=params,
        name="own_corr",
    )(at, a, b, *parts)


def side_corr_kernel(batch, steps, at_ref, a_ref, prev_ref, next_ref, pf_ref, nf_ref, *refs):
    keep_ref, send_ref, left_ref, right_ref = refs[-4:]
    step = pl.program_id(0)

    @pl.when(step == 0)
    def _():
        left_ref[...] = jnp.zeros_like(left_ref)
        right_ref[...] = jnp.zeros_like(right_ref)

    norm_a = a_ref[...]
    for acc_ref, b_ref, facts_ref in ((left_ref, prev_ref, pf_ref), (right_ref, next_ref, nf_ref)):
        norm_b = (b_ref[...] - facts_ref[2:3, :]) * facts_ref[3:4, :]
        acc_ref[...] += gram(norm_a, norm_b)

    @pl.when(step == steps - 1)
    def _():
        rows = keep_ref.shape[1] // 2
        for side, acc_ref in enumerate((left_ref, right_ref)):
            acc_ref[...] = acc_ref[...] / batch
            put_slots(at_ref, acc_ref, keep_ref, send_ref, side * rows, rows)


def side_corr(at, norm_a, prev_b, next_b, prev_facts, next_facts, batch, wait_for):
    rows, width = norm_a.shape
    steps = 4
    spec = pl.BlockSpec((rows // steps, width), lambda i: (i, 0))
    whole = pl.BlockSpec((8, width), lambda i: (0, 0))
    slots = pl.BlockSpec((4, width // 4, width), lambda i: (0, 0, 0))
    return pl.pallas_call(
        functools.partial(side_corr_kernel, batch, steps),
        grid=(steps,),
        in_specs=[smem_spec, spec, spec, spec, whole, whole] + [any_spec] * len(wait_for),
        out_specs=[slots, slots],
        out_shape=[shape(4, width // 4, width)] * 2,
        scratch_shapes=[pltpu.VMEM((width, width), f32)] * 2,
        compiler_params=params,
        name="side_corr",
    )(at, norm_a, prev_b, next_b, prev_facts, next_facts, *wait_for)


def fan_kernel(keep_ref, got_ref, *refs):
    outs = refs[-4:]
    for slot in range(4):
        outs[slot][...] = keep_ref[slot] + got_ref[slot]


def fan(keep, got, wait_for=()):
    return pl.pallas_call(
        fan_kernel,
        in_specs=[vmem_spec, vmem_spec] + [any_spec] * len(wait_for),
        out_specs=[vmem_spec] * 4,
        out_shape=[shape(*keep.shape[1:])] * 4,
        compiler_params=params,
        name="fan",
    )(keep, got, *wait_for)


def total_kernel(count, *refs):
    out = refs[0][...]
    for ref in refs[1:count]:
        out = out + ref[...]
    refs[-2][...] = out


def total(parts, carried, wait_for=()):
    count = len(parts)
    return pl.pallas_call(
        functools.partial(total_kernel, count),
        in_specs=[vmem_spec] * count + [any_spec] * (1 + len(wait_for)),
        out_specs=[vmem_spec, any_spec],
        out_shape=[shape(*parts[0].shape), shape(*carried.shape)],
        input_output_aliases={count: 1},
        compiler_params=params,
        name="total",
    )(*parts, carried, *wait_for)


def halves_kernel(a_ref, b_ref, *refs):
    out = a_ref[...] + b_ref[...]
    rows = out.shape[0] // 2
    refs[-2][...] = out[:rows]
    refs[-1][...] = out[rows:]


def halves(mine, got, wait_for=()):
    rows, width = mine.shape
    return pl.pallas_call(
        halves_kernel,
        in_specs=[vmem_spec] * 2 + [any_spec] * len(wait_for),
        out_specs=[vmem_spec] * 2,
        out_shape=[shape(rows // 2, width)] * 2,
        compiler_params=params,
        name="halves",
    )(mine, got, *wait_for)


def pack_kernel(*refs):
    out_ref = refs[4 if len(refs) == 5 else 5]
    for i in range(4):
        out_ref[i] = refs[i][...]


def pack(parts, carried=None):
    rows, width = parts[0].shape
    more = [] if carried is None else [carried]
    out = pl.pallas_call(
        pack_kernel,
        in_specs=[vmem_spec] * 4 + [any_spec] * len(more),
        out_specs=[vmem_spec] + [any_spec] * len(more),
        out_shape=[shape(4, rows, width)] + [shape(*c.shape) for c in more],
        input_output_aliases={4: 1} if more else {},
        compiler_params=params,
        name="pack",
    )(*parts, *more)
    return out[0] if carried is None else out


def row_of(at_ref, core_flip, slot, rows):
    core, x = at_ref[0], at_ref[1]
    core = 1 - core if core_flip else core
    return pl.multiple_of((core * 4 + ((x - slot) & 3)) * rows, rows)


def own_grad_kernel(at_ref, mine_ref, other_ref, a_ref, b_ref, facts_ref, *refs):
    ga_ref, gb_ref, sums_ref, corr_ref, pt_ref, p_ref = refs[-6:]
    width = corr_ref.shape[0]

    @pl.when(pl.program_id(0) == 0)
    def _():
        rows = mine_ref.shape[1]
        for flip, ref in ((False, mine_ref), (True, other_ref)):
            for slot in range(4):
                corr_ref[pl.ds(row_of(at_ref, flip, slot, rows), rows), :] = ref[slot]
        corr = corr_ref[...]
        row_index = lax.broadcasted_iota(jnp.int32, corr.shape, 0)
        column = lax.broadcasted_iota(jnp.int32, corr.shape, 1)
        pen = jnp.where(row_index == column, -2.0 * (1.0 - corr), 2.0 * off_weight * corr)
        cross = pen * corr
        pen_t = pen.T
        high, low = split(pen)
        p_ref[0:width, :] = high
        p_ref[width : 2 * width, :] = low
        p_ref[2 * width :, :] = high
        high, low = split(pen_t)
        pt_ref[0:width, :] = high
        pt_ref[width : 2 * width, :] = low
        pt_ref[2 * width :, :] = high
        left = thrice(facts_ref[...])
        sums_ref[0:1, :] = mm(left, pt_ref[...])[5:6]
        sums_ref[1:2, :] = jnp.sum(cross.T, axis=0, keepdims=True)
        sums_ref[2:3, :] = mm(left, p_ref[...])[4:5]
        sums_ref[3:4, :] = jnp.sum(cross, axis=0, keepdims=True)
        sums_ref[4:8, :] = jnp.zeros((4, width), f32)

    norm_b = (b_ref[...] - facts_ref[2:3, :]) * facts_ref[3:4, :]
    ga_ref[...] = mm(thrice(norm_b), pt_ref[...])
    gb_ref[...] = mm(thrice(a_ref[...]), p_ref[...])


def own_grad(at, mine, other, norm_a, b, facts, wait_for=()):
    rows, width = b.shape
    steps = 4
    spec = pl.BlockSpec((rows // steps, width), lambda i: (i, 0))
    whole = pl.BlockSpec((8, width), lambda i: (0, 0))
    slots = pl.BlockSpec(mine.shape, lambda i: (0, 0, 0))
    return pl.pallas_call(
        own_grad_kernel,
        grid=(steps,),
        in_specs=[smem_spec, slots, slots, spec, spec, whole] + [any_spec] * len(wait_for),
        out_specs=[spec, spec, whole],
        out_shape=[shape(rows, width)] * 2 + [shape(8, width)],
        scratch_shapes=[
            pltpu.VMEM((width, width), f32),
            pltpu.VMEM((3 * width, width), bf16),
            pltpu.VMEM((3 * width, width), bf16),
        ],
        compiler_params=params,
        name="own_grad",
    )(at, mine, other, norm_a, b, facts, *wait_for)


def finish_kernel(at_ref, *refs):
    packs, refs = refs[:8], refs[8:]
    facts_ref, pf_ref, nf_ref, sums_ref = refs[:4]
    ga_ref, gb_ref, na_ref, b_ref, pb_ref, nb_ref, pa_ref, xa_ref = refs[4:12]
    out_a_ref, out_b_ref, corr_ref, pt_ref, p_ref, vec_ref = refs[12:]
    width = corr_ref.shape[1]

    @pl.when(pl.program_id(0) == 0)
    def _():
        rows = packs[0].shape[1]
        for flip in (0, 1):
            for slot in range(4):
                at = row_of(at_ref, flip == 1, slot, rows)
                for kind in range(4):
                    corr_ref[kind, pl.ds(at, rows), :] = packs[4 * flip + slot][kind]
        vec = sums_ref[0:4, :]
        cross_a = vec[1:2]
        cross_b = vec[3:4]
        for kind in range(4):
            corr = corr_ref[kind]
            corr = corr.T if kind < 2 else corr
            pen = 2.0 * off_weight * corr
            cross = jnp.sum(pen * corr, axis=0, keepdims=True)
            into = pt_ref if kind < 2 else p_ref
            first = (kind % 2) * 3 * width
            high, low = split(pen)
            into[first : first + width, :] = high
            into[first + width : first + 2 * width, :] = low
            into[first + 2 * width : first + 3 * width, :] = high
            if kind < 2:
                cross_a = cross_a + cross
            else:
                cross_b = cross_b + cross
        left = jnp.concatenate([thrice(pf_ref[...]), thrice(nf_ref[...])], axis=1)
        vec_ref[0:1, :] = vec[0:1] + mm(left, pt_ref[...])[5:6]
        vec_ref[1:2, :] = cross_a
        vec_ref[2:3, :] = vec[2:3] + mm(left, p_ref[...])[4:5]
        vec_ref[3:4, :] = cross_b

    prev_b = (pb_ref[...] - pf_ref[2:3, :]) * pf_ref[3:4, :]
    next_b = (nb_ref[...] - nf_ref[2:3, :]) * nf_ref[3:4, :]
    ga = ga_ref[...] + mm(jnp.concatenate([thrice(prev_b), thrice(next_b)], axis=1), pt_ref[...])
    out_a_ref[...] = (ga - vec_ref[0:1, :] - na_ref[...] * vec_ref[1:2, :]) * facts_ref[1:2, :]
    both = jnp.concatenate([thrice(pa_ref[...]), thrice(xa_ref[...])], axis=1)
    gb = gb_ref[...] + mm(both, p_ref[...])
    norm_b = (b_ref[...] - facts_ref[2:3, :]) * facts_ref[3:4, :]
    out_b_ref[...] = (gb - vec_ref[2:3, :] - norm_b * vec_ref[3:4, :]) * facts_ref[3:4, :]


def finish(at, packs, facts, prev_facts, next_facts, sums, tiles):
    rows, width = tiles[0].shape
    steps = 4
    spec = pl.BlockSpec((rows // steps, width), lambda i: (i, 0))
    whole = pl.BlockSpec((8, width), lambda i: (0, 0))
    slots = pl.BlockSpec(packs[0].shape, lambda i: (0, 0, 0))
    return pl.pallas_call(
        finish_kernel,
        grid=(steps,),
        in_specs=[smem_spec] + [slots] * 8 + [whole] * 4 + [spec] * 8,
        out_specs=[spec, spec],
        out_shape=[shape(rows, width)] * 2,
        scratch_shapes=[
            pltpu.VMEM((4, width, width), f32),
            pltpu.VMEM((6 * width, width), bf16),
            pltpu.VMEM((6 * width, width), bf16),
            pltpu.VMEM((8, width), f32),
        ],
        compiler_params=params,
        name="finish",
    )(at, *packs, facts, prev_facts, next_facts, sums, *tiles)


def per_device(view_a, view_b):
    local_rows, width = view_a.shape
    batch = local_rows * lax.axis_size("row")
    index = lax.axis_index("row")
    at = jnp.stack([index & 1, (index >> 1) & 3])
    half = local_rows // 2

    sums = sums_of(view_a, view_b)
    sums = sums + to_y(sums)
    prev_raw = across(view_b, 1)
    next_raw = across(view_b, -1)
    sums = sums + to_core(sums)
    parts = [sums] + [to_x(sums, shift) for shift in (1, 2, 3)]

    norm_a, facts, keep, send = own_corr(at, view_a, view_b, parts, batch)
    prev_facts = across(facts, 1)
    next_facts = across(facts, -1)
    slots = fan(keep, to_core(send))
    got = [slots[0]] + [to_x(slots[shift], shift) for shift in (1, 2, 3)]
    own_chunk, norm_a = total(got, norm_a)
    prev_a = across(norm_a, 1)
    next_a = across(norm_a, -1)
    own_chunk = own_chunk + to_y(own_chunk)
    own_slots = [own_chunk] + [to_x(own_chunk, shift) for shift in (1, 2, 3)]

    keep, send = side_corr(
        at, norm_a, prev_raw, next_raw, prev_facts, next_facts, batch, [own_chunk]
    )
    own_mine = pack(own_slots)
    slots = fan(keep, to_core(send), [own_mine])
    own_other = to_core(own_mine)
    got = [slots[0]] + [to_x(slots[shift], shift) for shift in (1, 2, 3)]
    side_chunk, own_other = total(got, own_other)
    back = to_y(side_chunk)
    part_a, part_b, own_sums = own_grad(at, own_mine, own_other, norm_a, view_b, facts)
    left, right = halves(side_chunk, back, [own_sums])
    from_next = across(left, -1)
    from_prev = across(right, 1)
    packed = pack([left, right, from_prev, from_next])
    mine = [packed] + [to_x(packed, shift) for shift in (1, 2, 3)]
    other = [to_core(block) for block in mine]
    tiles = [part_a, part_b, norm_a, view_b, prev_raw, next_raw, prev_a, next_a]
    return tuple(
        finish(at, mine + other, facts, prev_facts, next_facts, own_sums, tiles)
    )


def solution(mesh):
    placed = (P("row", "grp"), P("row", "grp"))
    return jax.shard_map(
        per_device,
        mesh=mesh,
        in_specs=placed,
        out_specs=(P("row", "grp"), P("row", "grp")),
        check_vma=False,
    )
```

time: 377 us -> 221 us (0.59)
  waiting for transfers between devices: 230 us -> 134 us
  blocking collectives: 71.7 us -> 0 us
  starting transfers between devices: 8.1 us -> 47.3 us
  matrix products: 38.1 us -> 0 us
  Pallas kernels: 0 us -> 34.1 us
  between operations: 14.2 us -> 0.9 us
  other arithmetic: 11.7 us -> 0.82 us
    psum x1 -> x0, waiting for transfers between devices: 151 us -> none  [per_device(): corr = lax.psum(partial_corr, 'row')]
    psum x2 -> x0, blocking collectives: 71.7 us -> none  [the longest x1 36.2 us: per_device(): lax.psum((jnp.sum(view_a, axis=0), jnp.sum(view_a * view_a, axis=0), jnp....]
    ppermute x4 -> x34, waiting for transfers between devices: 79.7 us -> 134 us  [the longest x3 78.5 us: to_y(): return lax.ppermute(block, 'row', [(i, i ^ 8) for i in range(16)])]
    ppermute x4 -> x34, starting transfers between devices: 8.06 us -> 47.3 us  [the longest x8 15.5 us: to_core(): return lax.ppermute(block, 'row', [(i, i ^ 1) for i in range(16)])]
    dot_general x3 -> x0, matrix products: 38.1 us -> none  [the longest x1 13.9 us: per_device(): jnp.dot(norm_a, penalty, precision=highest, preferred_element_type=jnp.fl...]
    pallas_call x0 -> x12, Pallas kernels: none -> 34.1 us  [the longest x1 13.3 us: finish(): pl.pallas_call(finish_kernel, grid=(steps,), in_specs=[smem_spec] + [slot...]
    div x9 -> x0, other arithmetic: 6.41 us -> none  [the longest x1 4.23 us: per_device(): (grad_own - sums_back[0] / batch_rows - norm_a * (sums_back[1] / batch_ro...]
    reduce_sum x2 -> x0, other arithmetic: 5.33 us -> none  [the longest x1 2.93 us: per_device(): jnp.sum(view_a, axis=0)]
  transfers between devices with their start and end apart: 5 -> 34, of which waited for: 5 -> 20; matrix products, arithmetic and copies ran while one was open for 3% -> 0% of each run, Pallas kernels for 0% -> 7%
where the time goes in v1:
time: 221 us; the launch traced here: 220 us
  waiting for transfers between devices  134 us (61%)
  starting transfers between devices  47.3 us (21%)
  Pallas kernels  34.1 us (15%)
  local copies, waits for them, and re-layouts  2.73 us (1%)
    ppermute x3, waiting for transfers between devices, to_y(): return lax.ppermute(block, 'row', [(i, i ^ 8) for i in range(16)])  78.5 us
    ppermute x15, waiting for transfers between devices, to_x(): return lax.ppermute(block, 'row', pairs)  46.7 us
    ppermute x8, starting transfers between devices, to_core(): return lax.ppermute(block, 'row', [(i, i ^ 1) for i in range(16)])  15.5 us
    ppermute x15, starting transfers between devices, to_x(): return lax.ppermute(block, 'row', pairs)  14.5 us
    pallas_call x1, Pallas kernels, finish(): pl.pallas_call(finish_kernel, grid=(steps,), in_specs=[smem_spec] + [slot...  13.3 us
    ppermute x8, starting transfers between devices, across(): lax.ppermute(block, 'grp', [(i, (i + shift) % count) for i in range(count)])  12 us
    pallas_call x1, Pallas kernels, own_grad(): pl.pallas_call(own_grad_kernel, grid=(steps,), in_specs=[smem_spec, slots...  6.39 us
    pallas_call x1, Pallas kernels, side_corr(): pl.pallas_call(functools.partial(side_corr_kernel, batch, steps), grid=(s...  6.07 us
  transfers between devices with their start and end apart: 34, of which 20 were waited for; matrix products, arithmetic and copies ran while one was open for 0% of the time, Pallas kernels for 7%

profile of v1, /device:TPU:1, one launch (start us, length us, event | category | flops | bytes accessed | tf_op | source)
XLA Modules:
  0.0 220.2 jit_solution(768230960802220435)
XLA Ops:
  0.6 7.5 %collective-permute-start.10 = (f32[1024,512]{1,0:T(8,128)}, f32[1024,512]{1,0:T(8,128)}, u32[]{:S(2)}, u32[]{:S(2)}) collective-permute-start(f32[1024,512]{1,0:T(8,128)} %refs_15_.1), channel_id=1, source_target_pairs={{0,240},{16,0},{32,16},{48,32},{64,48},{80,64},{96,80},{112,96},{1... | collective-permute-start | bytes 6291464 | tf_op jit(solution)/shard_map/ppermute | solution.py:28
  8.1 3.7 %sums.1 = f32[8,512]{1,0:T(8,128)} custom-call(f32[1024,512]{1,0:T(8,128)} %a_ref.3, f32[1024,512]{1,0:T(8,128)} %refs_15_.1), custom_call_target="tpu_custom_call" | custom-call | tf_op jit(solution)/shard_map/sums/pallas_call | solution.py:81
  11.8 2.6 %collective-permute-start = (f32[8,512]{1,0:T(8,128)}, f32[8,512]{1,0:T(8,128)S(1)}, u32[]{:S(2)}, u32[]{:S(2)}) collective-permute-start(f32[8,512]{1,0:T(8,128)} %sums.1), channel_id=1, source_target_pairs={{0,8},{1,9},{2,10},{3,11},{4,12},{5,13},{6,14},{7,15},{8,0},{9,1},... | collective-permute-start | bytes 49160 | tf_op jit(solution)/shard_map/ppermute | solution.py:36
  14.4 45.5 %collective-permute-done = f32[8,512]{1,0:T(8,128)S(1)} collective-permute-done((f32[8,512]{1,0:T(8,128)}, f32[8,512]{1,0:T(8,128)S(1)}, u32[]{:S(2)}, u32[]{:S(2)}) %collective-permute-start) | collective-permute-done | bytes 16416 | tf_op jit(solution)/shard_map/ppermute | solution.py:36
  60.0 0.7 add.9
  61.2 0.8 collective-permute-done.1
  62.0 2.5 %collective-permute-start.4 = (f32[8,512]{1,0:T(8,128)S(1)}, f32[8,512]{1,0:T(8,128)S(1)}, u32[]{:S(2)}, u32[]{:S(2)}) collective-permute-start(f32[8,512]{1,0:T(8,128)S(1)} %add.10.refs_0_), channel_id=1, source_target_pairs={{0,6},{1,7},{2,0},{3,1},{4,2},{5,3},{6,4},{7,5},{8,14},{9,15},{10,... | collective-permute-start | bytes 49160 | tf_op jit(solution)/shard_map/ppermute | solution.py:41
  65.0 0.6 collective-permute-start.2
  65.7 2.9 %collective-permute-done.3.refs_2_ = f32[8,512]{1,0:T(8,128)S(1)} collective-permute-done((f32[8,512]{1,0:T(8,128)S(1)}, f32[8,512]{1,0:T(8,128)S(1)}, u32[]{:S(2)}, u32[]{:S(2)}) %collective-permute-start.3) | collective-permute-done | bytes 16416 | tf_op jit(solution)/shard_map/ppermute | solution.py:41
  68.8 4.3 %own_corr.1 = (f32[1024,512]{1,0:T(8,128)S(1)}, f32[8,512]{1,0:T(8,128)S(1)}, f32[4,64,512]{2,1,0:T(8,128)S(1)}, f32[4,64,512]{2,1,0:T(8,128)S(1)}) custom-call(s32[2]{0:T(128)S(1)} %pad_add_fusion.at_ref, f32[1024,512]{1,0:T(8,128)S(1)} %copy-done.1, f32[1024,512]{1,0:T(8,128)} %refs_15_.1, f32[8,512]{1,0:T(8,128)S(1)} %add.10.refs_0_, ...), custom_call_target="tpu_custom_call" | custom-call | tf_op jit(solution)/shard_map/own_corr/pallas_call | solution.py:140
  73.2 2.1 collective-permute-start.5
  75.3 1.5 collective-permute-done.5.got_ref
  77.0 1.3 collective-permute-start.7
  78.3 2.0 collective-permute-start.8
  80.3 5.5 %collective-permute-done.6.refs_1_ = f32[64,512]{1,0:T(8,128)S(1)} collective-permute-done((f32[64,512]{1,0:T(8,128)S(1)}, f32[64,512]{1,0:T(8,128)S(1)}, u32[]{:S(2)}, u32[]{:S(2)}) %collective-permute-start.6) | collective-permute-done | bytes 131104 | tf_op jit(solution)/shard_map/ppermute | solution.py:41
  86.2 1.5 collective-permute-start.11
  87.7 3.8 %collective-permute-done.13 = f32[64,512]{1,0:T(8,128)S(1)} collective-permute-done((f32[64,512]{1,0:T(8,128)S(1)}, f32[64,512]{1,0:T(8,128)S(1)}, u32[]{:S(2)}, u32[]{:S(2)}) %collective-permute-start.13) | collective-permute-done | bytes 131104 | tf_op jit(solution)/shard_map/ppermute | solution.py:36
  91.5 6.1 %side_corr.1 = (f32[4,128,512]{2,1,0:T(8,128)S(1)}, f32[4,128,512]{2,1,0:T(8,128)S(1)}) custom-call(s32[2]{0:T(128)S(1)} %pad_add_fusion.at_ref, f32[1024,512]{1,0:T(8,128)S(1)} %get-tuple-element.32.a_ref.refs_14_, f32[1024,512]{1,0:T(8,128)} %collective-permute-done.9.prev_ref.refs_16_, f32[1024,512]{1,0:T(8,128)} %collective-permute-done.10.next_ref.refs_17_, ...), custom_call_target="tpu_custom_call" | custom-call | tf_op jit(solution)/shard_map/side_corr/pallas_call | solution.py:180
  97.6 3.1 %collective-permute-start.14 = (f32[4,128,512]{2,1,0:T(8,128)S(1)}, f32[4,128,512]{2,1,0:T(8,128)S(1)}, u32[]{:S(2)}, u32[]{:S(2)}) collective-permute-start(f32[4,128,512]{2,1,0:T(8,128)S(1)} %get-tuple-element.36), channel_id=1, source_target_pairs={{0,1},{1,0},{2,3},{3,2},{4,5},{5,4},{6,7},{7,6},{8,9},{9,8},{10,11... | collective-permute-start | bytes 3145736 | tf_op jit(solution)/shard_map/ppermute | solution.py:32
  100.7 2.7 %collective-permute-start.17 = (f32[64,512]{1,0:T(8,128)S(1)}, f32[64,512]{1,0:T(8,128)S(1)}, u32[]{:S(2)}, u32[]{:S(2)}) collective-permute-start(f32[64,512]{1,0:T(8,128)S(1)} %add.11.refs_0_), channel_id=1, source_target_pairs={{0,6},{1,7},{2,0},{3,1},{4,2},{5,3},{6,4},{7,5},{8,14},{9,15},{10,... | collective-permute-start | bytes 393224 | tf_op jit(solution)/shard_map/ppermute | solution.py:41
  103.4 0.6 collective-permute-start.15
  103.9 4.8 %collective-permute-done.17.refs_3_ = f32[64,512]{1,0:T(8,128)S(1)} collective-permute-done((f32[64,512]{1,0:T(8,128)S(1)}, f32[64,512]{1,0:T(8,128)S(1)}, u32[]{:S(2)}, u32[]{:S(2)}) %collective-permute-start.17) | collective-permute-done | bytes 131104 | tf_op jit(solution)/shard_map/ppermute | solution.py:41
  108.8 0.8 collective-permute-done.16.refs_2_
  109.5 3.0 %collective-permute-done.15.refs_1_ = f32[64,512]{1,0:T(8,128)S(1)} collective-permute-done((f32[64,512]{1,0:T(8,128)S(1)}, f32[64,512]{1,0:T(8,128)S(1)}, u32[]{:S(2)}, u32[]{:S(2)}) %collective-permute-start.15) | collective-permute-done | bytes 131104 | tf_op jit(solution)/shard_map/ppermute | solution.py:41
  112.5 0.9 collective-permute-start.21
  113.4 1.5 collective-permute-start.32
  115.1 1.8 collective-permute-start.19
  116.9 0.9 collective-permute-start.20
  117.8 6.9 %collective-permute-done.18.refs_1_ = f32[128,512]{1,0:T(8,128)S(1)} collective-permute-done((f32[128,512]{1,0:T(8,128)S(1)}, f32[128,512]{1,0:T(8,128)S(1)}, u32[]{:S(2)}, u32[]{:S(2)}) %collective-permute-start.18) | collective-permute-done | bytes 262176 | tf_op jit(solution)/shard_map/ppermute | solution.py:41
  124.7 4.0 %collective-permute-done.19.refs_2_ = f32[128,512]{1,0:T(8,128)S(1)} collective-permute-done((f32[128,512]{1,0:T(8,128)S(1)}, f32[128,512]{1,0:T(8,128)S(1)}, u32[]{:S(2)}, u32[]{:S(2)}) %collective-permute-start.19) | collective-permute-done | bytes 262176 | tf_op jit(solution)/shard_map/ppermute | solution.py:41
  128.6 1.2 collective-permute-done.20.refs_3_
  129.9 2.5 %collective-permute-start.22 = (f32[128,512]{1,0:T(8,128)S(1)}, f32[128,512]{1,0:T(8,128)S(1)}, u32[]{:S(2)}, u32[]{:S(2)}) collective-permute-start(f32[128,512]{1,0:T(8,128)S(1)} %get-tuple-element.41.a_ref), channel_id=1, source_target_pairs={{0,8},{1,9},{2,10},{3,11},{4,12},{5,13},{6,14},{7,15},{8,0},{9,1},... | collective-permute-start | bytes 786440 | tf_op jit(solution)/shard_map/ppermute | solution.py:36
  132.4 6.4 %own_grad.1 = (f32[1024,512]{1,0:T(8,128)S(1)}, f32[1024,512]{1,0:T(8,128)S(1)}, f32[8,512]{1,0:T(8,128)S(1)}) custom-call(s32[2]{0:T(128)S(1)} %pad_add_fusion.at_ref, f32[4,64,512]{2,1,0:T(8,128)S(1)} %pack.2.refs_0_.mine_ref, f32[4,64,512]{2,1,0:T(8,128)S(1)} %get-tuple-element.42.other_ref, f32[1024,512]{1,0:T(8,128)} %copy-done, f32[1024,512]{1,0:T(8,128)} %refs_15_.1, ...), custom_call_target="tpu_custom_call" | custom-call | tf_op jit(solution)/shard_map/own_grad/pallas_call | solution.py:317
  138.8 1.4 copy-done.2
  140.2 1.3 copy-done.3
  141.5 29.2 %collective-permute-done.22.b_ref = f32[128,512]{1,0:T(8,128)S(1)} collective-permute-done((f32[128,512]{1,0:T(8,128)S(1)}, f32[128,512]{1,0:T(8,128)S(1)}, u32[]{:S(2)}, u32[]{:S(2)}) %collective-permute-start.22) | collective-permute-done | bytes 262176 | tf_op jit(solution)/shard_map/ppermute | solution.py:36
  170.8 1.5 collective-permute-start.23
  172.3 3.1 %collective-permute-done.24.refs_3_ = f32[64,512]{1,0:T(8,128)S(1)} collective-permute-done((f32[64,512]{1,0:T(8,128)S(1)}, f32[64,512]{1,0:T(8,128)S(1)}, u32[]{:S(2)}, u32[]{:S(2)}) %collective-permute-start.24) | collective-permute-done | bytes 131104 | tf_op jit(solution)/shard_map/ppermute | solution.py:28
  175.4 2.2 collective-permute-done.23.refs_2_
  177.6 0.7 collective-permute-start.27
  178.3 0.9 collective-permute-start.25
  179.2 1.9 collective-permute-start.28
  181.1 8.7 %collective-permute-done.27.refs_3_ = f32[4,64,512]{2,1,0:T(8,128)S(1)} collective-permute-done((f32[4,64,512]{2,1,0:T(8,128)S(1)}, f32[4,64,512]{2,1,0:T(8,128)S(1)}, u32[]{:S(2)}, u32[]{:S(2)}) %collective-permute-start.27) | collective-permute-done | bytes 524320 | tf_op jit(solution)/shard_map/ppermute | solution.py:41
  189.8 4.1 %collective-permute-start.31 = (f32[4,64,512]{2,1,0:T(8,128)S(1)}, f32[4,64,512]{2,1,0:T(8,128)S(1)}, u32[]{:S(2)}, u32[]{:S(2)}) collective-permute-start(f32[4,64,512]{2,1,0:T(8,128)S(1)} %collective-permute-done.27.refs_3_), channel_id=1, source_target_pairs={{0,1},{1,0},{2,3},{3,2},{4,5},{5,4},{6,7},{7,6},{8,9},{9,8},{10,11... | collective-permute-start | bytes 1572872 | tf_op jit(solution)/shard_map/ppermute | solution.py:32
  193.9 2.4 %collective-permute-start.30 = (f32[4,64,512]{2,1,0:T(8,128)S(1)}, f32[4,64,512]{2,1,0:T(8,128)S(1)}, u32[]{:S(2)}, u32[]{:S(2)}) collective-permute-start(f32[4,64,512]{2,1,0:T(8,128)S(1)} %collective-permute-done.26.refs_2_), channel_id=1, source_target_pairs={{0,1},{1,0},{2,3},{3,2},{4,5},{5,4},{6,7},{7,6},{8,9},{9,8},{10,11... | collective-permute-start | bytes 1572872 | tf_op jit(solution)/shard_map/ppermute | solution.py:32
  196.3 8.6 %collective-permute-done.25.refs_1_ = f32[4,64,512]{2,1,0:T(8,128)S(1)} collective-permute-done((f32[4,64,512]{2,1,0:T(8,128)S(1)}, f32[4,64,512]{2,1,0:T(8,128)S(1)}, u32[]{:S(2)}, u32[]{:S(2)}) %collective-permute-start.25) | collective-permute-done | bytes 524320 | tf_op jit(solution)/shard_map/ppermute | solution.py:41
  205.4 1.5 collective-permute-done.29.refs_5_
  206.9 13.3 %finish.1 = (f32[1024,512]{1,0:T(8,128)}, f32[1024,512]{1,0:T(8,128)}) custom-call(s32[2]{0:T(128)S(1)} %pad_add_fusion.at_ref, f32[4,64,512]{2,1,0:T(8,128)S(1)} %pack.3.refs_0_, f32[4,64,512]{2,1,0:T(8,128)S(1)} %collective-permute-done.25.refs_1_, f32[4,64,512]{2,1,0:T(8,128)S(1)} %collective-permute-done.26.refs_2_, ...), custom_call_target="tpu_custom_call" | custom-call | tf_op jit(solution)/shard_map/finish/pallas_call | solution.py:388
  (48 shorter events, 2.8 us)
Async XLA Ops:
  0.6 68.2 %copy-start.1 = (f32[1024,512]{1,0:T(8,128)S(1)}, f32[1024,512]{1,0:T(8,128)}, u32[]{:S(2)}) copy-start(f32[1024,512]{1,0:T(8,128)} %a_ref.3) | copy-start | bytes 6291460
  0.6 90.9 %collective-permute-start.10 = (f32[1024,512]{1,0:T(8,128)}, f32[1024,512]{1,0:T(8,128)}, u32[]{:S(2)}, u32[]{:S(2)}) collective-permute-start(f32[1024,512]{1,0:T(8,128)} %refs_15_.1), channel_id=1, source_target_pairs={{0,240},{16,0},{32,16},{48,32},{64,48},{80,64},{96,80},{112,96},{1... | collective-permute-start | bytes 6291464 | tf_op jit(solution)/shard_map/ppermute | solution.py:28
  8.1 83.4 %collective-permute-start.9 = (f32[1024,512]{1,0:T(8,128)}, f32[1024,512]{1,0:T(8,128)}, u32[]{:S(2)}, u32[]{:S(2)}) collective-permute-start(f32[1024,512]{1,0:T(8,128)} %refs_15_.1), channel_id=1, source_target_pairs={{0,16},{16,32},{32,48},{48,64},{64,80},{80,96},{96,112},{112,128},... | collective-permute-start | bytes 6291464 | tf_op jit(solution)/shard_map/ppermute | solution.py:28
  11.8 48.2 %collective-permute-start = (f32[8,512]{1,0:T(8,128)}, f32[8,512]{1,0:T(8,128)S(1)}, u32[]{:S(2)}, u32[]{:S(2)}) collective-permute-start(f32[8,512]{1,0:T(8,128)} %sums.1), channel_id=1, source_target_pairs={{0,8},{1,9},{2,10},{3,11},{4,12},{5,13},{6,14},{7,15},{8,0},{9,1},... | collective-permute-start | bytes 49160 | tf_op jit(solution)/shard_map/ppermute | solution.py:36
  60.7 1.3 collective-permute-start.1
  62.0 3.7 %collective-permute-start.4 = (f32[8,512]{1,0:T(8,128)S(1)}, f32[8,512]{1,0:T(8,128)S(1)}, u32[]{:S(2)}, u32[]{:S(2)}) collective-permute-start(f32[8,512]{1,0:T(8,128)S(1)} %add.10.refs_0_), channel_id=1, source_target_pairs={{0,6},{1,7},{2,0},{3,1},{4,2},{5,3},{6,4},{7,5},{8,14},{9,15},{10,... | collective-permute-start | bytes 49160 | tf_op jit(solution)/shard_map/ppermute | solution.py:41
  64.5 4.1 %collective-permute-start.3 = (f32[8,512]{1,0:T(8,128)S(1)}, f32[8,512]{1,0:T(8,128)S(1)}, u32[]{:S(2)}, u32[]{:S(2)}) collective-permute-start(f32[8,512]{1,0:T(8,128)S(1)} %add.10.refs_0_), channel_id=1, source_target_pairs={{0,4},{1,5},{2,6},{3,7},{4,0},{5,1},{6,2},{7,3},{8,12},{9,13},{10,... | collective-permute-start | bytes 49160 | tf_op jit(solution)/shard_map/ppermute | solution.py:41
  65.0 3.8 %collective-permute-start.2 = (f32[8,512]{1,0:T(8,128)S(1)}, f32[8,512]{1,0:T(8,128)S(1)}, u32[]{:S(2)}, u32[]{:S(2)}) collective-permute-start(f32[8,512]{1,0:T(8,128)S(1)} %add.10.refs_0_), channel_id=1, source_target_pairs={{0,2},{1,3},{2,4},{3,5},{4,6},{5,7},{6,0},{7,1},{8,10},{9,11},{10,... | collective-permute-start | bytes 49160 | tf_op jit(solution)/shard_map/ppermute | solution.py:41
  73.2 3.7 %collective-permute-start.5 = (f32[4,64,512]{2,1,0:T(8,128)S(1)}, f32[4,64,512]{2,1,0:T(8,128)S(1)}, u32[]{:S(2)}, u32[]{:S(2)}) collective-permute-start(f32[4,64,512]{2,1,0:T(8,128)S(1)} %get-tuple-element.26), channel_id=1, source_target_pairs={{0,1},{1,0},{2,3},{3,2},{4,5},{5,4},{6,7},{7,6},{8,9},{9,8},{10,11... | collective-permute-start | bytes 1572872 | tf_op jit(solution)/shard_map/ppermute | solution.py:32
  76.9 8.9 %collective-permute-start.6 = (f32[64,512]{1,0:T(8,128)S(1)}, f32[64,512]{1,0:T(8,128)S(1)}, u32[]{:S(2)}, u32[]{:S(2)}) collective-permute-start(f32[64,512]{1,0:T(8,128)S(1)} %get-tuple-element.28), channel_id=1, source_target_pairs={{0,2},{1,3},{2,4},{3,5},{4,6},{5,7},{6,0},{7,1},{8,10},{9,11},{10,... | collective-permute-start | bytes 393224 | tf_op jit(solution)/shard_map/ppermute | solution.py:41
  77.0 8.8 %collective-permute-start.7 = (f32[64,512]{1,0:T(8,128)S(1)}, f32[64,512]{1,0:T(8,128)S(1)}, u32[]{:S(2)}, u32[]{:S(2)}) collective-permute-start(f32[64,512]{1,0:T(8,128)S(1)} %get-tuple-element.29), channel_id=1, source_target_pairs={{0,4},{1,5},{2,6},{3,7},{4,0},{5,1},{6,2},{7,3},{8,12},{9,13},{10,... | collective-permute-start | bytes 393224 | tf_op jit(solution)/shard_map/ppermute | solution.py:41
  78.3 7.7 %collective-permute-start.8 = (f32[64,512]{1,0:T(8,128)S(1)}, f32[64,512]{1,0:T(8,128)S(1)}, u32[]{:S(2)}, u32[]{:S(2)}) collective-permute-start(f32[64,512]{1,0:T(8,128)S(1)} %get-tuple-element.30), channel_id=1, source_target_pairs={{0,6},{1,7},{2,0},{3,1},{4,2},{5,3},{6,4},{7,5},{8,14},{9,15},{10,... | collective-permute-start | bytes 393224 | tf_op jit(solution)/shard_map/ppermute | solution.py:41
  86.0 27.4 %copy-start = (f32[1024,512]{1,0:T(8,128)}, f32[1024,512]{1,0:T(8,128)S(1)}, u32[]{:S(2)}) copy-start(f32[1024,512]{1,0:T(8,128)S(1)} %get-tuple-element.32.a_ref.refs_14_) | copy-start | bytes 6291460
  86.0 5.4 %collective-permute-start.13 = (f32[64,512]{1,0:T(8,128)S(1)}, f32[64,512]{1,0:T(8,128)S(1)}, u32[]{:S(2)}, u32[]{:S(2)}) collective-permute-start(f32[64,512]{1,0:T(8,128)S(1)} %get-tuple-element.34), channel_id=1, source_target_pairs={{0,8},{1,9},{2,10},{3,11},{4,12},{5,13},{6,14},{7,15},{8,0},{9,1},... | collective-permute-start | bytes 393224 | tf_op jit(solution)/shard_map/ppermute | solution.py:36
  86.2 5.3 %collective-permute-start.12 = (f32[8,512]{1,0:T(8,128)S(1)}, f32[8,512]{1,0:T(8,128)S(1)}, u32[]{:S(2)}, u32[]{:S(2)}) collective-permute-start(f32[8,512]{1,0:T(8,128)S(1)} %get-tuple-element.33.facts_ref.refs_8_), channel_id=1, source_target_pairs={{0,240},{16,0},{32,16},{48,32},{64,48},{80,64},{96,80},{112,96},{1... | collective-permute-start | bytes 49160 | tf_op jit(solution)/shard_map/ppermute | solution.py:28
  86.2 5.3 %collective-permute-start.11 = (f32[8,512]{1,0:T(8,128)S(1)}, f32[8,512]{1,0:T(8,128)S(1)}, u32[]{:S(2)}, u32[]{:S(2)}) collective-permute-start(f32[8,512]{1,0:T(8,128)S(1)} %get-tuple-element.33.facts_ref.refs_8_), channel_id=1, source_target_pairs={{0,16},{16,32},{32,48},{48,64},{64,80},{80,96},{96,112},{112,128},... | collective-permute-start | bytes 49160 | tf_op jit(solution)/shard_map/ppermute | solution.py:28
  97.6 17.3 %collective-permute-start.14 = (f32[4,128,512]{2,1,0:T(8,128)S(1)}, f32[4,128,512]{2,1,0:T(8,128)S(1)}, u32[]{:S(2)}, u32[]{:S(2)}) collective-permute-start(f32[4,128,512]{2,1,0:T(8,128)S(1)} %get-tuple-element.36), channel_id=1, source_target_pairs={{0,1},{1,0},{2,3},{3,2},{4,5},{5,4},{6,7},{7,6},{8,9},{9,8},{10,11... | collective-permute-start | bytes 3145736 | tf_op jit(solution)/shard_map/ppermute | solution.py:32
  100.7 78.5 %collective-permute-start.33 = (f32[1024,512]{1,0:T(8,128)S(1)}, f32[1024,512]{1,0:T(8,128)S(1)}, u32[]{:S(2)}, u32[]{:S(2)}) collective-permute-start(f32[1024,512]{1,0:T(8,128)S(1)} %get-tuple-element.32.a_ref.refs_14_), channel_id=1, source_target_pairs={{0,240},{16,0},{32,16},{48,32},{64,48},{80,64},{96,80},{112,96},{1... | collective-permute-start | bytes 6291464 | tf_op jit(solution)/shard_map/ppermute | solution.py:28
  100.7 8.1 %collective-permute-start.17 = (f32[64,512]{1,0:T(8,128)S(1)}, f32[64,512]{1,0:T(8,128)S(1)}, u32[]{:S(2)}, u32[]{:S(2)}) collective-permute-start(f32[64,512]{1,0:T(8,128)S(1)} %add.11.refs_0_), channel_id=1, source_target_pairs={{0,6},{1,7},{2,0},{3,1},{4,2},{5,3},{6,4},{7,5},{8,14},{9,15},{10,... | collective-permute-start | bytes 393224 | tf_op jit(solution)/shard_map/ppermute | solution.py:41
  103.4 6.2 %collective-permute-start.16 = (f32[64,512]{1,0:T(8,128)S(1)}, f32[64,512]{1,0:T(8,128)S(1)}, u32[]{:S(2)}, u32[]{:S(2)}) collective-permute-start(f32[64,512]{1,0:T(8,128)S(1)} %add.11.refs_0_), channel_id=1, source_target_pairs={{0,4},{1,5},{2,6},{3,7},{4,0},{5,1},{6,2},{7,3},{8,12},{9,13},{10,... | collective-permute-start | bytes 393224 | tf_op jit(solution)/shard_map/ppermute | solution.py:41
  103.4 9.1 %collective-permute-start.15 = (f32[64,512]{1,0:T(8,128)S(1)}, f32[64,512]{1,0:T(8,128)S(1)}, u32[]{:S(2)}, u32[]{:S(2)}) collective-permute-start(f32[64,512]{1,0:T(8,128)S(1)} %add.11.refs_0_), channel_id=1, source_target_pairs={{0,2},{1,3},{2,4},{3,5},{4,6},{5,7},{6,0},{7,1},{8,10},{9,11},{10,... | collective-permute-start | bytes 393224 | tf_op jit(solution)/shard_map/ppermute | solution.py:41
  112.5 4.4 %collective-permute-start.21 = (f32[4,64,512]{2,1,0:T(8,128)S(1)}, f32[4,64,512]{2,1,0:T(8,128)S(1)}, u32[]{:S(2)}, u32[]{:S(2)}) collective-permute-start(f32[4,64,512]{2,1,0:T(8,128)S(1)} %pack.2.refs_0_.mine_ref), channel_id=1, source_target_pairs={{0,1},{1,0},{2,3},{3,2},{4,5},{5,4},{6,7},{7,6},{8,9},{9,8},{10,11... | collective-permute-start | bytes 1572872 | tf_op jit(solution)/shard_map/ppermute | solution.py:32
  113.4 91.9 %collective-permute-start.32 = (f32[1024,512]{1,0:T(8,128)S(1)}, f32[1024,512]{1,0:T(8,128)S(1)}, u32[]{:S(2)}, u32[]{:S(2)}) collective-permute-start(f32[1024,512]{1,0:T(8,128)S(1)} %get-tuple-element.32.a_ref.refs_14_), channel_id=1, source_target_pairs={{0,16},{16,32},{32,48},{48,64},{64,80},{80,96},{96,112},{112,128},... | collective-permute-start | bytes 6291464 | tf_op jit(solution)/shard_map/ppermute | solution.py:28
  115.0 9.6 %collective-permute-start.18 = (f32[128,512]{1,0:T(8,128)S(1)}, f32[128,512]{1,0:T(8,128)S(1)}, u32[]{:S(2)}, u32[]{:S(2)}) collective-permute-start(f32[128,512]{1,0:T(8,128)S(1)} %get-tuple-element.38), channel_id=1, source_target_pairs={{0,2},{1,3},{2,4},{3,5},{4,6},{5,7},{6,0},{7,1},{8,10},{9,11},{10,... | collective-permute-start | bytes 786440 | tf_op jit(solution)/shard_map/ppermute | solution.py:41
  115.1 13.5 %collective-permute-start.19 = (f32[128,512]{1,0:T(8,128)S(1)}, f32[128,512]{1,0:T(8,128)S(1)}, u32[]{:S(2)}, u32[]{:S(2)}) collective-permute-start(f32[128,512]{1,0:T(8,128)S(1)} %get-tuple-element.39), channel_id=1, source_target_pairs={{0,4},{1,5},{2,6},{3,7},{4,0},{5,1},{6,2},{7,3},{8,12},{9,13},{10,... | collective-permute-start | bytes 786440 | tf_op jit(solution)/shard_map/ppermute | solution.py:41
  116.9 12.9 %collective-permute-start.20 = (f32[128,512]{1,0:T(8,128)S(1)}, f32[128,512]{1,0:T(8,128)S(1)}, u32[]{:S(2)}, u32[]{:S(2)}) collective-permute-start(f32[128,512]{1,0:T(8,128)S(1)} %get-tuple-element.40), channel_id=1, source_target_pairs={{0,6},{1,7},{2,0},{3,1},{4,2},{5,3},{6,4},{7,5},{8,14},{9,15},{10,... | collective-permute-start | bytes 786440 | tf_op jit(solution)/shard_map/ppermute | solution.py:41
  129.9 40.8 %collective-permute-start.22 = (f32[128,512]{1,0:T(8,128)S(1)}, f32[128,512]{1,0:T(8,128)S(1)}, u32[]{:S(2)}, u32[]{:S(2)}) collective-permute-start(f32[128,512]{1,0:T(8,128)S(1)} %get-tuple-element.41.a_ref), channel_id=1, source_target_pairs={{0,8},{1,9},{2,10},{3,11},{4,12},{5,13},{6,14},{7,15},{8,0},{9,1},... | collective-permute-start | bytes 786440 | tf_op jit(solution)/shard_map/ppermute | solution.py:36
  138.8 1.4 copy-start.2
  140.2 1.3 copy-start.3
  170.7 4.7 %collective-permute-start.24 = (f32[64,512]{1,0:T(8,128)S(1)}, f32[64,512]{1,0:T(8,128)S(1)}, u32[]{:S(2)}, u32[]{:S(2)}) collective-permute-start(f32[64,512]{1,0:T(8,128)S(1)} %get-tuple-element.44.refs_0_), channel_id=1, source_target_pairs={{0,240},{16,0},{32,16},{48,32},{64,48},{80,64},{96,80},{112,96},{1... | collective-permute-start | bytes 393224 | tf_op jit(solution)/shard_map/ppermute | solution.py:28
  170.8 6.8 %collective-permute-start.23 = (f32[64,512]{1,0:T(8,128)S(1)}, f32[64,512]{1,0:T(8,128)S(1)}, u32[]{:S(2)}, u32[]{:S(2)}) collective-permute-start(f32[64,512]{1,0:T(8,128)S(1)} %get-tuple-element.45.refs_1_), channel_id=1, source_target_pairs={{0,16},{16,32},{32,48},{48,64},{64,80},{80,96},{96,112},{112,128},... | collective-permute-start | bytes 393224 | tf_op jit(solution)/shard_map/ppermute | solution.py:28
  177.6 12.2 %collective-permute-start.27 = (f32[4,64,512]{2,1,0:T(8,128)S(1)}, f32[4,64,512]{2,1,0:T(8,128)S(1)}, u32[]{:S(2)}, u32[]{:S(2)}) collective-permute-start(f32[4,64,512]{2,1,0:T(8,128)S(1)} %pack.3.refs_0_), channel_id=1, source_target_pairs={{0,6},{1,7},{2,0},{3,1},{4,2},{5,3},{6,4},{7,5},{8,14},{9,15},{10,... | collective-permute-start | bytes 1572872 | tf_op jit(solution)/shard_map/ppermute | solution.py:41
  178.3 15.6 %collective-permute-start.26 = (f32[4,64,512]{2,1,0:T(8,128)S(1)}, f32[4,64,512]{2,1,0:T(8,128)S(1)}, u32[]{:S(2)}, u32[]{:S(2)}) collective-permute-start(f32[4,64,512]{2,1,0:T(8,128)S(1)} %pack.3.refs_0_), channel_id=1, source_target_pairs={{0,4},{1,5},{2,6},{3,7},{4,0},{5,1},{6,2},{7,3},{8,12},{9,13},{10,... | collective-permute-start | bytes 1572872 | tf_op jit(solution)/shard_map/ppermute | solution.py:41
  178.3 26.6 %collective-permute-start.25 = (f32[4,64,512]{2,1,0:T(8,128)S(1)}, f32[4,64,512]{2,1,0:T(8,128)S(1)}, u32[]{:S(2)}, u32[]{:S(2)}) collective-permute-start(f32[4,64,512]{2,1,0:T(8,128)S(1)} %pack.3.refs_0_), channel_id=1, source_target_pairs={{0,2},{1,3},{2,4},{3,5},{4,6},{5,7},{6,0},{7,1},{8,10},{9,11},{10,... | collective-permute-start | bytes 1572872 | tf_op jit(solution)/shard_map/ppermute | solution.py:41
  179.2 27.7 %copy-start.4 = (f32[1024,512]{1,0:T(8,128)}, f32[1024,512]{1,0:T(8,128)S(1)}, u32[]{:S(2)}) copy-start(f32[1024,512]{1,0:T(8,128)S(1)} %collective-permute-done.33.refs_19_) | copy-start | bytes 6291460
  179.2 26.2 %collective-permute-start.28 = (f32[4,64,512]{2,1,0:T(8,128)S(1)}, f32[4,64,512]{2,1,0:T(8,128)S(1)}, u32[]{:S(2)}, u32[]{:S(2)}) collective-permute-start(f32[4,64,512]{2,1,0:T(8,128)S(1)} %pack.3.refs_0_), channel_id=1, source_target_pairs={{0,1},{1,0},{2,3},{3,2},{4,5},{5,4},{6,7},{7,6},{8,9},{9,8},{10,11... | collective-permute-start | bytes 1572872 | tf_op jit(solution)/shard_map/ppermute | solution.py:32
  189.8 15.6 %collective-permute-start.31 = (f32[4,64,512]{2,1,0:T(8,128)S(1)}, f32[4,64,512]{2,1,0:T(8,128)S(1)}, u32[]{:S(2)}, u32[]{:S(2)}) collective-permute-start(f32[4,64,512]{2,1,0:T(8,128)S(1)} %collective-permute-done.27.refs_3_), channel_id=1, source_target_pairs={{0,1},{1,0},{2,3},{3,2},{4,5},{5,4},{6,7},{7,6},{8,9},{9,8},{10,11... | collective-permute-start | bytes 1572872 | tf_op jit(solution)/shard_map/ppermute | solution.py:32
  193.9 11.5 %collective-permute-start.30 = (f32[4,64,512]{2,1,0:T(8,128)S(1)}, f32[4,64,512]{2,1,0:T(8,128)S(1)}, u32[]{:S(2)}, u32[]{:S(2)}) collective-permute-start(f32[4,64,512]{2,1,0:T(8,128)S(1)} %collective-permute-done.26.refs_2_), channel_id=1, source_target_pairs={{0,1},{1,0},{2,3},{3,2},{4,5},{5,4},{6,7},{7,6},{8,9},{9,8},{10,11... | collective-permute-start | bytes 1572872 | tf_op jit(solution)/shard_map/ppermute | solution.py:32
  204.9 2.0 collective-permute-start.29
  205.4 1.5 copy-start.5

commit v2 on v1

v2 whole, which is shorter than its diff:
```python
import functools

import jax
import jax.numpy as jnp
from jax import lax
from jax.experimental import pallas as pl
from jax.experimental.pallas import tpu as pltpu
from jax.sharding import PartitionSpec as P

epsilon = 1e-05
off_weight = 0.0051
f32 = jnp.float32
bf16 = jnp.bfloat16


any_spec = pl.BlockSpec(memory_space=pl.ANY)
smem_spec = pl.BlockSpec(memory_space=pltpu.SMEM)
vmem_spec = pl.BlockSpec(memory_space=pltpu.VMEM)
params = pltpu.CompilerParams(vmem_limit_bytes=48 * 1024 * 1024)
cheap = pl.CostEstimate(flops=1, transcendentals=0, bytes_accessed=1)
call = functools.partial(pl.pallas_call, compiler_params=params, cost_estimate=cheap)
top_rows = 384


def shape(*dims):
    return jax.ShapeDtypeStruct(dims, f32)


def across(block, shift):
    count = lax.axis_size("grp")
    return lax.ppermute(block, "grp", [(i, (i + shift) % count) for i in range(count)])


def to_core(block):
    return lax.ppermute(block, "row", [(i, i ^ 1) for i in range(16)])


def to_y(block):
    return lax.ppermute(block, "row", [(i, i ^ 8) for i in range(16)])


def to_x(block, shift):
    pairs = [(i, (i & 9) | ((((i >> 1) + shift) & 3) << 1)) for i in range(16)]
    return lax.ppermute(block, "row", pairs)


def split(value):
    high = value.astype(bf16)
    return high, (value - high.astype(f32)).astype(bf16)


def mm(a, b):
    return lax.dot_general(a, b, (((1,), (0,)), ((), ())), preferred_element_type=f32)


def gram(a, b):
    a_high, a_low = split(a.T)
    b_high, b_low = split(b)
    return mm(
        jnp.concatenate([a_high, a_high, a_low], axis=1),
        jnp.concatenate([b_high, b_low, b_high], axis=0),
    )


def thrice(value):
    high, low = split(value)
    return jnp.concatenate([high, high, low], axis=1)


def sums_kernel(a_ref, b_ref, out_ref):
    @pl.when(pl.program_id(0) == 0)
    def _():
        out_ref[...] = jnp.zeros_like(out_ref)

    a, b = a_ref[...], b_ref[...]
    for row, value in enumerate((a, a * a, b, b * b)):
        out_ref[row : row + 1, :] += jnp.sum(value, axis=0, keepdims=True)


def sums_of(a, b):
    rows, width = a.shape
    tile = rows // 4
    spec = pl.BlockSpec((tile, width), lambda i: (i, 0))
    return call(
        sums_kernel,
        grid=(4,),
        in_specs=[spec, spec],
        out_specs=pl.BlockSpec((8, width), lambda i: (0, 0)),
        out_shape=shape(8, width),
        name="sums",
    )(a, b)


def put_slots(at_ref, acc, keep_ref, send_ref, first, rows):
    core, x = at_ref[0], at_ref[1]
    for slot in range(4):
        chunk = (x + slot) & 3
        mine = pl.multiple_of((core * 4 + chunk) * rows, rows)
        theirs = pl.multiple_of(((1 - core) * 4 + chunk) * rows, rows)
        keep_ref[slot, first : first + rows, :] = acc[pl.ds(mine, rows), :]
        send_ref[slot, first : first + rows, :] = acc[pl.ds(theirs, rows), :]


def own_corr_kernel(half_rows, steps, top_steps, at_ref, a_ref, b_ref, *refs):
    parts, (top_ref, low_ref, facts_ref, keep_ref, send_ref, acc_ref) = refs[:4], refs[4:]
    step = pl.program_id(0)

    @pl.when(step == 0)
    def _():
        total = parts[0][...] + parts[1][...] + parts[2][...] + parts[3][...]
        total = total / half_rows
        for view in (0, 1):
            mean, square = total[2 * view : 2 * view + 1], total[2 * view + 1 : 2 * view + 2]
            scale = jnp.sqrt(square - mean * mean + epsilon)
            facts_ref[2 * view : 2 * view + 1, :] = mean
            facts_ref[2 * view + 1 : 2 * view + 2, :] = 1.0 / scale
            facts_ref[4 + view : 5 + view, :] = square
            facts_ref[6 + view : 7 + view, :] = scale
        acc_ref[...] = jnp.zeros_like(acc_ref)

    norm_a = (a_ref[...] - facts_ref[0:1, :]) * facts_ref[1:2, :]
    norm_b = (b_ref[...] - facts_ref[2:3, :]) * facts_ref[3:4, :]

    @pl.when(step < top_steps)
    def _():
        top_ref[...] = norm_a

    @pl.when(step >= top_steps)
    def _():
        low_ref[...] = norm_a

    acc_ref[...] += gram(norm_a, norm_b)

    @pl.when(step == steps - 1)
    def _():
        put_slots(at_ref, acc_ref, keep_ref, send_ref, 0, keep_ref.shape[1])


def own_corr(at, a, b, parts, half_rows):
    rows, width = a.shape
    tile = 128
    steps, top_steps = rows // tile, top_rows // tile
    spec = pl.BlockSpec((tile, width), lambda i: (i, 0))
    top_spec = pl.BlockSpec((tile, width), lambda i: (jnp.minimum(i, top_steps - 1), 0))
    low_spec = pl.BlockSpec((tile, width), lambda i: (jnp.maximum(i - top_steps, 0), 0))
    whole = pl.BlockSpec((8, width), lambda i: (0, 0))
    slots = pl.BlockSpec((4, width // 8, width), lambda i: (0, 0, 0))
    return call(
        functools.partial(own_corr_kernel, half_rows, steps, top_steps),
        grid=(steps,),
        in_specs=[smem_spec, spec, spec] + [whole] * 4,
        out_specs=[top_spec, low_spec, whole, slots, slots],
        out_shape=[shape(top_rows, width), shape(rows - top_rows, width), shape(8, width)]
        + [shape(4, width // 8, width)] * 2,
        scratch_shapes=[pltpu.VMEM((width, width), f32)],
        name="own_corr",
    )(at, a, b, *parts)


def side_corr_kernel(steps, at_ref, a_ref, prev_ref, next_ref, f_ref, pf_ref, nf_ref, *refs):
    keep_ref, send_ref, left_ref, right_ref = refs[-4:]
    step = pl.program_id(0)

    @pl.when(step == 0)
    def _():
        left_ref[...] = jnp.zeros_like(left_ref)
        right_ref[...] = jnp.zeros_like(right_ref)

    norm_a = (a_ref[...] - f_ref[0:1, :]) * f_ref[1:2, :]
    for acc_ref, b_ref, facts_ref in ((left_ref, prev_ref, pf_ref), (right_ref, next_ref, nf_ref)):
        norm_b = (b_ref[...] - facts_ref[2:3, :]) * facts_ref[3:4, :]
        acc_ref[...] += gram(norm_a, norm_b)

    @pl.when(step == steps - 1)
    def _():
        rows = keep_ref.shape[1] // 2
        put_slots(at_ref, left_ref, keep_ref, send_ref, 0, rows)
        put_slots(at_ref, right_ref, keep_ref, send_ref, rows, rows)


def side_corr(at, a, prev_b, next_b, facts, prev_facts, next_facts, wait_for):
    rows, width = a.shape
    steps = 4
    spec = pl.BlockSpec((rows // steps, width), lambda i: (i, 0))
    whole = pl.BlockSpec((8, width), lambda i: (0, 0))
    slots = pl.BlockSpec((4, width // 4, width), lambda i: (0, 0, 0))
    return call(
        functools.partial(side_corr_kernel, steps),
        grid=(steps,),
        in_specs=[smem_spec, spec, spec, spec] + [whole] * 3 + [any_spec] * len(wait_for),
        out_specs=[slots, slots],
        out_shape=[shape(4, width // 4, width)] * 2,
        scratch_shapes=[pltpu.VMEM((width, width), f32)] * 2,
        name="side_corr",
    )(at, a, prev_b, next_b, facts, prev_facts, next_facts, *wait_for)


def fan_kernel(keep_ref, got_ref, *refs):
    outs = refs[-4:]
    for slot in range(4):
        outs[slot][...] = keep_ref[slot] + got_ref[slot]


def fan(keep, got):
    return call(
        fan_kernel,
        in_specs=[vmem_spec, vmem_spec],
        out_specs=[vmem_spec] * 4,
        out_shape=[shape(*keep.shape[1:])] * 4,
        name="fan",
    )(keep, got)


def message_kernel(extra, *refs):
    out_ref = refs[4 + extra]
    rows = refs[0].shape[0]
    out_ref[0:rows, :] = refs[0][...] + refs[1][...] + refs[2][...] + refs[3][...]
    for i in range(extra):
        out_ref[rows + 8 * i : rows + 8 * i + 8, :] = refs[4 + i][...]


def message(parts, facts, carried=None):
    rows, width = parts[0].shape
    more = [] if carried is None else [carried]
    count = 4 + len(facts)

    def kernel(*refs):
        message_kernel(len(facts), *refs[:count], refs[count + len(more)])

    return call(
        kernel,
        in_specs=[vmem_spec] * count + [any_spec] * len(more),
        out_specs=[vmem_spec] + [any_spec] * len(more),
        out_shape=[shape(rows + 8 * len(facts), width)] + [shape(*c.shape) for c in more],
        input_output_aliases={count: 1} if more else {},
        name="message",
    )(*parts, *facts, *more)


def full_facts(mine, other):
    rows = []
    for view in (0, 1):
        mean = 0.5 * (mine[2 * view : 2 * view + 1] + other[2 * view : 2 * view + 1])
        square = 0.5 * (mine[4 + view : 5 + view] + other[4 + view : 5 + view])
        rows += [mean, 1.0 / jnp.sqrt(square - mean * mean + epsilon)]
    for view in (0, 1):
        average = 0.5 * (mine[2 * view : 2 * view + 1] + other[2 * view : 2 * view + 1])
        rows.append((average - rows[2 * view]) * rows[2 * view + 1])
    rows += [mine[6:7] * rows[1], (mine[0:1] - rows[0]) * rows[1]]
    return rows


def merged(mine, other, a_cols, b_mine, b_other, b_full, half_rows):
    scale0, scale1, diff0, diff1, inverse = (a_cols[:, i : i + 1] for i in range(5))
    out = mine * (scale0 * b_mine[7:8]) + other * (scale1 * b_other[7:8])
    shift0, shift1 = b_mine[2:3] - b_full[2], b_other[2:3] - b_full[2]
    out = out + half_rows * (diff0 * shift0 + diff1 * shift1)
    return out * (inverse * (b_full[3] * (0.5 / half_rows)))


def columns_of(at_ref, mine, other, full, cols_ref, rows):
    width = mine.shape[1]
    stack = [mine[6:7], other[6:7], mine[0:1] - full[0], other[0:1] - full[0], full[1]]
    stack = jnp.concatenate(stack + [jnp.zeros((123, width), f32)], axis=0)
    cols_ref[...] = stack.T
    first = pl.multiple_of((at_ref[0] * 4 + at_ref[1]) * rows, rows)
    return cols_ref[pl.ds(first, rows), :]


def own_merge_kernel(half_rows, at_ref, mine_ref, got_ref, _, chunk_ref, full_ref, __, cols_ref):
    rows = chunk_ref.shape[0]
    mine, other = mine_ref[rows:, :], got_ref[rows:, :]
    full = full_facts(mine, other)
    for i in range(8):
        full_ref[i : i + 1, :] = full[i]
    cols = columns_of(at_ref, mine, other, full, cols_ref, rows)
    chunk_ref[...] = merged(
        mine_ref[0:rows, :], got_ref[0:rows, :], cols, mine, other, full, half_rows
    )


def own_merge(at, mine, got, carried, half_rows):
    rows, width = mine.shape
    return call(
        functools.partial(own_merge_kernel, half_rows),
        in_specs=[smem_spec, vmem_spec, vmem_spec, any_spec],
        out_specs=[vmem_spec, vmem_spec, any_spec],
        out_shape=[shape(rows - 8, width), shape(8, width), shape(*carried.shape)],
        input_output_aliases={3: 2},
        scratch_shapes=[pltpu.VMEM((width, 128), f32)],
        name="own_merge",
    )(at, mine, got, carried)


def side_merge_kernel(half_rows, at_ref, mine_ref, got_ref, own_ref, own_got_ref, *refs):
    left_ref, right_ref, pf_ref, nf_ref, cols_ref = refs[-5:]
    rows = left_ref.shape[0]
    mine, other = own_ref[rows:, :], own_got_ref[rows:, :]
    cols = columns_of(at_ref, mine, other, full_facts(mine, other), cols_ref, rows)
    for side, (out_ref, facts_ref) in enumerate(((left_ref, pf_ref), (right_ref, nf_ref))):
        first = side * rows
        fact = 2 * rows + 8 * side
        b_mine, b_other = mine_ref[fact : fact + 8, :], got_ref[fact : fact + 8, :]
        full = full_facts(b_mine, b_other)
        for i in range(8):
            facts_ref[i : i + 1, :] = full[i]
        out_ref[...] = merged(
            mine_ref[first : first + rows, :],
            got_ref[first : first + rows, :],
            cols,
            b_mine,
            b_other,
            full,
            half_rows,
        )


def side_merge(at, mine, got, own, own_got, half_rows, wait_for):
    rows, width = own.shape
    return call(
        functools.partial(side_merge_kernel, half_rows),
        in_specs=[smem_spec] + [vmem_spec] * 4 + [any_spec] * len(wait_for),
        out_specs=[vmem_spec] * 4,
        out_shape=[shape(rows - 8, width)] * 2 + [shape(8, width)] * 2,
        scratch_shapes=[pltpu.VMEM((width, 128), f32)],
        name="side_merge",
    )(at, mine, got, own, own_got, *wait_for)


def pack(parts, carried=None, wait_for=()):
    rows, width = parts[0].shape
    more = [] if carried is None else [carried]
    at_out = 4 + len(more) + len(wait_for)

    def kernel(*refs):
        for i in range(4):
            refs[at_out][i] = refs[i][...]

    out = call(
        kernel,
        in_specs=[vmem_spec] * 4 + [any_spec] * (len(more) + len(wait_for)),
        out_specs=[vmem_spec] + [any_spec] * len(more),
        out_shape=[shape(4, rows, width)] + [shape(*c.shape) for c in more],
        input_output_aliases={4: 1} if more else {},
        name="pack",
    )(*parts, *more, *wait_for)
    return out[0] if carried is None else out


def row_of(at_ref, core_flip, slot, rows):
    core, x = at_ref[0], at_ref[1]
    core = 1 - core if core_flip else core
    return pl.multiple_of((core * 4 + ((x - slot) & 3)) * rows, rows)


def own_grad_kernel(at_ref, mine_ref, other_ref, a_ref, b_ref, facts_ref, *refs):
    ga_ref, gb_ref, sums_ref, corr_ref, pt_ref, p_ref = refs[-6:]
    width = corr_ref.shape[0]

    @pl.when(pl.program_id(0) == 0)
    def _():
        rows = mine_ref.shape[1]
        for flip, ref in ((False, mine_ref), (True, other_ref)):
            for slot in range(4):
                corr_ref[pl.ds(row_of(at_ref, flip, slot, rows), rows), :] = ref[slot]
        corr = corr_ref[...]
        row_index = lax.broadcasted_iota(jnp.int32, corr.shape, 0)
        column = lax.broadcasted_iota(jnp.int32, corr.shape, 1)
        pen = jnp.where(row_index == column, -2.0 * (1.0 - corr), 2.0 * off_weight * corr)
        cross = pen * corr
        pen_t = pen.T
        high, low = split(pen)
        p_ref[0:width, :] = high
        p_ref[width : 2 * width, :] = low
        p_ref[2 * width :, :] = high
        high, low = split(pen_t)
        pt_ref[0:width, :] = high
        pt_ref[width : 2 * width, :] = low
        pt_ref[2 * width :, :] = high
        left = thrice(facts_ref[...])
        sums_ref[0:1, :] = mm(left, pt_ref[...])[5:6]
        sums_ref[1:2, :] = jnp.sum(cross.T, axis=0, keepdims=True)
        sums_ref[2:3, :] = mm(left, p_ref[...])[4:5]
        sums_ref[3:4, :] = jnp.sum(cross, axis=0, keepdims=True)
        sums_ref[4:8, :] = jnp.zeros((4, width), f32)

    norm_b = (b_ref[...] - facts_ref[2:3, :]) * facts_ref[3:4, :]
    ga_ref[...] = mm(thrice(norm_b), pt_ref[...])
    norm_a = (a_ref[...] - facts_ref[0:1, :]) * facts_ref[1:2, :]
    gb_ref[...] = mm(thrice(norm_a), p_ref[...])


def own_grad(at, mine, other, a, b, facts):
    rows, width = b.shape
    steps = 4
    spec = pl.BlockSpec((rows // steps, width), lambda i: (i, 0))
    whole = pl.BlockSpec((8, width), lambda i: (0, 0))
    slots = pl.BlockSpec(mine.shape, lambda i: (0, 0, 0))
    return call(
        own_grad_kernel,
        grid=(steps,),
        in_specs=[smem_spec, slots, slots, spec, spec, whole],
        out_specs=[spec, spec, whole],
        out_shape=[shape(rows, width)] * 2 + [shape(8, width)],
        scratch_shapes=[
            pltpu.VMEM((width, width), f32),
            pltpu.VMEM((3 * width, width), bf16),
            pltpu.VMEM((3 * width, width), bf16),
        ],
        name="own_grad",
    )(at, mine, other, a, b, facts)


def prep_kernel(at_ref, *refs):
    packs, refs = refs[:8], refs[8:]
    pf_ref, nf_ref, sums_ref, pt_ref, p_ref, vec_ref, corr_ref = refs
    width = corr_ref.shape[1]
    rows = packs[0].shape[1]
    for flip in (0, 1):
        for slot in range(4):
            at = row_of(at_ref, flip == 1, slot, rows)
            for kind in range(4):
                corr_ref[kind, pl.ds(at, rows), :] = packs[4 * flip + slot][kind]
    vec = sums_ref[0:4, :]
    cross_a = vec[1:2]
    cross_b = vec[3:4]
    for kind in range(4):
        corr = corr_ref[kind]
        corr = corr.T if kind < 2 else corr
        pen = 2.0 * off_weight * corr
        cross = jnp.sum(pen * corr, axis=0, keepdims=True)
        into = pt_ref if kind < 2 else p_ref
        first = (kind % 2) * 3 * width
        high, low = split(pen)
        into[first : first + width, :] = high
        into[first + width : first + 2 * width, :] = low
        into[first + 2 * width : first + 3 * width, :] = high
        if kind < 2:
            cross_a = cross_a + cross
        else:
            cross_b = cross_b + cross
    left = jnp.concatenate([thrice(pf_ref[...]), thrice(nf_ref[...])], axis=1)
    vec_ref[0:1, :] = vec[0:1] + mm(left, pt_ref[...])[5:6]
    vec_ref[1:2, :] = cross_a
    vec_ref[2:3, :] = vec[2:3] + mm(left, p_ref[...])[4:5]
    vec_ref[3:4, :] = cross_b
    vec_ref[4:8, :] = jnp.zeros((4, width), f32)


def prep(at, packs, prev_facts, next_facts, sums):
    width = sums.shape[1]
    return call(
        prep_kernel,
        in_specs=[smem_spec] + [vmem_spec] * 11,
        out_specs=[vmem_spec] * 3,
        out_shape=[jax.ShapeDtypeStruct((6 * width, width), bf16)] * 2 + [shape(8, width)],
        scratch_shapes=[pltpu.VMEM((4, width, width), f32)],
        name="prep",
    )(at, *packs, prev_facts, next_facts, sums)


def finish_kernel(pt_ref, p_ref, vec_ref, f_ref, pf_ref, nf_ref, *refs):
    ga_ref, gb_ref, a_ref, b_ref, pb_ref, nb_ref, pa_ref, xa_ref = refs[:8]
    out_a_ref, out_b_ref = refs[-2:]
    prev_b = (pb_ref[...] - pf_ref[2:3, :]) * pf_ref[3:4, :]
    next_b = (nb_ref[...] - nf_ref[2:3, :]) * nf_ref[3:4, :]
    ga = ga_ref[...] + mm(jnp.concatenate([thrice(prev_b), thrice(next_b)], axis=1), pt_ref[...])
    norm_a = (a_ref[...] - f_ref[0:1, :]) * f_ref[1:2, :]
    out_a_ref[...] = (ga - vec_ref[0:1, :] - norm_a * vec_ref[1:2, :]) * f_ref[1:2, :]
    prev_a = pa_ref[...] * pf_ref[6:7, :] + pf_ref[7:8, :]
    next_a = xa_ref[...] * nf_ref[6:7, :] + nf_ref[7:8, :]
    gb = gb_ref[...] + mm(jnp.concatenate([thrice(prev_a), thrice(next_a)], axis=1), p_ref[...])
    norm_b = (b_ref[...] - f_ref[2:3, :]) * f_ref[3:4, :]
    out_b_ref[...] = (gb - vec_ref[2:3, :] - norm_b * vec_ref[3:4, :]) * f_ref[3:4, :]


def finish(first, tile, mats, facts, whole_tiles, halo_tiles, partial=()):
    rows, width = whole_tiles[0].shape
    steps = halo_tiles[0].shape[0] // tile
    at = pl.BlockSpec((pl.Element(tile), pl.Element(width)), lambda i: (pl.multiple_of(first + i * tile, 64), 0))
    halo = pl.BlockSpec((tile, width), lambda i: (i, 0))
    whole = pl.BlockSpec((8, width), lambda i: (0, 0))
    mat = pl.BlockSpec(mats[0].shape, lambda i: (0, 0))
    count = 6 + 8
    return call(
        finish_kernel,
        grid=(steps,),
        in_specs=[mat, mat] + [whole] * 4 + [at] * 6 + [halo] * 2 + [any_spec] * len(partial),
        out_specs=[at, at],
        out_shape=[shape(rows, width)] * 2,
        input_output_aliases={count: 0, count + 1: 1} if partial else {},
        name="finish",
    )(*mats, *facts, *whole_tiles, *halo_tiles, *partial)


def per_device(view_a, view_b):
    local_rows, width = view_a.shape
    half_rows = local_rows * lax.axis_size("row") // 2
    index = lax.axis_index("row")
    at = jnp.stack([index & 1, (index >> 1) & 3])

    prev_raw = across(view_b, 1)
    next_raw = across(view_b, -1)
    sums = sums_of(view_a, view_b)
    sums = sums + to_core(sums)
    parts = [sums] + [to_x(sums, shift) for shift in (1, 2, 3)]

    a_top, a_low, half_facts, keep, send = own_corr(at, view_a, view_b, parts, half_rows)
    prev_half = across(half_facts, 1)
    next_half = across(half_facts, -1)
    slots = fan(keep, to_core(send))
    got = [slots[0]] + [to_x(slots[shift], shift) for shift in (1, 2, 3)]
    (own_mine,) = message(got, [half_facts])
    own_got = to_y(own_mine)
    own_chunk, facts, a_top = own_merge(at, own_mine, own_got, a_top, half_rows)
    prev_top = across(a_top, 1)
    next_top = across(a_top, -1)

    keep, send = side_corr(
        at, view_a, prev_raw, next_raw, half_facts, prev_half, next_half, [own_chunk]
    )
    slots = fan(keep, to_core(send))
    got = [slots[0]] + [to_x(slots[shift], shift) for shift in (1, 2, 3)]
    side_mine, own_chunk = message(got, [prev_half, next_half], own_chunk)
    own_slots = [own_chunk] + [to_x(own_chunk, shift) for shift in (1, 2, 3)]
    left, right, prev_facts, next_facts = side_merge(
        at, side_mine, to_y(side_mine), own_mine, own_got, half_rows, [prev_top, next_top]
    )
    from_next = across(left, -1)
    from_prev = across(right, 1)
    own_pack = pack(own_slots, None, [left])
    own_other = to_core(own_pack)
    packed, a_low = pack([left, right, from_prev, from_next], a_low, [own_other])
    prev_low = across(a_low, 1)
    next_low = across(a_low, -1)
    mine = [packed] + [to_x(packed, shift) for shift in (1, 2, 3)]
    part_a, part_b, own_sums = own_grad(at, own_pack, own_other, view_a, view_b, facts)
    other = [to_core(block) for block in mine]
    mats = prep(at, mine + other, prev_facts, next_facts, own_sums)
    all_facts = [facts, prev_facts, next_facts]
    whole = [part_a, part_b, view_a, view_b, prev_raw, next_raw]
    done = finish(0, top_rows, mats, all_facts, whole, [prev_top, next_top])
    low = (local_rows - top_rows) // 2
    return tuple(finish(top_rows, low, mats, all_facts, whole, [prev_low, next_low], done))


def solution(mesh):
    placed = (P("row", "grp"), P("row", "grp"))
    return jax.shard_map(
        per_device,
        mesh=mesh,
        in_specs=placed,
        out_specs=(P("row", "grp"), P("row", "grp")),
        check_vma=False,
    )
```

time: 221 us -> 170 us (0.77)
  waiting for transfers between devices: 134 us -> 64.2 us
  starting transfers between devices: 47.3 us -> 58.2 us
  Pallas kernels: 34.1 us -> 43.4 us
    ppermute x3 -> x2, waiting for transfers between devices: 78.5 us -> 22 us  [to_y(): return lax.ppermute(block, 'row', [(i, i ^ 8) for i in range(16)])]
    ppermute x15, waiting for transfers between devices: 46.7 us -> 35.4 us  [to_x(): return lax.ppermute(block, 'row', pairs)]
    pallas_call x12 -> x15, Pallas kernels: 34.1 us -> 43.4 us  [the longest x2 17.3 us: finish(): call(finish_kernel, grid=(steps,), in_specs=[mat, mat] + [whole] * 4 + [a...]
    ppermute x8 -> x10, starting transfers between devices: 12 us -> 19.4 us  [across(): lax.ppermute(block, 'grp', [(i, (i + shift) % count) for i in range(count)])]
    ppermute x15, starting transfers between devices: 14.5 us -> 17.9 us  [to_x(): return lax.ppermute(block, 'row', pairs)]
    ppermute x8, starting transfers between devices: 15.5 us -> 18 us  [to_core(): return lax.ppermute(block, 'row', [(i, i ^ 1) for i in range(16)])]
    ppermute x3 -> x2, starting transfers between devices: 5.28 us -> 2.85 us  [to_y(): return lax.ppermute(block, 'row', [(i, i ^ 8) for i in range(16)])]
    ppermute x8 -> x10, waiting for transfers between devices: 5.32 us -> 3.6 us  [across(): lax.ppermute(block, 'grp', [(i, (i + shift) % count) for i in range(count)])]
  transfers between devices with their start and end apart: 34 -> 35, of which waited for: 20 -> 15; matrix products, arithmetic and copies ran while one was open for 0% -> 0% of each run, Pallas kernels for 7% -> 16%
where the time goes in v2:
time: 170 us
  waiting for transfers between devices  64.2 us (38%)
  starting transfers between devices  58.2 us (34%)
  Pallas kernels  43.4 us (26%)
  local copies, waits for them, and re-layouts  3.19 us (2%)
    ppermute x15, waiting for transfers between devices, to_x(): return lax.ppermute(block, 'row', pairs)  35.4 us
    ppermute x2, waiting for transfers between devices, to_y(): return lax.ppermute(block, 'row', [(i, i ^ 8) for i in range(16)])  22 us
    ppermute x10, starting transfers between devices, across(): lax.ppermute(block, 'grp', [(i, (i + shift) % count) for i in range(count)])  19.4 us
    ppermute x8, starting transfers between devices, to_core(): return lax.ppermute(block, 'row', [(i, i ^ 1) for i in range(16)])  18 us
    ppermute x15, starting transfers between devices, to_x(): return lax.ppermute(block, 'row', pairs)  17.9 us
    pallas_call x2, Pallas kernels, finish(): call(finish_kernel, grid=(steps,), in_specs=[mat, mat] + [whole] * 4 + [a...  17.3 us
    pallas_call x1, Pallas kernels, own_corr(): call(functools.partial(own_corr_kernel, half_rows, steps, top_steps), gri...  6.97 us
    pallas_call x1, Pallas kernels, own_grad(): call(own_grad_kernel, grid=(steps,), in_specs=[smem_spec, slots, slots, s...  6.39 us
  transfers between devices with their start and end apart: 35, of which 15 were waited for; matrix products, arithmetic and copies ran while one was open for 0% of the time, Pallas kernels for 16%

profile of v2, /device:TPU:1, one launch (start us, length us, event | category | flops | bytes accessed | tf_op | source)
XLA Modules:
  0.0 169.9 jit_solution(1448440837723329792)
XLA Ops:
  0.6 7.5 %collective-permute-start.1 = (f32[1024,512]{1,0:T(8,128)}, f32[1024,512]{1,0:T(8,128)}, u32[]{:S(2)}, u32[]{:S(2)}) collective-permute-start(f32[1024,512]{1,0:T(8,128)} %refs_3_.3), channel_id=1, source_target_pairs={{0,240},{16,0},{32,16},{48,32},{64,48},{80,64},{96,80},{112,96},{1... | collective-permute-start | bytes 6291464 | tf_op jit(solution)/shard_map/ppermute | solution.py:31
  8.1 1.6 copy-done
  9.7 1.6 copy-done.2
  11.3 0.6 sums.1
  11.9 1.0 collective-permute-start.2
  13.0 0.8 collective-permute-done.2
  13.8 2.5 %collective-permute-start.5 = (f32[8,512]{1,0:T(8,128)S(1)}, f32[8,512]{1,0:T(8,128)S(1)}, u32[]{:S(2)}, u32[]{:S(2)}) collective-permute-start(f32[8,512]{1,0:T(8,128)S(1)} %add.3.refs_0_), channel_id=1, source_target_pairs={{0,6},{1,7},{2,0},{3,1},{4,2},{5,3},{6,4},{7,5},{8,14},{9,15},{10,... | collective-permute-start | bytes 49160 | tf_op jit(solution)/shard_map/ppermute | solution.py:44
  16.3 0.5 collective-permute-start.4
  16.8 0.6 collective-permute-start.3
  17.5 3.3 %collective-permute-done.4.refs_2_ = f32[8,512]{1,0:T(8,128)S(1)} collective-permute-done((f32[8,512]{1,0:T(8,128)S(1)}, f32[8,512]{1,0:T(8,128)S(1)}, u32[]{:S(2)}, u32[]{:S(2)}) %collective-permute-start.4) | collective-permute-done | bytes 16416 | tf_op jit(solution)/shard_map/ppermute | solution.py:44
  21.0 7.0 %own_corr.1 = (f32[384,512]{1,0:T(8,128)S(1)}, f32[640,512]{1,0:T(8,128)S(1)}, f32[8,512]{1,0:T(8,128)S(1)}, f32[4,64,512]{2,1,0:T(8,128)S(1)}, f32[4,64,512]{2,1,0:T(8,128)S(1)}) custom-call(s32[2]{0:T(128)S(1)} %pad_add_fusion.at_ref, f32[1024,512]{1,0:T(8,128)S(1)} %copy-done.1, f32[1024,512]{1,0:T(8,128)} %refs_3_.3, f32[8,512]{1,0:T(8,128)S(1)} %add.3.refs_0_, ...), custom_call_target="tpu_custom_call" | custom-call | flops 1 | bytes 1 | tf_op jit(solution)/shard_map/own_corr/pallas_call | solution.py:148
  28.0 1.7 %collective-permute-start.8 = (f32[4,64,512]{2,1,0:T(8,128)S(1)}, f32[4,64,512]{2,1,0:T(8,128)S(1)}, u32[]{:S(2)}, u32[]{:S(2)}) collective-permute-start(f32[4,64,512]{2,1,0:T(8,128)S(1)} %get-tuple-element.38), channel_id=1, source_target_pairs={{0,1},{1,0},{2,3},{3,2},{4,5},{5,4},{6,7},{7,6},{8,9},{9,8},{10,11... | collective-permute-start | bytes 1572872 | tf_op jit(solution)/shard_map/ppermute | solution.py:35
  29.7 1.5 collective-permute-done.8.got_ref
  31.4 1.3 collective-permute-start.10
  32.8 2.0 %collective-permute-start.11 = (f32[64,512]{1,0:T(8,128)S(1)}, f32[64,512]{1,0:T(8,128)S(1)}, u32[]{:S(2)}, u32[]{:S(2)}) collective-permute-start(f32[64,512]{1,0:T(8,128)S(1)} %get-tuple-element.42), channel_id=1, source_target_pairs={{0,6},{1,7},{2,0},{3,1},{4,2},{5,3},{6,4},{7,5},{8,14},{9,15},{10,... | collective-permute-start | bytes 393224 | tf_op jit(solution)/shard_map/ppermute | solution.py:44
  34.7 5.6 %collective-permute-done.9.refs_1_ = f32[64,512]{1,0:T(8,128)S(1)} collective-permute-done((f32[64,512]{1,0:T(8,128)S(1)}, f32[64,512]{1,0:T(8,128)S(1)}, u32[]{:S(2)}, u32[]{:S(2)}) %collective-permute-start.9) | collective-permute-done | bytes 131104 | tf_op jit(solution)/shard_map/ppermute | solution.py:44
  40.5 2.7 %collective-permute-start.12 = (f32[72,512]{1,0:T(8,128)S(1)}, f32[72,512]{1,0:T(8,128)S(1)}, u32[]{:S(2)}, u32[]{:S(2)}) collective-permute-start(f32[72,512]{1,0:T(8,128)S(1)} %message.2.mine_ref.own_ref), channel_id=1, source_target_pairs={{0,8},{1,9},{2,10},{3,11},{4,12},{5,13},{6,14},{7,15},{8,0},{9,1},... | collective-permute-start | bytes 442376 | tf_op jit(solution)/shard_map/ppermute | solution.py:39
  43.2 3.2 %collective-permute-start.7 = (f32[8,512]{1,0:T(8,128)S(1)}, f32[8,512]{1,0:T(8,128)S(1)}, u32[]{:S(2)}, u32[]{:S(2)}) collective-permute-start(f32[8,512]{1,0:T(8,128)S(1)} %get-tuple-element.36.refs_4_.f_ref), channel_id=1, source_target_pairs={{0,240},{16,0},{32,16},{48,32},{64,48},{80,64},{96,80},{112,96},{1... | collective-permute-start | bytes 49160 | tf_op jit(solution)/shard_map/ppermute | solution.py:31
  46.5 16.6 %collective-permute-done.12.got_ref.own_got_ref = f32[72,512]{1,0:T(8,128)S(1)} collective-permute-done((f32[72,512]{1,0:T(8,128)S(1)}, f32[72,512]{1,0:T(8,128)S(1)}, u32[]{:S(2)}, u32[]{:S(2)}) %collective-permute-start.12) | collective-permute-done | bytes 147488 | tf_op jit(solution)/shard_map/ppermute | solution.py:39
  63.1 0.8 own_merge.1
  64.0 6.0 %side_corr.1 = (f32[4,128,512]{2,1,0:T(8,128)S(1)}, f32[4,128,512]{2,1,0:T(8,128)S(1)}) custom-call(s32[2]{0:T(128)S(1)} %pad_add_fusion.at_ref, f32[1024,512]{1,0:T(8,128)S(1)} %copy-done.1, f32[1024,512]{1,0:T(8,128)} %collective-permute-done.prev_ref.refs_4_, f32[1024,512]{1,0:T(8,128)} %collective-permute-done.1.next_ref.refs_5_, ...), custom_call_target="tpu_custom_call" | custom-call | flops 1 | bytes 1 | tf_op jit(solution)/shard_map/side_corr/pallas_call | solution.py:187
  70.0 0.6 collective-permute-start.13
  70.6 1.5 collective-permute-start.18
  72.0 0.8 collective-permute-done.13.got_ref
  73.0 1.3 collective-permute-start.14
  74.3 2.5 %collective-permute-start.15 = (f32[128,512]{1,0:T(8,128)S(1)}, f32[128,512]{1,0:T(8,128)S(1)}, u32[]{:S(2)}, u32[]{:S(2)}) collective-permute-start(f32[128,512]{1,0:T(8,128)S(1)} %get-tuple-element.49), channel_id=1, source_target_pairs={{0,4},{1,5},{2,6},{3,7},{4,0},{5,1},{6,2},{7,3},{8,12},{9,13},{10,... | collective-permute-start | bytes 786440 | tf_op jit(solution)/shard_map/ppermute | solution.py:44
  76.7 1.2 collective-permute-start.16
  77.9 3.9 %collective-permute-done.14.refs_1_ = f32[128,512]{1,0:T(8,128)S(1)} collective-permute-done((f32[128,512]{1,0:T(8,128)S(1)}, f32[128,512]{1,0:T(8,128)S(1)}, u32[]{:S(2)}, u32[]{:S(2)}) %collective-permute-start.14) | collective-permute-done | bytes 262176 | tf_op jit(solution)/shard_map/ppermute | solution.py:44
  81.8 6.6 %collective-permute-done.15.refs_2_ = f32[128,512]{1,0:T(8,128)S(1)} collective-permute-done((f32[128,512]{1,0:T(8,128)S(1)}, f32[128,512]{1,0:T(8,128)S(1)}, u32[]{:S(2)}, u32[]{:S(2)}) %collective-permute-start.15) | collective-permute-done | bytes 262176 | tf_op jit(solution)/shard_map/ppermute | solution.py:44
  88.6 2.7 %collective-permute-start.24 = (f32[64,512]{1,0:T(8,128)S(1)}, f32[64,512]{1,0:T(8,128)S(1)}, u32[]{:S(2)}, u32[]{:S(2)}) collective-permute-start(f32[64,512]{1,0:T(8,128)S(1)} %get-tuple-element.56.refs_0_), channel_id=1, source_target_pairs={{0,6},{1,7},{2,0},{3,1},{4,2},{5,3},{6,4},{7,5},{8,14},{9,15},{10,... | collective-permute-start | bytes 393224 | tf_op jit(solution)/shard_map/ppermute | solution.py:44
  91.4 0.5 collective-permute-start.22
  92.0 5.3 %collective-permute-done.17.got_ref = f32[144,512]{1,0:T(8,128)S(1)} collective-permute-done((f32[144,512]{1,0:T(8,128)S(1)}, f32[144,512]{1,0:T(8,128)S(1)}, u32[]{:S(2)}, u32[]{:S(2)}) %collective-permute-start.17) | collective-permute-done | bytes 294944 | tf_op jit(solution)/shard_map/ppermute | solution.py:39
  97.3 0.9 side_merge.1
  98.3 1.9 %collective-permute-done.22.refs_1_ = f32[64,512]{1,0:T(8,128)S(1)} collective-permute-done((f32[64,512]{1,0:T(8,128)S(1)}, f32[64,512]{1,0:T(8,128)S(1)}, u32[]{:S(2)}, u32[]{:S(2)}) %collective-permute-start.22) | collective-permute-done | bytes 131104 | tf_op jit(solution)/shard_map/ppermute | solution.py:44
  100.3 1.2 collective-permute-start.25
  101.5 3.6 %collective-permute-start.21 = (f32[64,512]{1,0:T(8,128)S(1)}, f32[64,512]{1,0:T(8,128)S(1)}, u32[]{:S(2)}, u32[]{:S(2)}) collective-permute-start(f32[64,512]{1,0:T(8,128)S(1)} %get-tuple-element.53.refs_4_.refs_0_), channel_id=1, source_target_pairs={{0,240},{16,0},{32,16},{48,32},{64,48},{80,64},{96,80},{112,96},{1... | collective-permute-start | bytes 393224 | tf_op jit(solution)/shard_map/ppermute | solution.py:31
  105.1 3.6 %collective-permute-done.20.refs_2_ = f32[64,512]{1,0:T(8,128)S(1)} collective-permute-done((f32[64,512]{1,0:T(8,128)S(1)}, f32[64,512]{1,0:T(8,128)S(1)}, u32[]{:S(2)}, u32[]{:S(2)}) %collective-permute-start.20) | collective-permute-done | bytes 131104 | tf_op jit(solution)/shard_map/ppermute | solution.py:31
  108.7 1.0 collective-permute-start.29
  109.7 3.6 %collective-permute-start.34 = (f32[640,512]{1,0:T(8,128)S(1)}, f32[640,512]{1,0:T(8,128)S(1)}, u32[]{:S(2)}, u32[]{:S(2)}) collective-permute-start(f32[640,512]{1,0:T(8,128)S(1)} %get-tuple-element.67), channel_id=1, source_target_pairs={{0,240},{16,0},{32,16},{48,32},{64,48},{80,64},{96,80},{112,96},{1... | collective-permute-start | bytes 3932168 | tf_op jit(solution)/shard_map/ppermute | solution.py:31
  113.3 1.7 %collective-permute-start.28 = (f32[4,64,512]{2,1,0:T(8,128)S(1)}, f32[4,64,512]{2,1,0:T(8,128)S(1)}, u32[]{:S(2)}, u32[]{:S(2)}) collective-permute-start(f32[4,64,512]{2,1,0:T(8,128)S(1)} %get-tuple-element.57.refs_0_), channel_id=1, source_target_pairs={{0,6},{1,7},{2,0},{3,1},{4,2},{5,3},{6,4},{7,5},{8,14},{9,15},{10,... | collective-permute-start | bytes 1572872 | tf_op jit(solution)/shard_map/ppermute | solution.py:44
  115.3 0.6 collective-permute-start.26
  115.9 10.5 %collective-permute-done.28.refs_3_ = f32[4,64,512]{2,1,0:T(8,128)S(1)} collective-permute-done((f32[4,64,512]{2,1,0:T(8,128)S(1)}, f32[4,64,512]{2,1,0:T(8,128)S(1)}, u32[]{:S(2)}, u32[]{:S(2)}) %collective-permute-start.28) | collective-permute-done | bytes 524320 | tf_op jit(solution)/shard_map/ppermute | solution.py:44
  126.4 12.0 %collective-permute-start.32 = (f32[4,64,512]{2,1,0:T(8,128)S(1)}, f32[4,64,512]{2,1,0:T(8,128)S(1)}, u32[]{:S(2)}, u32[]{:S(2)}) collective-permute-start(f32[4,64,512]{2,1,0:T(8,128)S(1)} %collective-permute-done.28.refs_3_), channel_id=1, source_target_pairs={{0,1},{1,0},{2,3},{3,2},{4,5},{5,4},{6,7},{7,6},{8,9},{9,8},{10,11... | collective-permute-start | bytes 1572872 | tf_op jit(solution)/shard_map/ppermute | solution.py:35
  138.4 3.2 %collective-permute-done.26.refs_1_ = f32[4,64,512]{2,1,0:T(8,128)S(1)} collective-permute-done((f32[4,64,512]{2,1,0:T(8,128)S(1)}, f32[4,64,512]{2,1,0:T(8,128)S(1)}, u32[]{:S(2)}, u32[]{:S(2)}) %collective-permute-start.26) | collective-permute-done | bytes 524320 | tf_op jit(solution)/shard_map/ppermute | solution.py:44
  142.1 6.4 %own_grad.1 = (f32[1024,512]{1,0:T(8,128)S(1)}, f32[1024,512]{1,0:T(8,128)S(1)}, f32[8,512]{1,0:T(8,128)S(1)}) custom-call(s32[2]{0:T(128)S(1)} %pad_add_fusion.at_ref, f32[4,64,512]{2,1,0:T(8,128)S(1)} %pack.2.mine_ref, f32[4,64,512]{2,1,0:T(8,128)S(1)} %collective-permute-done.25.refs_5_.other_ref, f32[1024,512]{1,0:T(8,128)} %refs_2_.3, ...), custom_call_target="tpu_custom_call" | custom-call | flops 1 | bytes 1 | tf_op jit(solution)/shard_map/own_grad/pallas_call | solution.py:399
  148.5 4.1 %prep.1 = (bf16[3072,512]{1,0:T(8,128)(2,1)}, bf16[3072,512]{1,0:T(8,128)(2,1)}, f32[8,512]{1,0:T(8,128)S(1)}) custom-call(s32[2]{0:T(128)S(1)} %pad_add_fusion.at_ref, f32[4,64,512]{2,1,0:T(8,128)S(1)} %get-tuple-element.57.refs_0_, f32[4,64,512]{2,1,0:T(8,128)S(1)} %collective-permute-done.26.refs_1_, f32[4,64,512]{2,1,0:T(8,128)S(1)} %collective-permute-done.27.refs_2_, ...), custom_call_target="tpu_custom_call" | custom-call | flops 1 | bytes 1 | tf_op jit(solution)/shard_map/prep/pallas_call | solution.py:452
  152.7 7.3 %finish.2 = (f32[1024,512]{1,0:T(8,128)}, f32[1024,512]{1,0:T(8,128)}) custom-call(bf16[3072,512]{1,0:T(8,128)(2,1)} %get-tuple-element.62.pt_ref, bf16[3072,512]{1,0:T(8,128)(2,1)} %get-tuple-element.63.p_ref, f32[8,512]{1,0:T(8,128)S(1)} %get-tuple-element.64.vec_ref, f32[8,512]{1,0:T(8,128)S(1)} %get-tuple-element.60.facts_ref.f_ref, ...), custom_call_target="tpu_custom_call" | custom-call | flops 1 | bytes 1 | tf_op jit(solution)/shard_map/finish/pallas_call | solution.py:485
  160.0 9.9 %finish.3 = (f32[1024,512]{1,0:T(8,128)}, f32[1024,512]{1,0:T(8,128)}) custom-call(bf16[3072,512]{1,0:T(8,128)(2,1)} %get-tuple-element.62.pt_ref, bf16[3072,512]{1,0:T(8,128)(2,1)} %get-tuple-element.63.p_ref, f32[8,512]{1,0:T(8,128)S(1)} %get-tuple-element.64.vec_ref, ...), custom_call_target="tpu_custom_call", output_to_operand_aliasing={{0}: (14, {}), {1}: (15, {})} | custom-call | flops 1 | bytes 1 | tf_op jit(solution)/shard_map/finish/pallas_call | solution.py:485
  (47 shorter events, 2.0 us)
Async XLA Ops:
  0.6 63.4 %collective-permute-start.1 = (f32[1024,512]{1,0:T(8,128)}, f32[1024,512]{1,0:T(8,128)}, u32[]{:S(2)}, u32[]{:S(2)}) collective-permute-start(f32[1024,512]{1,0:T(8,128)} %refs_3_.3), channel_id=1, source_target_pairs={{0,240},{16,0},{32,16},{48,32},{64,48},{80,64},{96,80},{112,96},{1... | collective-permute-start | bytes 6291464 | tf_op jit(solution)/shard_map/ppermute | solution.py:31
  8.1 55.9 %collective-permute-start = (f32[1024,512]{1,0:T(8,128)}, f32[1024,512]{1,0:T(8,128)}, u32[]{:S(2)}, u32[]{:S(2)}) collective-permute-start(f32[1024,512]{1,0:T(8,128)} %refs_3_.3), channel_id=1, source_target_pairs={{0,16},{16,32},{32,48},{48,64},{64,80},{80,96},{96,112},{112,128},... | collective-permute-start | bytes 6291464 | tf_op jit(solution)/shard_map/ppermute | solution.py:31
  8.1 1.6 copy-start
  9.7 1.6 copy-start.2
  11.3 9.7 %copy-start.1 = (f32[1024,512]{1,0:T(8,128)S(1)}, f32[1024,512]{1,0:T(8,128)}, u32[]{:S(2)}) copy-start(f32[1024,512]{1,0:T(8,128)} %refs_2_.3) | copy-start | bytes 6291460
  11.9 1.9 %collective-permute-start.2 = (f32[8,512]{1,0:T(8,128)S(1)}, f32[8,512]{1,0:T(8,128)S(1)}, u32[]{:S(2)}, u32[]{:S(2)}) collective-permute-start(f32[8,512]{1,0:T(8,128)S(1)} %sums.1), channel_id=1, source_target_pairs={{0,1},{1,0},{2,3},{3,2},{4,5},{5,4},{6,7},{7,6},{8,9},{9,8},{10,11... | collective-permute-start | bytes 49160 | tf_op jit(solution)/shard_map/ppermute | solution.py:35
  13.8 3.7 %collective-permute-start.5 = (f32[8,512]{1,0:T(8,128)S(1)}, f32[8,512]{1,0:T(8,128)S(1)}, u32[]{:S(2)}, u32[]{:S(2)}) collective-permute-start(f32[8,512]{1,0:T(8,128)S(1)} %add.3.refs_0_), channel_id=1, source_target_pairs={{0,6},{1,7},{2,0},{3,1},{4,2},{5,3},{6,4},{7,5},{8,14},{9,15},{10,... | collective-permute-start | bytes 49160 | tf_op jit(solution)/shard_map/ppermute | solution.py:44
  16.3 4.5 %collective-permute-start.4 = (f32[8,512]{1,0:T(8,128)S(1)}, f32[8,512]{1,0:T(8,128)S(1)}, u32[]{:S(2)}, u32[]{:S(2)}) collective-permute-start(f32[8,512]{1,0:T(8,128)S(1)} %add.3.refs_0_), channel_id=1, source_target_pairs={{0,4},{1,5},{2,6},{3,7},{4,0},{5,1},{6,2},{7,3},{8,12},{9,13},{10,... | collective-permute-start | bytes 49160 | tf_op jit(solution)/shard_map/ppermute | solution.py:44
  16.8 4.2 %collective-permute-start.3 = (f32[8,512]{1,0:T(8,128)S(1)}, f32[8,512]{1,0:T(8,128)S(1)}, u32[]{:S(2)}, u32[]{:S(2)}) collective-permute-start(f32[8,512]{1,0:T(8,128)S(1)} %add.3.refs_0_), channel_id=1, source_target_pairs={{0,2},{1,3},{2,4},{3,5},{4,6},{5,7},{6,0},{7,1},{8,10},{9,11},{10,... | collective-permute-start | bytes 49160 | tf_op jit(solution)/shard_map/ppermute | solution.py:44
  28.0 3.3 %collective-permute-start.8 = (f32[4,64,512]{2,1,0:T(8,128)S(1)}, f32[4,64,512]{2,1,0:T(8,128)S(1)}, u32[]{:S(2)}, u32[]{:S(2)}) collective-permute-start(f32[4,64,512]{2,1,0:T(8,128)S(1)} %get-tuple-element.38), channel_id=1, source_target_pairs={{0,1},{1,0},{2,3},{3,2},{4,5},{5,4},{6,7},{7,6},{8,9},{9,8},{10,11... | collective-permute-start | bytes 1572872 | tf_op jit(solution)/shard_map/ppermute | solution.py:35
  31.3 9.0 %collective-permute-start.9 = (f32[64,512]{1,0:T(8,128)S(1)}, f32[64,512]{1,0:T(8,128)S(1)}, u32[]{:S(2)}, u32[]{:S(2)}) collective-permute-start(f32[64,512]{1,0:T(8,128)S(1)} %get-tuple-element.40), channel_id=1, source_target_pairs={{0,2},{1,3},{2,4},{3,5},{4,6},{5,7},{6,0},{7,1},{8,10},{9,11},{10,... | collective-permute-start | bytes 393224 | tf_op jit(solution)/shard_map/ppermute | solution.py:44
  31.4 8.9 %collective-permute-start.10 = (f32[64,512]{1,0:T(8,128)S(1)}, f32[64,512]{1,0:T(8,128)S(1)}, u32[]{:S(2)}, u32[]{:S(2)}) collective-permute-start(f32[64,512]{1,0:T(8,128)S(1)} %get-tuple-element.41), channel_id=1, source_target_pairs={{0,4},{1,5},{2,6},{3,7},{4,0},{5,1},{6,2},{7,3},{8,12},{9,13},{10,... | collective-permute-start | bytes 393224 | tf_op jit(solution)/shard_map/ppermute | solution.py:44
  32.8 7.7 %collective-permute-start.11 = (f32[64,512]{1,0:T(8,128)S(1)}, f32[64,512]{1,0:T(8,128)S(1)}, u32[]{:S(2)}, u32[]{:S(2)}) collective-permute-start(f32[64,512]{1,0:T(8,128)S(1)} %get-tuple-element.42), channel_id=1, source_target_pairs={{0,6},{1,7},{2,0},{3,1},{4,2},{5,3},{6,4},{7,5},{8,14},{9,15},{10,... | collective-permute-start | bytes 393224 | tf_op jit(solution)/shard_map/ppermute | solution.py:44
  40.5 22.6 %collective-permute-start.12 = (f32[72,512]{1,0:T(8,128)S(1)}, f32[72,512]{1,0:T(8,128)S(1)}, u32[]{:S(2)}, u32[]{:S(2)}) collective-permute-start(f32[72,512]{1,0:T(8,128)S(1)} %message.2.mine_ref.own_ref), channel_id=1, source_target_pairs={{0,8},{1,9},{2,10},{3,11},{4,12},{5,13},{6,14},{7,15},{8,0},{9,1},... | collective-permute-start | bytes 442376 | tf_op jit(solution)/shard_map/ppermute | solution.py:39
  43.2 20.7 %collective-permute-start.7 = (f32[8,512]{1,0:T(8,128)S(1)}, f32[8,512]{1,0:T(8,128)S(1)}, u32[]{:S(2)}, u32[]{:S(2)}) collective-permute-start(f32[8,512]{1,0:T(8,128)S(1)} %get-tuple-element.36.refs_4_.f_ref), channel_id=1, source_target_pairs={{0,240},{16,0},{32,16},{48,32},{64,48},{80,64},{96,80},{112,96},{1... | collective-permute-start | bytes 49160 | tf_op jit(solution)/shard_map/ppermute | solution.py:31
  46.5 17.5 %collective-permute-start.6 = (f32[8,512]{1,0:T(8,128)S(1)}, f32[8,512]{1,0:T(8,128)S(1)}, u32[]{:S(2)}, u32[]{:S(2)}) collective-permute-start(f32[8,512]{1,0:T(8,128)S(1)} %get-tuple-element.36.refs_4_.f_ref), channel_id=1, source_target_pairs={{0,16},{16,32},{32,48},{48,64},{64,80},{80,96},{96,112},{112,128},... | collective-permute-start | bytes 49160 | tf_op jit(solution)/shard_map/ppermute | solution.py:31
  70.0 2.9 %collective-permute-start.13 = (f32[4,128,512]{2,1,0:T(8,128)S(1)}, f32[4,128,512]{2,1,0:T(8,128)S(1)}, u32[]{:S(2)}, u32[]{:S(2)}) collective-permute-start(f32[4,128,512]{2,1,0:T(8,128)S(1)} %get-tuple-element.46), channel_id=1, source_target_pairs={{0,1},{1,0},{2,3},{3,2},{4,5},{5,4},{6,7},{7,6},{8,9},{9,8},{10,11... | collective-permute-start | bytes 3145736 | tf_op jit(solution)/shard_map/ppermute | solution.py:35
  70.6 20.9 %collective-permute-start.19 = (f32[384,512]{1,0:T(8,128)S(1)}, f32[384,512]{1,0:T(8,128)S(1)}, u32[]{:S(2)}, u32[]{:S(2)}) collective-permute-start(f32[384,512]{1,0:T(8,128)S(1)} %get-tuple-element.52), channel_id=1, source_target_pairs={{0,240},{16,0},{32,16},{48,32},{64,48},{80,64},{96,80},{112,96},{1... | collective-permute-start | bytes 2359304 | tf_op jit(solution)/shard_map/ppermute | solution.py:31
  70.6 21.4 %collective-permute-start.18 = (f32[384,512]{1,0:T(8,128)S(1)}, f32[384,512]{1,0:T(8,128)S(1)}, u32[]{:S(2)}, u32[]{:S(2)}) collective-permute-start(f32[384,512]{1,0:T(8,128)S(1)} %get-tuple-element.52), channel_id=1, source_target_pairs={{0,16},{16,32},{32,48},{48,64},{64,80},{80,96},{96,112},{112,128},... | collective-permute-start | bytes 2359304 | tf_op jit(solution)/shard_map/ppermute | solution.py:31
  73.0 8.8 %collective-permute-start.14 = (f32[128,512]{1,0:T(8,128)S(1)}, f32[128,512]{1,0:T(8,128)S(1)}, u32[]{:S(2)}, u32[]{:S(2)}) collective-permute-start(f32[128,512]{1,0:T(8,128)S(1)} %get-tuple-element.48), channel_id=1, source_target_pairs={{0,2},{1,3},{2,4},{3,5},{4,6},{5,7},{6,0},{7,1},{8,10},{9,11},{10,... | collective-permute-start | bytes 786440 | tf_op jit(solution)/shard_map/ppermute | solution.py:44
  74.3 14.1 %collective-permute-start.15 = (f32[128,512]{1,0:T(8,128)S(1)}, f32[128,512]{1,0:T(8,128)S(1)}, u32[]{:S(2)}, u32[]{:S(2)}) collective-permute-start(f32[128,512]{1,0:T(8,128)S(1)} %get-tuple-element.49), channel_id=1, source_target_pairs={{0,4},{1,5},{2,6},{3,7},{4,0},{5,1},{6,2},{7,3},{8,12},{9,13},{10,... | collective-permute-start | bytes 786440 | tf_op jit(solution)/shard_map/ppermute | solution.py:44
  76.7 11.7 %collective-permute-start.16 = (f32[128,512]{1,0:T(8,128)S(1)}, f32[128,512]{1,0:T(8,128)S(1)}, u32[]{:S(2)}, u32[]{:S(2)}) collective-permute-start(f32[128,512]{1,0:T(8,128)S(1)} %get-tuple-element.50), channel_id=1, source_target_pairs={{0,6},{1,7},{2,0},{3,1},{4,2},{5,3},{6,4},{7,5},{8,14},{9,15},{10,... | collective-permute-start | bytes 786440 | tf_op jit(solution)/shard_map/ppermute | solution.py:44
  88.4 8.9 %collective-permute-start.17 = (f32[144,512]{1,0:T(8,128)S(1)}, f32[144,512]{1,0:T(8,128)S(1)}, u32[]{:S(2)}, u32[]{:S(2)}) collective-permute-start(f32[144,512]{1,0:T(8,128)S(1)} %get-tuple-element.51.mine_ref), channel_id=1, source_target_pairs={{0,8},{1,9},{2,10},{3,11},{4,12},{5,13},{6,14},{7,15},{8,0},{9,1},... | collective-permute-start | bytes 884744 | tf_op jit(solution)/shard_map/ppermute | solution.py:39
  88.6 9.7 %collective-permute-start.24 = (f32[64,512]{1,0:T(8,128)S(1)}, f32[64,512]{1,0:T(8,128)S(1)}, u32[]{:S(2)}, u32[]{:S(2)}) collective-permute-start(f32[64,512]{1,0:T(8,128)S(1)} %get-tuple-element.56.refs_0_), channel_id=1, source_target_pairs={{0,6},{1,7},{2,0},{3,1},{4,2},{5,3},{6,4},{7,5},{8,14},{9,15},{10,... | collective-permute-start | bytes 393224 | tf_op jit(solution)/shard_map/ppermute | solution.py:44
  91.3 7.0 %collective-permute-start.23 = (f32[64,512]{1,0:T(8,128)S(1)}, f32[64,512]{1,0:T(8,128)S(1)}, u32[]{:S(2)}, u32[]{:S(2)}) collective-permute-start(f32[64,512]{1,0:T(8,128)S(1)} %get-tuple-element.56.refs_0_), channel_id=1, source_target_pairs={{0,4},{1,5},{2,6},{3,7},{4,0},{5,1},{6,2},{7,3},{8,12},{9,13},{10,... | collective-permute-start | bytes 393224 | tf_op jit(solution)/shard_map/ppermute | solution.py:44
  91.4 8.8 %collective-permute-start.22 = (f32[64,512]{1,0:T(8,128)S(1)}, f32[64,512]{1,0:T(8,128)S(1)}, u32[]{:S(2)}, u32[]{:S(2)}) collective-permute-start(f32[64,512]{1,0:T(8,128)S(1)} %get-tuple-element.56.refs_0_), channel_id=1, source_target_pairs={{0,2},{1,3},{2,4},{3,5},{4,6},{5,7},{6,0},{7,1},{8,10},{9,11},{10,... | collective-permute-start | bytes 393224 | tf_op jit(solution)/shard_map/ppermute | solution.py:44
  100.3 8.4 %collective-permute-start.25 = (f32[4,64,512]{2,1,0:T(8,128)S(1)}, f32[4,64,512]{2,1,0:T(8,128)S(1)}, u32[]{:S(2)}, u32[]{:S(2)}) collective-permute-start(f32[4,64,512]{2,1,0:T(8,128)S(1)} %pack.2.mine_ref), channel_id=1, source_target_pairs={{0,1},{1,0},{2,3},{3,2},{4,5},{5,4},{6,7},{7,6},{8,9},{9,8},{10,11... | collective-permute-start | bytes 1572872 | tf_op jit(solution)/shard_map/ppermute | solution.py:35
  101.5 7.2 %collective-permute-start.20 = (f32[64,512]{1,0:T(8,128)S(1)}, f32[64,512]{1,0:T(8,128)S(1)}, u32[]{:S(2)}, u32[]{:S(2)}) collective-permute-start(f32[64,512]{1,0:T(8,128)S(1)} %get-tuple-element.54.refs_1_), channel_id=1, source_target_pairs={{0,16},{16,32},{32,48},{48,64},{64,80},{80,96},{96,112},{112,128},... | collective-permute-start | bytes 393224 | tf_op jit(solution)/shard_map/ppermute | solution.py:31
  101.5 7.2 %collective-permute-start.21 = (f32[64,512]{1,0:T(8,128)S(1)}, f32[64,512]{1,0:T(8,128)S(1)}, u32[]{:S(2)}, u32[]{:S(2)}) collective-permute-start(f32[64,512]{1,0:T(8,128)S(1)} %get-tuple-element.53.refs_4_.refs_0_), channel_id=1, source_target_pairs={{0,240},{16,0},{32,16},{48,32},{64,48},{80,64},{96,80},{112,96},{1... | collective-permute-start | bytes 393224 | tf_op jit(solution)/shard_map/ppermute | solution.py:31
  108.7 6.6 %collective-permute-start.29 = (f32[4,64,512]{2,1,0:T(8,128)S(1)}, f32[4,64,512]{2,1,0:T(8,128)S(1)}, u32[]{:S(2)}, u32[]{:S(2)}) collective-permute-start(f32[4,64,512]{2,1,0:T(8,128)S(1)} %get-tuple-element.57.refs_0_), channel_id=1, source_target_pairs={{0,1},{1,0},{2,3},{3,2},{4,5},{5,4},{6,7},{7,6},{8,9},{9,8},{10,11... | collective-permute-start | bytes 1572872 | tf_op jit(solution)/shard_map/ppermute | solution.py:35
  109.7 50.3 %collective-permute-start.34 = (f32[640,512]{1,0:T(8,128)S(1)}, f32[640,512]{1,0:T(8,128)S(1)}, u32[]{:S(2)}, u32[]{:S(2)}) collective-permute-start(f32[640,512]{1,0:T(8,128)S(1)} %get-tuple-element.67), channel_id=1, source_target_pairs={{0,240},{16,0},{32,16},{48,32},{64,48},{80,64},{96,80},{112,96},{1... | collective-permute-start | bytes 3932168 | tf_op jit(solution)/shard_map/ppermute | solution.py:31
  113.3 46.7 %collective-permute-start.33 = (f32[640,512]{1,0:T(8,128)S(1)}, f32[640,512]{1,0:T(8,128)S(1)}, u32[]{:S(2)}, u32[]{:S(2)}) collective-permute-start(f32[640,512]{1,0:T(8,128)S(1)} %get-tuple-element.67), channel_id=1, source_target_pairs={{0,16},{16,32},{32,48},{48,64},{64,80},{80,96},{96,112},{112,128},... | collective-permute-start | bytes 3932168 | tf_op jit(solution)/shard_map/ppermute | solution.py:31
  113.3 13.2 %collective-permute-start.28 = (f32[4,64,512]{2,1,0:T(8,128)S(1)}, f32[4,64,512]{2,1,0:T(8,128)S(1)}, u32[]{:S(2)}, u32[]{:S(2)}) collective-permute-start(f32[4,64,512]{2,1,0:T(8,128)S(1)} %get-tuple-element.57.refs_0_), channel_id=1, source_target_pairs={{0,6},{1,7},{2,0},{3,1},{4,2},{5,3},{6,4},{7,5},{8,14},{9,15},{10,... | collective-permute-start | bytes 1572872 | tf_op jit(solution)/shard_map/ppermute | solution.py:44
  115.0 23.4 %collective-permute-start.27 = (f32[4,64,512]{2,1,0:T(8,128)S(1)}, f32[4,64,512]{2,1,0:T(8,128)S(1)}, u32[]{:S(2)}, u32[]{:S(2)}) collective-permute-start(f32[4,64,512]{2,1,0:T(8,128)S(1)} %get-tuple-element.57.refs_0_), channel_id=1, source_target_pairs={{0,4},{1,5},{2,6},{3,7},{4,0},{5,1},{6,2},{7,3},{8,12},{9,13},{10,... | collective-permute-start | bytes 1572872 | tf_op jit(solution)/shard_map/ppermute | solution.py:44
  115.3 26.3 %collective-permute-start.26 = (f32[4,64,512]{2,1,0:T(8,128)S(1)}, f32[4,64,512]{2,1,0:T(8,128)S(1)}, u32[]{:S(2)}, u32[]{:S(2)}) collective-permute-start(f32[4,64,512]{2,1,0:T(8,128)S(1)} %get-tuple-element.57.refs_0_), channel_id=1, source_target_pairs={{0,2},{1,3},{2,4},{3,5},{4,6},{5,7},{6,0},{7,1},{8,10},{9,11},{10,... | collective-permute-start | bytes 1572872 | tf_op jit(solution)/shard_map/ppermute | solution.py:44
  126.4 22.1 %collective-permute-start.32 = (f32[4,64,512]{2,1,0:T(8,128)S(1)}, f32[4,64,512]{2,1,0:T(8,128)S(1)}, u32[]{:S(2)}, u32[]{:S(2)}) collective-permute-start(f32[4,64,512]{2,1,0:T(8,128)S(1)} %collective-permute-done.28.refs_3_), channel_id=1, source_target_pairs={{0,1},{1,0},{2,3},{3,2},{4,5},{5,4},{6,7},{7,6},{8,9},{9,8},{10,11... | collective-permute-start | bytes 1572872 | tf_op jit(solution)/shard_map/ppermute | solution.py:35
  138.4 10.1 %collective-permute-start.31 = (f32[4,64,512]{2,1,0:T(8,128)S(1)}, f32[4,64,512]{2,1,0:T(8,128)S(1)}, u32[]{:S(2)}, u32[]{:S(2)}) collective-permute-start(f32[4,64,512]{2,1,0:T(8,128)S(1)} %collective-permute-done.27.refs_2_), channel_id=1, source_target_pairs={{0,1},{1,0},{2,3},{3,2},{4,5},{5,4},{6,7},{7,6},{8,9},{9,8},{10,11... | collective-permute-start | bytes 1572872 | tf_op jit(solution)/shard_map/ppermute | solution.py:35
  141.6 6.9 %collective-permute-start.30 = (f32[4,64,512]{2,1,0:T(8,128)S(1)}, f32[4,64,512]{2,1,0:T(8,128)S(1)}, u32[]{:S(2)}, u32[]{:S(2)}) collective-permute-start(f32[4,64,512]{2,1,0:T(8,128)S(1)} %collective-permute-done.26.refs_1_), channel_id=1, source_target_pairs={{0,1},{1,0},{2,3},{3,2},{4,5},{5,4},{6,7},{7,6},{8,9},{9,8},{10,11... | collective-permute-start | bytes 1572872 | tf_op jit(solution)/shard_map/ppermute | solution.py:35
  148.5 4.2 %copy-start.3 = (f32[1024,512]{1,0:T(8,128)}, f32[1024,512]{1,0:T(8,128)S(1)}, u32[]{:S(2)}) copy-start(f32[1024,512]{1,0:T(8,128)S(1)} %get-tuple-element.66.refs_1_) | copy-start | bytes 6291460

commit v3 on v2

--- a/solution.py
+++ b/solution.py
@@ -16,10 +16,13 @@
 any_spec = pl.BlockSpec(memory_space=pl.ANY)
 smem_spec = pl.BlockSpec(memory_space=pltpu.SMEM)
 vmem_spec = pl.BlockSpec(memory_space=pltpu.VMEM)
-params = pltpu.CompilerParams(vmem_limit_bytes=48 * 1024 * 1024)
 cheap = pl.CostEstimate(flops=1, transcendentals=0, bytes_accessed=1)
-call = functools.partial(pl.pallas_call, compiler_params=params, cost_estimate=cheap)
-top_rows = 384
+top_rows = 256
+
+
+def call(kernel, mib=8, **rest):
+    params = pltpu.CompilerParams(vmem_limit_bytes=mib * 1024 * 1024)
+    return pl.pallas_call(kernel, compiler_params=params, cost_estimate=cheap, **rest)
 
 
 def shape(*dims):
@@ -138,7 +141,7 @@
 
 def own_corr(at, a, b, parts, half_rows):
     rows, width = a.shape
-    tile = 128
+    tile = 256
     steps, top_steps = rows // tile, top_rows // tile
     spec = pl.BlockSpec((tile, width), lambda i: (i, 0))
     top_spec = pl.BlockSpec((tile, width), lambda i: (jnp.minimum(i, top_steps - 1), 0))
@@ -153,6 +156,7 @@
         out_shape=[shape(top_rows, width), shape(rows - top_rows, width), shape(8, width)]
         + [shape(4, width // 8, width)] * 2,
         scratch_shapes=[pltpu.VMEM((width, width), f32)],
+        mib=16,
         name="own_corr",
     )(at, a, b, *parts)
 
@@ -191,6 +195,7 @@
         out_specs=[slots, slots],
         out_shape=[shape(4, width // 4, width)] * 2,
         scratch_shapes=[pltpu.VMEM((width, width), f32)] * 2,
+        mib=24,
         name="side_corr",
     )(at, a, prev_b, next_b, facts, prev_facts, next_facts, *wait_for)
 
@@ -267,7 +272,8 @@
     return cols_ref[pl.ds(first, rows), :]
 
 
-def own_merge_kernel(half_rows, at_ref, mine_ref, got_ref, _, chunk_ref, full_ref, __, cols_ref):
+def own_merge_kernel(half_rows, at_ref, mine_ref, got_ref, *refs):
+    chunk_ref, full_ref, _, cols_ref = refs[-4:]
     rows = chunk_ref.shape[0]
     mine, other = mine_ref[rows:, :], got_ref[rows:, :]
     full = full_facts(mine, other)
@@ -279,21 +285,21 @@
     )
 
 
-def own_merge(at, mine, got, carried, half_rows):
+def own_merge(at, mine, got, carried, half_rows, wait_for):
     rows, width = mine.shape
     return call(
         functools.partial(own_merge_kernel, half_rows),
-        in_specs=[smem_spec, vmem_spec, vmem_spec, any_spec],
+        in_specs=[smem_spec, vmem_spec, vmem_spec, any_spec] + [any_spec] * len(wait_for),
         out_specs=[vmem_spec, vmem_spec, any_spec],
         out_shape=[shape(rows - 8, width), shape(8, width), shape(*carried.shape)],
         input_output_aliases={3: 2},
         scratch_shapes=[pltpu.VMEM((width, 128), f32)],
         name="own_merge",
-    )(at, mine, got, carried)
+    )(at, mine, got, carried, *wait_for)
 
 
 def side_merge_kernel(half_rows, at_ref, mine_ref, got_ref, own_ref, own_got_ref, *refs):
-    left_ref, right_ref, pf_ref, nf_ref, cols_ref = refs[-5:]
+    left_ref, right_ref, both_ref, pf_ref, nf_ref, cols_ref = refs[-6:]
     rows = left_ref.shape[0]
     mine, other = own_ref[rows:, :], own_got_ref[rows:, :]
     cols = columns_of(at_ref, mine, other, full_facts(mine, other), cols_ref, rows)
@@ -304,7 +310,7 @@
         full = full_facts(b_mine, b_other)
         for i in range(8):
             facts_ref[i : i + 1, :] = full[i]
-        out_ref[...] = merged(
+        chunk = merged(
             mine_ref[first : first + rows, :],
             got_ref[first : first + rows, :],
             cols,
@@ -313,6 +319,8 @@
             full,
             half_rows,
         )
+        out_ref[...] = chunk
+        both_ref[first : first + rows, :] = chunk
 
 
 def side_merge(at, mine, got, own, own_got, half_rows, wait_for):
@@ -320,31 +328,46 @@
     return call(
         functools.partial(side_merge_kernel, half_rows),
         in_specs=[smem_spec] + [vmem_spec] * 4 + [any_spec] * len(wait_for),
-        out_specs=[vmem_spec] * 4,
-        out_shape=[shape(rows - 8, width)] * 2 + [shape(8, width)] * 2,
+        out_specs=[vmem_spec] * 5,
+        out_shape=[shape(rows - 8, width)] * 2
+        + [shape(2 * (rows - 8), width)]
+        + [shape(8, width)] * 2,
         scratch_shapes=[pltpu.VMEM((width, 128), f32)],
         name="side_merge",
     )(at, mine, got, own, own_got, *wait_for)
 
 
-def pack(parts, carried=None, wait_for=()):
+def pack(parts, wait_for=()):
     rows, width = parts[0].shape
-    more = [] if carried is None else [carried]
-    at_out = 4 + len(more) + len(wait_for)
 
     def kernel(*refs):
         for i in range(4):
-            refs[at_out][i] = refs[i][...]
-
-    out = call(
+            refs[-1][i] = refs[i][...]
+
+    return call(
         kernel,
-        in_specs=[vmem_spec] * 4 + [any_spec] * (len(more) + len(wait_for)),
-        out_specs=[vmem_spec] + [any_spec] * len(more),
-        out_shape=[shape(4, rows, width)] + [shape(*c.shape) for c in more],
-        input_output_aliases={4: 1} if more else {},
+        in_specs=[vmem_spec] * 4 + [any_spec] * len(wait_for),
+        out_specs=vmem_spec,
+        out_shape=shape(4, rows, width),
         name="pack",
-    )(*parts, *more, *wait_for)
-    return out[0] if carried is None else out
+    )(*parts, *wait_for)
+
+
+def join(first, second, carried, wait_for=()):
+    rows, width = first.shape
+
+    def kernel(first_ref, second_ref, *refs):
+        refs[-2][0:rows, :] = first_ref[...]
+        refs[-2][rows:, :] = second_ref[...]
+
+    return call(
+        kernel,
+        in_specs=[vmem_spec] * 2 + [any_spec] * (1 + len(wait_for)),
+        out_specs=[vmem_spec, any_spec],
+        out_shape=[shape(2 * rows, width), shape(*carried.shape)],
+        input_output_aliases={2: 1},
+        name="join",
+    )(first, second, carried, *wait_for)
 
 
 def row_of(at_ref, core_flip, slot, rows):
@@ -390,7 +413,7 @@
     gb_ref[...] = mm(thrice(norm_a), p_ref[...])
 
 
-def own_grad(at, mine, other, a, b, facts):
+def own_grad(at, mine, other, a, b, facts, wait_for):
     rows, width = b.shape
     steps = 4
     spec = pl.BlockSpec((rows // steps, width), lambda i: (i, 0))
@@ -399,7 +422,7 @@
     return call(
         own_grad_kernel,
         grid=(steps,),
-        in_specs=[smem_spec, slots, slots, spec, spec, whole],
+        in_specs=[smem_spec, slots, slots, spec, spec, whole] + [any_spec] * len(wait_for),
         out_specs=[spec, spec, whole],
         out_shape=[shape(rows, width)] * 2 + [shape(8, width)],
         scratch_shapes=[
@@ -407,90 +430,85 @@
             pltpu.VMEM((3 * width, width), bf16),
             pltpu.VMEM((3 * width, width), bf16),
         ],
+        mib=24,
         name="own_grad",
-    )(at, mine, other, a, b, facts)
-
-
-def prep_kernel(at_ref, *refs):
-    packs, refs = refs[:8], refs[8:]
-    pf_ref, nf_ref, sums_ref, pt_ref, p_ref, vec_ref, corr_ref = refs
+    )(at, mine, other, a, b, facts, *wait_for)
+
+
+def build(at_ref, mine_ref, other_ref, corr_ref, pen_ref, transposed):
+    rows = mine_ref.shape[1] // 2
     width = corr_ref.shape[1]
-    rows = packs[0].shape[1]
-    for flip in (0, 1):
+    for flip, ref in ((False, mine_ref), (True, other_ref)):
         for slot in range(4):
-            at = row_of(at_ref, flip == 1, slot, rows)
-            for kind in range(4):
-                corr_ref[kind, pl.ds(at, rows), :] = packs[4 * flip + slot][kind]
-    vec = sums_ref[0:4, :]
-    cross_a = vec[1:2]
-    cross_b = vec[3:4]
-    for kind in range(4):
-        corr = corr_ref[kind]
-        corr = corr.T if kind < 2 else corr
+            at = row_of(at_ref, flip, slot, rows)
+            for side in (0, 1):
+                corr_ref[side, pl.ds(at, rows), :] = ref[slot, side * rows : (side + 1) * rows, :]
+    cross = jnp.zeros((1, width), f32)
+    for side in (0, 1):
+        corr = corr_ref[side]
+        corr = corr.T if transposed else corr
         pen = 2.0 * off_weight * corr
-        cross = jnp.sum(pen * corr, axis=0, keepdims=True)
-        into = pt_ref if kind < 2 else p_ref
-        first = (kind % 2) * 3 * width
+        cross = cross + jnp.sum(pen * corr, axis=0, keepdims=True)
         high, low = split(pen)
-        into[first : first + width, :] = high
-        into[first + width : first + 2 * width, :] = low
-        into[first + 2 * width : first + 3 * width, :] = high
-        if kind < 2:
-            cross_a = cross_a + cross
-        else:
-            cross_b = cross_b + cross
-    left = jnp.concatenate([thrice(pf_ref[...]), thrice(nf_ref[...])], axis=1)
-    vec_ref[0:1, :] = vec[0:1] + mm(left, pt_ref[...])[5:6]
-    vec_ref[1:2, :] = cross_a
-    vec_ref[2:3, :] = vec[2:3] + mm(left, p_ref[...])[4:5]
-    vec_ref[3:4, :] = cross_b
-    vec_ref[4:8, :] = jnp.zeros((4, width), f32)
-
-
-def prep(at, packs, prev_facts, next_facts, sums):
-    width = sums.shape[1]
-    return call(
-        prep_kernel,
-        in_specs=[smem_spec] + [vmem_spec] * 11,
-        out_specs=[vmem_spec] * 3,
-        out_shape=[jax.ShapeDtypeStruct((6 * width, width), bf16)] * 2 + [shape(8, width)],
-        scratch_shapes=[pltpu.VMEM((4, width, width), f32)],
-        name="prep",
-    )(at, *packs, prev_facts, next_facts, sums)
-
-
-def finish_kernel(pt_ref, p_ref, vec_ref, f_ref, pf_ref, nf_ref, *refs):
-    ga_ref, gb_ref, a_ref, b_ref, pb_ref, nb_ref, pa_ref, xa_ref = refs[:8]
-    out_a_ref, out_b_ref = refs[-2:]
-    prev_b = (pb_ref[...] - pf_ref[2:3, :]) * pf_ref[3:4, :]
-    next_b = (nb_ref[...] - nf_ref[2:3, :]) * nf_ref[3:4, :]
-    ga = ga_ref[...] + mm(jnp.concatenate([thrice(prev_b), thrice(next_b)], axis=1), pt_ref[...])
-    norm_a = (a_ref[...] - f_ref[0:1, :]) * f_ref[1:2, :]
-    out_a_ref[...] = (ga - vec_ref[0:1, :] - norm_a * vec_ref[1:2, :]) * f_ref[1:2, :]
-    prev_a = pa_ref[...] * pf_ref[6:7, :] + pf_ref[7:8, :]
-    next_a = xa_ref[...] * nf_ref[6:7, :] + nf_ref[7:8, :]
-    gb = gb_ref[...] + mm(jnp.concatenate([thrice(prev_a), thrice(next_a)], axis=1), p_ref[...])
-    norm_b = (b_ref[...] - f_ref[2:3, :]) * f_ref[3:4, :]
-    out_b_ref[...] = (gb - vec_ref[2:3, :] - norm_b * vec_ref[3:4, :]) * f_ref[3:4, :]
-
-
-def finish(first, tile, mats, facts, whole_tiles, halo_tiles, partial=()):
-    rows, width = whole_tiles[0].shape
-    steps = halo_tiles[0].shape[0] // tile
-    at = pl.BlockSpec((pl.Element(tile), pl.Element(width)), lambda i: (pl.multiple_of(first + i * tile, 64), 0))
-    halo = pl.BlockSpec((tile, width), lambda i: (i, 0))
+        first = side * 3 * width
+        pen_ref[first : first + width, :] = high
+        pen_ref[first + width : first + 2 * width, :] = low
+        pen_ref[first + 2 * width : first + 3 * width, :] = high
+    return cross
+
+
+def finish_kernel(for_a, at_ref, mine_ref, other_ref, f_ref, pf_ref, nf_ref, sums_ref, *refs):
+    part_ref, view_ref = refs[:2]
+    out_ref, corr_ref, pen_ref, vec_ref = refs[-4:]
+    own = 0 if for_a else 2
+
+    @pl.when(pl.program_id(0) == 0)
+    def _():
+        cross = build(at_ref, mine_ref, other_ref, corr_ref, pen_ref, for_a)
+        left = jnp.concatenate([thrice(pf_ref[...]), thrice(nf_ref[...])], axis=1)
+        mean = 5 if for_a else 4
+        vec_ref[0:1, :] = sums_ref[own : own + 1, :] + mm(left, pen_ref[...])[mean : mean + 1]
+        vec_ref[1:2, :] = sums_ref[own + 1 : own + 2, :] + cross
+
+    if for_a:
+        prev = (refs[2][...] - pf_ref[2:3, :]) * pf_ref[3:4, :]
+        next_ = (refs[3][...] - nf_ref[2:3, :]) * nf_ref[3:4, :]
+    else:
+        in_top = pl.program_id(0) == 0
+        prev = jnp.where(in_top, refs[2][...], refs[3][...]) * pf_ref[6:7, :] + pf_ref[7:8, :]
+        next_ = jnp.where(in_top, refs[4][...], refs[5][...]) * nf_ref[6:7, :] + nf_ref[7:8, :]
+    both = jnp.concatenate([thrice(prev), thrice(next_)], axis=1)
+    grad = part_ref[...] + mm(both, pen_ref[...])
+    inverse = f_ref[own + 1 : own + 2, :]
+    normed = (view_ref[...] - f_ref[own : own + 1, :]) * inverse
+    out_ref[...] = (grad - vec_ref[0:1, :] - normed * vec_ref[1:2, :]) * inverse
+
+
+def finish(for_a, at, mine, other, facts, sums, part, view, halos):
+    rows, width = view.shape
+    tile = 256
+    spec = pl.BlockSpec((tile, width), lambda i: (i, 0))
+    top = pl.BlockSpec((tile, width), lambda i: (0, 0))
+    low = pl.BlockSpec((tile, width), lambda i: (jnp.maximum(i - 1, 0), 0))
     whole = pl.BlockSpec((8, width), lambda i: (0, 0))
-    mat = pl.BlockSpec(mats[0].shape, lambda i: (0, 0))
-    count = 6 + 8
-    return call(
-        finish_kernel,
-        grid=(steps,),
-        in_specs=[mat, mat] + [whole] * 4 + [at] * 6 + [halo] * 2 + [any_spec] * len(partial),
-        out_specs=[at, at],
-        out_shape=[shape(rows, width)] * 2,
-        input_output_aliases={count: 0, count + 1: 1} if partial else {},
-        name="finish",
-    )(*mats, *facts, *whole_tiles, *halo_tiles, *partial)
+    slots = pl.BlockSpec(mine.shape, lambda i: (0, 0, 0))
+    return call(
+        functools.partial(finish_kernel, for_a),
+        mib=24,
+        grid=(rows // tile,),
+        in_specs=[smem_spec, slots, slots]
+        + [whole] * 4
+        + [spec] * 2
+        + ([spec] * 2 if for_a else [top, low] * 2),
+        out_specs=spec,
+        out_shape=shape(rows, width),
+        scratch_shapes=[
+            pltpu.VMEM((2, width, width), f32),
+            pltpu.VMEM((6 * width, width), bf16),
+            pltpu.VMEM((8, width), f32),
+        ],
+        name="finish_a" if for_a else "finish_b",
+    )(at, mine, other, *facts, sums, part, view, *halos)
 
 
 def per_device(view_a, view_b):
@@ -512,36 +530,41 @@
     got = [slots[0]] + [to_x(slots[shift], shift) for shift in (1, 2, 3)]
     (own_mine,) = message(got, [half_facts])
     own_got = to_y(own_mine)
-    own_chunk, facts, a_top = own_merge(at, own_mine, own_got, a_top, half_rows)
+
+    keep, send = side_corr(
+        at, view_a, prev_raw, next_raw, half_facts, prev_half, next_half, [own_mine]
+    )
+    own_chunk, facts, a_top = own_merge(at, own_mine, own_got, a_top, half_rows, [keep])
     prev_top = across(a_top, 1)
     next_top = across(a_top, -1)
-
-    keep, send = side_corr(
-        at, view_a, prev_raw, next_raw, half_facts, prev_half, next_half, [own_chunk]
-    )
     slots = fan(keep, to_core(send))
     got = [slots[0]] + [to_x(slots[shift], shift) for shift in (1, 2, 3)]
     side_mine, own_chunk = message(got, [prev_half, next_half], own_chunk)
     own_slots = [own_chunk] + [to_x(own_chunk, shift) for shift in (1, 2, 3)]
-    left, right, prev_facts, next_facts = side_merge(
+    left, right, sides, prev_facts, next_facts = side_merge(
         at, side_mine, to_y(side_mine), own_mine, own_got, half_rows, [prev_top, next_top]
     )
     from_next = across(left, -1)
     from_prev = across(right, 1)
-    own_pack = pack(own_slots, None, [left])
+    side_slots = [sides] + [to_x(sides, shift) for shift in (1, 2, 3)]
+    own_pack = pack(own_slots)
     own_other = to_core(own_pack)
-    packed, a_low = pack([left, right, from_prev, from_next], a_low, [own_other])
+    ends, a_low = join(from_prev, from_next, a_low, [own_other])
     prev_low = across(a_low, 1)
     next_low = across(a_low, -1)
-    mine = [packed] + [to_x(packed, shift) for shift in (1, 2, 3)]
-    part_a, part_b, own_sums = own_grad(at, own_pack, own_other, view_a, view_b, facts)
-    other = [to_core(block) for block in mine]
-    mats = prep(at, mine + other, prev_facts, next_facts, own_sums)
+    end_slots = [ends] + [to_x(ends, shift) for shift in (1, 2, 3)]
+    part_a, part_b, own_sums = own_grad(at, own_pack, own_other, view_a, view_b, facts, [ends])
     all_facts = [facts, prev_facts, next_facts]
-    whole = [part_a, part_b, view_a, view_b, prev_raw, next_raw]
-    done = finish(0, top_rows, mats, all_facts, whole, [prev_top, next_top])
-    low = (local_rows - top_rows) // 2
-    return tuple(finish(top_rows, low, mats, all_facts, whole, [prev_low, next_low], done))
+    mine = pack(side_slots, [own_sums])
+    grad_a = finish(
+        True, at, mine, to_core(mine), all_facts, own_sums, part_a, view_a, [prev_raw, next_raw]
+    )
+    mine = pack(end_slots, [grad_a])
+    halos = [prev_top, prev_low, next_top, next_low]
+    grad_b = finish(
+        False, at, mine, to_core(mine), all_facts, own_sums, part_b, view_b, halos
+    )
+    return (grad_a, grad_b)
 
 
 def solution(mesh):

time: 170 us -> 164 us (0.965)
  Pallas kernels: 43.4 us -> 32.5 us
  starting transfers between devices: 58.2 us -> 63.8 us
  waiting for transfers between devices: 64.2 us -> 59.7 us
  local copies, waits for them, and re-layouts: 3.19 us -> 6.37 us
    ppermute x10, waiting for transfers between devices: 3.6 us -> 34.4 us  [across(): lax.ppermute(block, 'grp', [(i, (i + shift) % count) for i in range(count)])]
    ppermute x15 -> x18, waiting for transfers between devices: 35.4 us -> 14.9 us  [to_x(): return lax.ppermute(block, 'row', pairs)]
    ppermute x2, waiting for transfers between devices: 22 us -> 5.63 us  [to_y(): return lax.ppermute(block, 'row', [(i, i ^ 8) for i in range(16)])]
    ppermute x15 -> x18, starting transfers between devices: 17.9 us -> 26.3 us  [to_x(): return lax.ppermute(block, 'row', pairs)]
    pallas_call x5 -> x6, Pallas kernels: 21.5 us -> 14.4 us  [the longest x2 14.2 us: finish(): call(functools.partial(finish_kernel, for_a), mib=24, grid=(rows // tile,...]
    ppermute x8 -> x6, starting transfers between devices: 18 us -> 13.3 us  [to_core(): return lax.ppermute(block, 'row', [(i, i ^ 1) for i in range(16)])]
    unnamed x8 -> x12, local copies, waits for them, and re-layouts: 3.19 us -> 6.37 us
    pallas_call x1, Pallas kernels: 6.97 us -> 4.02 us  [own_corr(): call(functools.partial(own_corr_kernel, half_rows, steps, top_steps), gri...]
  transfers between devices with their start and end apart: 35 -> 36, of which waited for: 15 -> 18; matrix products, arithmetic and copies ran while one was open for 0% -> 0% of each run, Pallas kernels for 16% -> 12%
where the time goes in v3:
time: 164 us; the launch traced here: 163 us
  starting transfers between devices  63.8 us (39%)
  waiting for transfers between devices  59.7 us (36%)
  Pallas kernels  32.5 us (20%)
  local copies, waits for them, and re-layouts  6.37 us (4%)
    ppermute x10, waiting for transfers between devices, across(): lax.ppermute(block, 'grp', [(i, (i + shift) % count) for i in range(count)])  34.4 us
    ppermute x18, starting transfers between devices, to_x(): return lax.ppermute(block, 'row', pairs)  26.3 us
    ppermute x10, starting transfers between devices, across(): lax.ppermute(block, 'grp', [(i, (i + shift) % count) for i in range(count)])  18.9 us
    ppermute x18, waiting for transfers between devices, to_x(): return lax.ppermute(block, 'row', pairs)  14.9 us
    pallas_call x2, Pallas kernels, finish(): call(functools.partial(finish_kernel, for_a), mib=24, grid=(rows // tile,...  14.2 us
    ppermute x6, starting transfers between devices, to_core(): return lax.ppermute(block, 'row', [(i, i ^ 1) for i in range(16)])  13.3 us
    unnamed x12, local copies, waits for them, and re-layouts  6.37 us
    pallas_call x1, Pallas kernels, side_corr(): call(functools.partial(side_corr_kernel, steps), grid=(steps,), in_specs=...  5.96 us
  transfers between devices with their start and end apart: 36, of which 18 were waited for; matrix products, arithmetic and copies ran while one was open for 0% of the time, Pallas kernels for 12%

profile of v3, /device:TPU:1, one launch (start us, length us, event | category | flops | bytes accessed | tf_op | source)
XLA Modules:
  0.0 163.2 jit_solution(6711106221964632285)
XLA Ops:
  0.6 2.5 %collective-permute-start = (f32[1024,512]{1,0:T(8,128)}, f32[1024,512]{1,0:T(8,128)}, u32[]{:S(2)}, u32[]{:S(2)}) collective-permute-start(f32[1024,512]{1,0:T(8,128)} %refs_1_.3), channel_id=1, source_target_pairs={{0,16},{16,32},{32,48},{48,64},{64,80},{80,96},{96,112},{112,128},... | collective-permute-start | bytes 6291464 | tf_op jit(solution)/shard_map/ppermute | solution.py:34
  3.2 5.0 %collective-permute-start.1 = (f32[1024,512]{1,0:T(8,128)}, f32[1024,512]{1,0:T(8,128)}, u32[]{:S(2)}, u32[]{:S(2)}) collective-permute-start(f32[1024,512]{1,0:T(8,128)} %refs_1_.3), channel_id=1, source_target_pairs={{0,240},{16,0},{32,16},{48,32},{64,48},{80,64},{96,80},{112,96},{1... | collective-permute-start | bytes 6291464 | tf_op jit(solution)/shard_map/ppermute | solution.py:34
  8.2 1.6 copy-done
  9.8 1.6 copy-done.2
  13.9 1.2 collective-permute-start.3
  15.1 2.5 %collective-permute-start.4 = (f32[8,512]{1,0:T(8,128)S(1)}, f32[8,512]{1,0:T(8,128)S(1)}, u32[]{:S(2)}, u32[]{:S(2)}) collective-permute-start(f32[8,512]{1,0:T(8,128)S(1)} %add.3.refs_0_), channel_id=1, source_target_pairs={{0,4},{1,5},{2,6},{3,7},{4,0},{5,1},{6,2},{7,3},{8,12},{9,13},{10,... | collective-permute-start | bytes 49160 | tf_op jit(solution)/shard_map/ppermute | solution.py:47
  17.6 1.2 collective-permute-start.5
  20.6 1.6 copy-done.3
  22.2 4.0 %own_corr.1 = (f32[256,512]{1,0:T(8,128)S(1)}, f32[768,512]{1,0:T(8,128)S(1)}, f32[8,512]{1,0:T(8,128)S(1)}, f32[4,64,512]{2,1,0:T(8,128)S(1)}, f32[4,64,512]{2,1,0:T(8,128)S(1)}) custom-call(s32[2]{0:T(128)S(1)} %pad_add_fusion.at_ref, f32[1024,512]{1,0:T(8,128)S(1)} %copy-done.1, f32[1024,512]{1,0:T(8,128)S(1)} %copy-done.3, f32[8,512]{1,0:T(8,128)S(1)} %add.3.refs_0_, ...), custom_call_target="tpu_custom_call" | custom-call | flops 1 | bytes 1 | tf_op jit(solution)/shard_map/own_corr/pallas_call | solution.py:151
  26.2 1.7 %collective-permute-start.8 = (f32[4,64,512]{2,1,0:T(8,128)S(1)}, f32[4,64,512]{2,1,0:T(8,128)S(1)}, u32[]{:S(2)}, u32[]{:S(2)}) collective-permute-start(f32[4,64,512]{2,1,0:T(8,128)S(1)} %get-tuple-element.34), channel_id=1, source_target_pairs={{0,1},{1,0},{2,3},{3,2},{4,5},{5,4},{6,7},{7,6},{8,9},{9,8},{10,11... | collective-permute-start | bytes 1572872 | tf_op jit(solution)/shard_map/ppermute | solution.py:38
  27.9 1.5 collective-permute-done.8.got_ref
  29.5 1.3 collective-permute-start.10
  30.8 1.2 collective-permute-start.11
  32.6 3.4 %collective-permute-done.10.refs_2_ = f32[64,512]{1,0:T(8,128)S(1)} collective-permute-done((f32[64,512]{1,0:T(8,128)S(1)}, f32[64,512]{1,0:T(8,128)S(1)}, u32[]{:S(2)}, u32[]{:S(2)}) %collective-permute-start.10) | collective-permute-done | bytes 131104 | tf_op jit(solution)/shard_map/ppermute | solution.py:47
  35.9 2.8 %collective-permute-done.11.refs_3_ = f32[64,512]{1,0:T(8,128)S(1)} collective-permute-done((f32[64,512]{1,0:T(8,128)S(1)}, f32[64,512]{1,0:T(8,128)S(1)}, u32[]{:S(2)}, u32[]{:S(2)}) %collective-permute-start.11) | collective-permute-done | bytes 131104 | tf_op jit(solution)/shard_map/ppermute | solution.py:47
  38.8 1.7 %collective-permute-start.7 = (f32[8,512]{1,0:T(8,128)S(1)}, f32[8,512]{1,0:T(8,128)S(1)}, u32[]{:S(2)}, u32[]{:S(2)}) collective-permute-start(f32[8,512]{1,0:T(8,128)S(1)} %get-tuple-element.32.refs_4_.f_ref), channel_id=1, source_target_pairs={{0,240},{16,0},{32,16},{48,32},{64,48},{80,64},{96,80},{112,96},{1... | collective-permute-start | bytes 49160 | tf_op jit(solution)/shard_map/ppermute | solution.py:34
  40.5 13.7 %collective-permute-done.6.pf_ref.refs_4_ = f32[8,512]{1,0:T(8,128)S(1)} collective-permute-done((f32[8,512]{1,0:T(8,128)S(1)}, f32[8,512]{1,0:T(8,128)S(1)}, u32[]{:S(2)}, u32[]{:S(2)}) %collective-permute-start.6) | collective-permute-done | bytes 16416 | tf_op jit(solution)/shard_map/ppermute | solution.py:34
  54.2 6.0 %side_corr.1 = (f32[4,128,512]{2,1,0:T(8,128)S(1)}, f32[4,128,512]{2,1,0:T(8,128)S(1)}) custom-call(s32[2]{0:T(128)S(1)} %pad_add_fusion.at_ref, f32[1024,512]{1,0:T(8,128)S(1)} %copy-done.1, f32[1024,512]{1,0:T(8,128)} %collective-permute-done.prev_ref.refs_2_, f32[1024,512]{1,0:T(8,128)} %collective-permute-done.1.next_ref.refs_3_, ...), custom_call_target="tpu_custom_call" | custom-call | flops 1 | bytes 1 | tf_op jit(solution)/shard_map/side_corr/pallas_call | solution.py:191
  60.1 1.2 collective-permute-start.12
  61.3 2.3 %collective-permute-done.12.got_ref = f32[4,128,512]{2,1,0:T(8,128)S(1)} collective-permute-done((f32[4,128,512]{2,1,0:T(8,128)S(1)}, f32[4,128,512]{2,1,0:T(8,128)S(1)}, u32[]{:S(2)}, u32[]{:S(2)}) %collective-permute-start.12) | collective-permute-done | bytes 1048608 | tf_op jit(solution)/shard_map/ppermute | solution.py:38
  63.7 1.5 collective-permute-start.13
  65.2 2.5 %collective-permute-start.14 = (f32[128,512]{1,0:T(8,128)S(1)}, f32[128,512]{1,0:T(8,128)S(1)}, u32[]{:S(2)}, u32[]{:S(2)}) collective-permute-start(f32[128,512]{1,0:T(8,128)S(1)} %get-tuple-element.43), channel_id=1, source_target_pairs={{0,4},{1,5},{2,6},{3,7},{4,0},{5,1},{6,2},{7,3},{8,12},{9,13},{10,... | collective-permute-start | bytes 786440 | tf_op jit(solution)/shard_map/ppermute | solution.py:47
  67.7 1.1 collective-permute-start.15
  68.8 2.6 %collective-permute-start.16 = (f32[72,512]{1,0:T(8,128)S(1)}, f32[72,512]{1,0:T(8,128)S(1)}, u32[]{:S(2)}, u32[]{:S(2)}) collective-permute-start(f32[72,512]{1,0:T(8,128)S(1)} %message.2.refs_0_.mine_ref.own_ref), channel_id=1, source_target_pairs={{0,8},{1,9},{2,10},{3,11},{4,12},{5,13},{6,14},{7,15},{8,0},{9,1},... | collective-permute-start | bytes 442376 | tf_op jit(solution)/shard_map/ppermute | solution.py:42
  71.4 2.9 %collective-permute-done.16.got_ref.own_got_ref = f32[72,512]{1,0:T(8,128)S(1)} collective-permute-done((f32[72,512]{1,0:T(8,128)S(1)}, f32[72,512]{1,0:T(8,128)S(1)}, u32[]{:S(2)}, u32[]{:S(2)}) %collective-permute-start.16) | collective-permute-done | bytes 147488 | tf_op jit(solution)/shard_map/ppermute | solution.py:42
  75.2 3.7 %collective-permute-start.19 = (f32[256,512]{1,0:T(8,128)S(1)}, f32[256,512]{1,0:T(8,128)S(1)}, u32[]{:S(2)}, u32[]{:S(2)}) collective-permute-start(f32[256,512]{1,0:T(8,128)S(1)} %get-tuple-element.48), channel_id=1, source_target_pairs={{0,240},{16,0},{32,16},{48,32},{64,48},{80,64},{96,80},{112,96},{1... | collective-permute-start | bytes 1572872 | tf_op jit(solution)/shard_map/ppermute | solution.py:34
  80.5 2.8 %collective-permute-start.24 = (f32[64,512]{1,0:T(8,128)S(1)}, f32[64,512]{1,0:T(8,128)S(1)}, u32[]{:S(2)}, u32[]{:S(2)}) collective-permute-start(f32[64,512]{1,0:T(8,128)S(1)} %get-tuple-element.50.refs_0_), channel_id=1, source_target_pairs={{0,4},{1,5},{2,6},{3,7},{4,0},{5,1},{6,2},{7,3},{8,12},{9,13},{10,... | collective-permute-start | bytes 393224 | tf_op jit(solution)/shard_map/ppermute | solution.py:47
  83.6 1.2 collective-permute-done.23.refs_1_
  84.8 2.6 %collective-permute-start.17 = (f32[144,512]{1,0:T(8,128)S(1)}, f32[144,512]{1,0:T(8,128)S(1)}, u32[]{:S(2)}, u32[]{:S(2)}) collective-permute-start(f32[144,512]{1,0:T(8,128)S(1)} %get-tuple-element.47.mine_ref), channel_id=1, source_target_pairs={{0,8},{1,9},{2,10},{3,11},{4,12},{5,13},{6,14},{7,15},{8,0},{9,1},... | collective-permute-start | bytes 884744 | tf_op jit(solution)/shard_map/ppermute | solution.py:42
  87.4 1.8 %collective-permute-done.24.refs_2_ = f32[64,512]{1,0:T(8,128)S(1)} collective-permute-done((f32[64,512]{1,0:T(8,128)S(1)}, f32[64,512]{1,0:T(8,128)S(1)}, u32[]{:S(2)}, u32[]{:S(2)}) %collective-permute-start.24) | collective-permute-done | bytes 131104 | tf_op jit(solution)/shard_map/ppermute | solution.py:47
  89.3 4.6 %collective-permute-start.26 = (f32[4,64,512]{2,1,0:T(8,128)S(1)}, f32[4,64,512]{2,1,0:T(8,128)S(1)}, u32[]{:S(2)}, u32[]{:S(2)}) collective-permute-start(f32[4,64,512]{2,1,0:T(8,128)S(1)} %pack.3.mine_ref), channel_id=1, source_target_pairs={{0,1},{1,0},{2,3},{3,2},{4,5},{5,4},{6,7},{7,6},{8,9},{9,8},{10,11... | collective-permute-start | bytes 1572872 | tf_op jit(solution)/shard_map/ppermute | solution.py:38
  93.9 2.8 %collective-permute-done.17.got_ref = f32[144,512]{1,0:T(8,128)S(1)} collective-permute-done((f32[144,512]{1,0:T(8,128)S(1)}, f32[144,512]{1,0:T(8,128)S(1)}, u32[]{:S(2)}, u32[]{:S(2)}) %collective-permute-start.17) | collective-permute-done | bytes 294944 | tf_op jit(solution)/shard_map/ppermute | solution.py:42
  97.7 3.2 %collective-permute-start.20 = (f32[128,512]{1,0:T(8,128)S(1)}, f32[128,512]{1,0:T(8,128)S(1)}, u32[]{:S(2)}, u32[]{:S(2)}) collective-permute-start(f32[128,512]{1,0:T(8,128)S(1)} %get-tuple-element.49.refs_0_), channel_id=1, source_target_pairs={{0,2},{1,3},{2,4},{3,5},{4,6},{5,7},{6,0},{7,1},{8,10},{9,11},{10,... | collective-permute-start | bytes 786440 | tf_op jit(solution)/shard_map/ppermute | solution.py:47
  101.7 1.7 %collective-permute-start.22 = (f32[128,512]{1,0:T(8,128)S(1)}, f32[128,512]{1,0:T(8,128)S(1)}, u32[]{:S(2)}, u32[]{:S(2)}) collective-permute-start(f32[128,512]{1,0:T(8,128)S(1)} %get-tuple-element.49.refs_0_), channel_id=1, source_target_pairs={{0,6},{1,7},{2,0},{3,1},{4,2},{5,3},{6,4},{7,5},{8,14},{9,15},{10,... | collective-permute-start | bytes 786440 | tf_op jit(solution)/shard_map/ppermute | solution.py:47
  103.4 2.2 %collective-permute-done.27.first_ref = f32[64,512]{1,0:T(8,128)S(1)} collective-permute-done((f32[64,512]{1,0:T(8,128)S(1)}, f32[64,512]{1,0:T(8,128)S(1)}, u32[]{:S(2)}, u32[]{:S(2)}) %collective-permute-start.27) | collective-permute-done | bytes 131104 | tf_op jit(solution)/shard_map/ppermute | solution.py:34
  105.6 2.2 %collective-permute-start.28 = (f32[64,512]{1,0:T(8,128)S(1)}, f32[64,512]{1,0:T(8,128)S(1)}, u32[]{:S(2)}, u32[]{:S(2)}) collective-permute-start(f32[64,512]{1,0:T(8,128)S(1)} %get-tuple-element.53), channel_id=1, source_target_pairs={{0,240},{16,0},{32,16},{48,32},{64,48},{80,64},{96,80},{112,96},{1... | collective-permute-start | bytes 393224 | tf_op jit(solution)/shard_map/ppermute | solution.py:34
  107.8 1.9 %collective-permute-done.28.second_ref = f32[64,512]{1,0:T(8,128)S(1)} collective-permute-done((f32[64,512]{1,0:T(8,128)S(1)}, f32[64,512]{1,0:T(8,128)S(1)}, u32[]{:S(2)}, u32[]{:S(2)}) %collective-permute-start.28) | collective-permute-done | bytes 131104 | tf_op jit(solution)/shard_map/ppermute | solution.py:34
  109.8 5.5 %own_grad.1 = (f32[1024,512]{1,0:T(8,128)S(1)}, f32[1024,512]{1,0:T(8,128)S(1)}, f32[8,512]{1,0:T(8,128)S(1)}) custom-call(s32[2]{0:T(128)S(1)} %pad_add_fusion.at_ref, f32[4,64,512]{2,1,0:T(8,128)S(1)} %pack.3.mine_ref, f32[4,64,512]{2,1,0:T(8,128)S(1)} %collective-permute-done.26.refs_1_.other_ref, f32[1024,512]{1,0:T(8,128)S(1)} %copy-done.1, ...), custom_call_target="tpu_custom_call" | custom-call | flops 1 | bytes 1 | tf_op jit(solution)/shard_map/own_grad/pallas_call | solution.py:422
  115.5 3.1 %collective-permute-start.29 = (f32[4,128,512]{2,1,0:T(8,128)S(1)}, f32[4,128,512]{2,1,0:T(8,128)S(1)}, u32[]{:S(2)}, u32[]{:S(2)}) collective-permute-start(f32[4,128,512]{2,1,0:T(8,128)S(1)} %pack.4.mine_ref), channel_id=1, source_target_pairs={{0,1},{1,0},{2,3},{3,2},{4,5},{5,4},{6,7},{7,6},{8,9},{9,8},{10,11... | collective-permute-start | bytes 3145736 | tf_op jit(solution)/shard_map/ppermute | solution.py:38
  118.5 3.6 %collective-permute-start.35 = (f32[768,512]{1,0:T(8,128)S(1)}, f32[768,512]{1,0:T(8,128)S(1)}, u32[]{:S(2)}, u32[]{:S(2)}) collective-permute-start(f32[768,512]{1,0:T(8,128)S(1)} %get-tuple-element.61), channel_id=1, source_target_pairs={{0,240},{16,0},{32,16},{48,32},{64,48},{80,64},{96,80},{112,96},{1... | collective-permute-start | bytes 4718600 | tf_op jit(solution)/shard_map/ppermute | solution.py:34
  124.0 1.6 collective-permute-start.32
  125.6 7.6 %finish_a.1.refs_4_ = f32[1024,512]{1,0:T(8,128)} custom-call(s32[2]{0:T(128)S(1)} %pad_add_fusion.at_ref, f32[4,128,512]{2,1,0:T(8,128)S(1)} %pack.4.mine_ref, f32[4,128,512]{2,1,0:T(8,128)S(1)} %collective-permute-done.29.other_ref, f32[8,512]{1,0:T(8,128)S(1)} %get-tuple-element.51.facts_ref.f_ref, f32[8,512]{1,0:T(8,128)S(1)} %get-tuple-element.57.pf_ref, ...), custom_call_target="tpu_custom_call" | custom-call | flops 1 | bytes 1 | tf_op jit(solution)/shard_map/finish_a/pallas_call | solution.py:495
  133.1 2.3 %collective-permute-done.31.refs_2_ = f32[128,512]{1,0:T(8,128)S(1)} collective-permute-done((f32[128,512]{1,0:T(8,128)S(1)}, f32[128,512]{1,0:T(8,128)S(1)}, u32[]{:S(2)}, u32[]{:S(2)}) %collective-permute-start.31) | collective-permute-done | bytes 262176 | tf_op jit(solution)/shard_map/ppermute | solution.py:47
  135.4 1.3 collective-permute-done.32.refs_3_
  136.7 1.6 copy-done.5
  138.4 1.6 %collective-permute-start.33 = (f32[4,128,512]{2,1,0:T(8,128)S(1)}, f32[4,128,512]{2,1,0:T(8,128)S(1)}, u32[]{:S(2)}, u32[]{:S(2)}) collective-permute-start(f32[4,128,512]{2,1,0:T(8,128)S(1)} %pack.5.mine_ref), channel_id=1, source_target_pairs={{0,1},{1,0},{2,3},{3,2},{4,5},{5,4},{6,7},{7,6},{8,9},{9,8},{10,11... | collective-permute-start | bytes 3145736 | tf_op jit(solution)/shard_map/ppermute | solution.py:38
  140.0 16.6 %collective-permute-done.34.refs_3_ = f32[768,512]{1,0:T(8,128)S(1)} collective-permute-done((f32[768,512]{1,0:T(8,128)S(1)}, f32[768,512]{1,0:T(8,128)S(1)}, u32[]{:S(2)}, u32[]{:S(2)}) %collective-permute-start.34) | collective-permute-done | bytes 1572896 | tf_op jit(solution)/shard_map/ppermute | solution.py:34
  156.6 6.6 %finish_b.1 = f32[1024,512]{1,0:T(8,128)} custom-call(s32[2]{0:T(128)S(1)} %pad_add_fusion.at_ref, f32[4,128,512]{2,1,0:T(8,128)S(1)} %pack.5.mine_ref, f32[4,128,512]{2,1,0:T(8,128)S(1)} %collective-permute-done.33.other_ref, f32[8,512]{1,0:T(8,128)S(1)} %get-tuple-element.51.facts_ref.f_ref, f32[8,512]{1,0:T(8,128)S(1)} %get-tuple-element.57.pf_ref, ...), custom_call_target="tpu_custom_call" | custom-call | flops 1 | bytes 1 | tf_op jit(solution)/shard_map/finish_b/pallas_call | solution.py:495
  (54 shorter events, 11.7 us)
Async XLA Ops:
  0.6 53.5 %collective-permute-start = (f32[1024,512]{1,0:T(8,128)}, f32[1024,512]{1,0:T(8,128)}, u32[]{:S(2)}, u32[]{:S(2)}) collective-permute-start(f32[1024,512]{1,0:T(8,128)} %refs_1_.3), channel_id=1, source_target_pairs={{0,16},{16,32},{32,48},{48,64},{64,80},{80,96},{96,112},{112,128},... | collective-permute-start | bytes 6291464 | tf_op jit(solution)/shard_map/ppermute | solution.py:34
  3.2 51.0 %collective-permute-start.1 = (f32[1024,512]{1,0:T(8,128)}, f32[1024,512]{1,0:T(8,128)}, u32[]{:S(2)}, u32[]{:S(2)}) collective-permute-start(f32[1024,512]{1,0:T(8,128)} %refs_1_.3), channel_id=1, source_target_pairs={{0,240},{16,0},{32,16},{48,32},{64,48},{80,64},{96,80},{112,96},{1... | collective-permute-start | bytes 6291464 | tf_op jit(solution)/shard_map/ppermute | solution.py:34
  8.2 1.6 copy-start
  9.8 1.6 copy-start.2
  11.4 9.2 %copy-start.1 = (f32[1024,512]{1,0:T(8,128)S(1)}, f32[1024,512]{1,0:T(8,128)}, u32[]{:S(2)}) copy-start(f32[1024,512]{1,0:T(8,128)} %refs_1_.2) | copy-start | bytes 6291460
  12.0 1.9 %collective-permute-start.2 = (f32[8,512]{1,0:T(8,128)S(1)}, f32[8,512]{1,0:T(8,128)S(1)}, u32[]{:S(2)}, u32[]{:S(2)}) collective-permute-start(f32[8,512]{1,0:T(8,128)S(1)} %sums.1), channel_id=1, source_target_pairs={{0,1},{1,0},{2,3},{3,2},{4,5},{5,4},{6,7},{7,6},{8,9},{9,8},{10,11... | collective-permute-start | bytes 49160 | tf_op jit(solution)/shard_map/ppermute | solution.py:38
  13.9 4.9 %collective-permute-start.3 = (f32[8,512]{1,0:T(8,128)S(1)}, f32[8,512]{1,0:T(8,128)S(1)}, u32[]{:S(2)}, u32[]{:S(2)}) collective-permute-start(f32[8,512]{1,0:T(8,128)S(1)} %add.3.refs_0_), channel_id=1, source_target_pairs={{0,2},{1,3},{2,4},{3,5},{4,6},{5,7},{6,0},{7,1},{8,10},{9,11},{10,... | collective-permute-start | bytes 49160 | tf_op jit(solution)/shard_map/ppermute | solution.py:47
  15.1 4.5 %collective-permute-start.4 = (f32[8,512]{1,0:T(8,128)S(1)}, f32[8,512]{1,0:T(8,128)S(1)}, u32[]{:S(2)}, u32[]{:S(2)}) collective-permute-start(f32[8,512]{1,0:T(8,128)S(1)} %add.3.refs_0_), channel_id=1, source_target_pairs={{0,4},{1,5},{2,6},{3,7},{4,0},{5,1},{6,2},{7,3},{8,12},{9,13},{10,... | collective-permute-start | bytes 49160 | tf_op jit(solution)/shard_map/ppermute | solution.py:47
  17.6 3.0 %collective-permute-start.5 = (f32[8,512]{1,0:T(8,128)S(1)}, f32[8,512]{1,0:T(8,128)S(1)}, u32[]{:S(2)}, u32[]{:S(2)}) collective-permute-start(f32[8,512]{1,0:T(8,128)S(1)} %add.3.refs_0_), channel_id=1, source_target_pairs={{0,6},{1,7},{2,0},{3,1},{4,2},{5,3},{6,4},{7,5},{8,14},{9,15},{10,... | collective-permute-start | bytes 49160 | tf_op jit(solution)/shard_map/ppermute | solution.py:47
  20.6 1.6 copy-start.3
  26.2 3.3 %collective-permute-start.8 = (f32[4,64,512]{2,1,0:T(8,128)S(1)}, f32[4,64,512]{2,1,0:T(8,128)S(1)}, u32[]{:S(2)}, u32[]{:S(2)}) collective-permute-start(f32[4,64,512]{2,1,0:T(8,128)S(1)} %get-tuple-element.34), channel_id=1, source_target_pairs={{0,1},{1,0},{2,3},{3,2},{4,5},{5,4},{6,7},{7,6},{8,9},{9,8},{10,11... | collective-permute-start | bytes 1572872 | tf_op jit(solution)/shard_map/ppermute | solution.py:38
  29.5 6.4 %collective-permute-start.10 = (f32[64,512]{1,0:T(8,128)S(1)}, f32[64,512]{1,0:T(8,128)S(1)}, u32[]{:S(2)}, u32[]{:S(2)}) collective-permute-start(f32[64,512]{1,0:T(8,128)S(1)} %get-tuple-element.37), channel_id=1, source_target_pairs={{0,4},{1,5},{2,6},{3,7},{4,0},{5,1},{6,2},{7,3},{8,12},{9,13},{10,... | collective-permute-start | bytes 393224 | tf_op jit(solution)/shard_map/ppermute | solution.py:47
  30.8 7.9 %collective-permute-start.11 = (f32[64,512]{1,0:T(8,128)S(1)}, f32[64,512]{1,0:T(8,128)S(1)}, u32[]{:S(2)}, u32[]{:S(2)}) collective-permute-start(f32[64,512]{1,0:T(8,128)S(1)} %get-tuple-element.38), channel_id=1, source_target_pairs={{0,6},{1,7},{2,0},{3,1},{4,2},{5,3},{6,4},{7,5},{8,14},{9,15},{10,... | collective-permute-start | bytes 393224 | tf_op jit(solution)/shard_map/ppermute | solution.py:47
  32.1 8.3 %collective-permute-start.9 = (f32[64,512]{1,0:T(8,128)S(1)}, f32[64,512]{1,0:T(8,128)S(1)}, u32[]{:S(2)}, u32[]{:S(2)}) collective-permute-start(f32[64,512]{1,0:T(8,128)S(1)} %get-tuple-element.36), channel_id=1, source_target_pairs={{0,2},{1,3},{2,4},{3,5},{4,6},{5,7},{6,0},{7,1},{8,10},{9,11},{10,... | collective-permute-start | bytes 393224 | tf_op jit(solution)/shard_map/ppermute | solution.py:47
  35.9 18.2 %collective-permute-start.6 = (f32[8,512]{1,0:T(8,128)S(1)}, f32[8,512]{1,0:T(8,128)S(1)}, u32[]{:S(2)}, u32[]{:S(2)}) collective-permute-start(f32[8,512]{1,0:T(8,128)S(1)} %get-tuple-element.32.refs_4_.f_ref), channel_id=1, source_target_pairs={{0,16},{16,32},{32,48},{48,64},{64,80},{80,96},{96,112},{112,128},... | collective-permute-start | bytes 49160 | tf_op jit(solution)/shard_map/ppermute | solution.py:34
  38.8 15.4 %collective-permute-start.7 = (f32[8,512]{1,0:T(8,128)S(1)}, f32[8,512]{1,0:T(8,128)S(1)}, u32[]{:S(2)}, u32[]{:S(2)}) collective-permute-start(f32[8,512]{1,0:T(8,128)S(1)} %get-tuple-element.32.refs_4_.f_ref), channel_id=1, source_target_pairs={{0,240},{16,0},{32,16},{48,32},{64,48},{80,64},{96,80},{112,96},{1... | collective-permute-start | bytes 49160 | tf_op jit(solution)/shard_map/ppermute | solution.py:34
  60.1 3.5 %collective-permute-start.12 = (f32[4,128,512]{2,1,0:T(8,128)S(1)}, f32[4,128,512]{2,1,0:T(8,128)S(1)}, u32[]{:S(2)}, u32[]{:S(2)}) collective-permute-start(f32[4,128,512]{2,1,0:T(8,128)S(1)} %get-tuple-element.40), channel_id=1, source_target_pairs={{0,1},{1,0},{2,3},{3,2},{4,5},{5,4},{6,7},{7,6},{8,9},{9,8},{10,11... | collective-permute-start | bytes 3145736 | tf_op jit(solution)/shard_map/ppermute | solution.py:38
  63.7 15.2 %collective-permute-start.13 = (f32[128,512]{1,0:T(8,128)S(1)}, f32[128,512]{1,0:T(8,128)S(1)}, u32[]{:S(2)}, u32[]{:S(2)}) collective-permute-start(f32[128,512]{1,0:T(8,128)S(1)} %get-tuple-element.42), channel_id=1, source_target_pairs={{0,2},{1,3},{2,4},{3,5},{4,6},{5,7},{6,0},{7,1},{8,10},{9,11},{10,... | collective-permute-start | bytes 786440 | tf_op jit(solution)/shard_map/ppermute | solution.py:47
  65.2 14.1 %collective-permute-start.14 = (f32[128,512]{1,0:T(8,128)S(1)}, f32[128,512]{1,0:T(8,128)S(1)}, u32[]{:S(2)}, u32[]{:S(2)}) collective-permute-start(f32[128,512]{1,0:T(8,128)S(1)} %get-tuple-element.43), channel_id=1, source_target_pairs={{0,4},{1,5},{2,6},{3,7},{4,0},{5,1},{6,2},{7,3},{8,12},{9,13},{10,... | collective-permute-start | bytes 786440 | tf_op jit(solution)/shard_map/ppermute | solution.py:47
  67.7 11.7 %collective-permute-start.15 = (f32[128,512]{1,0:T(8,128)S(1)}, f32[128,512]{1,0:T(8,128)S(1)}, u32[]{:S(2)}, u32[]{:S(2)}) collective-permute-start(f32[128,512]{1,0:T(8,128)S(1)} %get-tuple-element.44), channel_id=1, source_target_pairs={{0,6},{1,7},{2,0},{3,1},{4,2},{5,3},{6,4},{7,5},{8,14},{9,15},{10,... | collective-permute-start | bytes 786440 | tf_op jit(solution)/shard_map/ppermute | solution.py:47
  68.8 5.5 %collective-permute-start.16 = (f32[72,512]{1,0:T(8,128)S(1)}, f32[72,512]{1,0:T(8,128)S(1)}, u32[]{:S(2)}, u32[]{:S(2)}) collective-permute-start(f32[72,512]{1,0:T(8,128)S(1)} %message.2.refs_0_.mine_ref.own_ref), channel_id=1, source_target_pairs={{0,8},{1,9},{2,10},{3,11},{4,12},{5,13},{6,14},{7,15},{8,0},{9,1},... | collective-permute-start | bytes 442376 | tf_op jit(solution)/shard_map/ppermute | solution.py:42
  75.2 18.8 %collective-permute-start.18 = (f32[256,512]{1,0:T(8,128)S(1)}, f32[256,512]{1,0:T(8,128)S(1)}, u32[]{:S(2)}, u32[]{:S(2)}) collective-permute-start(f32[256,512]{1,0:T(8,128)S(1)} %get-tuple-element.48), channel_id=1, source_target_pairs={{0,16},{16,32},{32,48},{48,64},{64,80},{80,96},{96,112},{112,128},... | collective-permute-start | bytes 1572872 | tf_op jit(solution)/shard_map/ppermute | solution.py:34
  75.2 18.7 %collective-permute-start.19 = (f32[256,512]{1,0:T(8,128)S(1)}, f32[256,512]{1,0:T(8,128)S(1)}, u32[]{:S(2)}, u32[]{:S(2)}) collective-permute-start(f32[256,512]{1,0:T(8,128)S(1)} %get-tuple-element.48), channel_id=1, source_target_pairs={{0,240},{16,0},{32,16},{48,32},{64,48},{80,64},{96,80},{112,96},{1... | collective-permute-start | bytes 1572872 | tf_op jit(solution)/shard_map/ppermute | solution.py:34
  79.4 5.4 %collective-permute-start.23 = (f32[64,512]{1,0:T(8,128)S(1)}, f32[64,512]{1,0:T(8,128)S(1)}, u32[]{:S(2)}, u32[]{:S(2)}) collective-permute-start(f32[64,512]{1,0:T(8,128)S(1)} %get-tuple-element.50.refs_0_), channel_id=1, source_target_pairs={{0,2},{1,3},{2,4},{3,5},{4,6},{5,7},{6,0},{7,1},{8,10},{9,11},{10,... | collective-permute-start | bytes 393224 | tf_op jit(solution)/shard_map/ppermute | solution.py:47
  80.5 8.7 %collective-permute-start.24 = (f32[64,512]{1,0:T(8,128)S(1)}, f32[64,512]{1,0:T(8,128)S(1)}, u32[]{:S(2)}, u32[]{:S(2)}) collective-permute-start(f32[64,512]{1,0:T(8,128)S(1)} %get-tuple-element.50.refs_0_), channel_id=1, source_target_pairs={{0,4},{1,5},{2,6},{3,7},{4,0},{5,1},{6,2},{7,3},{8,12},{9,13},{10,... | collective-permute-start | bytes 393224 | tf_op jit(solution)/shard_map/ppermute | solution.py:47
  83.3 5.9 %collective-permute-start.25 = (f32[64,512]{1,0:T(8,128)S(1)}, f32[64,512]{1,0:T(8,128)S(1)}, u32[]{:S(2)}, u32[]{:S(2)}) collective-permute-start(f32[64,512]{1,0:T(8,128)S(1)} %get-tuple-element.50.refs_0_), channel_id=1, source_target_pairs={{0,6},{1,7},{2,0},{3,1},{4,2},{5,3},{6,4},{7,5},{8,14},{9,15},{10,... | collective-permute-start | bytes 393224 | tf_op jit(solution)/shard_map/ppermute | solution.py:47
  84.8 11.9 %collective-permute-start.17 = (f32[144,512]{1,0:T(8,128)S(1)}, f32[144,512]{1,0:T(8,128)S(1)}, u32[]{:S(2)}, u32[]{:S(2)}) collective-permute-start(f32[144,512]{1,0:T(8,128)S(1)} %get-tuple-element.47.mine_ref), channel_id=1, source_target_pairs={{0,8},{1,9},{2,10},{3,11},{4,12},{5,13},{6,14},{7,15},{8,0},{9,1},... | collective-permute-start | bytes 884744 | tf_op jit(solution)/shard_map/ppermute | solution.py:42
  89.3 20.5 %copy-start.4 = (f32[1024,512]{1,0:T(8,128)S(1)}, f32[1024,512]{1,0:T(8,128)}, u32[]{:S(2)}) copy-start(f32[1024,512]{1,0:T(8,128)} %refs_1_.3) | copy-start | bytes 6291460
  89.3 20.5 %collective-permute-start.26 = (f32[4,64,512]{2,1,0:T(8,128)S(1)}, f32[4,64,512]{2,1,0:T(8,128)S(1)}, u32[]{:S(2)}, u32[]{:S(2)}) collective-permute-start(f32[4,64,512]{2,1,0:T(8,128)S(1)} %pack.3.mine_ref), channel_id=1, source_target_pairs={{0,1},{1,0},{2,3},{3,2},{4,5},{5,4},{6,7},{7,6},{8,9},{9,8},{10,11... | collective-permute-start | bytes 1572872 | tf_op jit(solution)/shard_map/ppermute | solution.py:38
  97.6 8.0 %collective-permute-start.27 = (f32[64,512]{1,0:T(8,128)S(1)}, f32[64,512]{1,0:T(8,128)S(1)}, u32[]{:S(2)}, u32[]{:S(2)}) collective-permute-start(f32[64,512]{1,0:T(8,128)S(1)} %get-tuple-element.52), channel_id=1, source_target_pairs={{0,16},{16,32},{32,48},{48,64},{64,80},{80,96},{96,112},{112,128},... | collective-permute-start | bytes 393224 | tf_op jit(solution)/shard_map/ppermute | solution.py:34
  97.7 17.7 %collective-permute-start.20 = (f32[128,512]{1,0:T(8,128)S(1)}, f32[128,512]{1,0:T(8,128)S(1)}, u32[]{:S(2)}, u32[]{:S(2)}) collective-permute-start(f32[128,512]{1,0:T(8,128)S(1)} %get-tuple-element.49.refs_0_), channel_id=1, source_target_pairs={{0,2},{1,3},{2,4},{3,5},{4,6},{5,7},{6,0},{7,1},{8,10},{9,11},{10,... | collective-permute-start | bytes 786440 | tf_op jit(solution)/shard_map/ppermute | solution.py:47
  100.9 14.5 %collective-permute-start.21 = (f32[128,512]{1,0:T(8,128)S(1)}, f32[128,512]{1,0:T(8,128)S(1)}, u32[]{:S(2)}, u32[]{:S(2)}) collective-permute-start(f32[128,512]{1,0:T(8,128)S(1)} %get-tuple-element.49.refs_0_), channel_id=1, source_target_pairs={{0,4},{1,5},{2,6},{3,7},{4,0},{5,1},{6,2},{7,3},{8,12},{9,13},{10,... | collective-permute-start | bytes 786440 | tf_op jit(solution)/shard_map/ppermute | solution.py:47
  101.7 13.6 %collective-permute-start.22 = (f32[128,512]{1,0:T(8,128)S(1)}, f32[128,512]{1,0:T(8,128)S(1)}, u32[]{:S(2)}, u32[]{:S(2)}) collective-permute-start(f32[128,512]{1,0:T(8,128)S(1)} %get-tuple-element.49.refs_0_), channel_id=1, source_target_pairs={{0,6},{1,7},{2,0},{3,1},{4,2},{5,3},{6,4},{7,5},{8,14},{9,15},{10,... | collective-permute-start | bytes 786440 | tf_op jit(solution)/shard_map/ppermute | solution.py:47
  105.6 4.2 %collective-permute-start.28 = (f32[64,512]{1,0:T(8,128)S(1)}, f32[64,512]{1,0:T(8,128)S(1)}, u32[]{:S(2)}, u32[]{:S(2)}) collective-permute-start(f32[64,512]{1,0:T(8,128)S(1)} %get-tuple-element.53), channel_id=1, source_target_pairs={{0,240},{16,0},{32,16},{48,32},{64,48},{80,64},{96,80},{112,96},{1... | collective-permute-start | bytes 393224 | tf_op jit(solution)/shard_map/ppermute | solution.py:34
  115.5 8.5 %collective-permute-start.29 = (f32[4,128,512]{2,1,0:T(8,128)S(1)}, f32[4,128,512]{2,1,0:T(8,128)S(1)}, u32[]{:S(2)}, u32[]{:S(2)}) collective-permute-start(f32[4,128,512]{2,1,0:T(8,128)S(1)} %pack.4.mine_ref), channel_id=1, source_target_pairs={{0,1},{1,0},{2,3},{3,2},{4,5},{5,4},{6,7},{7,6},{8,9},{9,8},{10,11... | collective-permute-start | bytes 3145736 | tf_op jit(solution)/shard_map/ppermute | solution.py:38
  118.5 38.1 %collective-permute-start.34 = (f32[768,512]{1,0:T(8,128)S(1)}, f32[768,512]{1,0:T(8,128)S(1)}, u32[]{:S(2)}, u32[]{:S(2)}) collective-permute-start(f32[768,512]{1,0:T(8,128)S(1)} %get-tuple-element.61), channel_id=1, source_target_pairs={{0,16},{16,32},{32,48},{48,64},{64,80},{80,96},{96,112},{112,128},... | collective-permute-start | bytes 4718600 | tf_op jit(solution)/shard_map/ppermute | solution.py:34
  118.5 38.1 %collective-permute-start.35 = (f32[768,512]{1,0:T(8,128)S(1)}, f32[768,512]{1,0:T(8,128)S(1)}, u32[]{:S(2)}, u32[]{:S(2)}) collective-permute-start(f32[768,512]{1,0:T(8,128)S(1)} %get-tuple-element.61), channel_id=1, source_target_pairs={{0,240},{16,0},{32,16},{48,32},{64,48},{80,64},{96,80},{112,96},{1... | collective-permute-start | bytes 4718600 | tf_op jit(solution)/shard_map/ppermute | solution.py:34
  122.1 11.0 %collective-permute-start.30 = (f32[128,512]{1,0:T(8,128)S(1)}, f32[128,512]{1,0:T(8,128)S(1)}, u32[]{:S(2)}, u32[]{:S(2)}) collective-permute-start(f32[128,512]{1,0:T(8,128)S(1)} %get-tuple-element.55.refs_0_), channel_id=1, source_target_pairs={{0,2},{1,3},{2,4},{3,5},{4,6},{5,7},{6,0},{7,1},{8,10},{9,11},{10,... | collective-permute-start | bytes 786440 | tf_op jit(solution)/shard_map/ppermute | solution.py:47
  123.2 12.2 %collective-permute-start.31 = (f32[128,512]{1,0:T(8,128)S(1)}, f32[128,512]{1,0:T(8,128)S(1)}, u32[]{:S(2)}, u32[]{:S(2)}) collective-permute-start(f32[128,512]{1,0:T(8,128)S(1)} %get-tuple-element.55.refs_0_), channel_id=1, source_target_pairs={{0,4},{1,5},{2,6},{3,7},{4,0},{5,1},{6,2},{7,3},{8,12},{9,13},{10,... | collective-permute-start | bytes 786440 | tf_op jit(solution)/shard_map/ppermute | solution.py:47
  124.0 12.7 %collective-permute-start.32 = (f32[128,512]{1,0:T(8,128)S(1)}, f32[128,512]{1,0:T(8,128)S(1)}, u32[]{:S(2)}, u32[]{:S(2)}) collective-permute-start(f32[128,512]{1,0:T(8,128)S(1)} %get-tuple-element.55.refs_0_), channel_id=1, source_target_pairs={{0,6},{1,7},{2,0},{3,1},{4,2},{5,3},{6,4},{7,5},{8,14},{9,15},{10,... | collective-permute-start | bytes 786440 | tf_op jit(solution)/shard_map/ppermute | solution.py:47
  136.7 1.6 copy-start.5
  138.4 18.2 %collective-permute-start.33 = (f32[4,128,512]{2,1,0:T(8,128)S(1)}, f32[4,128,512]{2,1,0:T(8,128)S(1)}, u32[]{:S(2)}, u32[]{:S(2)}) collective-permute-start(f32[4,128,512]{2,1,0:T(8,128)S(1)} %pack.5.mine_ref), channel_id=1, source_target_pairs={{0,1},{1,0},{2,3},{3,2},{4,5},{5,4},{6,7},{7,6},{8,9},{9,8},{10,11... | collective-permute-start | bytes 3145736 | tf_op jit(solution)/shard_map/ppermute | solution.py:38

commit v4 on v3

v4 whole, which is shorter than its diff:
```python
import functools

import jax
import jax.numpy as jnp
from jax import lax
from jax.experimental import pallas as pl
from jax.experimental.pallas import tpu as pltpu
from jax.sharding import PartitionSpec as P

epsilon = 1e-05
off_weight = 0.0051
f32 = jnp.float32
bf16 = jnp.bfloat16


any_spec = pl.BlockSpec(memory_space=pl.ANY)
smem_spec = pl.BlockSpec(memory_space=pltpu.SMEM)
vmem_spec = pl.BlockSpec(memory_space=pltpu.VMEM)
cheap = pl.CostEstimate(flops=1, transcendentals=0, bytes_accessed=1)
top_rows, mid_rows = 512, 128


def call(kernel, mib=8, **rest):
    params = pltpu.CompilerParams(vmem_limit_bytes=mib * 1024 * 1024)
    return pl.pallas_call(kernel, compiler_params=params, cost_estimate=cheap, **rest)


def shape(*dims):
    return jax.ShapeDtypeStruct(dims, f32)


def across(block, shift):
    count = lax.axis_size("grp")
    return lax.ppermute(block, "grp", [(i, (i + shift) % count) for i in range(count)])


def to_core(block):
    return lax.ppermute(block, "row", [(i, i ^ 1) for i in range(16)])


def to_y(block):
    return lax.ppermute(block, "row", [(i, i ^ 8) for i in range(16)])


def to_x(block, shift):
    pairs = [(i, (i & 9) | ((((i >> 1) + shift) & 3) << 1)) for i in range(16)]
    return lax.ppermute(block, "row", pairs)


def split(value):
    high = value.astype(bf16)
    return high, (value - high.astype(f32)).astype(bf16)


def mm(a, b):
    return lax.dot_general(a, b, (((1,), (0,)), ((), ())), preferred_element_type=f32)


def gram(a, b):
    a_high, a_low = split(a.T)
    b_high, b_low = split(b)
    return mm(
        jnp.concatenate([a_high, a_high, a_low], axis=1),
        jnp.concatenate([b_high, b_low, b_high], axis=0),
    )


def thrice(value):
    high, low = split(value)
    return jnp.concatenate([high, high, low], axis=1)


def sums_kernel(a_ref, b_ref, out_ref):
    @pl.when(pl.program_id(0) == 0)
    def _():
        out_ref[...] = jnp.zeros_like(out_ref)

    a, b = a_ref[...], b_ref[...]
    for row, value in enumerate((a, a * a, b, b * b)):
        out_ref[row : row + 1, :] += jnp.sum(value, axis=0, keepdims=True)


def sums_of(a, b):
    rows, width = a.shape
    tile = rows // 4
    spec = pl.BlockSpec((tile, width), lambda i: (i, 0))
    return call(
        sums_kernel,
        grid=(4,),
        in_specs=[spec, spec],
        out_specs=pl.BlockSpec((8, width), lambda i: (0, 0)),
        out_shape=shape(8, width),
        name="sums",
    )(a, b)


def put_slots(at_ref, acc, keep_ref, sends, first, rows):
    core, x = at_ref[0], at_ref[1]
    for slot in range(4):
        chunk = (x + slot) & 3
        mine = pl.multiple_of((core * 4 + chunk) * rows, rows)
        theirs = pl.multiple_of(((1 - core) * 4 + chunk) * rows, rows)
        keep_ref[slot, first : first + rows, :] = acc[pl.ds(mine, rows), :]
        each = 4 // len(sends)
        sends[slot // each][slot % each, first : first + rows, :] = acc[pl.ds(theirs, rows), :]


def own_corr_kernel(half_rows, steps, bounds, at_ref, a_ref, b_ref, *refs):
    parts, halos, (facts_ref, keep_ref, send_ref, acc_ref) = refs[:4], refs[4:7], refs[7:]
    step = pl.program_id(0)

    @pl.when(step == 0)
    def _():
        total = parts[0][...] + parts[1][...] + parts[2][...] + parts[3][...]
        total = total / half_rows
        for view in (0, 1):
            mean, square = total[2 * view : 2 * view + 1], total[2 * view + 1 : 2 * view + 2]
            scale = jnp.sqrt(square - mean * mean + epsilon)
            facts_ref[2 * view : 2 * view + 1, :] = mean
            facts_ref[2 * view + 1 : 2 * view + 2, :] = 1.0 / scale
            facts_ref[4 + view : 5 + view, :] = square
            facts_ref[6 + view : 7 + view, :] = scale
        acc_ref[...] = jnp.zeros_like(acc_ref)

    norm_a = (a_ref[...] - facts_ref[0:1, :]) * facts_ref[1:2, :]
    norm_b = (b_ref[...] - facts_ref[2:3, :]) * facts_ref[3:4, :]

    for ref, first, last in zip(halos, bounds[:-1], bounds[1:]):

        @pl.when((step >= first) & (step < last))
        def _(ref=ref):
            ref[...] = norm_a

    acc_ref[...] += gram(norm_a, norm_b)

    @pl.when(step == steps - 1)
    def _():
        put_slots(at_ref, acc_ref, keep_ref, [send_ref], 0, keep_ref.shape[1])


def halo_cuts(rows, tile):
    sizes = (top_rows, mid_rows, rows - top_rows - mid_rows)
    bounds = (0, sizes[0] // tile, (sizes[0] + sizes[1]) // tile, rows // tile)

    def spec(first, last):
        return lambda i: (jnp.clip(i - first, 0, last - first - 1), 0)

    maps = [spec(first, last) for first, last in zip(bounds[:-1], bounds[1:])]
    return sizes, bounds, maps


def own_corr(at, a, b, parts, half_rows):
    rows, width = a.shape
    tile = 128
    sizes, bounds, maps = halo_cuts(rows, tile)
    spec = pl.BlockSpec((tile, width), lambda i: (i, 0))
    whole = pl.BlockSpec((8, width), lambda i: (0, 0))
    slots = pl.BlockSpec((4, width // 8, width), lambda i: (0, 0, 0))
    return call(
        functools.partial(own_corr_kernel, half_rows, rows // tile, bounds),
        grid=(rows // tile,),
        in_specs=[smem_spec, spec, spec] + [whole] * 4,
        out_specs=[pl.BlockSpec((tile, width), part) for part in maps] + [whole, slots, slots],
        out_shape=[shape(size, width) for size in sizes]
        + [shape(8, width)]
        + [shape(4, width // 8, width)] * 2,
        scratch_shapes=[pltpu.VMEM((width, width), f32)],
        mib=16,
        name="own_corr",
    )(at, a, b, *parts)


def side_corr_kernel(steps, at_ref, a_ref, prev_ref, next_ref, f_ref, *refs):
    keep_ref, *sends, left_ref, right_ref = refs[-5:]
    step = pl.program_id(0)

    @pl.when(step == 0)
    def _():
        left_ref[...] = jnp.zeros_like(left_ref)
        right_ref[...] = jnp.zeros_like(right_ref)

    norm_a = (a_ref[...] - f_ref[0:1, :]) * f_ref[1:2, :]
    for acc_ref, b_ref in ((left_ref, prev_ref), (right_ref, next_ref)):
        acc_ref[...] += gram(norm_a, b_ref[...])

    @pl.when(step == steps - 1)
    def _():
        rows = keep_ref.shape[1] // 2
        put_slots(at_ref, left_ref, keep_ref, sends, 0, rows)
        put_slots(at_ref, right_ref, keep_ref, sends, rows, rows)


def side_corr(at, a, prev_b, next_b, facts, wait_for):
    rows, width = a.shape
    steps = 4
    spec = pl.BlockSpec((rows // steps, width), lambda i: (i, 0))
    whole = pl.BlockSpec((8, width), lambda i: (0, 0))
    slots = pl.BlockSpec((4, width // 4, width), lambda i: (0, 0, 0))
    pair = pl.BlockSpec((2, width // 4, width), lambda i: (0, 0, 0))
    return call(
        functools.partial(side_corr_kernel, steps),
        grid=(steps,),
        in_specs=[smem_spec, spec, spec, spec, whole] + [any_spec] * len(wait_for),
        out_specs=[slots, pair, pair],
        out_shape=[shape(4, width // 4, width)] + [shape(2, width // 4, width)] * 2,
        scratch_shapes=[pltpu.VMEM((width, width), f32)] * 2,
        mib=24,
        name="side_corr",
    )(at, a, prev_b, next_b, facts, *wait_for)


def fan_kernel(keep_ref, *refs):
    gots, outs = refs[:-4], refs[-4:]
    each = 4 // len(gots)
    for slot in range(4):
        outs[slot][...] = keep_ref[slot] + gots[slot // each][slot % each]


def fan(keep, *gots):
    return call(
        fan_kernel,
        in_specs=[vmem_spec] * (1 + len(gots)),
        out_specs=[vmem_spec] * 4,
        out_shape=[shape(*keep.shape[1:])] * 4,
        name="fan",
    )(keep, *gots)


def own_sum_kernel(*refs):
    top_ref, facts_ref, sum_ref, halo_ref = refs[4:]
    sum_ref[...] = refs[0][...] + refs[1][...] + refs[2][...] + refs[3][...]
    rows = top_ref.shape[0]
    halo_ref[0:rows, :] = top_ref[...]
    halo_ref[rows:, :] = facts_ref[...]


def own_sum(parts, top, facts):
    rows, width = top.shape
    return call(
        own_sum_kernel,
        in_specs=[vmem_spec] * 6,
        out_specs=[vmem_spec] * 2,
        out_shape=[shape(*parts[0].shape), shape(rows + 8, width)],
        name="own_sum",
    )(*parts, top, facts)


def message_kernel(own_ref, *refs):
    side, facts, out_ref = refs[:4], refs[4:7], refs[7]
    first = own_ref.shape[0]
    last = first + side[0].shape[0]
    out_ref[0:first, :] = own_ref[...]
    out_ref[first:last, :] = side[0][...] + side[1][...] + side[2][...] + side[3][...]
    for i, ref in enumerate(facts):
        out_ref[last + 8 * i : last + 8 * i + 8, :] = ref[...]


def message(own, side, facts, prev_top, next_top):
    rows = own.shape[0] + side[0].shape[0] + 24
    width = own.shape[1]
    below = pl.BlockSpec((8, width), lambda i: (top_rows // 8, 0))
    wholes = [pl.BlockSpec(block.shape, lambda i: (0, 0)) for block in (own, *side, facts)]
    return call(
        message_kernel,
        grid=(1,),
        in_specs=wholes + [below] * 2,
        out_specs=pl.BlockSpec((rows, width), lambda i: (0, 0)),
        out_shape=shape(rows, width),
        name="message",
    )(own, *side, facts, prev_top, next_top)


def full_facts(mine, other):
    rows = []
    for view in (0, 1):
        mean = 0.5 * (mine[2 * view : 2 * view + 1] + other[2 * view : 2 * view + 1])
        square = 0.5 * (mine[4 + view : 5 + view] + other[4 + view : 5 + view])
        rows += [mean, 1.0 / jnp.sqrt(square - mean * mean + epsilon)]
    for view in (0, 1):
        average = 0.5 * (mine[2 * view : 2 * view + 1] + other[2 * view : 2 * view + 1])
        rows.append((average - rows[2 * view]) * rows[2 * view + 1])
    rows += [mine[6:7] * rows[1], (mine[0:1] - rows[0]) * rows[1]]
    return rows


def merged(mine, other, a_cols, b_mine, b_other, b_full, half_rows, raw_b):
    scale0, scale1, diff0, diff1, inverse = (a_cols[:, i : i + 1] for i in range(5))
    if not raw_b:
        mine, other = mine * b_mine[7:8], other * b_other[7:8]
    out = mine * scale0 + other * scale1
    shift0, shift1 = b_mine[2:3] - b_full[2], b_other[2:3] - b_full[2]
    out = out + half_rows * (diff0 * shift0 + diff1 * shift1)
    return out * (inverse * (b_full[3] * (0.5 / half_rows)))


def columns_of(at_ref, mine, other, full, cols_ref, rows):
    width = mine.shape[1]
    stack = [mine[6:7], other[6:7], mine[0:1] - full[0], other[0:1] - full[0], full[1]]
    stack = jnp.concatenate(stack + [jnp.zeros((123, width), f32)], axis=0)
    cols_ref[...] = stack.T
    first = pl.multiple_of((at_ref[0] * 4 + at_ref[1]) * rows, rows)
    return cols_ref[pl.ds(first, rows), :]


def merge_kernel(half_rows, at_ref, mine_ref, got_ref, *refs):
    left_ref, right_ref, trio_ref, *facts_refs, cols_ref = refs[-7:]
    rows = left_ref.shape[0]
    facts = [
        (mine_ref[first : first + 8, :], got_ref[first : first + 8, :])
        for first in (3 * rows, 3 * rows + 8, 3 * rows + 16)
    ]
    full = [full_facts(*both) for both in facts]
    for ref, values in zip(facts_refs, full):
        for i in range(8):
            ref[i : i + 1, :] = values[i]
    cols = columns_of(at_ref, *facts[0], full[0], cols_ref, rows)
    for kind in range(3):
        first = kind * rows
        chunk = merged(
            mine_ref[first : first + rows, :],
            got_ref[first : first + rows, :],
            cols,
            *facts[kind],
            full[kind],
            half_rows,
            kind > 0,
        )
        trio_ref[first : first + rows, :] = chunk
        if kind == 1:
            left_ref[...] = chunk
        if kind == 2:
            right_ref[...] = chunk


def merge(at, mine, got, half_rows):
    width = mine.shape[1]
    rows = (mine.shape[0] - 24) // 3
    return call(
        functools.partial(merge_kernel, half_rows),
        in_specs=[smem_spec] + [vmem_spec] * 2,
        out_specs=[vmem_spec] * 6,
        out_shape=[shape(rows, width)] * 2 + [shape(3 * rows, width)] + [shape(8, width)] * 3,
        scratch_shapes=[pltpu.VMEM((width, 128), f32)],
        name="merge",
    )(at, mine, got)


def pack(parts, wait_for=()):
    rows, width = parts[0].shape

    def kernel(*refs):
        for i in range(4):
            refs[-1][i] = refs[i][...]

    return call(
        kernel,
        in_specs=[vmem_spec] * 4 + [any_spec] * len(wait_for),
        out_specs=vmem_spec,
        out_shape=shape(4, rows, width),
        name="pack",
    )(*parts, *wait_for)


def join(first, second, carried):
    rows, width = first.shape
    count = len(carried)

    def kernel(first_ref, second_ref, *refs):
        refs[count][0:rows, :] = first_ref[...]
        refs[count][rows:, :] = second_ref[...]

    return call(
        kernel,
        in_specs=[vmem_spec] * 2 + [any_spec] * count,
        out_specs=[vmem_spec] + [any_spec] * count,
        out_shape=[shape(2 * rows, width)] + [shape(*c.shape) for c in carried],
        input_output_aliases={2 + i: 1 + i for i in range(count)},
        name="join",
    )(first, second, *carried)


def row_of(at_ref, core_flip, slot, rows):
    core, x = at_ref[0], at_ref[1]
    core = 1 - core if core_flip else core
    return pl.multiple_of((core * 4 + ((x - slot) & 3)) * rows, rows)


def build(at_ref, mine_ref, other_ref, kinds, own, corr_ref, pen_ref, transposed):
    width = corr_ref.shape[1]
    rows = width // 8
    for flip, ref in ((False, mine_ref), (True, other_ref)):
        for slot in range(4):
            at = row_of(at_ref, flip, slot, rows)
            for i, kind in enumerate(kinds):
                corr_ref[i, pl.ds(at, rows), :] = ref[slot, kind * rows : (kind + 1) * rows, :]
    cross = jnp.zeros((1, width), f32)
    for i, kind in enumerate(kinds):
        corr = corr_ref[i]
        corr = corr.T if transposed else corr
        pen = 2.0 * off_weight * corr
        if kind == own:
            row_index = lax.broadcasted_iota(jnp.int32, corr.shape, 0)
            column = lax.broadcasted_iota(jnp.int32, corr.shape, 1)
            pen = jnp.where(row_index == column, -2.0 * (1.0 - corr), pen)
        cross = cross + jnp.sum(pen * corr, axis=0, keepdims=True)
        high, low = split(pen)
        first = i * 3 * width
        pen_ref[first : first + width, :] = high
        pen_ref[first + width : first + 2 * width, :] = low
        pen_ref[first + 2 * width : first + 3 * width, :] = high
    return cross


def scratch_for(kinds, width):
    return [
        pltpu.VMEM((kinds, width, width), f32),
        pltpu.VMEM((3 * kinds * width, width), bf16),
        pltpu.VMEM((8, width), f32),
    ]


def finish_a_kernel(at_ref, mine_ref, other_ref, *refs):
    facts, (a_ref, *b_refs) = refs[:3], refs[3:7]
    out_ref, corr_ref, pen_ref, vec_ref = refs[-4:]

    @pl.when(pl.program_id(0) == 0)
    def _():
        kinds = (0, 1, 2)
        cross = build(at_ref, mine_ref, other_ref, kinds, 0, corr_ref, pen_ref, True)
        left = jnp.concatenate([thrice(ref[...]) for ref in facts], axis=1)
        vec_ref[0:1, :] = mm(left, pen_ref[...])[5:6]
        vec_ref[1:2, :] = cross

    norms = [
        thrice((b_ref[...] - ref[2:3, :]) * ref[3:4, :]) for b_ref, ref in zip(b_refs, facts)
    ]
    grad = mm(jnp.concatenate(norms, axis=1), pen_ref[...])
    inverse = facts[0][1:2, :]
    normed = (a_ref[...] - facts[0][0:1, :]) * inverse
    out_ref[...] = (grad - vec_ref[0:1, :] - normed * vec_ref[1:2, :]) * inverse


def finish_a(at, mine, other, facts, a, b, prev_b, next_b):
    rows, width = a.shape
    tile = 256
    spec = pl.BlockSpec((tile, width), lambda i: (i, 0))
    whole = pl.BlockSpec((8, width), lambda i: (0, 0))
    slots = pl.BlockSpec(mine.shape, lambda i: (0, 0, 0))
    return call(
        finish_a_kernel,
        mib=40,
        grid=(rows // tile,),
        in_specs=[smem_spec, slots, slots] + [whole] * 3 + [spec] * 4,
        out_specs=spec,
        out_shape=shape(rows, width),
        scratch_shapes=scratch_for(3, width),
        name="finish_a",
    )(at, mine, other, *facts, a, b, prev_b, next_b)


def own_b_kernel(at_ref, mine_ref, other_ref, facts_ref, a_ref, *refs):
    out_ref, sums_ref, corr_ref, pen_ref, _ = refs[-5:]

    @pl.when(pl.program_id(0) == 0)
    def _():
        sums_ref[...] = jnp.zeros_like(sums_ref)
        cross = build(at_ref, mine_ref, other_ref, (0,), 0, corr_ref, pen_ref, False)
        sums_ref[0:1, :] = mm(thrice(facts_ref[...]), pen_ref[...])[4:5]
        sums_ref[1:2, :] = cross

    norm_a = (a_ref[...] - facts_ref[0:1, :]) * facts_ref[1:2, :]
    out_ref[...] = mm(thrice(norm_a), pen_ref[...])


def own_b(at, mine, other, facts, a, wait_for):
    rows, width = a.shape
    tile = 256
    spec = pl.BlockSpec((tile, width), lambda i: (i, 0))
    whole = pl.BlockSpec((8, width), lambda i: (0, 0))
    slots = pl.BlockSpec(mine.shape, lambda i: (0, 0, 0))
    return call(
        own_b_kernel,
        mib=24,
        grid=(rows // tile,),
        in_specs=[smem_spec, slots, slots, whole, spec] + [any_spec] * len(wait_for),
        out_specs=[spec, whole],
        out_shape=[shape(rows, width), shape(8, width)],
        scratch_shapes=scratch_for(1, width),
        name="own_b",
    )(at, mine, other, facts, a, *wait_for)


def finish_b_kernel(bounds, at_ref, mine_ref, other_ref, f_ref, pf_ref, nf_ref, *refs):
    sums_ref, part_ref, b_ref, *halos = refs[:9]
    out_ref, corr_ref, pen_ref, vec_ref = refs[-4:]
    step = pl.program_id(0)

    @pl.when(step == 0)
    def _():
        cross = build(at_ref, mine_ref, other_ref, (0, 1), 2, corr_ref, pen_ref, False)
        left = jnp.concatenate([thrice(pf_ref[...]), thrice(nf_ref[...])], axis=1)
        vec_ref[0:1, :] = sums_ref[0:1, :] + mm(left, pen_ref[...])[4:5]
        vec_ref[1:2, :] = sums_ref[1:2, :] + cross

    def current(parts):
        rest = jnp.where(step < bounds[2], parts[1][...], parts[2][...])
        return jnp.where(step < bounds[1], parts[0][...], rest)

    prev = current(halos[:3]) * pf_ref[6:7, :] + pf_ref[7:8, :]
    next_ = current(halos[3:]) * nf_ref[6:7, :] + nf_ref[7:8, :]
    both = jnp.concatenate([thrice(prev), thrice(next_)], axis=1)
    grad = part_ref[...] + mm(both, pen_ref[...])
    normed = (b_ref[...] - f_ref[2:3, :]) * f_ref[3:4, :]
    out_ref[...] = (grad - vec_ref[0:1, :] - normed * vec_ref[1:2, :]) * f_ref[3:4, :]


def finish_b(at, mine, other, facts, sums, part, b, halos):
    rows, width = b.shape
    tile = 128
    _, bounds, maps = halo_cuts(rows, tile)
    spec = pl.BlockSpec((tile, width), lambda i: (i, 0))
    parts = [pl.BlockSpec((tile, width), part) for part in maps]
    whole = pl.BlockSpec((8, width), lambda i: (0, 0))
    slots = pl.BlockSpec(mine.shape, lambda i: (0, 0, 0))
    return call(
        functools.partial(finish_b_kernel, bounds),
        mib=24,
        grid=(rows // tile,),
        in_specs=[smem_spec, slots, slots] + [whole] * 4 + [spec] * 2 + parts * 2,
        out_specs=spec,
        out_shape=shape(rows, width),
        scratch_shapes=scratch_for(2, width),
        name="finish_b",
    )(at, mine, other, *facts, sums, part, b, *halos)


def per_device(view_a, view_b):
    local_rows, width = view_a.shape
    half_rows = local_rows * lax.axis_size("row") // 2
    index = lax.axis_index("row")
    at = jnp.stack([index & 1, (index >> 1) & 3])

    prev_raw = across(view_b, 1)
    next_raw = across(view_b, -1)
    sums = sums_of(view_a, view_b)
    sums = sums + to_core(sums)
    parts = [sums] + [to_x(sums, shift) for shift in (1, 2, 3)]

    a_top, a_mid, a_low, half_facts, keep, send = own_corr(at, view_a, view_b, parts, half_rows)
    slots = fan(keep, to_core(send))
    own_parts = [slots[0]] + [to_x(slots[shift], shift) for shift in (1, 2, 3)]
    own, a_top = own_sum(own_parts, a_top, half_facts)
    prev_top = across(a_top, 1)
    next_top = across(a_top, -1)

    keep, *sends = side_corr(at, view_a, prev_raw, next_raw, half_facts, [own])
    slots = fan(keep, *[to_core(send) for send in sends])
    side_parts = [slots[0]] + [to_x(slots[shift], shift) for shift in (1, 2, 3)]
    mine = message(own, side_parts, half_facts, prev_top, next_top)
    left, right, trio, *facts = merge(at, mine, to_y(mine), half_rows)
    from_next = across(left, -1)
    from_prev = across(right, 1)
    trio_slots = [trio] + [to_x(trio, shift) for shift in (1, 2, 3)]
    ends, a_mid, a_low = join(from_prev, from_next, [a_mid, a_low])
    prev_mid = across(a_mid, 1)
    next_mid = across(a_mid, -1)
    prev_low = across(a_low, 1)
    next_low = across(a_low, -1)
    end_slots = [ends] + [to_x(ends, shift) for shift in (1, 2, 3)]
    mine = pack(trio_slots, [ends, prev_mid, next_mid])
    other = to_core(mine)
    grad_a = finish_a(at, mine, other, facts, view_a, view_b, prev_raw, next_raw)
    ends = pack(end_slots, [grad_a, prev_low, next_low])
    part_b, sums = own_b(at, mine, other, facts[0], view_a, [ends])
    halos = [prev_top, prev_mid, prev_low, next_top, next_mid, next_low]
    grad_b = finish_b(at, ends, to_core(ends), facts, sums, part_b, view_b, halos)
    return (grad_a, grad_b)


def solution(mesh):
    placed = (P("row", "grp"), P("row", "grp"))
    return jax.shard_map(
        per_device,
        mesh=mesh,
        in_specs=placed,
        out_specs=(P("row", "grp"), P("row", "grp")),
        check_vma=False,
    )
```

time: 164 us -> 156 us (0.951)
  starting transfers between devices: 63.8 us -> 54.6 us
    ppermute x10, waiting for transfers between devices: 34.4 us -> 23.3 us  [across(): lax.ppermute(block, 'grp', [(i, (i + shift) % count) for i in range(count)])]
    ppermute x18 -> x15, waiting for transfers between devices: 14.9 us -> 22.6 us  [to_x(): return lax.ppermute(block, 'row', pairs)]
    ppermute x18 -> x15, starting transfers between devices: 26.3 us -> 21.1 us  [to_x(): return lax.ppermute(block, 'row', pairs)]
    ppermute x6, starting transfers between devices: 13.3 us -> 8.18 us  [to_core(): return lax.ppermute(block, 'row', [(i, i ^ 1) for i in range(16)])]
    ppermute x2 -> x1, waiting for transfers between devices: 5.63 us -> 9.34 us  [to_y(): return lax.ppermute(block, 'row', [(i, i ^ 8) for i in range(16)])]
    ppermute x10, starting transfers between devices: 18.9 us -> 22.6 us  [across(): lax.ppermute(block, 'grp', [(i, (i + shift) % count) for i in range(count)])]
    ppermute x2 -> x1, starting transfers between devices: 5.24 us -> 2.71 us  [to_y(): return lax.ppermute(block, 'row', [(i, i ^ 8) for i in range(16)])]
    pallas_call x11 -> x10, Pallas kernels: 25.7 us -> 27 us  [the longest x1 9.13 us: finish_a(): call(finish_a_kernel, mib=40, grid=(rows // tile,), in_specs=[smem_spec,...]
  transfers between devices with their start and end apart: 36 -> 32, of which waited for: 18 -> 18; matrix products, arithmetic and copies ran while one was open for 0% -> 0% of each run, Pallas kernels for 12% -> 16%
where the time goes in v4:
time: 156 us; the launch traced here: 155 us
  waiting for transfers between devices  59.8 us (38%)
  starting transfers between devices  54.6 us (35%)
  Pallas kernels  33.7 us (22%)
  local copies, waits for them, and re-layouts  6.37 us (4%)
    ppermute x10, waiting for transfers between devices, across(): lax.ppermute(block, 'grp', [(i, (i + shift) % count) for i in range(count)])  23.3 us
    ppermute x15, waiting for transfers between devices, to_x(): return lax.ppermute(block, 'row', pairs)  22.6 us
    ppermute x10, starting transfers between devices, across(): lax.ppermute(block, 'grp', [(i, (i + shift) % count) for i in range(count)])  22.6 us
    ppermute x15, starting transfers between devices, to_x(): return lax.ppermute(block, 'row', pairs)  21.1 us
    ppermute x1, waiting for transfers between devices, to_y(): return lax.ppermute(block, 'row', [(i, i ^ 8) for i in range(16)])  9.34 us
    pallas_call x1, Pallas kernels, finish_a(): call(finish_a_kernel, mib=40, grid=(rows // tile,), in_specs=[smem_spec,...  9.13 us
    ppermute x6, starting transfers between devices, to_core(): return lax.ppermute(block, 'row', [(i, i ^ 1) for i in range(16)])  8.18 us
    pallas_call x1, Pallas kernels, finish_b(): call(functools.partial(finish_b_kernel, bounds), mib=24, grid=(rows // ti...  7.71 us
  transfers between devices with their start and end apart: 32, of which 18 were waited for; matrix products, arithmetic and copies ran while one was open for 0% of the time, Pallas kernels for 16%

profile of v4, /device:TPU:1, one launch (start us, length us, event | category | flops | bytes accessed | tf_op | source)
XLA Modules:
  0.0 155.4 jit_solution(3549516713844663664)
XLA Ops:
  0.6 2.5 %collective-permute-start.8 = (f32[1024,512]{1,0:T(8,128)}, f32[1024,512]{1,0:T(8,128)}, u32[]{:S(2)}, u32[]{:S(2)}) collective-permute-start(f32[1024,512]{1,0:T(8,128)} %refs_2_.1), channel_id=1, source_target_pairs={{0,16},{16,32},{32,48},{48,64},{64,80},{80,96},{96,112},{112,128},... | collective-permute-start | bytes 6291464 | tf_op jit(solution)/shard_map/ppermute | solution.py:34
  3.2 5.0 %collective-permute-start.9 = (f32[1024,512]{1,0:T(8,128)}, f32[1024,512]{1,0:T(8,128)}, u32[]{:S(2)}, u32[]{:S(2)}) collective-permute-start(f32[1024,512]{1,0:T(8,128)} %refs_2_.1), channel_id=1, source_target_pairs={{0,240},{16,0},{32,16},{48,32},{64,48},{80,64},{96,80},{112,96},{1... | collective-permute-start | bytes 6291464 | tf_op jit(solution)/shard_map/ppermute | solution.py:34
  8.2 1.6 %copy-done = f32[1024,512]{1,0:T(8,128)S(1)} copy-done((f32[1024,512]{1,0:T(8,128)S(1)}, f32[1024,512]{1,0:T(8,128)}, u32[]{:S(2)}) %copy-start) | copy-done | bytes 2097176
  9.8 1.6 %copy-done.2 = f32[1024,512]{1,0:T(8,128)S(1)} copy-done((f32[1024,512]{1,0:T(8,128)S(1)}, f32[1024,512]{1,0:T(8,128)}, u32[]{:S(2)}) %copy-start.2) | copy-done | bytes 2097176
  12.0 1.0 collective-permute-start
  13.1 0.8 collective-permute-done
  13.9 1.2 collective-permute-start.1
  15.1 2.5 %collective-permute-start.2 = (f32[8,512]{1,0:T(8,128)S(1)}, f32[8,512]{1,0:T(8,128)S(1)}, u32[]{:S(2)}, u32[]{:S(2)}) collective-permute-start(f32[8,512]{1,0:T(8,128)S(1)} %add.3.refs_0_), channel_id=1, source_target_pairs={{0,4},{1,5},{2,6},{3,7},{4,0},{5,1},{6,2},{7,3},{8,12},{9,13},{10,... | collective-permute-start | bytes 49160 | tf_op jit(solution)/shard_map/ppermute | solution.py:47
  17.6 1.2 collective-permute-start.3
  18.8 0.8 collective-permute-done.2.refs_2_
  19.6 0.9 collective-permute-done.3.refs_3_
  20.6 1.6 %copy-done.3 = f32[1024,512]{1,0:T(8,128)S(1)} copy-done((f32[1024,512]{1,0:T(8,128)S(1)}, f32[1024,512]{1,0:T(8,128)}, u32[]{:S(2)}) %copy-start.3) | copy-done | bytes 2097176
  22.2 5.4 %own_corr.1 = (f32[512,512]{1,0:T(8,128)S(1)}, f32[128,512]{1,0:T(8,128)S(1)}, f32[384,512]{1,0:T(8,128)S(1)}, f32[8,512]{1,0:T(8,128)S(1)}, f32[4,64,512]{2,1,0:T(8,128)S(1)}, /*index=5*/f32[4,64,512]{2,1,0:T(8,128)S(1)}) custom-call(s32[2]{0:T(128)S(1)} %pad_add_fusion.at_ref, f32[1024,512]{1,0:T(8,128)S(1)} %copy-done.1, f32[1024,512]{1,0:T(8,128)S(1)} %copy-done.3, ...), custom_call_target="tpu_custom_call" | custom-call | flops 1 | bytes 1 | tf_op jit(solution)/shard_map/own_corr/pallas_call | solution.py:159
  27.6 1.7 %collective-permute-start.4 = (f32[4,64,512]{2,1,0:T(8,128)S(1)}, f32[4,64,512]{2,1,0:T(8,128)S(1)}, u32[]{:S(2)}, u32[]{:S(2)}) collective-permute-start(f32[4,64,512]{2,1,0:T(8,128)S(1)} %get-tuple-element.33), channel_id=1, source_target_pairs={{0,1},{1,0},{2,3},{3,2},{4,5},{5,4},{6,7},{7,6},{8,9},{9,8},{10,11... | collective-permute-start | bytes 1572872 | tf_op jit(solution)/shard_map/ppermute | solution.py:38
  29.3 1.5 collective-permute-done.4.refs_0_
  31.0 3.5 %collective-permute-start.6 = (f32[64,512]{1,0:T(8,128)S(1)}, f32[64,512]{1,0:T(8,128)S(1)}, u32[]{:S(2)}, u32[]{:S(2)}) collective-permute-start(f32[64,512]{1,0:T(8,128)S(1)} %get-tuple-element.36), channel_id=1, source_target_pairs={{0,4},{1,5},{2,6},{3,7},{4,0},{5,1},{6,2},{7,3},{8,12},{9,13},{10,... | collective-permute-start | bytes 393224 | tf_op jit(solution)/shard_map/ppermute | solution.py:47
  34.6 2.5 %collective-permute-done.5.refs_1_ = f32[64,512]{1,0:T(8,128)S(1)} collective-permute-done((f32[64,512]{1,0:T(8,128)S(1)}, f32[64,512]{1,0:T(8,128)S(1)}, u32[]{:S(2)}, u32[]{:S(2)}) %collective-permute-start.5) | collective-permute-done | bytes 131104 | tf_op jit(solution)/shard_map/ppermute | solution.py:47
  37.0 3.7 %collective-permute-done.6.refs_2_ = f32[64,512]{1,0:T(8,128)S(1)} collective-permute-done((f32[64,512]{1,0:T(8,128)S(1)}, f32[64,512]{1,0:T(8,128)S(1)}, u32[]{:S(2)}, u32[]{:S(2)}) %collective-permute-start.6) | collective-permute-done | bytes 131104 | tf_op jit(solution)/shard_map/ppermute | solution.py:47
  40.9 3.6 %collective-permute-start.16 = (f32[520,512]{1,0:T(8,128)S(1)}, f32[520,512]{1,0:T(8,128)S(1)}, u32[]{:S(2)}, u32[]{:S(2)}) collective-permute-start(f32[520,512]{1,0:T(8,128)S(1)} %get-tuple-element.48), channel_id=1, source_target_pairs={{0,240},{16,0},{32,16},{48,32},{64,48},{80,64},{96,80},{112,96},{1... | collective-permute-start | bytes 3194888 | tf_op jit(solution)/shard_map/ppermute | solution.py:34
  44.5 9.3 %collective-permute-done.8.prev_ref.refs_5_ = f32[1024,512]{1,0:T(8,128)} collective-permute-done((f32[1024,512]{1,0:T(8,128)}, f32[1024,512]{1,0:T(8,128)}, u32[]{:S(2)}, u32[]{:S(2)}) %collective-permute-start.8) | collective-permute-done | bytes 2097184 | tf_op jit(solution)/shard_map/ppermute | solution.py:34
  53.8 5.9 %side_corr.1 = (f32[4,128,512]{2,1,0:T(8,128)S(1)}, f32[2,128,512]{2,1,0:T(8,128)S(1)}, f32[2,128,512]{2,1,0:T(8,128)S(1)}) custom-call(s32[2]{0:T(128)S(1)} %pad_add_fusion.at_ref, f32[1024,512]{1,0:T(8,128)S(1)} %copy-done.1, f32[1024,512]{1,0:T(8,128)} %collective-permute-done.8.prev_ref.refs_5_, f32[1024,512]{1,0:T(8,128)} %collective-permute-done.9.next_ref.refs_6_, ...), custom_call_target="tpu_custom_call" | custom-call | flops 1 | bytes 1 | tf_op jit(solution)/shard_map/side_corr/pallas_call | solution.py:200
  59.7 2.1 %collective-permute-start.10 = (f32[2,128,512]{2,1,0:T(8,128)S(1)}, f32[2,128,512]{2,1,0:T(8,128)S(1)}, u32[]{:S(2)}, u32[]{:S(2)}) collective-permute-start(f32[2,128,512]{2,1,0:T(8,128)S(1)} %get-tuple-element.42), channel_id=1, source_target_pairs={{0,1},{1,0},{2,3},{3,2},{4,5},{5,4},{6,7},{7,6},{8,9},{9,8},{10,11... | collective-permute-start | bytes 1572872 | tf_op jit(solution)/shard_map/ppermute | solution.py:38
  61.9 1.4 collective-permute-done.10.refs_0_
  63.4 0.7 collective-permute-done.11.refs_1_
  64.2 1.5 collective-permute-start.12
  65.7 2.5 %collective-permute-start.13 = (f32[128,512]{1,0:T(8,128)S(1)}, f32[128,512]{1,0:T(8,128)S(1)}, u32[]{:S(2)}, u32[]{:S(2)}) collective-permute-start(f32[128,512]{1,0:T(8,128)S(1)} %get-tuple-element.46), channel_id=1, source_target_pairs={{0,4},{1,5},{2,6},{3,7},{4,0},{5,1},{6,2},{7,3},{8,12},{9,13},{10,... | collective-permute-start | bytes 786440 | tf_op jit(solution)/shard_map/ppermute | solution.py:47
  68.1 1.2 collective-permute-start.14
  69.3 7.2 %collective-permute-done.15.refs_5_.refs_3_ = f32[520,512]{1,0:T(8,128)S(1)} collective-permute-done((f32[520,512]{1,0:T(8,128)S(1)}, f32[520,512]{1,0:T(8,128)S(1)}, u32[]{:S(2)}, u32[]{:S(2)}) %collective-permute-start.15) | collective-permute-done | bytes 1064992 | tf_op jit(solution)/shard_map/ppermute | solution.py:34
  76.5 3.3 %collective-permute-done.13.refs_2_ = f32[128,512]{1,0:T(8,128)S(1)} collective-permute-done((f32[128,512]{1,0:T(8,128)S(1)}, f32[128,512]{1,0:T(8,128)S(1)}, u32[]{:S(2)}, u32[]{:S(2)}) %collective-permute-start.13) | collective-permute-done | bytes 262176 | tf_op jit(solution)/shard_map/ppermute | solution.py:47
  79.9 2.7 %collective-permute-start.17 = (f32[216,512]{1,0:T(8,128)S(1)}, f32[216,512]{1,0:T(8,128)S(1)}, u32[]{:S(2)}, u32[]{:S(2)}) collective-permute-start(f32[216,512]{1,0:T(8,128)S(1)} %message.1.mine_ref), channel_id=1, source_target_pairs={{0,8},{1,9},{2,10},{3,11},{4,12},{5,13},{6,14},{7,15},{8,0},{9,1},... | collective-permute-start | bytes 1327112 | tf_op jit(solution)/shard_map/ppermute | solution.py:42
  82.6 9.3 %collective-permute-done.17.got_ref = f32[216,512]{1,0:T(8,128)S(1)} collective-permute-done((f32[216,512]{1,0:T(8,128)S(1)}, f32[216,512]{1,0:T(8,128)S(1)}, u32[]{:S(2)}, u32[]{:S(2)}) %collective-permute-start.17) | collective-permute-done | bytes 442400 | tf_op jit(solution)/shard_map/ppermute | solution.py:42
  91.9 1.0 merge.1
  93.0 4.0 %collective-permute-start.22 = (f32[64,512]{1,0:T(8,128)S(1)}, f32[64,512]{1,0:T(8,128)S(1)}, u32[]{:S(2)}, u32[]{:S(2)}) collective-permute-start(f32[64,512]{1,0:T(8,128)S(1)} %get-tuple-element.51), channel_id=1, source_target_pairs={{0,240},{16,0},{32,16},{48,32},{64,48},{80,64},{96,80},{112,96},{1... | collective-permute-start | bytes 393224 | tf_op jit(solution)/shard_map/ppermute | solution.py:34
  97.1 1.0 collective-permute-start.18
  98.1 3.6 %collective-permute-start.19 = (f32[192,512]{1,0:T(8,128)S(1)}, f32[192,512]{1,0:T(8,128)S(1)}, u32[]{:S(2)}, u32[]{:S(2)}) collective-permute-start(f32[192,512]{1,0:T(8,128)S(1)} %get-tuple-element.49.refs_0_), channel_id=1, source_target_pairs={{0,4},{1,5},{2,6},{3,7},{4,0},{5,1},{6,2},{7,3},{8,12},{9,13},{10,... | collective-permute-start | bytes 1179656 | tf_op jit(solution)/shard_map/ppermute | solution.py:47
  101.9 3.6 %collective-permute-start.24 = (f32[128,512]{1,0:T(8,128)S(1)}, f32[128,512]{1,0:T(8,128)S(1)}, u32[]{:S(2)}, u32[]{:S(2)}) collective-permute-start(f32[128,512]{1,0:T(8,128)S(1)} %get-tuple-element.55), channel_id=1, source_target_pairs={{0,240},{16,0},{32,16},{48,32},{64,48},{80,64},{96,80},{112,96},{1... | collective-permute-start | bytes 786440 | tf_op jit(solution)/shard_map/ppermute | solution.py:34
  105.4 3.8 %collective-permute-done.23.refs_5_.refs_4_ = f32[128,512]{1,0:T(8,128)S(1)} collective-permute-done((f32[128,512]{1,0:T(8,128)S(1)}, f32[128,512]{1,0:T(8,128)S(1)}, u32[]{:S(2)}, u32[]{:S(2)}) %collective-permute-start.23) | collective-permute-done | bytes 262176 | tf_op jit(solution)/shard_map/ppermute | solution.py:34
  109.2 8.5 %collective-permute-done.19.refs_2_ = f32[192,512]{1,0:T(8,128)S(1)} collective-permute-done((f32[192,512]{1,0:T(8,128)S(1)}, f32[192,512]{1,0:T(8,128)S(1)}, u32[]{:S(2)}, u32[]{:S(2)}) %collective-permute-start.19) | collective-permute-done | bytes 393248 | tf_op jit(solution)/shard_map/ppermute | solution.py:47
  118.2 2.2 %collective-permute-start.25 = (f32[4,192,512]{2,1,0:T(8,128)S(1)}, f32[4,192,512]{2,1,0:T(8,128)S(1)}, u32[]{:S(2)}, u32[]{:S(2)}) collective-permute-start(f32[4,192,512]{2,1,0:T(8,128)S(1)} %pack.2.mine_ref), channel_id=1, source_target_pairs={{0,1},{1,0},{2,3},{3,2},{4,5},{5,4},{6,7},{7,6},{8,9},{9,8},{10,11... | collective-permute-start | bytes 4718600 | tf_op jit(solution)/shard_map/ppermute | solution.py:38
  120.4 3.6 %collective-permute-start.30 = (f32[384,512]{1,0:T(8,128)S(1)}, f32[384,512]{1,0:T(8,128)S(1)}, u32[]{:S(2)}, u32[]{:S(2)}) collective-permute-start(f32[384,512]{1,0:T(8,128)S(1)} %get-tuple-element.59), channel_id=1, source_target_pairs={{0,240},{16,0},{32,16},{48,32},{64,48},{80,64},{96,80},{112,96},{1... | collective-permute-start | bytes 2359304 | tf_op jit(solution)/shard_map/ppermute | solution.py:34
  124.0 3.0 %collective-permute-start.27 = (f32[128,512]{1,0:T(8,128)S(1)}, f32[128,512]{1,0:T(8,128)S(1)}, u32[]{:S(2)}, u32[]{:S(2)}) collective-permute-start(f32[128,512]{1,0:T(8,128)S(1)} %get-tuple-element.54.refs_4_.refs_0_), channel_id=1, source_target_pairs={{0,4},{1,5},{2,6},{3,7},{4,0},{5,1},{6,2},{7,3},{8,12},{9,13},{10,... | collective-permute-start | bytes 786440 | tf_op jit(solution)/shard_map/ppermute | solution.py:47
  127.0 9.1 %finish_a.1.refs_4_ = f32[1024,512]{1,0:T(8,128)} custom-call(s32[2]{0:T(128)S(1)} %pad_add_fusion.at_ref, f32[4,192,512]{2,1,0:T(8,128)S(1)} %pack.2.mine_ref, f32[4,192,512]{2,1,0:T(8,128)S(1)} %collective-permute-done.25.other_ref, f32[8,512]{1,0:T(8,128)S(1)} %get-tuple-element.56.refs_0_.facts_ref.f_ref, f32[8,512]{1,0:T(8,128)S(1)} %get-tuple-element.57.refs_1_.pf_ref, ...), custom_call_target="tpu_custom_call" | custom-call | flops 1 | bytes 1 | tf_op jit(solution)/shard_map/finish_a/pallas_call | solution.py:449
  136.1 2.2 %collective-permute-done.27.refs_2_ = f32[128,512]{1,0:T(8,128)S(1)} collective-permute-done((f32[128,512]{1,0:T(8,128)S(1)}, f32[128,512]{1,0:T(8,128)S(1)}, u32[]{:S(2)}, u32[]{:S(2)}) %collective-permute-start.27) | collective-permute-done | bytes 262176 | tf_op jit(solution)/shard_map/ppermute | solution.py:47
  138.6 3.0 %collective-permute-done.29.refs_5_ = f32[384,512]{1,0:T(8,128)S(1)} collective-permute-done((f32[384,512]{1,0:T(8,128)S(1)}, f32[384,512]{1,0:T(8,128)S(1)}, u32[]{:S(2)}, u32[]{:S(2)}) %collective-permute-start.29) | collective-permute-done | bytes 786464 | tf_op jit(solution)/shard_map/ppermute | solution.py:34
  141.6 1.6 %copy-done.5 = f32[1024,512]{1,0:T(8,128)S(1)} copy-done((f32[1024,512]{1,0:T(8,128)S(1)}, f32[1024,512]{1,0:T(8,128)}, u32[]{:S(2)}) %copy-start.5) | copy-done | bytes 2097176
  143.3 1.0 collective-permute-start.31
  144.2 3.4 %own_b.1 = (f32[1024,512]{1,0:T(8,128)S(1)}, f32[8,512]{1,0:T(8,128)S(1)}) custom-call(s32[2]{0:T(128)S(1)} %pad_add_fusion.at_ref, f32[4,192,512]{2,1,0:T(8,128)S(1)} %pack.2.mine_ref, f32[4,192,512]{2,1,0:T(8,128)S(1)} %collective-permute-done.25.other_ref, f32[8,512]{1,0:T(8,128)S(1)} %get-tuple-element.56.refs_0_.facts_ref.f_ref, ...), custom_call_target="tpu_custom_call" | custom-call | flops 1 | bytes 1 | tf_op jit(solution)/shard_map/own_b/pallas_call | solution.py:481
  147.7 7.7 %finish_b.1 = f32[1024,512]{1,0:T(8,128)} custom-call(s32[2]{0:T(128)S(1)} %pad_add_fusion.at_ref, f32[4,128,512]{2,1,0:T(8,128)S(1)} %pack.3.refs_0_.mine_ref, f32[4,128,512]{2,1,0:T(8,128)S(1)} %collective-permute-done.31.other_ref, f32[8,512]{1,0:T(8,128)S(1)} %get-tuple-element.56.refs_0_.facts_ref.f_ref, f32[8,512]{1,0:T(8,128)S(1)} %get-tuple-element.57.refs_1_.pf_ref, ...), custom_call_target="tpu_custom_call" | custom-call | flops 1 | bytes 1 | tf_op jit(solution)/shard_map/finish_b/pallas_call | solution.py:525
  (44 shorter events, 2.4 us)
Async XLA Ops:
  0.6 53.2 %collective-permute-start.8 = (f32[1024,512]{1,0:T(8,128)}, f32[1024,512]{1,0:T(8,128)}, u32[]{:S(2)}, u32[]{:S(2)}) collective-permute-start(f32[1024,512]{1,0:T(8,128)} %refs_2_.1), channel_id=1, source_target_pairs={{0,16},{16,32},{32,48},{48,64},{64,80},{80,96},{96,112},{112,128},... | collective-permute-start | bytes 6291464 | tf_op jit(solution)/shard_map/ppermute | solution.py:34
  3.2 50.6 %collective-permute-start.9 = (f32[1024,512]{1,0:T(8,128)}, f32[1024,512]{1,0:T(8,128)}, u32[]{:S(2)}, u32[]{:S(2)}) collective-permute-start(f32[1024,512]{1,0:T(8,128)} %refs_2_.1), channel_id=1, source_target_pairs={{0,240},{16,0},{32,16},{48,32},{64,48},{80,64},{96,80},{112,96},{1... | collective-permute-start | bytes 6291464 | tf_op jit(solution)/shard_map/ppermute | solution.py:34
  8.2 1.6 %copy-start = (f32[1024,512]{1,0:T(8,128)S(1)}, f32[1024,512]{1,0:T(8,128)}, u32[]{:S(2)}) copy-start(f32[1024,512]{1,0:T(8,128)} %a_ref.7) | copy-start | bytes 6291460
  9.8 1.6 %copy-start.2 = (f32[1024,512]{1,0:T(8,128)S(1)}, f32[1024,512]{1,0:T(8,128)}, u32[]{:S(2)}) copy-start(f32[1024,512]{1,0:T(8,128)} %refs_2_.1) | copy-start | bytes 6291460
  11.4 9.2 %copy-start.1 = (f32[1024,512]{1,0:T(8,128)S(1)}, f32[1024,512]{1,0:T(8,128)}, u32[]{:S(2)}) copy-start(f32[1024,512]{1,0:T(8,128)} %a_ref.7) | copy-start | bytes 6291460
  12.0 1.9 %collective-permute-start = (f32[8,512]{1,0:T(8,128)S(1)}, f32[8,512]{1,0:T(8,128)S(1)}, u32[]{:S(2)}, u32[]{:S(2)}) collective-permute-start(f32[8,512]{1,0:T(8,128)S(1)} %sums.1), channel_id=1, source_target_pairs={{0,1},{1,0},{2,3},{3,2},{4,5},{5,4},{6,7},{7,6},{8,9},{9,8},{10,11... | collective-permute-start | bytes 49160 | tf_op jit(solution)/shard_map/ppermute | solution.py:38
  13.9 4.9 %collective-permute-start.1 = (f32[8,512]{1,0:T(8,128)S(1)}, f32[8,512]{1,0:T(8,128)S(1)}, u32[]{:S(2)}, u32[]{:S(2)}) collective-permute-start(f32[8,512]{1,0:T(8,128)S(1)} %add.3.refs_0_), channel_id=1, source_target_pairs={{0,2},{1,3},{2,4},{3,5},{4,6},{5,7},{6,0},{7,1},{8,10},{9,11},{10,... | collective-permute-start | bytes 49160 | tf_op jit(solution)/shard_map/ppermute | solution.py:47
  15.1 4.5 %collective-permute-start.2 = (f32[8,512]{1,0:T(8,128)S(1)}, f32[8,512]{1,0:T(8,128)S(1)}, u32[]{:S(2)}, u32[]{:S(2)}) collective-permute-start(f32[8,512]{1,0:T(8,128)S(1)} %add.3.refs_0_), channel_id=1, source_target_pairs={{0,4},{1,5},{2,6},{3,7},{4,0},{5,1},{6,2},{7,3},{8,12},{9,13},{10,... | collective-permute-start | bytes 49160 | tf_op jit(solution)/shard_map/ppermute | solution.py:47
  17.6 3.0 %collective-permute-start.3 = (f32[8,512]{1,0:T(8,128)S(1)}, f32[8,512]{1,0:T(8,128)S(1)}, u32[]{:S(2)}, u32[]{:S(2)}) collective-permute-start(f32[8,512]{1,0:T(8,128)S(1)} %add.3.refs_0_), channel_id=1, source_target_pairs={{0,6},{1,7},{2,0},{3,1},{4,2},{5,3},{6,4},{7,5},{8,14},{9,15},{10,... | collective-permute-start | bytes 49160 | tf_op jit(solution)/shard_map/ppermute | solution.py:47
  20.6 1.6 %copy-start.3 = (f32[1024,512]{1,0:T(8,128)S(1)}, f32[1024,512]{1,0:T(8,128)}, u32[]{:S(2)}) copy-start(f32[1024,512]{1,0:T(8,128)} %refs_2_.1) | copy-start | bytes 6291460
  27.6 3.3 %collective-permute-start.4 = (f32[4,64,512]{2,1,0:T(8,128)S(1)}, f32[4,64,512]{2,1,0:T(8,128)S(1)}, u32[]{:S(2)}, u32[]{:S(2)}) collective-permute-start(f32[4,64,512]{2,1,0:T(8,128)S(1)} %get-tuple-element.33), channel_id=1, source_target_pairs={{0,1},{1,0},{2,3},{3,2},{4,5},{5,4},{6,7},{7,6},{8,9},{9,8},{10,11... | collective-permute-start | bytes 1572872 | tf_op jit(solution)/shard_map/ppermute | solution.py:38
  30.9 6.1 %collective-permute-start.5 = (f32[64,512]{1,0:T(8,128)S(1)}, f32[64,512]{1,0:T(8,128)S(1)}, u32[]{:S(2)}, u32[]{:S(2)}) collective-permute-start(f32[64,512]{1,0:T(8,128)S(1)} %get-tuple-element.35), channel_id=1, source_target_pairs={{0,2},{1,3},{2,4},{3,5},{4,6},{5,7},{6,0},{7,1},{8,10},{9,11},{10,... | collective-permute-start | bytes 393224 | tf_op jit(solution)/shard_map/ppermute | solution.py:47
  31.0 9.7 %collective-permute-start.6 = (f32[64,512]{1,0:T(8,128)S(1)}, f32[64,512]{1,0:T(8,128)S(1)}, u32[]{:S(2)}, u32[]{:S(2)}) collective-permute-start(f32[64,512]{1,0:T(8,128)S(1)} %get-tuple-element.36), channel_id=1, source_target_pairs={{0,4},{1,5},{2,6},{3,7},{4,0},{5,1},{6,2},{7,3},{8,12},{9,13},{10,... | collective-permute-start | bytes 393224 | tf_op jit(solution)/shard_map/ppermute | solution.py:47
  34.6 6.2 %collective-permute-start.7 = (f32[64,512]{1,0:T(8,128)S(1)}, f32[64,512]{1,0:T(8,128)S(1)}, u32[]{:S(2)}, u32[]{:S(2)}) collective-permute-start(f32[64,512]{1,0:T(8,128)S(1)} %get-tuple-element.37), channel_id=1, source_target_pairs={{0,6},{1,7},{2,0},{3,1},{4,2},{5,3},{6,4},{7,5},{8,14},{9,15},{10,... | collective-permute-start | bytes 393224 | tf_op jit(solution)/shard_map/ppermute | solution.py:47
  40.8 35.7 %collective-permute-start.15 = (f32[520,512]{1,0:T(8,128)S(1)}, f32[520,512]{1,0:T(8,128)S(1)}, u32[]{:S(2)}, u32[]{:S(2)}) collective-permute-start(f32[520,512]{1,0:T(8,128)S(1)} %get-tuple-element.48), channel_id=1, source_target_pairs={{0,16},{16,32},{32,48},{48,64},{64,80},{80,96},{96,112},{112,128},... | collective-permute-start | bytes 3194888 | tf_op jit(solution)/shard_map/ppermute | solution.py:34
  40.9 35.6 %collective-permute-start.16 = (f32[520,512]{1,0:T(8,128)S(1)}, f32[520,512]{1,0:T(8,128)S(1)}, u32[]{:S(2)}, u32[]{:S(2)}) collective-permute-start(f32[520,512]{1,0:T(8,128)S(1)} %get-tuple-element.48), channel_id=1, source_target_pairs={{0,240},{16,0},{32,16},{48,32},{64,48},{80,64},{96,80},{112,96},{1... | collective-permute-start | bytes 3194888 | tf_op jit(solution)/shard_map/ppermute | solution.py:34
  59.7 3.7 %collective-permute-start.10 = (f32[2,128,512]{2,1,0:T(8,128)S(1)}, f32[2,128,512]{2,1,0:T(8,128)S(1)}, u32[]{:S(2)}, u32[]{:S(2)}) collective-permute-start(f32[2,128,512]{2,1,0:T(8,128)S(1)} %get-tuple-element.42), channel_id=1, source_target_pairs={{0,1},{1,0},{2,3},{3,2},{4,5},{5,4},{6,7},{7,6},{8,9},{9,8},{10,11... | collective-permute-start | bytes 1572872 | tf_op jit(solution)/shard_map/ppermute | solution.py:38
  61.8 2.3 %collective-permute-start.11 = (f32[2,128,512]{2,1,0:T(8,128)S(1)}, f32[2,128,512]{2,1,0:T(8,128)S(1)}, u32[]{:S(2)}, u32[]{:S(2)}) collective-permute-start(f32[2,128,512]{2,1,0:T(8,128)S(1)} %get-tuple-element.43), channel_id=1, source_target_pairs={{0,1},{1,0},{2,3},{3,2},{4,5},{5,4},{6,7},{7,6},{8,9},{9,8},{10,11... | collective-permute-start | bytes 1572872 | tf_op jit(solution)/shard_map/ppermute | solution.py:38
  64.2 12.3 %collective-permute-start.12 = (f32[128,512]{1,0:T(8,128)S(1)}, f32[128,512]{1,0:T(8,128)S(1)}, u32[]{:S(2)}, u32[]{:S(2)}) collective-permute-start(f32[128,512]{1,0:T(8,128)S(1)} %get-tuple-element.45), channel_id=1, source_target_pairs={{0,2},{1,3},{2,4},{3,5},{4,6},{5,7},{6,0},{7,1},{8,10},{9,11},{10,... | collective-permute-start | bytes 786440 | tf_op jit(solution)/shard_map/ppermute | solution.py:47
  65.7 14.1 %collective-permute-start.13 = (f32[128,512]{1,0:T(8,128)S(1)}, f32[128,512]{1,0:T(8,128)S(1)}, u32[]{:S(2)}, u32[]{:S(2)}) collective-permute-start(f32[128,512]{1,0:T(8,128)S(1)} %get-tuple-element.46), channel_id=1, source_target_pairs={{0,4},{1,5},{2,6},{3,7},{4,0},{5,1},{6,2},{7,3},{8,12},{9,13},{10,... | collective-permute-start | bytes 786440 | tf_op jit(solution)/shard_map/ppermute | solution.py:47
  68.1 11.7 %collective-permute-start.14 = (f32[128,512]{1,0:T(8,128)S(1)}, f32[128,512]{1,0:T(8,128)S(1)}, u32[]{:S(2)}, u32[]{:S(2)}) collective-permute-start(f32[128,512]{1,0:T(8,128)S(1)} %get-tuple-element.47), channel_id=1, source_target_pairs={{0,6},{1,7},{2,0},{3,1},{4,2},{5,3},{6,4},{7,5},{8,14},{9,15},{10,... | collective-permute-start | bytes 786440 | tf_op jit(solution)/shard_map/ppermute | solution.py:47
  79.9 12.1 %collective-permute-start.17 = (f32[216,512]{1,0:T(8,128)S(1)}, f32[216,512]{1,0:T(8,128)S(1)}, u32[]{:S(2)}, u32[]{:S(2)}) collective-permute-start(f32[216,512]{1,0:T(8,128)S(1)} %message.1.mine_ref), channel_id=1, source_target_pairs={{0,8},{1,9},{2,10},{3,11},{4,12},{5,13},{6,14},{7,15},{8,0},{9,1},... | collective-permute-start | bytes 1327112 | tf_op jit(solution)/shard_map/ppermute | solution.py:42
  92.9 8.8 %collective-permute-start.21 = (f32[64,512]{1,0:T(8,128)S(1)}, f32[64,512]{1,0:T(8,128)S(1)}, u32[]{:S(2)}, u32[]{:S(2)}) collective-permute-start(f32[64,512]{1,0:T(8,128)S(1)} %get-tuple-element.50), channel_id=1, source_target_pairs={{0,16},{16,32},{32,48},{48,64},{64,80},{80,96},{96,112},{112,128},... | collective-permute-start | bytes 393224 | tf_op jit(solution)/shard_map/ppermute | solution.py:34
  93.0 8.7 %collective-permute-start.22 = (f32[64,512]{1,0:T(8,128)S(1)}, f32[64,512]{1,0:T(8,128)S(1)}, u32[]{:S(2)}, u32[]{:S(2)}) collective-permute-start(f32[64,512]{1,0:T(8,128)S(1)} %get-tuple-element.51), channel_id=1, source_target_pairs={{0,240},{16,0},{32,16},{48,32},{64,48},{80,64},{96,80},{112,96},{1... | collective-permute-start | bytes 393224 | tf_op jit(solution)/shard_map/ppermute | solution.py:34
  97.1 12.1 %collective-permute-start.18 = (f32[192,512]{1,0:T(8,128)S(1)}, f32[192,512]{1,0:T(8,128)S(1)}, u32[]{:S(2)}, u32[]{:S(2)}) collective-permute-start(f32[192,512]{1,0:T(8,128)S(1)} %get-tuple-element.49.refs_0_), channel_id=1, source_target_pairs={{0,2},{1,3},{2,4},{3,5},{4,6},{5,7},{6,0},{7,1},{8,10},{9,11},{10,... | collective-permute-start | bytes 1179656 | tf_op jit(solution)/shard_map/ppermute | solution.py:47
  98.1 19.6 %collective-permute-start.19 = (f32[192,512]{1,0:T(8,128)S(1)}, f32[192,512]{1,0:T(8,128)S(1)}, u32[]{:S(2)}, u32[]{:S(2)}) collective-permute-start(f32[192,512]{1,0:T(8,128)S(1)} %get-tuple-element.49.refs_0_), channel_id=1, source_target_pairs={{0,4},{1,5},{2,6},{3,7},{4,0},{5,1},{6,2},{7,3},{8,12},{9,13},{10,... | collective-permute-start | bytes 1179656 | tf_op jit(solution)/shard_map/ppermute | solution.py:47
  101.7 16.4 %collective-permute-start.20 = (f32[192,512]{1,0:T(8,128)S(1)}, f32[192,512]{1,0:T(8,128)S(1)}, u32[]{:S(2)}, u32[]{:S(2)}) collective-permute-start(f32[192,512]{1,0:T(8,128)S(1)} %get-tuple-element.49.refs_0_), channel_id=1, source_target_pairs={{0,6},{1,7},{2,0},{3,1},{4,2},{5,3},{6,4},{7,5},{8,14},{9,15},{10,... | collective-permute-start | bytes 1179656 | tf_op jit(solution)/shard_map/ppermute | solution.py:47
  101.8 25.2 %copy-start.4 = (f32[1024,512]{1,0:T(8,128)S(1)}, f32[1024,512]{1,0:T(8,128)}, u32[]{:S(2)}) copy-start(f32[1024,512]{1,0:T(8,128)} %refs_2_.1) | copy-start | bytes 6291460
  101.8 7.4 %collective-permute-start.23 = (f32[128,512]{1,0:T(8,128)S(1)}, f32[128,512]{1,0:T(8,128)S(1)}, u32[]{:S(2)}, u32[]{:S(2)}) collective-permute-start(f32[128,512]{1,0:T(8,128)S(1)} %get-tuple-element.55), channel_id=1, source_target_pairs={{0,16},{16,32},{32,48},{48,64},{64,80},{80,96},{96,112},{112,128},... | collective-permute-start | bytes 786440 | tf_op jit(solution)/shard_map/ppermute | solution.py:34
  101.9 7.3 %collective-permute-start.24 = (f32[128,512]{1,0:T(8,128)S(1)}, f32[128,512]{1,0:T(8,128)S(1)}, u32[]{:S(2)}, u32[]{:S(2)}) collective-permute-start(f32[128,512]{1,0:T(8,128)S(1)} %get-tuple-element.55), channel_id=1, source_target_pairs={{0,240},{16,0},{32,16},{48,32},{64,48},{80,64},{96,80},{112,96},{1... | collective-permute-start | bytes 786440 | tf_op jit(solution)/shard_map/ppermute | solution.py:34
  118.2 8.8 %collective-permute-start.25 = (f32[4,192,512]{2,1,0:T(8,128)S(1)}, f32[4,192,512]{2,1,0:T(8,128)S(1)}, u32[]{:S(2)}, u32[]{:S(2)}) collective-permute-start(f32[4,192,512]{2,1,0:T(8,128)S(1)} %pack.2.mine_ref), channel_id=1, source_target_pairs={{0,1},{1,0},{2,3},{3,2},{4,5},{5,4},{6,7},{7,6},{8,9},{9,8},{10,11... | collective-permute-start | bytes 4718600 | tf_op jit(solution)/shard_map/ppermute | solution.py:38
  120.4 21.2 %collective-permute-start.29 = (f32[384,512]{1,0:T(8,128)S(1)}, f32[384,512]{1,0:T(8,128)S(1)}, u32[]{:S(2)}, u32[]{:S(2)}) collective-permute-start(f32[384,512]{1,0:T(8,128)S(1)} %get-tuple-element.59), channel_id=1, source_target_pairs={{0,16},{16,32},{32,48},{48,64},{64,80},{80,96},{96,112},{112,128},... | collective-permute-start | bytes 2359304 | tf_op jit(solution)/shard_map/ppermute | solution.py:34
  120.4 21.2 %collective-permute-start.30 = (f32[384,512]{1,0:T(8,128)S(1)}, f32[384,512]{1,0:T(8,128)S(1)}, u32[]{:S(2)}, u32[]{:S(2)}) collective-permute-start(f32[384,512]{1,0:T(8,128)S(1)} %get-tuple-element.59), channel_id=1, source_target_pairs={{0,240},{16,0},{32,16},{48,32},{64,48},{80,64},{96,80},{112,96},{1... | collective-permute-start | bytes 2359304 | tf_op jit(solution)/shard_map/ppermute | solution.py:34
  124.0 12.1 %collective-permute-start.26 = (f32[128,512]{1,0:T(8,128)S(1)}, f32[128,512]{1,0:T(8,128)S(1)}, u32[]{:S(2)}, u32[]{:S(2)}) collective-permute-start(f32[128,512]{1,0:T(8,128)S(1)} %get-tuple-element.54.refs_4_.refs_0_), channel_id=1, source_target_pairs={{0,2},{1,3},{2,4},{3,5},{4,6},{5,7},{6,0},{7,1},{8,10},{9,11},{10,... | collective-permute-start | bytes 786440 | tf_op jit(solution)/shard_map/ppermute | solution.py:47
  124.0 14.3 %collective-permute-start.27 = (f32[128,512]{1,0:T(8,128)S(1)}, f32[128,512]{1,0:T(8,128)S(1)}, u32[]{:S(2)}, u32[]{:S(2)}) collective-permute-start(f32[128,512]{1,0:T(8,128)S(1)} %get-tuple-element.54.refs_4_.refs_0_), channel_id=1, source_target_pairs={{0,4},{1,5},{2,6},{3,7},{4,0},{5,1},{6,2},{7,3},{8,12},{9,13},{10,... | collective-permute-start | bytes 786440 | tf_op jit(solution)/shard_map/ppermute | solution.py:47
  127.0 11.6 %collective-permute-start.28 = (f32[128,512]{1,0:T(8,128)S(1)}, f32[128,512]{1,0:T(8,128)S(1)}, u32[]{:S(2)}, u32[]{:S(2)}) collective-permute-start(f32[128,512]{1,0:T(8,128)S(1)} %get-tuple-element.54.refs_4_.refs_0_), channel_id=1, source_target_pairs={{0,6},{1,7},{2,0},{3,1},{4,2},{5,3},{6,4},{7,5},{8,14},{9,15},{10,... | collective-permute-start | bytes 786440 | tf_op jit(solution)/shard_map/ppermute | solution.py:47
  141.6 1.6 %copy-start.5 = (f32[1024,512]{1,0:T(8,128)S(1)}, f32[1024,512]{1,0:T(8,128)}, u32[]{:S(2)}) copy-start(f32[1024,512]{1,0:T(8,128)} %finish_a.1.refs_4_) | copy-start | bytes 6291460
  143.3 4.4 %collective-permute-start.31 = (f32[4,128,512]{2,1,0:T(8,128)S(1)}, f32[4,128,512]{2,1,0:T(8,128)S(1)}, u32[]{:S(2)}, u32[]{:S(2)}) collective-permute-start(f32[4,128,512]{2,1,0:T(8,128)S(1)} %pack.3.refs_0_.mine_ref), channel_id=1, source_target_pairs={{0,1},{1,0},{2,3},{3,2},{4,5},{5,4},{6,7},{7,6},{8,9},{9,8},{10,11... | collective-permute-start | bytes 3145736 | tf_op jit(solution)/shard_map/ppermute | solution.py:38

commit v5 on v4

--- a/solution.py
+++ b/solution.py
@@ -17,7 +17,7 @@
 smem_spec = pl.BlockSpec(memory_space=pltpu.SMEM)
 vmem_spec = pl.BlockSpec(memory_space=pltpu.VMEM)
 cheap = pl.CostEstimate(flops=1, transcendentals=0, bytes_accessed=1)
-top_rows, mid_rows = 512, 128
+top_rows, mid_rows = 640, 128
 
 
 def call(kernel, mib=8, **rest):
@@ -421,10 +421,11 @@
 
 def finish_a_kernel(at_ref, mine_ref, other_ref, *refs):
     facts, (a_ref, *b_refs) = refs[:3], refs[3:7]
-    out_ref, corr_ref, pen_ref, vec_ref = refs[-4:]
+    out_ref, ready_ref, corr_ref, pen_ref, vec_ref = refs[-5:]
 
     @pl.when(pl.program_id(0) == 0)
     def _():
+        ready_ref[...] = jnp.zeros_like(ready_ref)
         kinds = (0, 1, 2)
         cross = build(at_ref, mine_ref, other_ref, kinds, 0, corr_ref, pen_ref, True)
         left = jnp.concatenate([thrice(ref[...]) for ref in facts], axis=1)
@@ -451,8 +452,8 @@
         mib=40,
         grid=(rows // tile,),
         in_specs=[smem_spec, slots, slots] + [whole] * 3 + [spec] * 4,
-        out_specs=spec,
-        out_shape=shape(rows, width),
+        out_specs=[spec, whole],
+        out_shape=[shape(rows, width), shape(8, width)],
         scratch_shapes=scratch_for(3, width),
         name="finish_a",
     )(at, mine, other, *facts, a, b, prev_b, next_b)
@@ -569,8 +570,8 @@
     end_slots = [ends] + [to_x(ends, shift) for shift in (1, 2, 3)]
     mine = pack(trio_slots, [ends, prev_mid, next_mid])
     other = to_core(mine)
-    grad_a = finish_a(at, mine, other, facts, view_a, view_b, prev_raw, next_raw)
-    ends = pack(end_slots, [grad_a, prev_low, next_low])
+    grad_a, ready = finish_a(at, mine, other, facts, view_a, view_b, prev_raw, next_raw)
+    ends = pack(end_slots, [ready, prev_low, next_low])
     part_b, sums = own_b(at, mine, other, facts[0], view_a, [ends])
     halos = [prev_top, prev_mid, prev_low, next_top, next_mid, next_low]
     grad_b = finish_b(at, ends, to_core(ends), facts, sums, part_b, view_b, halos)

time: 156 us -> 153 us (0.981)
  waiting for transfers between devices: 59.8 us -> 56.4 us
  starting transfers between devices: 54.6 us -> 56.6 us
  local copies, waits for them, and re-layouts: 6.37 us -> 4.78 us
    ppermute x15, waiting for transfers between devices: 22.6 us -> 16.6 us  [to_x(): return lax.ppermute(block, 'row', pairs)]
    ppermute x10, waiting for transfers between devices: 23.3 us -> 25.9 us  [across(): lax.ppermute(block, 'grp', [(i, (i + shift) % count) for i in range(count)])]
    ppermute x15, starting transfers between devices: 21.1 us -> 22.8 us  [to_x(): return lax.ppermute(block, 'row', pairs)]
    unnamed x12 -> x10, local copies, waits for them, and re-layouts: 6.37 us -> 4.78 us
  transfers between devices with their start and end apart: 32 -> 32, of which waited for: 18 -> 16; matrix products, arithmetic and copies ran while one was open for 0% -> 0% of each run, Pallas kernels for 16% -> 16%
where the time goes in v5:
time: 153 us; the launch traced here: 152 us
  starting transfers between devices  56.6 us (37%)
  waiting for transfers between devices  56.4 us (37%)
  Pallas kernels  33.6 us (22%)
  local copies, waits for them, and re-layouts  4.78 us (3%)
    ppermute x10, waiting for transfers between devices, across(): lax.ppermute(block, 'grp', [(i, (i + shift) % count) for i in range(count)])  25.9 us
    ppermute x15, starting transfers between devices, to_x(): return lax.ppermute(block, 'row', pairs)  22.8 us
    ppermute x10, starting transfers between devices, across(): lax.ppermute(block, 'grp', [(i, (i + shift) % count) for i in range(count)])  22.1 us
    ppermute x15, waiting for transfers between devices, to_x(): return lax.ppermute(block, 'row', pairs)  16.6 us
    ppermute x1, waiting for transfers between devices, to_y(): return lax.ppermute(block, 'row', [(i, i ^ 8) for i in range(16)])  9.32 us
    pallas_call x1, Pallas kernels, finish_a(): call(finish_a_kernel, mib=40, grid=(rows // tile,), in_specs=[smem_spec,...  9.11 us
    ppermute x6, starting transfers between devices, to_core(): return lax.ppermute(block, 'row', [(i, i ^ 1) for i in range(16)])  8.99 us
    pallas_call x1, Pallas kernels, finish_b(): call(functools.partial(finish_b_kernel, bounds), mib=24, grid=(rows // ti...  7.65 us
  transfers between devices with their start and end apart: 32, of which 16 were waited for; matrix products, arithmetic and copies ran while one was open for 0% of the time, Pallas kernels for 16%

profile of v5, /device:TPU:1, one launch (start us, length us, event | category | flops | bytes accessed | tf_op | source)
XLA Modules:
  0.0 152.3 jit_solution(5577947516789505036)
XLA Ops:
  0.6 2.5 %collective-permute-start.8 = (f32[1024,512]{1,0:T(8,128)}, f32[1024,512]{1,0:T(8,128)}, u32[]{:S(2)}, u32[]{:S(2)}) collective-permute-start(f32[1024,512]{1,0:T(8,128)} %refs_2_.1), channel_id=1, source_target_pairs={{0,16},{16,32},{32,48},{48,64},{64,80},{80,96},{96,112},{112,128},... | collective-permute-start | bytes 6291464 | tf_op jit(solution)/shard_map/ppermute | solution.py:34
  3.2 5.0 %collective-permute-start.9 = (f32[1024,512]{1,0:T(8,128)}, f32[1024,512]{1,0:T(8,128)}, u32[]{:S(2)}, u32[]{:S(2)}) collective-permute-start(f32[1024,512]{1,0:T(8,128)} %refs_2_.1), channel_id=1, source_target_pairs={{0,240},{16,0},{32,16},{48,32},{64,48},{80,64},{96,80},{112,96},{1... | collective-permute-start | bytes 6291464 | tf_op jit(solution)/shard_map/ppermute | solution.py:34
  8.2 1.6 %copy-done = f32[1024,512]{1,0:T(8,128)S(1)} copy-done((f32[1024,512]{1,0:T(8,128)S(1)}, f32[1024,512]{1,0:T(8,128)}, u32[]{:S(2)}) %copy-start) | copy-done | bytes 2097176
  9.8 1.6 %copy-done.2 = f32[1024,512]{1,0:T(8,128)S(1)} copy-done((f32[1024,512]{1,0:T(8,128)S(1)}, f32[1024,512]{1,0:T(8,128)}, u32[]{:S(2)}) %copy-start.2) | copy-done | bytes 2097176
  12.0 1.0 collective-permute-start
  13.1 0.8 collective-permute-done
  13.9 1.2 collective-permute-start.1
  15.1 2.5 %collective-permute-start.2 = (f32[8,512]{1,0:T(8,128)S(1)}, f32[8,512]{1,0:T(8,128)S(1)}, u32[]{:S(2)}, u32[]{:S(2)}) collective-permute-start(f32[8,512]{1,0:T(8,128)S(1)} %add.3.refs_0_), channel_id=1, source_target_pairs={{0,4},{1,5},{2,6},{3,7},{4,0},{5,1},{6,2},{7,3},{8,12},{9,13},{10,... | collective-permute-start | bytes 49160 | tf_op jit(solution)/shard_map/ppermute | solution.py:47
  17.6 1.2 collective-permute-start.3
  18.8 0.8 collective-permute-done.2.refs_2_
  19.6 0.9 collective-permute-done.3.refs_3_
  20.6 1.6 %copy-done.3 = f32[1024,512]{1,0:T(8,128)S(1)} copy-done((f32[1024,512]{1,0:T(8,128)S(1)}, f32[1024,512]{1,0:T(8,128)}, u32[]{:S(2)}) %copy-start.3) | copy-done | bytes 2097176
  22.2 5.4 %own_corr.1 = (f32[640,512]{1,0:T(8,128)S(1)}, f32[128,512]{1,0:T(8,128)S(1)}, f32[256,512]{1,0:T(8,128)S(1)}, f32[8,512]{1,0:T(8,128)S(1)}, f32[4,64,512]{2,1,0:T(8,128)S(1)}, /*index=5*/f32[4,64,512]{2,1,0:T(8,128)S(1)}) custom-call(s32[2]{0:T(128)S(1)} %pad_add_fusion.at_ref, f32[1024,512]{1,0:T(8,128)S(1)} %copy-done.1, f32[1024,512]{1,0:T(8,128)S(1)} %copy-done.3, ...), custom_call_target="tpu_custom_call" | custom-call | flops 1 | bytes 1 | tf_op jit(solution)/shard_map/own_corr/pallas_call | solution.py:159
  27.6 1.7 %collective-permute-start.4 = (f32[4,64,512]{2,1,0:T(8,128)S(1)}, f32[4,64,512]{2,1,0:T(8,128)S(1)}, u32[]{:S(2)}, u32[]{:S(2)}) collective-permute-start(f32[4,64,512]{2,1,0:T(8,128)S(1)} %get-tuple-element.35), channel_id=1, source_target_pairs={{0,1},{1,0},{2,3},{3,2},{4,5},{5,4},{6,7},{7,6},{8,9},{9,8},{10,11... | collective-permute-start | bytes 1572872 | tf_op jit(solution)/shard_map/ppermute | solution.py:38
  29.3 1.5 %collective-permute-done.4.refs_0_ = f32[4,64,512]{2,1,0:T(8,128)S(1)} collective-permute-done((f32[4,64,512]{2,1,0:T(8,128)S(1)}, f32[4,64,512]{2,1,0:T(8,128)S(1)}, u32[]{:S(2)}, u32[]{:S(2)}) %collective-permute-start.4) | collective-permute-done | bytes 524320 | tf_op jit(solution)/shard_map/ppermute | solution.py:38
  31.0 3.5 %collective-permute-start.6 = (f32[64,512]{1,0:T(8,128)S(1)}, f32[64,512]{1,0:T(8,128)S(1)}, u32[]{:S(2)}, u32[]{:S(2)}) collective-permute-start(f32[64,512]{1,0:T(8,128)S(1)} %get-tuple-element.38), channel_id=1, source_target_pairs={{0,4},{1,5},{2,6},{3,7},{4,0},{5,1},{6,2},{7,3},{8,12},{9,13},{10,... | collective-permute-start | bytes 393224 | tf_op jit(solution)/shard_map/ppermute | solution.py:47
  34.6 2.5 %collective-permute-done.5.refs_1_ = f32[64,512]{1,0:T(8,128)S(1)} collective-permute-done((f32[64,512]{1,0:T(8,128)S(1)}, f32[64,512]{1,0:T(8,128)S(1)}, u32[]{:S(2)}, u32[]{:S(2)}) %collective-permute-start.5) | collective-permute-done | bytes 131104 | tf_op jit(solution)/shard_map/ppermute | solution.py:47
  37.0 3.7 %collective-permute-done.6.refs_2_ = f32[64,512]{1,0:T(8,128)S(1)} collective-permute-done((f32[64,512]{1,0:T(8,128)S(1)}, f32[64,512]{1,0:T(8,128)S(1)}, u32[]{:S(2)}, u32[]{:S(2)}) %collective-permute-start.6) | collective-permute-done | bytes 131104 | tf_op jit(solution)/shard_map/ppermute | solution.py:47
  40.9 3.6 %collective-permute-start.16 = (f32[648,512]{1,0:T(8,128)S(1)}, f32[648,512]{1,0:T(8,128)S(1)}, u32[]{:S(2)}, u32[]{:S(2)}) collective-permute-start(f32[648,512]{1,0:T(8,128)S(1)} %get-tuple-element.50), channel_id=1, source_target_pairs={{0,240},{16,0},{32,16},{48,32},{64,48},{80,64},{96,80},{112,96},{1... | collective-permute-start | bytes 3981320 | tf_op jit(solution)/shard_map/ppermute | solution.py:34
  44.5 9.3 %collective-permute-done.8.prev_ref.refs_5_ = f32[1024,512]{1,0:T(8,128)} collective-permute-done((f32[1024,512]{1,0:T(8,128)}, f32[1024,512]{1,0:T(8,128)}, u32[]{:S(2)}, u32[]{:S(2)}) %collective-permute-start.8) | collective-permute-done | bytes 2097184 | tf_op jit(solution)/shard_map/ppermute | solution.py:34
  53.8 5.9 %side_corr.1 = (f32[4,128,512]{2,1,0:T(8,128)S(1)}, f32[2,128,512]{2,1,0:T(8,128)S(1)}, f32[2,128,512]{2,1,0:T(8,128)S(1)}) custom-call(s32[2]{0:T(128)S(1)} %pad_add_fusion.at_ref, f32[1024,512]{1,0:T(8,128)S(1)} %copy-done.1, f32[1024,512]{1,0:T(8,128)} %collective-permute-done.8.prev_ref.refs_5_, f32[1024,512]{1,0:T(8,128)} %collective-permute-done.9.next_ref.refs_6_, ...), custom_call_target="tpu_custom_call" | custom-call | flops 1 | bytes 1 | tf_op jit(solution)/shard_map/side_corr/pallas_call | solution.py:200
  59.7 2.1 %collective-permute-start.10 = (f32[2,128,512]{2,1,0:T(8,128)S(1)}, f32[2,128,512]{2,1,0:T(8,128)S(1)}, u32[]{:S(2)}, u32[]{:S(2)}) collective-permute-start(f32[2,128,512]{2,1,0:T(8,128)S(1)} %get-tuple-element.44), channel_id=1, source_target_pairs={{0,1},{1,0},{2,3},{3,2},{4,5},{5,4},{6,7},{7,6},{8,9},{9,8},{10,11... | collective-permute-start | bytes 1572872 | tf_op jit(solution)/shard_map/ppermute | solution.py:38
  61.9 1.4 collective-permute-done.10.refs_0_
  64.2 1.5 collective-permute-start.12
  65.7 2.5 %collective-permute-start.13 = (f32[128,512]{1,0:T(8,128)S(1)}, f32[128,512]{1,0:T(8,128)S(1)}, u32[]{:S(2)}, u32[]{:S(2)}) collective-permute-start(f32[128,512]{1,0:T(8,128)S(1)} %get-tuple-element.48), channel_id=1, source_target_pairs={{0,4},{1,5},{2,6},{3,7},{4,0},{5,1},{6,2},{7,3},{8,12},{9,13},{10,... | collective-permute-start | bytes 786440 | tf_op jit(solution)/shard_map/ppermute | solution.py:47
  68.1 1.2 collective-permute-start.14
  69.3 12.8 %collective-permute-done.15.refs_5_.refs_3_ = f32[648,512]{1,0:T(8,128)S(1)} collective-permute-done((f32[648,512]{1,0:T(8,128)S(1)}, f32[648,512]{1,0:T(8,128)S(1)}, u32[]{:S(2)}, u32[]{:S(2)}) %collective-permute-start.15) | collective-permute-done | bytes 1327136 | tf_op jit(solution)/shard_map/ppermute | solution.py:34
  82.2 2.7 %collective-permute-start.17 = (f32[216,512]{1,0:T(8,128)S(1)}, f32[216,512]{1,0:T(8,128)S(1)}, u32[]{:S(2)}, u32[]{:S(2)}) collective-permute-start(f32[216,512]{1,0:T(8,128)S(1)} %message.1.mine_ref), channel_id=1, source_target_pairs={{0,8},{1,9},{2,10},{3,11},{4,12},{5,13},{6,14},{7,15},{8,0},{9,1},... | collective-permute-start | bytes 1327112 | tf_op jit(solution)/shard_map/ppermute | solution.py:42
  84.9 9.3 %collective-permute-done.17.got_ref = f32[216,512]{1,0:T(8,128)S(1)} collective-permute-done((f32[216,512]{1,0:T(8,128)S(1)}, f32[216,512]{1,0:T(8,128)S(1)}, u32[]{:S(2)}, u32[]{:S(2)}) %collective-permute-start.17) | collective-permute-done | bytes 442400 | tf_op jit(solution)/shard_map/ppermute | solution.py:42
  94.3 1.0 merge.1
  95.3 3.6 %collective-permute-start.22 = (f32[64,512]{1,0:T(8,128)S(1)}, f32[64,512]{1,0:T(8,128)S(1)}, u32[]{:S(2)}, u32[]{:S(2)}) collective-permute-start(f32[64,512]{1,0:T(8,128)S(1)} %get-tuple-element.53), channel_id=1, source_target_pairs={{0,240},{16,0},{32,16},{48,32},{64,48},{80,64},{96,80},{112,96},{1... | collective-permute-start | bytes 393224 | tf_op jit(solution)/shard_map/ppermute | solution.py:34
  98.9 1.2 collective-permute-start.18
  100.1 2.5 %collective-permute-start.19 = (f32[192,512]{1,0:T(8,128)S(1)}, f32[192,512]{1,0:T(8,128)S(1)}, u32[]{:S(2)}, u32[]{:S(2)}) collective-permute-start(f32[192,512]{1,0:T(8,128)S(1)} %get-tuple-element.51.refs_0_), channel_id=1, source_target_pairs={{0,4},{1,5},{2,6},{3,7},{4,0},{5,1},{6,2},{7,3},{8,12},{9,13},{10,... | collective-permute-start | bytes 1179656 | tf_op jit(solution)/shard_map/ppermute | solution.py:47
  102.5 1.2 collective-permute-start.20
  103.8 3.6 %collective-permute-start.24 = (f32[128,512]{1,0:T(8,128)S(1)}, f32[128,512]{1,0:T(8,128)S(1)}, u32[]{:S(2)}, u32[]{:S(2)}) collective-permute-start(f32[128,512]{1,0:T(8,128)S(1)} %get-tuple-element.57), channel_id=1, source_target_pairs={{0,240},{16,0},{32,16},{48,32},{64,48},{80,64},{96,80},{112,96},{1... | collective-permute-start | bytes 786440 | tf_op jit(solution)/shard_map/ppermute | solution.py:34
  107.4 3.8 %collective-permute-done.23.refs_5_.refs_4_ = f32[128,512]{1,0:T(8,128)S(1)} collective-permute-done((f32[128,512]{1,0:T(8,128)S(1)}, f32[128,512]{1,0:T(8,128)S(1)}, u32[]{:S(2)}, u32[]{:S(2)}) %collective-permute-start.23) | collective-permute-done | bytes 262176 | tf_op jit(solution)/shard_map/ppermute | solution.py:34
  111.2 6.2 %collective-permute-done.19.refs_2_ = f32[192,512]{1,0:T(8,128)S(1)} collective-permute-done((f32[192,512]{1,0:T(8,128)S(1)}, f32[192,512]{1,0:T(8,128)S(1)}, u32[]{:S(2)}, u32[]{:S(2)}) %collective-permute-start.19) | collective-permute-done | bytes 393248 | tf_op jit(solution)/shard_map/ppermute | solution.py:47
  117.4 1.4 collective-permute-done.20.refs_3_
  118.9 2.3 %collective-permute-start.25 = (f32[4,192,512]{2,1,0:T(8,128)S(1)}, f32[4,192,512]{2,1,0:T(8,128)S(1)}, u32[]{:S(2)}, u32[]{:S(2)}) collective-permute-start(f32[4,192,512]{2,1,0:T(8,128)S(1)} %pack.2.mine_ref), channel_id=1, source_target_pairs={{0,1},{1,0},{2,3},{3,2},{4,5},{5,4},{6,7},{7,6},{8,9},{9,8},{10,11... | collective-permute-start | bytes 4718600 | tf_op jit(solution)/shard_map/ppermute | solution.py:38
  121.2 3.6 %collective-permute-start.30 = (f32[256,512]{1,0:T(8,128)S(1)}, f32[256,512]{1,0:T(8,128)S(1)}, u32[]{:S(2)}, u32[]{:S(2)}) collective-permute-start(f32[256,512]{1,0:T(8,128)S(1)} %get-tuple-element.63), channel_id=1, source_target_pairs={{0,240},{16,0},{32,16},{48,32},{64,48},{80,64},{96,80},{112,96},{1... | collective-permute-start | bytes 1572872 | tf_op jit(solution)/shard_map/ppermute | solution.py:34
  124.8 1.1 collective-permute-start.26
  125.9 2.1 %collective-permute-start.27 = (f32[128,512]{1,0:T(8,128)S(1)}, f32[128,512]{1,0:T(8,128)S(1)}, u32[]{:S(2)}, u32[]{:S(2)}) collective-permute-start(f32[128,512]{1,0:T(8,128)S(1)} %get-tuple-element.56.refs_4_.refs_0_), channel_id=1, source_target_pairs={{0,4},{1,5},{2,6},{3,7},{4,0},{5,1},{6,2},{7,3},{8,12},{9,13},{10,... | collective-permute-start | bytes 786440 | tf_op jit(solution)/shard_map/ppermute | solution.py:47
  128.0 1.3 collective-permute-start.28
  129.3 9.1 %finish_a.1 = (f32[1024,512]{1,0:T(8,128)}, f32[8,512]{1,0:T(8,128)S(1)}) custom-call(s32[2]{0:T(128)S(1)} %pad_add_fusion.at_ref, f32[4,192,512]{2,1,0:T(8,128)S(1)} %pack.2.mine_ref, f32[4,192,512]{2,1,0:T(8,128)S(1)} %collective-permute-done.25.other_ref, f32[8,512]{1,0:T(8,128)S(1)} %get-tuple-element.58.refs_0_.facts_ref.f_ref, ...), custom_call_target="tpu_custom_call" | custom-call | flops 1 | bytes 1 | tf_op jit(solution)/shard_map/finish_a/pallas_call | solution.py:450
  138.4 1.0 collective-permute-done.27.refs_2_
  139.5 1.6 %collective-permute-start.31 = (f32[4,128,512]{2,1,0:T(8,128)S(1)}, f32[4,128,512]{2,1,0:T(8,128)S(1)}, u32[]{:S(2)}, u32[]{:S(2)}) collective-permute-start(f32[4,128,512]{2,1,0:T(8,128)S(1)} %pack.3.refs_0_.mine_ref), channel_id=1, source_target_pairs={{0,1},{1,0},{2,3},{3,2},{4,5},{5,4},{6,7},{7,6},{8,9},{9,8},{10,11... | collective-permute-start | bytes 3145736 | tf_op jit(solution)/shard_map/ppermute | solution.py:38
  141.2 3.4 %own_b.1 = (f32[1024,512]{1,0:T(8,128)S(1)}, f32[8,512]{1,0:T(8,128)S(1)}) custom-call(s32[2]{0:T(128)S(1)} %pad_add_fusion.at_ref, f32[4,192,512]{2,1,0:T(8,128)S(1)} %pack.2.mine_ref, f32[4,192,512]{2,1,0:T(8,128)S(1)} %collective-permute-done.25.other_ref, f32[8,512]{1,0:T(8,128)S(1)} %get-tuple-element.58.refs_0_.facts_ref.f_ref, ...), custom_call_target="tpu_custom_call" | custom-call | flops 1 | bytes 1 | tf_op jit(solution)/shard_map/own_b/pallas_call | solution.py:482
  144.6 7.6 %finish_b.1 = f32[1024,512]{1,0:T(8,128)} custom-call(s32[2]{0:T(128)S(1)} %pad_add_fusion.at_ref, f32[4,128,512]{2,1,0:T(8,128)S(1)} %pack.3.refs_0_.mine_ref, f32[4,128,512]{2,1,0:T(8,128)S(1)} %collective-permute-done.31.other_ref, f32[8,512]{1,0:T(8,128)S(1)} %get-tuple-element.58.refs_0_.facts_ref.f_ref, f32[8,512]{1,0:T(8,128)S(1)} %get-tuple-element.59.refs_1_.pf_ref, ...), custom_call_target="tpu_custom_call" | custom-call | flops 1 | bytes 1 | tf_op jit(solution)/shard_map/finish_b/pallas_call | solution.py:526
  (42 shorter events, 2.5 us)
Async XLA Ops:
  0.6 53.2 %collective-permute-start.8 = (f32[1024,512]{1,0:T(8,128)}, f32[1024,512]{1,0:T(8,128)}, u32[]{:S(2)}, u32[]{:S(2)}) collective-permute-start(f32[1024,512]{1,0:T(8,128)} %refs_2_.1), channel_id=1, source_target_pairs={{0,16},{16,32},{32,48},{48,64},{64,80},{80,96},{96,112},{112,128},... | collective-permute-start | bytes 6291464 | tf_op jit(solution)/shard_map/ppermute | solution.py:34
  3.2 50.6 %collective-permute-start.9 = (f32[1024,512]{1,0:T(8,128)}, f32[1024,512]{1,0:T(8,128)}, u32[]{:S(2)}, u32[]{:S(2)}) collective-permute-start(f32[1024,512]{1,0:T(8,128)} %refs_2_.1), channel_id=1, source_target_pairs={{0,240},{16,0},{32,16},{48,32},{64,48},{80,64},{96,80},{112,96},{1... | collective-permute-start | bytes 6291464 | tf_op jit(solution)/shard_map/ppermute | solution.py:34
  8.2 1.6 %copy-start = (f32[1024,512]{1,0:T(8,128)S(1)}, f32[1024,512]{1,0:T(8,128)}, u32[]{:S(2)}) copy-start(f32[1024,512]{1,0:T(8,128)} %a_ref.7) | copy-start | bytes 6291460
  9.8 1.6 %copy-start.2 = (f32[1024,512]{1,0:T(8,128)S(1)}, f32[1024,512]{1,0:T(8,128)}, u32[]{:S(2)}) copy-start(f32[1024,512]{1,0:T(8,128)} %refs_2_.1) | copy-start | bytes 6291460
  11.4 9.2 %copy-start.1 = (f32[1024,512]{1,0:T(8,128)S(1)}, f32[1024,512]{1,0:T(8,128)}, u32[]{:S(2)}) copy-start(f32[1024,512]{1,0:T(8,128)} %a_ref.7) | copy-start | bytes 6291460
  12.0 1.9 %collective-permute-start = (f32[8,512]{1,0:T(8,128)S(1)}, f32[8,512]{1,0:T(8,128)S(1)}, u32[]{:S(2)}, u32[]{:S(2)}) collective-permute-start(f32[8,512]{1,0:T(8,128)S(1)} %sums.1), channel_id=1, source_target_pairs={{0,1},{1,0},{2,3},{3,2},{4,5},{5,4},{6,7},{7,6},{8,9},{9,8},{10,11... | collective-permute-start | bytes 49160 | tf_op jit(solution)/shard_map/ppermute | solution.py:38
  13.9 4.9 %collective-permute-start.1 = (f32[8,512]{1,0:T(8,128)S(1)}, f32[8,512]{1,0:T(8,128)S(1)}, u32[]{:S(2)}, u32[]{:S(2)}) collective-permute-start(f32[8,512]{1,0:T(8,128)S(1)} %add.3.refs_0_), channel_id=1, source_target_pairs={{0,2},{1,3},{2,4},{3,5},{4,6},{5,7},{6,0},{7,1},{8,10},{9,11},{10,... | collective-permute-start | bytes 49160 | tf_op jit(solution)/shard_map/ppermute | solution.py:47
  15.1 4.5 %collective-permute-start.2 = (f32[8,512]{1,0:T(8,128)S(1)}, f32[8,512]{1,0:T(8,128)S(1)}, u32[]{:S(2)}, u32[]{:S(2)}) collective-permute-start(f32[8,512]{1,0:T(8,128)S(1)} %add.3.refs_0_), channel_id=1, source_target_pairs={{0,4},{1,5},{2,6},{3,7},{4,0},{5,1},{6,2},{7,3},{8,12},{9,13},{10,... | collective-permute-start | bytes 49160 | tf_op jit(solution)/shard_map/ppermute | solution.py:47
  17.6 3.0 %collective-permute-start.3 = (f32[8,512]{1,0:T(8,128)S(1)}, f32[8,512]{1,0:T(8,128)S(1)}, u32[]{:S(2)}, u32[]{:S(2)}) collective-permute-start(f32[8,512]{1,0:T(8,128)S(1)} %add.3.refs_0_), channel_id=1, source_target_pairs={{0,6},{1,7},{2,0},{3,1},{4,2},{5,3},{6,4},{7,5},{8,14},{9,15},{10,... | collective-permute-start | bytes 49160 | tf_op jit(solution)/shard_map/ppermute | solution.py:47
  20.6 1.6 %copy-start.3 = (f32[1024,512]{1,0:T(8,128)S(1)}, f32[1024,512]{1,0:T(8,128)}, u32[]{:S(2)}) copy-start(f32[1024,512]{1,0:T(8,128)} %refs_2_.1) | copy-start | bytes 6291460
  27.6 3.3 %collective-permute-start.4 = (f32[4,64,512]{2,1,0:T(8,128)S(1)}, f32[4,64,512]{2,1,0:T(8,128)S(1)}, u32[]{:S(2)}, u32[]{:S(2)}) collective-permute-start(f32[4,64,512]{2,1,0:T(8,128)S(1)} %get-tuple-element.35), channel_id=1, source_target_pairs={{0,1},{1,0},{2,3},{3,2},{4,5},{5,4},{6,7},{7,6},{8,9},{9,8},{10,11... | collective-permute-start | bytes 1572872 | tf_op jit(solution)/shard_map/ppermute | solution.py:38
  30.9 6.1 %collective-permute-start.5 = (f32[64,512]{1,0:T(8,128)S(1)}, f32[64,512]{1,0:T(8,128)S(1)}, u32[]{:S(2)}, u32[]{:S(2)}) collective-permute-start(f32[64,512]{1,0:T(8,128)S(1)} %get-tuple-element.37), channel_id=1, source_target_pairs={{0,2},{1,3},{2,4},{3,5},{4,6},{5,7},{6,0},{7,1},{8,10},{9,11},{10,... | collective-permute-start | bytes 393224 | tf_op jit(solution)/shard_map/ppermute | solution.py:47
  31.0 9.7 %collective-permute-start.6 = (f32[64,512]{1,0:T(8,128)S(1)}, f32[64,512]{1,0:T(8,128)S(1)}, u32[]{:S(2)}, u32[]{:S(2)}) collective-permute-start(f32[64,512]{1,0:T(8,128)S(1)} %get-tuple-element.38), channel_id=1, source_target_pairs={{0,4},{1,5},{2,6},{3,7},{4,0},{5,1},{6,2},{7,3},{8,12},{9,13},{10,... | collective-permute-start | bytes 393224 | tf_op jit(solution)/shard_map/ppermute | solution.py:47
  34.6 6.2 %collective-permute-start.7 = (f32[64,512]{1,0:T(8,128)S(1)}, f32[64,512]{1,0:T(8,128)S(1)}, u32[]{:S(2)}, u32[]{:S(2)}) collective-permute-start(f32[64,512]{1,0:T(8,128)S(1)} %get-tuple-element.39), channel_id=1, source_target_pairs={{0,6},{1,7},{2,0},{3,1},{4,2},{5,3},{6,4},{7,5},{8,14},{9,15},{10,... | collective-permute-start | bytes 393224 | tf_op jit(solution)/shard_map/ppermute | solution.py:47
  40.8 41.3 %collective-permute-start.15 = (f32[648,512]{1,0:T(8,128)S(1)}, f32[648,512]{1,0:T(8,128)S(1)}, u32[]{:S(2)}, u32[]{:S(2)}) collective-permute-start(f32[648,512]{1,0:T(8,128)S(1)} %get-tuple-element.50), channel_id=1, source_target_pairs={{0,16},{16,32},{32,48},{48,64},{64,80},{80,96},{96,112},{112,128},... | collective-permute-start | bytes 3981320 | tf_op jit(solution)/shard_map/ppermute | solution.py:34
  40.9 41.2 %collective-permute-start.16 = (f32[648,512]{1,0:T(8,128)S(1)}, f32[648,512]{1,0:T(8,128)S(1)}, u32[]{:S(2)}, u32[]{:S(2)}) collective-permute-start(f32[648,512]{1,0:T(8,128)S(1)} %get-tuple-element.50), channel_id=1, source_target_pairs={{0,240},{16,0},{32,16},{48,32},{64,48},{80,64},{96,80},{112,96},{1... | collective-permute-start | bytes 3981320 | tf_op jit(solution)/shard_map/ppermute | solution.py:34
  59.7 3.7 %collective-permute-start.10 = (f32[2,128,512]{2,1,0:T(8,128)S(1)}, f32[2,128,512]{2,1,0:T(8,128)S(1)}, u32[]{:S(2)}, u32[]{:S(2)}) collective-permute-start(f32[2,128,512]{2,1,0:T(8,128)S(1)} %get-tuple-element.44), channel_id=1, source_target_pairs={{0,1},{1,0},{2,3},{3,2},{4,5},{5,4},{6,7},{7,6},{8,9},{9,8},{10,11... | collective-permute-start | bytes 1572872 | tf_op jit(solution)/shard_map/ppermute | solution.py:38
  61.8 2.3 %collective-permute-start.11 = (f32[2,128,512]{2,1,0:T(8,128)S(1)}, f32[2,128,512]{2,1,0:T(8,128)S(1)}, u32[]{:S(2)}, u32[]{:S(2)}) collective-permute-start(f32[2,128,512]{2,1,0:T(8,128)S(1)} %get-tuple-element.45), channel_id=1, source_target_pairs={{0,1},{1,0},{2,3},{3,2},{4,5},{5,4},{6,7},{7,6},{8,9},{9,8},{10,11... | collective-permute-start | bytes 1572872 | tf_op jit(solution)/shard_map/ppermute | solution.py:38
  64.2 17.9 %collective-permute-start.12 = (f32[128,512]{1,0:T(8,128)S(1)}, f32[128,512]{1,0:T(8,128)S(1)}, u32[]{:S(2)}, u32[]{:S(2)}) collective-permute-start(f32[128,512]{1,0:T(8,128)S(1)} %get-tuple-element.47), channel_id=1, source_target_pairs={{0,2},{1,3},{2,4},{3,5},{4,6},{5,7},{6,0},{7,1},{8,10},{9,11},{10,... | collective-permute-start | bytes 786440 | tf_op jit(solution)/shard_map/ppermute | solution.py:47
  65.7 16.4 %collective-permute-start.13 = (f32[128,512]{1,0:T(8,128)S(1)}, f32[128,512]{1,0:T(8,128)S(1)}, u32[]{:S(2)}, u32[]{:S(2)}) collective-permute-start(f32[128,512]{1,0:T(8,128)S(1)} %get-tuple-element.48), channel_id=1, source_target_pairs={{0,4},{1,5},{2,6},{3,7},{4,0},{5,1},{6,2},{7,3},{8,12},{9,13},{10,... | collective-permute-start | bytes 786440 | tf_op jit(solution)/shard_map/ppermute | solution.py:47
  68.1 14.0 %collective-permute-start.14 = (f32[128,512]{1,0:T(8,128)S(1)}, f32[128,512]{1,0:T(8,128)S(1)}, u32[]{:S(2)}, u32[]{:S(2)}) collective-permute-start(f32[128,512]{1,0:T(8,128)S(1)} %get-tuple-element.49), channel_id=1, source_target_pairs={{0,6},{1,7},{2,0},{3,1},{4,2},{5,3},{6,4},{7,5},{8,14},{9,15},{10,... | collective-permute-start | bytes 786440 | tf_op jit(solution)/shard_map/ppermute | solution.py:47
  82.2 12.0 %collective-permute-start.17 = (f32[216,512]{1,0:T(8,128)S(1)}, f32[216,512]{1,0:T(8,128)S(1)}, u32[]{:S(2)}, u32[]{:S(2)}) collective-permute-start(f32[216,512]{1,0:T(8,128)S(1)} %message.1.mine_ref), channel_id=1, source_target_pairs={{0,8},{1,9},{2,10},{3,11},{4,12},{5,13},{6,14},{7,15},{8,0},{9,1},... | collective-permute-start | bytes 1327112 | tf_op jit(solution)/shard_map/ppermute | solution.py:42
  95.2 8.5 %collective-permute-start.21 = (f32[64,512]{1,0:T(8,128)S(1)}, f32[64,512]{1,0:T(8,128)S(1)}, u32[]{:S(2)}, u32[]{:S(2)}) collective-permute-start(f32[64,512]{1,0:T(8,128)S(1)} %get-tuple-element.52), channel_id=1, source_target_pairs={{0,16},{16,32},{32,48},{48,64},{64,80},{80,96},{96,112},{112,128},... | collective-permute-start | bytes 393224 | tf_op jit(solution)/shard_map/ppermute | solution.py:34
  95.3 8.4 %collective-permute-start.22 = (f32[64,512]{1,0:T(8,128)S(1)}, f32[64,512]{1,0:T(8,128)S(1)}, u32[]{:S(2)}, u32[]{:S(2)}) collective-permute-start(f32[64,512]{1,0:T(8,128)S(1)} %get-tuple-element.53), channel_id=1, source_target_pairs={{0,240},{16,0},{32,16},{48,32},{64,48},{80,64},{96,80},{112,96},{1... | collective-permute-start | bytes 393224 | tf_op jit(solution)/shard_map/ppermute | solution.py:34
  98.9 12.3 %collective-permute-start.18 = (f32[192,512]{1,0:T(8,128)S(1)}, f32[192,512]{1,0:T(8,128)S(1)}, u32[]{:S(2)}, u32[]{:S(2)}) collective-permute-start(f32[192,512]{1,0:T(8,128)S(1)} %get-tuple-element.51.refs_0_), channel_id=1, source_target_pairs={{0,2},{1,3},{2,4},{3,5},{4,6},{5,7},{6,0},{7,1},{8,10},{9,11},{10,... | collective-permute-start | bytes 1179656 | tf_op jit(solution)/shard_map/ppermute | solution.py:47
  100.1 17.3 %collective-permute-start.19 = (f32[192,512]{1,0:T(8,128)S(1)}, f32[192,512]{1,0:T(8,128)S(1)}, u32[]{:S(2)}, u32[]{:S(2)}) collective-permute-start(f32[192,512]{1,0:T(8,128)S(1)} %get-tuple-element.51.refs_0_), channel_id=1, source_target_pairs={{0,4},{1,5},{2,6},{3,7},{4,0},{5,1},{6,2},{7,3},{8,12},{9,13},{10,... | collective-permute-start | bytes 1179656 | tf_op jit(solution)/shard_map/ppermute | solution.py:47
  102.5 16.3 %collective-permute-start.20 = (f32[192,512]{1,0:T(8,128)S(1)}, f32[192,512]{1,0:T(8,128)S(1)}, u32[]{:S(2)}, u32[]{:S(2)}) collective-permute-start(f32[192,512]{1,0:T(8,128)S(1)} %get-tuple-element.51.refs_0_), channel_id=1, source_target_pairs={{0,6},{1,7},{2,0},{3,1},{4,2},{5,3},{6,4},{7,5},{8,14},{9,15},{10,... | collective-permute-start | bytes 1179656 | tf_op jit(solution)/shard_map/ppermute | solution.py:47
  103.7 25.6 %copy-start.4 = (f32[1024,512]{1,0:T(8,128)S(1)}, f32[1024,512]{1,0:T(8,128)}, u32[]{:S(2)}) copy-start(f32[1024,512]{1,0:T(8,128)} %refs_2_.1) | copy-start | bytes 6291460
  103.7 7.4 %collective-permute-start.23 = (f32[128,512]{1,0:T(8,128)S(1)}, f32[128,512]{1,0:T(8,128)S(1)}, u32[]{:S(2)}, u32[]{:S(2)}) collective-permute-start(f32[128,512]{1,0:T(8,128)S(1)} %get-tuple-element.57), channel_id=1, source_target_pairs={{0,16},{16,32},{32,48},{48,64},{64,80},{80,96},{96,112},{112,128},... | collective-permute-start | bytes 786440 | tf_op jit(solution)/shard_map/ppermute | solution.py:34
  103.8 7.3 %collective-permute-start.24 = (f32[128,512]{1,0:T(8,128)S(1)}, f32[128,512]{1,0:T(8,128)S(1)}, u32[]{:S(2)}, u32[]{:S(2)}) collective-permute-start(f32[128,512]{1,0:T(8,128)S(1)} %get-tuple-element.57), channel_id=1, source_target_pairs={{0,240},{16,0},{32,16},{48,32},{64,48},{80,64},{96,80},{112,96},{1... | collective-permute-start | bytes 786440 | tf_op jit(solution)/shard_map/ppermute | solution.py:34
  118.9 9.1 %collective-permute-start.25 = (f32[4,192,512]{2,1,0:T(8,128)S(1)}, f32[4,192,512]{2,1,0:T(8,128)S(1)}, u32[]{:S(2)}, u32[]{:S(2)}) collective-permute-start(f32[4,192,512]{2,1,0:T(8,128)S(1)} %pack.2.mine_ref), channel_id=1, source_target_pairs={{0,1},{1,0},{2,3},{3,2},{4,5},{5,4},{6,7},{7,6},{8,9},{9,8},{10,11... | collective-permute-start | bytes 4718600 | tf_op jit(solution)/shard_map/ppermute | solution.py:38
  121.2 18.2 %collective-permute-start.29 = (f32[256,512]{1,0:T(8,128)S(1)}, f32[256,512]{1,0:T(8,128)S(1)}, u32[]{:S(2)}, u32[]{:S(2)}) collective-permute-start(f32[256,512]{1,0:T(8,128)S(1)} %get-tuple-element.63), channel_id=1, source_target_pairs={{0,16},{16,32},{32,48},{48,64},{64,80},{80,96},{96,112},{112,128},... | collective-permute-start | bytes 1572872 | tf_op jit(solution)/shard_map/ppermute | solution.py:34
  121.2 18.2 %collective-permute-start.30 = (f32[256,512]{1,0:T(8,128)S(1)}, f32[256,512]{1,0:T(8,128)S(1)}, u32[]{:S(2)}, u32[]{:S(2)}) collective-permute-start(f32[256,512]{1,0:T(8,128)S(1)} %get-tuple-element.63), channel_id=1, source_target_pairs={{0,240},{16,0},{32,16},{48,32},{64,48},{80,64},{96,80},{112,96},{1... | collective-permute-start | bytes 1572872 | tf_op jit(solution)/shard_map/ppermute | solution.py:34
  124.8 13.6 %collective-permute-start.26 = (f32[128,512]{1,0:T(8,128)S(1)}, f32[128,512]{1,0:T(8,128)S(1)}, u32[]{:S(2)}, u32[]{:S(2)}) collective-permute-start(f32[128,512]{1,0:T(8,128)S(1)} %get-tuple-element.56.refs_4_.refs_0_), channel_id=1, source_target_pairs={{0,2},{1,3},{2,4},{3,5},{4,6},{5,7},{6,0},{7,1},{8,10},{9,11},{10,... | collective-permute-start | bytes 786440 | tf_op jit(solution)/shard_map/ppermute | solution.py:47
  125.9 13.5 %collective-permute-start.27 = (f32[128,512]{1,0:T(8,128)S(1)}, f32[128,512]{1,0:T(8,128)S(1)}, u32[]{:S(2)}, u32[]{:S(2)}) collective-permute-start(f32[128,512]{1,0:T(8,128)S(1)} %get-tuple-element.56.refs_4_.refs_0_), channel_id=1, source_target_pairs={{0,4},{1,5},{2,6},{3,7},{4,0},{5,1},{6,2},{7,3},{8,12},{9,13},{10,... | collective-permute-start | bytes 786440 | tf_op jit(solution)/shard_map/ppermute | solution.py:47
  128.0 11.4 %collective-permute-start.28 = (f32[128,512]{1,0:T(8,128)S(1)}, f32[128,512]{1,0:T(8,128)S(1)}, u32[]{:S(2)}, u32[]{:S(2)}) collective-permute-start(f32[128,512]{1,0:T(8,128)S(1)} %get-tuple-element.56.refs_4_.refs_0_), channel_id=1, source_target_pairs={{0,6},{1,7},{2,0},{3,1},{4,2},{5,3},{6,4},{7,5},{8,14},{9,15},{10,... | collective-permute-start | bytes 786440 | tf_op jit(solution)/shard_map/ppermute | solution.py:47
  139.5 5.1 %collective-permute-start.31 = (f32[4,128,512]{2,1,0:T(8,128)S(1)}, f32[4,128,512]{2,1,0:T(8,128)S(1)}, u32[]{:S(2)}, u32[]{:S(2)}) collective-permute-start(f32[4,128,512]{2,1,0:T(8,128)S(1)} %pack.3.refs_0_.mine_ref), channel_id=1, source_target_pairs={{0,1},{1,0},{2,3},{3,2},{4,5},{5,4},{6,7},{7,6},{8,9},{9,8},{10,11... | collective-permute-start | bytes 3145736 | tf_op jit(solution)/shard_map/ppermute | solution.py:38

commit v6 on v5

--- a/solution.py
+++ b/solution.py
@@ -17,7 +17,7 @@
 smem_spec = pl.BlockSpec(memory_space=pltpu.SMEM)
 vmem_spec = pl.BlockSpec(memory_space=pltpu.VMEM)
 cheap = pl.CostEstimate(flops=1, transcendentals=0, bytes_accessed=1)
-top_rows, mid_rows = 640, 128
+top_rows, mid_rows = 384, 128
 
 
 def call(kernel, mib=8, **rest):
@@ -170,60 +170,56 @@
     )(at, a, b, *parts)
 
 
-def side_corr_kernel(steps, at_ref, a_ref, prev_ref, next_ref, f_ref, *refs):
-    keep_ref, *sends, left_ref, right_ref = refs[-5:]
+def side_corr_kernel(steps, at_ref, a_ref, b_ref, f_ref, *refs):
+    keep_ref, send_ref, acc_ref = refs[-3:]
     step = pl.program_id(0)
 
     @pl.when(step == 0)
     def _():
-        left_ref[...] = jnp.zeros_like(left_ref)
-        right_ref[...] = jnp.zeros_like(right_ref)
+        acc_ref[...] = jnp.zeros_like(acc_ref)
 
     norm_a = (a_ref[...] - f_ref[0:1, :]) * f_ref[1:2, :]
-    for acc_ref, b_ref in ((left_ref, prev_ref), (right_ref, next_ref)):
-        acc_ref[...] += gram(norm_a, b_ref[...])
+    acc_ref[...] += gram(norm_a, b_ref[...])
 
     @pl.when(step == steps - 1)
     def _():
-        rows = keep_ref.shape[1] // 2
-        put_slots(at_ref, left_ref, keep_ref, sends, 0, rows)
-        put_slots(at_ref, right_ref, keep_ref, sends, rows, rows)
-
-
-def side_corr(at, a, prev_b, next_b, facts, wait_for):
+        put_slots(at_ref, acc_ref, keep_ref, [send_ref], 0, keep_ref.shape[1])
+
+
+def side_corr(at, a, b, facts, wait_for):
     rows, width = a.shape
     steps = 4
     spec = pl.BlockSpec((rows // steps, width), lambda i: (i, 0))
     whole = pl.BlockSpec((8, width), lambda i: (0, 0))
-    slots = pl.BlockSpec((4, width // 4, width), lambda i: (0, 0, 0))
-    pair = pl.BlockSpec((2, width // 4, width), lambda i: (0, 0, 0))
+    slots = pl.BlockSpec((4, width // 8, width), lambda i: (0, 0, 0))
     return call(
         functools.partial(side_corr_kernel, steps),
         grid=(steps,),
-        in_specs=[smem_spec, spec, spec, spec, whole] + [any_spec] * len(wait_for),
-        out_specs=[slots, pair, pair],
-        out_shape=[shape(4, width // 4, width)] + [shape(2, width // 4, width)] * 2,
-        scratch_shapes=[pltpu.VMEM((width, width), f32)] * 2,
-        mib=24,
+        in_specs=[smem_spec, spec, spec, whole] + [any_spec] * len(wait_for),
+        out_specs=[slots, slots],
+        out_shape=[shape(4, width // 8, width)] * 2,
+        scratch_shapes=[pltpu.VMEM((width, width), f32)],
+        mib=16,
         name="side_corr",
-    )(at, a, prev_b, next_b, facts, *wait_for)
-
-
-def fan_kernel(keep_ref, *refs):
-    gots, outs = refs[:-4], refs[-4:]
-    each = 4 // len(gots)
-    for slot in range(4):
-        outs[slot][...] = keep_ref[slot] + gots[slot // each][slot % each]
-
-
-def fan(keep, *gots):
-    return call(
-        fan_kernel,
-        in_specs=[vmem_spec] * (1 + len(gots)),
-        out_specs=[vmem_spec] * 4,
-        out_shape=[shape(*keep.shape[1:])] * 4,
+    )(at, a, b, facts, *wait_for)
+
+
+def fan_kernel(count, *refs):
+    keeps, gots, outs = refs[:count], refs[count : 2 * count], refs[2 * count :]
+    for i in range(count):
+        for slot in range(4):
+            outs[4 * i + slot][...] = keeps[i][slot] + gots[i][slot]
+
+
+def fan(keeps, gots):
+    count = len(keeps)
+    return call(
+        functools.partial(fan_kernel, count),
+        in_specs=[vmem_spec] * (2 * count),
+        out_specs=[vmem_spec] * (4 * count),
+        out_shape=[shape(*keep.shape[1:]) for keep in keeps for _ in range(4)],
         name="fan",
-    )(keep, *gots)
+    )(*keeps, *gots)
 
 
 def own_sum_kernel(*refs):
@@ -245,29 +241,37 @@
     )(*parts, top, facts)
 
 
-def message_kernel(own_ref, *refs):
-    side, facts, out_ref = refs[:4], refs[4:7], refs[7]
-    first = own_ref.shape[0]
-    last = first + side[0].shape[0]
-    out_ref[0:first, :] = own_ref[...]
-    out_ref[first:last, :] = side[0][...] + side[1][...] + side[2][...] + side[3][...]
-    for i, ref in enumerate(facts):
-        out_ref[last + 8 * i : last + 8 * i + 8, :] = ref[...]
-
-
-def message(own, side, facts, prev_top, next_top):
-    rows = own.shape[0] + side[0].shape[0] + 24
-    width = own.shape[1]
+def message_kernel(whole, summed, facts, *refs):
+    out_ref = refs[-1]
+    first = 0
+    for ref in refs[:whole]:
+        out_ref[first : first + ref.shape[0], :] = ref[...]
+        first += ref.shape[0]
+    parts = refs[whole : whole + summed]
+    rows = parts[0].shape[0]
+    out_ref[first : first + rows, :] = parts[0][...] + parts[1][...] + parts[2][...] + parts[3][...]
+    first += rows
+    for ref in refs[whole + summed : whole + summed + facts]:
+        out_ref[first : first + 8, :] = ref[...]
+        first += 8
+
+
+def message(whole, summed, facts, halo_tops):
+    rows, width = summed[0].shape
     below = pl.BlockSpec((8, width), lambda i: (top_rows // 8, 0))
-    wholes = [pl.BlockSpec(block.shape, lambda i: (0, 0)) for block in (own, *side, facts)]
-    return call(
-        message_kernel,
+    blocks = [*whole, *summed, *facts]
+    size = rows * (len(whole) + 1) + 8 * (len(facts) + len(halo_tops))
+    return call(
+        functools.partial(
+            message_kernel, len(whole), len(summed), len(facts) + len(halo_tops)
+        ),
         grid=(1,),
-        in_specs=wholes + [below] * 2,
-        out_specs=pl.BlockSpec((rows, width), lambda i: (0, 0)),
-        out_shape=shape(rows, width),
+        in_specs=[pl.BlockSpec(block.shape, lambda i: (0, 0)) for block in blocks]
+        + [below] * len(halo_tops),
+        out_specs=pl.BlockSpec((size, width), lambda i: (0, 0)),
+        out_shape=shape(size, width),
         name="message",
-    )(own, *side, facts, prev_top, next_top)
+    )(*blocks, *halo_tops)
 
 
 def full_facts(mine, other):
@@ -302,47 +306,45 @@
     return cols_ref[pl.ds(first, rows), :]
 
 
-def merge_kernel(half_rows, at_ref, mine_ref, got_ref, *refs):
-    left_ref, right_ref, trio_ref, *facts_refs, cols_ref = refs[-7:]
+def merge_kernel(half_rows, at_ref, first_ref, first_got_ref, second_ref, second_got_ref, *refs):
+    left_ref, right_ref, trio_ref, *facts_refs, cols_ref = refs
     rows = left_ref.shape[0]
-    facts = [
-        (mine_ref[first : first + 8, :], got_ref[first : first + 8, :])
-        for first in (3 * rows, 3 * rows + 8, 3 * rows + 16)
-    ]
+    one, two = (first_ref, first_got_ref), (second_ref, second_got_ref)
+    places = ((one, 2 * rows), (one, 2 * rows + 8), (one, 2 * rows + 16))
+    facts = [tuple(ref[first : first + 8, :] for ref in both) for both, first in places]
     full = [full_facts(*both) for both in facts]
     for ref, values in zip(facts_refs, full):
         for i in range(8):
             ref[i : i + 1, :] = values[i]
     cols = columns_of(at_ref, *facts[0], full[0], cols_ref, rows)
-    for kind in range(3):
-        first = kind * rows
+    for kind, (both, first) in enumerate(((one, 0), (one, rows), (two, 0))):
         chunk = merged(
-            mine_ref[first : first + rows, :],
-            got_ref[first : first + rows, :],
+            both[0][first : first + rows, :],
+            both[1][first : first + rows, :],
             cols,
             *facts[kind],
             full[kind],
             half_rows,
             kind > 0,
         )
-        trio_ref[first : first + rows, :] = chunk
+        trio_ref[kind * rows : (kind + 1) * rows, :] = chunk
         if kind == 1:
             left_ref[...] = chunk
         if kind == 2:
             right_ref[...] = chunk
 
 
-def merge(at, mine, got, half_rows):
-    width = mine.shape[1]
-    rows = (mine.shape[0] - 24) // 3
+def merge(at, messages, half_rows):
+    width = messages[0].shape[1]
+    rows = width // 8
     return call(
         functools.partial(merge_kernel, half_rows),
-        in_specs=[smem_spec] + [vmem_spec] * 2,
+        in_specs=[smem_spec] + [vmem_spec] * 4,
         out_specs=[vmem_spec] * 6,
         out_shape=[shape(rows, width)] * 2 + [shape(3 * rows, width)] + [shape(8, width)] * 3,
         scratch_shapes=[pltpu.VMEM((width, 128), f32)],
         name="merge",
-    )(at, mine, got)
+    )(at, *messages)
 
 
 def pack(parts, wait_for=()):
@@ -492,7 +494,7 @@
 
 
 def finish_b_kernel(bounds, at_ref, mine_ref, other_ref, f_ref, pf_ref, nf_ref, *refs):
-    sums_ref, part_ref, b_ref, *halos = refs[:9]
+    sums_ref, part_ref, b_ref, *halos = refs[:15]
     out_ref, corr_ref, pen_ref, vec_ref = refs[-4:]
     step = pl.program_id(0)
 
@@ -504,11 +506,15 @@
         vec_ref[1:2, :] = sums_ref[1:2, :] + cross
 
     def current(parts):
-        rest = jnp.where(step < bounds[2], parts[1][...], parts[2][...])
-        return jnp.where(step < bounds[1], parts[0][...], rest)
-
-    prev = current(halos[:3]) * pf_ref[6:7, :] + pf_ref[7:8, :]
-    next_ = current(halos[3:]) * nf_ref[6:7, :] + nf_ref[7:8, :]
+        blocks = []
+        for i in (0, 1):
+            at = 2 * step + i
+            rest = jnp.where(at < bounds[2], parts[3 * i + 1][...], parts[3 * i + 2][...])
+            blocks.append(jnp.where(at < bounds[1], parts[3 * i][...], rest))
+        return jnp.concatenate(blocks, axis=0)
+
+    prev = current(halos[:6]) * pf_ref[6:7, :] + pf_ref[7:8, :]
+    next_ = current(halos[6:]) * nf_ref[6:7, :] + nf_ref[7:8, :]
     both = jnp.concatenate([thrice(prev), thrice(next_)], axis=1)
     grad = part_ref[...] + mm(both, pen_ref[...])
     normed = (b_ref[...] - f_ref[2:3, :]) * f_ref[3:4, :]
@@ -517,10 +523,15 @@
 
 def finish_b(at, mine, other, facts, sums, part, b, halos):
     rows, width = b.shape
-    tile = 128
-    _, bounds, maps = halo_cuts(rows, tile)
+    block = 128
+    tile = 2 * block
+    _, bounds, maps = halo_cuts(rows, block)
     spec = pl.BlockSpec((tile, width), lambda i: (i, 0))
-    parts = [pl.BlockSpec((tile, width), part) for part in maps]
+    parts = [
+        pl.BlockSpec((block, width), lambda i, half=half, part=part: part(2 * i + half))
+        for half in (0, 1)
+        for part in maps
+    ]
     whole = pl.BlockSpec((8, width), lambda i: (0, 0))
     slots = pl.BlockSpec(mine.shape, lambda i: (0, 0, 0))
     return call(
@@ -532,7 +543,7 @@
         out_shape=shape(rows, width),
         scratch_shapes=scratch_for(2, width),
         name="finish_b",
-    )(at, mine, other, *facts, sums, part, b, *halos)
+    )(at, mine, other, *facts, sums, part, b, *halos[:3] * 2, *halos[3:] * 2)
 
 
 def per_device(view_a, view_b):
@@ -548,17 +559,24 @@
     parts = [sums] + [to_x(sums, shift) for shift in (1, 2, 3)]
 
     a_top, a_mid, a_low, half_facts, keep, send = own_corr(at, view_a, view_b, parts, half_rows)
-    slots = fan(keep, to_core(send))
+    slots = fan([keep], [to_core(send)])
     own_parts = [slots[0]] + [to_x(slots[shift], shift) for shift in (1, 2, 3)]
     own, a_top = own_sum(own_parts, a_top, half_facts)
     prev_top = across(a_top, 1)
     next_top = across(a_top, -1)
 
-    keep, *sends = side_corr(at, view_a, prev_raw, next_raw, half_facts, [own])
-    slots = fan(keep, *[to_core(send) for send in sends])
-    side_parts = [slots[0]] + [to_x(slots[shift], shift) for shift in (1, 2, 3)]
-    mine = message(own, side_parts, half_facts, prev_top, next_top)
-    left, right, trio, *facts = merge(at, mine, to_y(mine), half_rows)
+    left_keep, left_send = side_corr(at, view_a, prev_raw, half_facts, [own])
+    right_keep, right_send = side_corr(at, view_a, next_raw, half_facts, [own])
+    fans = fan([left_keep, right_keep], [to_core(left_send), to_core(right_send)])
+    halves = []
+    for slots, whole, known, tops in (
+        (fans[:4], [own], [half_facts], [prev_top, next_top]),
+        (fans[4:], [], [], []),
+    ):
+        summed = [slots[0]] + [to_x(slots[shift], shift) for shift in (1, 2, 3)]
+        mine = message(whole, summed, known, tops)
+        halves += [mine, to_y(mine)]
+    left, right, trio, *facts = merge(at, halves, half_rows)
     from_next = across(left, -1)
     from_prev = across(right, 1)
     trio_slots = [trio] + [to_x(trio, shift) for shift in (1, 2, 3)]

time: 153 us -> 158 us (1.033)
  starting transfers between devices: 56.6 us -> 63.1 us
  waiting for transfers between devices: 56.4 us -> 53.8 us
  Pallas kernels: 33.6 us -> 35.3 us
    ppermute x15 -> x18, waiting for transfers between devices: 16.6 us -> 21.6 us  [to_x(): return lax.ppermute(block, 'row', pairs)]
    ppermute x15 -> x18, starting transfers between devices: 22.8 us -> 27.3 us  [to_x(): return lax.ppermute(block, 'row', pairs)]
    ppermute x1 -> x2, waiting for transfers between devices: 9.32 us -> 5.13 us  [to_y(): return lax.ppermute(block, 'row', [(i, i ^ 8) for i in range(16)])]
    ppermute x10, waiting for transfers between devices: 25.9 us -> 23.1 us  [across(): lax.ppermute(block, 'grp', [(i, (i + shift) % count) for i in range(count)])]
    pallas_call x1 -> x2, Pallas kernels: 5.88 us -> 8.38 us  [side_corr(): call(functools.partial(side_corr_kernel, steps), grid=(steps,), in_specs=...]
  transfers between devices with their start and end apart: 32 -> 36, of which waited for: 16 -> 18; matrix products, arithmetic and copies ran while one was open for 0% -> 0% of each run, Pallas kernels for 16% -> 17%
where the time goes in v6:
time: 158 us
  starting transfers between devices  63.1 us (40%)
  waiting for transfers between devices  53.8 us (34%)
  Pallas kernels  35.3 us (22%)
  local copies, waits for them, and re-layouts  4.78 us (3%)
    ppermute x18, starting transfers between devices, to_x(): return lax.ppermute(block, 'row', pairs)  27.3 us
    ppermute x10, waiting for transfers between devices, across(): lax.ppermute(block, 'grp', [(i, (i + shift) % count) for i in range(count)])  23.1 us
    ppermute x10, starting transfers between devices, across(): lax.ppermute(block, 'grp', [(i, (i + shift) % count) for i in range(count)])  22.8 us
    ppermute x18, waiting for transfers between devices, to_x(): return lax.ppermute(block, 'row', pairs)  21.6 us
    ppermute x6, starting transfers between devices, to_core(): return lax.ppermute(block, 'row', [(i, i ^ 1) for i in range(16)])  9.98 us
    pallas_call x1, Pallas kernels, finish_a(): call(finish_a_kernel, mib=40, grid=(rows // tile,), in_specs=[smem_spec,...  9.11 us
    pallas_call x2, Pallas kernels, side_corr(): call(functools.partial(side_corr_kernel, steps), grid=(steps,), in_specs=...  8.38 us
    pallas_call x1, Pallas kernels, finish_b(): call(functools.partial(finish_b_kernel, bounds), mib=24, grid=(rows // ti...  6.84 us
  transfers between devices with their start and end apart: 36, of which 18 were waited for; matrix products, arithmetic and copies ran while one was open for 0% of the time, Pallas kernels for 17%

profile of v6, /device:TPU:1, one launch (start us, length us, event | category | flops | bytes accessed | tf_op | source)
XLA Modules:
  0.0 157.8 jit_solution(16717914296372191534)
XLA Ops:
  0.6 7.5 %collective-permute-start.9 = (f32[1024,512]{1,0:T(8,128)}, f32[1024,512]{1,0:T(8,128)}, u32[]{:S(2)}, u32[]{:S(2)}) collective-permute-start(f32[1024,512]{1,0:T(8,128)} %refs_2_.1), channel_id=1, source_target_pairs={{0,240},{16,0},{32,16},{48,32},{64,48},{80,64},{96,80},{112,96},{1... | collective-permute-start | bytes 6291464 | tf_op jit(solution)/shard_map/ppermute | solution.py:34
  8.1 1.6 %copy-done = f32[1024,512]{1,0:T(8,128)S(1)} copy-done((f32[1024,512]{1,0:T(8,128)S(1)}, f32[1024,512]{1,0:T(8,128)}, u32[]{:S(2)}) %copy-start) | copy-done | bytes 2097176
  9.7 1.6 %copy-done.2 = f32[1024,512]{1,0:T(8,128)S(1)} copy-done((f32[1024,512]{1,0:T(8,128)S(1)}, f32[1024,512]{1,0:T(8,128)}, u32[]{:S(2)}) %copy-start.2) | copy-done | bytes 2097176
  11.9 1.0 collective-permute-start
  13.8 1.2 collective-permute-start.1
  15.0 2.5 %collective-permute-start.2 = (f32[8,512]{1,0:T(8,128)S(1)}, f32[8,512]{1,0:T(8,128)S(1)}, u32[]{:S(2)}, u32[]{:S(2)}) collective-permute-start(f32[8,512]{1,0:T(8,128)S(1)} %add.3.refs_0_), channel_id=1, source_target_pairs={{0,4},{1,5},{2,6},{3,7},{4,0},{5,1},{6,2},{7,3},{8,12},{9,13},{10,... | collective-permute-start | bytes 49160 | tf_op jit(solution)/shard_map/ppermute | solution.py:47
  17.5 1.2 collective-permute-start.3
  20.5 1.6 %copy-done.3 = f32[1024,512]{1,0:T(8,128)S(1)} copy-done((f32[1024,512]{1,0:T(8,128)S(1)}, f32[1024,512]{1,0:T(8,128)}, u32[]{:S(2)}) %copy-start.3) | copy-done | bytes 2097176
  22.1 5.4 %own_corr.1 = (f32[384,512]{1,0:T(8,128)S(1)}, f32[128,512]{1,0:T(8,128)S(1)}, f32[512,512]{1,0:T(8,128)S(1)}, f32[8,512]{1,0:T(8,128)S(1)}, f32[4,64,512]{2,1,0:T(8,128)S(1)}, /*index=5*/f32[4,64,512]{2,1,0:T(8,128)S(1)}) custom-call(s32[2]{0:T(128)S(1)} %pad_add_fusion.at_ref, f32[1024,512]{1,0:T(8,128)S(1)} %copy-done.1, f32[1024,512]{1,0:T(8,128)S(1)} %copy-done.3, ...), custom_call_target="tpu_custom_call" | custom-call | flops 1 | bytes 1 | tf_op jit(solution)/shard_map/own_corr/pallas_call | solution.py:159
  27.5 1.7 %collective-permute-start.4 = (f32[4,64,512]{2,1,0:T(8,128)S(1)}, f32[4,64,512]{2,1,0:T(8,128)S(1)}, u32[]{:S(2)}, u32[]{:S(2)}) collective-permute-start(f32[4,64,512]{2,1,0:T(8,128)S(1)} %get-tuple-element.40), channel_id=1, source_target_pairs={{0,1},{1,0},{2,3},{3,2},{4,5},{5,4},{6,7},{7,6},{8,9},{9,8},{10,11... | collective-permute-start | bytes 1572872 | tf_op jit(solution)/shard_map/ppermute | solution.py:38
  29.3 1.5 collective-permute-done.4.refs_1_
  30.9 3.5 %collective-permute-start.6 = (f32[64,512]{1,0:T(8,128)S(1)}, f32[64,512]{1,0:T(8,128)S(1)}, u32[]{:S(2)}, u32[]{:S(2)}) collective-permute-start(f32[64,512]{1,0:T(8,128)S(1)} %get-tuple-element.43), channel_id=1, source_target_pairs={{0,4},{1,5},{2,6},{3,7},{4,0},{5,1},{6,2},{7,3},{8,12},{9,13},{10,... | collective-permute-start | bytes 393224 | tf_op jit(solution)/shard_map/ppermute | solution.py:47
  34.5 2.5 %collective-permute-done.5.refs_1_ = f32[64,512]{1,0:T(8,128)S(1)} collective-permute-done((f32[64,512]{1,0:T(8,128)S(1)}, f32[64,512]{1,0:T(8,128)S(1)}, u32[]{:S(2)}, u32[]{:S(2)}) %collective-permute-start.5) | collective-permute-done | bytes 131104 | tf_op jit(solution)/shard_map/ppermute | solution.py:47
  37.0 3.7 %collective-permute-done.6.refs_2_ = f32[64,512]{1,0:T(8,128)S(1)} collective-permute-done((f32[64,512]{1,0:T(8,128)S(1)}, f32[64,512]{1,0:T(8,128)S(1)}, u32[]{:S(2)}, u32[]{:S(2)}) %collective-permute-start.6) | collective-permute-done | bytes 131104 | tf_op jit(solution)/shard_map/ppermute | solution.py:47
  40.8 3.9 %collective-permute-start.16 = (f32[392,512]{1,0:T(8,128)S(1)}, f32[392,512]{1,0:T(8,128)S(1)}, u32[]{:S(2)}, u32[]{:S(2)}) collective-permute-start(f32[392,512]{1,0:T(8,128)S(1)} %get-tuple-element.56), channel_id=1, source_target_pairs={{0,240},{16,0},{32,16},{48,32},{64,48},{80,64},{96,80},{112,96},{1... | collective-permute-start | bytes 2408456 | tf_op jit(solution)/shard_map/ppermute | solution.py:34
  44.7 8.0 %collective-permute-done.9.b_ref.refs_6_ = f32[1024,512]{1,0:T(8,128)} collective-permute-done((f32[1024,512]{1,0:T(8,128)}, f32[1024,512]{1,0:T(8,128)}, u32[]{:S(2)}, u32[]{:S(2)}) %collective-permute-start.9) | collective-permute-done | bytes 2097184 | tf_op jit(solution)/shard_map/ppermute | solution.py:34
  52.7 4.2 %side_corr.3 = (f32[4,64,512]{2,1,0:T(8,128)S(1)}, f32[4,64,512]{2,1,0:T(8,128)S(1)}) custom-call(s32[2]{0:T(128)S(1)} %pad_add_fusion.at_ref, f32[1024,512]{1,0:T(8,128)S(1)} %copy-done.1, f32[1024,512]{1,0:T(8,128)} %collective-permute-done.9.b_ref.refs_6_, f32[8,512]{1,0:T(8,128)S(1)} %get-tuple-element.46.refs_5_.f_ref, ...), custom_call_target="tpu_custom_call" | custom-call | flops 1 | bytes 1 | tf_op jit(solution)/shard_map/side_corr/pallas_call | solution.py:195
  56.9 2.8 %collective-permute-start.11 = (f32[4,64,512]{2,1,0:T(8,128)S(1)}, f32[4,64,512]{2,1,0:T(8,128)S(1)}, u32[]{:S(2)}, u32[]{:S(2)}) collective-permute-start(f32[4,64,512]{2,1,0:T(8,128)S(1)} %get-tuple-element.51), channel_id=1, source_target_pairs={{0,1},{1,0},{2,3},{3,2},{4,5},{5,4},{6,7},{7,6},{8,9},{9,8},{10,11... | collective-permute-start | bytes 1572872 | tf_op jit(solution)/shard_map/ppermute | solution.py:38
  59.7 4.2 %side_corr.2 = (f32[4,64,512]{2,1,0:T(8,128)S(1)}, f32[4,64,512]{2,1,0:T(8,128)S(1)}) custom-call(s32[2]{0:T(128)S(1)} %pad_add_fusion.at_ref, f32[1024,512]{1,0:T(8,128)S(1)} %copy-done.1, f32[1024,512]{1,0:T(8,128)} %collective-permute-done.8.b_ref.refs_5_, f32[8,512]{1,0:T(8,128)S(1)} %get-tuple-element.46.refs_5_.f_ref, ...), custom_call_target="tpu_custom_call" | custom-call | flops 1 | bytes 1 | tf_op jit(solution)/shard_map/side_corr/pallas_call | solution.py:195
  64.3 1.6 collective-permute-done.10.refs_2_
  66.0 1.5 collective-permute-start.12
  67.5 2.4 %collective-permute-start.13 = (f32[64,512]{1,0:T(8,128)S(1)}, f32[64,512]{1,0:T(8,128)S(1)}, u32[]{:S(2)}, u32[]{:S(2)}) collective-permute-start(f32[64,512]{1,0:T(8,128)S(1)} %get-tuple-element.54), channel_id=1, source_target_pairs={{0,4},{1,5},{2,6},{3,7},{4,0},{5,1},{6,2},{7,3},{8,12},{9,13},{10,... | collective-permute-start | bytes 393224 | tf_op jit(solution)/shard_map/ppermute | solution.py:47
  69.9 1.2 collective-permute-start.14
  71.1 2.7 %collective-permute-done.15.refs_6_.refs_3_ = f32[392,512]{1,0:T(8,128)S(1)} collective-permute-done((f32[392,512]{1,0:T(8,128)S(1)}, f32[392,512]{1,0:T(8,128)S(1)}, u32[]{:S(2)}, u32[]{:S(2)}) %collective-permute-start.15) | collective-permute-done | bytes 802848 | tf_op jit(solution)/shard_map/ppermute | solution.py:34
  73.8 2.2 %collective-permute-done.13.refs_3_ = f32[64,512]{1,0:T(8,128)S(1)} collective-permute-done((f32[64,512]{1,0:T(8,128)S(1)}, f32[64,512]{1,0:T(8,128)S(1)}, u32[]{:S(2)}, u32[]{:S(2)}) %collective-permute-start.13) | collective-permute-done | bytes 131104 | tf_op jit(solution)/shard_map/ppermute | solution.py:47
  76.1 2.7 %collective-permute-start.17 = (f32[152,512]{1,0:T(8,128)S(1)}, f32[152,512]{1,0:T(8,128)S(1)}, u32[]{:S(2)}, u32[]{:S(2)}) collective-permute-start(f32[152,512]{1,0:T(8,128)S(1)} %message.2.first_ref), channel_id=1, source_target_pairs={{0,8},{1,9},{2,10},{3,11},{4,12},{5,13},{6,14},{7,15},{8,0},{9,1},... | collective-permute-start | bytes 933896 | tf_op jit(solution)/shard_map/ppermute | solution.py:42
  78.8 1.0 collective-permute-start.18
  79.8 2.2 %collective-permute-start.19 = (f32[64,512]{1,0:T(8,128)S(1)}, f32[64,512]{1,0:T(8,128)S(1)}, u32[]{:S(2)}, u32[]{:S(2)}) collective-permute-start(f32[64,512]{1,0:T(8,128)S(1)} %get-tuple-element.59), channel_id=1, source_target_pairs={{0,4},{1,5},{2,6},{3,7},{4,0},{5,1},{6,2},{7,3},{8,12},{9,13},{10,... | collective-permute-start | bytes 393224 | tf_op jit(solution)/shard_map/ppermute | solution.py:47
  83.0 1.2 collective-permute-done.18.refs_1_
  84.1 2.8 %collective-permute-done.19.refs_2_ = f32[64,512]{1,0:T(8,128)S(1)} collective-permute-done((f32[64,512]{1,0:T(8,128)S(1)}, f32[64,512]{1,0:T(8,128)S(1)}, u32[]{:S(2)}, u32[]{:S(2)}) %collective-permute-start.19) | collective-permute-done | bytes 131104 | tf_op jit(solution)/shard_map/ppermute | solution.py:47
  87.2 5.1 %collective-permute-done.21.second_got_ref = f32[64,512]{1,0:T(8,128)S(1)} collective-permute-done((f32[64,512]{1,0:T(8,128)S(1)}, f32[64,512]{1,0:T(8,128)S(1)}, u32[]{:S(2)}, u32[]{:S(2)}) %collective-permute-start.21) | collective-permute-done | bytes 131104 | tf_op jit(solution)/shard_map/ppermute | solution.py:42
  93.4 3.9 %collective-permute-start.26 = (f32[64,512]{1,0:T(8,128)S(1)}, f32[64,512]{1,0:T(8,128)S(1)}, u32[]{:S(2)}, u32[]{:S(2)}) collective-permute-start(f32[64,512]{1,0:T(8,128)S(1)} %get-tuple-element.63), channel_id=1, source_target_pairs={{0,240},{16,0},{32,16},{48,32},{64,48},{80,64},{96,80},{112,96},{1... | collective-permute-start | bytes 393224 | tf_op jit(solution)/shard_map/ppermute | solution.py:34
  97.4 2.6 %collective-permute-start.22 = (f32[192,512]{1,0:T(8,128)S(1)}, f32[192,512]{1,0:T(8,128)S(1)}, u32[]{:S(2)}, u32[]{:S(2)}) collective-permute-start(f32[192,512]{1,0:T(8,128)S(1)} %get-tuple-element.61.refs_0_), channel_id=1, source_target_pairs={{0,2},{1,3},{2,4},{3,5},{4,6},{5,7},{6,0},{7,1},{8,10},{9,11},{10,... | collective-permute-start | bytes 1179656 | tf_op jit(solution)/shard_map/ppermute | solution.py:47
  99.9 1.0 collective-permute-start.23
  100.9 1.4 collective-permute-start.24
  102.5 3.6 %collective-permute-start.28 = (f32[128,512]{1,0:T(8,128)S(1)}, f32[128,512]{1,0:T(8,128)S(1)}, u32[]{:S(2)}, u32[]{:S(2)}) collective-permute-start(f32[128,512]{1,0:T(8,128)S(1)} %get-tuple-element.67), channel_id=1, source_target_pairs={{0,240},{16,0},{32,16},{48,32},{64,48},{80,64},{96,80},{112,96},{1... | collective-permute-start | bytes 786440 | tf_op jit(solution)/shard_map/ppermute | solution.py:34
  106.0 3.8 %collective-permute-done.27.refs_5_.refs_4_.refs_7_ = f32[128,512]{1,0:T(8,128)S(1)} collective-permute-done((f32[128,512]{1,0:T(8,128)S(1)}, f32[128,512]{1,0:T(8,128)S(1)}, u32[]{:S(2)}, u32[]{:S(2)}) %collective-permute-start.27) | collective-permute-done | bytes 262176 | tf_op jit(solution)/shard_map/ppermute | solution.py:34
  109.8 4.6 %collective-permute-done.23.refs_2_ = f32[192,512]{1,0:T(8,128)S(1)} collective-permute-done((f32[192,512]{1,0:T(8,128)S(1)}, f32[192,512]{1,0:T(8,128)S(1)}, u32[]{:S(2)}, u32[]{:S(2)}) %collective-permute-start.23) | collective-permute-done | bytes 393248 | tf_op jit(solution)/shard_map/ppermute | solution.py:47
  114.4 2.1 %collective-permute-done.24.refs_3_ = f32[192,512]{1,0:T(8,128)S(1)} collective-permute-done((f32[192,512]{1,0:T(8,128)S(1)}, f32[192,512]{1,0:T(8,128)S(1)}, u32[]{:S(2)}, u32[]{:S(2)}) %collective-permute-start.24) | collective-permute-done | bytes 393248 | tf_op jit(solution)/shard_map/ppermute | solution.py:47
  116.6 3.0 %collective-permute-start.29 = (f32[4,192,512]{2,1,0:T(8,128)S(1)}, f32[4,192,512]{2,1,0:T(8,128)S(1)}, u32[]{:S(2)}, u32[]{:S(2)}) collective-permute-start(f32[4,192,512]{2,1,0:T(8,128)S(1)} %pack.2.mine_ref), channel_id=1, source_target_pairs={{0,1},{1,0},{2,3},{3,2},{4,5},{5,4},{6,7},{7,6},{8,9},{9,8},{10,11... | collective-permute-start | bytes 4718600 | tf_op jit(solution)/shard_map/ppermute | solution.py:38
  119.6 3.6 %collective-permute-start.34 = (f32[512,512]{1,0:T(8,128)S(1)}, f32[512,512]{1,0:T(8,128)S(1)}, u32[]{:S(2)}, u32[]{:S(2)}) collective-permute-start(f32[512,512]{1,0:T(8,128)S(1)} %get-tuple-element.73), channel_id=1, source_target_pairs={{0,240},{16,0},{32,16},{48,32},{64,48},{80,64},{96,80},{112,96},{1... | collective-permute-start | bytes 3145736 | tf_op jit(solution)/shard_map/ppermute | solution.py:34
  123.2 1.6 %collective-permute-start.30 = (f32[128,512]{1,0:T(8,128)S(1)}, f32[128,512]{1,0:T(8,128)S(1)}, u32[]{:S(2)}, u32[]{:S(2)}) collective-permute-start(f32[128,512]{1,0:T(8,128)S(1)} %get-tuple-element.66.refs_4_.refs_0_), channel_id=1, source_target_pairs={{0,2},{1,3},{2,4},{3,5},{4,6},{5,7},{6,0},{7,1},{8,10},{9,11},{10,... | collective-permute-start | bytes 786440 | tf_op jit(solution)/shard_map/ppermute | solution.py:47
  124.9 1.6 %collective-permute-start.31 = (f32[128,512]{1,0:T(8,128)S(1)}, f32[128,512]{1,0:T(8,128)S(1)}, u32[]{:S(2)}, u32[]{:S(2)}) collective-permute-start(f32[128,512]{1,0:T(8,128)S(1)} %get-tuple-element.66.refs_4_.refs_0_), channel_id=1, source_target_pairs={{0,4},{1,5},{2,6},{3,7},{4,0},{5,1},{6,2},{7,3},{8,12},{9,13},{10,... | collective-permute-start | bytes 786440 | tf_op jit(solution)/shard_map/ppermute | solution.py:47
  126.5 1.4 collective-permute-start.32
  127.9 9.1 %finish_a.1 = (f32[1024,512]{1,0:T(8,128)}, f32[8,512]{1,0:T(8,128)S(1)}) custom-call(s32[2]{0:T(128)S(1)} %pad_add_fusion.at_ref, f32[4,192,512]{2,1,0:T(8,128)S(1)} %pack.2.mine_ref, f32[4,192,512]{2,1,0:T(8,128)S(1)} %collective-permute-done.29.other_ref, f32[8,512]{1,0:T(8,128)S(1)} %get-tuple-element.68.refs_0_.facts_ref.f_ref, ...), custom_call_target="tpu_custom_call" | custom-call | flops 1 | bytes 1 | tf_op jit(solution)/shard_map/finish_a/pallas_call | solution.py:452
  137.8 8.6 %collective-permute-done.33.refs_5_.refs_8_ = f32[512,512]{1,0:T(8,128)S(1)} collective-permute-done((f32[512,512]{1,0:T(8,128)S(1)}, f32[512,512]{1,0:T(8,128)S(1)}, u32[]{:S(2)}, u32[]{:S(2)}) %collective-permute-start.33) | collective-permute-done | bytes 1048608 | tf_op jit(solution)/shard_map/ppermute | solution.py:34
  147.5 3.4 %own_b.1 = (f32[1024,512]{1,0:T(8,128)S(1)}, f32[8,512]{1,0:T(8,128)S(1)}) custom-call(s32[2]{0:T(128)S(1)} %pad_add_fusion.at_ref, f32[4,192,512]{2,1,0:T(8,128)S(1)} %pack.2.mine_ref, f32[4,192,512]{2,1,0:T(8,128)S(1)} %collective-permute-done.29.other_ref, f32[8,512]{1,0:T(8,128)S(1)} %get-tuple-element.68.refs_0_.facts_ref.f_ref, ...), custom_call_target="tpu_custom_call" | custom-call | flops 1 | bytes 1 | tf_op jit(solution)/shard_map/own_b/pallas_call | solution.py:484
  151.0 6.8 %finish_b.1 = f32[1024,512]{1,0:T(8,128)} custom-call(s32[2]{0:T(128)S(1)} %pad_add_fusion.at_ref, f32[4,128,512]{2,1,0:T(8,128)S(1)} %pack.3.refs_0_.mine_ref, f32[4,128,512]{2,1,0:T(8,128)S(1)} %collective-permute-done.35.other_ref, f32[8,512]{1,0:T(8,128)S(1)} %get-tuple-element.68.refs_0_.facts_ref.f_ref, f32[8,512]{1,0:T(8,128)S(1)} %get-tuple-element.69.refs_1_.pf_ref, ...), custom_call_target="tpu_custom_call" | custom-call | flops 1 | bytes 1 | tf_op jit(solution)/shard_map/finish_b/pallas_call | solution.py:537
  (52 shorter events, 8.6 us)
Async XLA Ops:
  0.6 52.1 %collective-permute-start.9 = (f32[1024,512]{1,0:T(8,128)}, f32[1024,512]{1,0:T(8,128)}, u32[]{:S(2)}, u32[]{:S(2)}) collective-permute-start(f32[1024,512]{1,0:T(8,128)} %refs_2_.1), channel_id=1, source_target_pairs={{0,240},{16,0},{32,16},{48,32},{64,48},{80,64},{96,80},{112,96},{1... | collective-permute-start | bytes 6291464 | tf_op jit(solution)/shard_map/ppermute | solution.py:34
  8.1 51.6 %collective-permute-start.8 = (f32[1024,512]{1,0:T(8,128)}, f32[1024,512]{1,0:T(8,128)}, u32[]{:S(2)}, u32[]{:S(2)}) collective-permute-start(f32[1024,512]{1,0:T(8,128)} %refs_2_.1), channel_id=1, source_target_pairs={{0,16},{16,32},{32,48},{48,64},{64,80},{80,96},{96,112},{112,128},... | collective-permute-start | bytes 6291464 | tf_op jit(solution)/shard_map/ppermute | solution.py:34
  8.1 1.6 %copy-start = (f32[1024,512]{1,0:T(8,128)S(1)}, f32[1024,512]{1,0:T(8,128)}, u32[]{:S(2)}) copy-start(f32[1024,512]{1,0:T(8,128)} %a_ref.9) | copy-start | bytes 6291460
  9.7 1.6 %copy-start.2 = (f32[1024,512]{1,0:T(8,128)S(1)}, f32[1024,512]{1,0:T(8,128)}, u32[]{:S(2)}) copy-start(f32[1024,512]{1,0:T(8,128)} %refs_2_.1) | copy-start | bytes 6291460
  11.3 9.2 %copy-start.1 = (f32[1024,512]{1,0:T(8,128)S(1)}, f32[1024,512]{1,0:T(8,128)}, u32[]{:S(2)}) copy-start(f32[1024,512]{1,0:T(8,128)} %a_ref.9) | copy-start | bytes 6291460
  11.9 1.9 %collective-permute-start = (f32[8,512]{1,0:T(8,128)S(1)}, f32[8,512]{1,0:T(8,128)S(1)}, u32[]{:S(2)}, u32[]{:S(2)}) collective-permute-start(f32[8,512]{1,0:T(8,128)S(1)} %sums.1), channel_id=1, source_target_pairs={{0,1},{1,0},{2,3},{3,2},{4,5},{5,4},{6,7},{7,6},{8,9},{9,8},{10,11... | collective-permute-start | bytes 49160 | tf_op jit(solution)/shard_map/ppermute | solution.py:38
  13.8 4.9 %collective-permute-start.1 = (f32[8,512]{1,0:T(8,128)S(1)}, f32[8,512]{1,0:T(8,128)S(1)}, u32[]{:S(2)}, u32[]{:S(2)}) collective-permute-start(f32[8,512]{1,0:T(8,128)S(1)} %add.3.refs_0_), channel_id=1, source_target_pairs={{0,2},{1,3},{2,4},{3,5},{4,6},{5,7},{6,0},{7,1},{8,10},{9,11},{10,... | collective-permute-start | bytes 49160 | tf_op jit(solution)/shard_map/ppermute | solution.py:47
  15.0 4.5 %collective-permute-start.2 = (f32[8,512]{1,0:T(8,128)S(1)}, f32[8,512]{1,0:T(8,128)S(1)}, u32[]{:S(2)}, u32[]{:S(2)}) collective-permute-start(f32[8,512]{1,0:T(8,128)S(1)} %add.3.refs_0_), channel_id=1, source_target_pairs={{0,4},{1,5},{2,6},{3,7},{4,0},{5,1},{6,2},{7,3},{8,12},{9,13},{10,... | collective-permute-start | bytes 49160 | tf_op jit(solution)/shard_map/ppermute | solution.py:47
  17.5 3.0 %collective-permute-start.3 = (f32[8,512]{1,0:T(8,128)S(1)}, f32[8,512]{1,0:T(8,128)S(1)}, u32[]{:S(2)}, u32[]{:S(2)}) collective-permute-start(f32[8,512]{1,0:T(8,128)S(1)} %add.3.refs_0_), channel_id=1, source_target_pairs={{0,6},{1,7},{2,0},{3,1},{4,2},{5,3},{6,4},{7,5},{8,14},{9,15},{10,... | collective-permute-start | bytes 49160 | tf_op jit(solution)/shard_map/ppermute | solution.py:47
  20.5 1.6 %copy-start.3 = (f32[1024,512]{1,0:T(8,128)S(1)}, f32[1024,512]{1,0:T(8,128)}, u32[]{:S(2)}) copy-start(f32[1024,512]{1,0:T(8,128)} %refs_2_.1) | copy-start | bytes 6291460
  27.5 3.3 %collective-permute-start.4 = (f32[4,64,512]{2,1,0:T(8,128)S(1)}, f32[4,64,512]{2,1,0:T(8,128)S(1)}, u32[]{:S(2)}, u32[]{:S(2)}) collective-permute-start(f32[4,64,512]{2,1,0:T(8,128)S(1)} %get-tuple-element.40), channel_id=1, source_target_pairs={{0,1},{1,0},{2,3},{3,2},{4,5},{5,4},{6,7},{7,6},{8,9},{9,8},{10,11... | collective-permute-start | bytes 1572872 | tf_op jit(solution)/shard_map/ppermute | solution.py:38
  30.8 6.1 %collective-permute-start.5 = (f32[64,512]{1,0:T(8,128)S(1)}, f32[64,512]{1,0:T(8,128)S(1)}, u32[]{:S(2)}, u32[]{:S(2)}) collective-permute-start(f32[64,512]{1,0:T(8,128)S(1)} %get-tuple-element.42), channel_id=1, source_target_pairs={{0,2},{1,3},{2,4},{3,5},{4,6},{5,7},{6,0},{7,1},{8,10},{9,11},{10,... | collective-permute-start | bytes 393224 | tf_op jit(solution)/shard_map/ppermute | solution.py:47
  30.9 9.7 %collective-permute-start.6 = (f32[64,512]{1,0:T(8,128)S(1)}, f32[64,512]{1,0:T(8,128)S(1)}, u32[]{:S(2)}, u32[]{:S(2)}) collective-permute-start(f32[64,512]{1,0:T(8,128)S(1)} %get-tuple-element.43), channel_id=1, source_target_pairs={{0,4},{1,5},{2,6},{3,7},{4,0},{5,1},{6,2},{7,3},{8,12},{9,13},{10,... | collective-permute-start | bytes 393224 | tf_op jit(solution)/shard_map/ppermute | solution.py:47
  34.5 6.2 %collective-permute-start.7 = (f32[64,512]{1,0:T(8,128)S(1)}, f32[64,512]{1,0:T(8,128)S(1)}, u32[]{:S(2)}, u32[]{:S(2)}) collective-permute-start(f32[64,512]{1,0:T(8,128)S(1)} %get-tuple-element.44), channel_id=1, source_target_pairs={{0,6},{1,7},{2,0},{3,1},{4,2},{5,3},{6,4},{7,5},{8,14},{9,15},{10,... | collective-permute-start | bytes 393224 | tf_op jit(solution)/shard_map/ppermute | solution.py:47
  40.7 33.1 %collective-permute-start.15 = (f32[392,512]{1,0:T(8,128)S(1)}, f32[392,512]{1,0:T(8,128)S(1)}, u32[]{:S(2)}, u32[]{:S(2)}) collective-permute-start(f32[392,512]{1,0:T(8,128)S(1)} %get-tuple-element.56), channel_id=1, source_target_pairs={{0,16},{16,32},{32,48},{48,64},{64,80},{80,96},{96,112},{112,128},... | collective-permute-start | bytes 2408456 | tf_op jit(solution)/shard_map/ppermute | solution.py:34
  40.8 33.0 %collective-permute-start.16 = (f32[392,512]{1,0:T(8,128)S(1)}, f32[392,512]{1,0:T(8,128)S(1)}, u32[]{:S(2)}, u32[]{:S(2)}) collective-permute-start(f32[392,512]{1,0:T(8,128)S(1)} %get-tuple-element.56), channel_id=1, source_target_pairs={{0,240},{16,0},{32,16},{48,32},{64,48},{80,64},{96,80},{112,96},{1... | collective-permute-start | bytes 2408456 | tf_op jit(solution)/shard_map/ppermute | solution.py:34
  56.9 7.4 %collective-permute-start.11 = (f32[4,64,512]{2,1,0:T(8,128)S(1)}, f32[4,64,512]{2,1,0:T(8,128)S(1)}, u32[]{:S(2)}, u32[]{:S(2)}) collective-permute-start(f32[4,64,512]{2,1,0:T(8,128)S(1)} %get-tuple-element.51), channel_id=1, source_target_pairs={{0,1},{1,0},{2,3},{3,2},{4,5},{5,4},{6,7},{7,6},{8,9},{9,8},{10,11... | collective-permute-start | bytes 1572872 | tf_op jit(solution)/shard_map/ppermute | solution.py:38
  63.9 2.0 %collective-permute-start.10 = (f32[4,64,512]{2,1,0:T(8,128)S(1)}, f32[4,64,512]{2,1,0:T(8,128)S(1)}, u32[]{:S(2)}, u32[]{:S(2)}) collective-permute-start(f32[4,64,512]{2,1,0:T(8,128)S(1)} %get-tuple-element.50), channel_id=1, source_target_pairs={{0,1},{1,0},{2,3},{3,2},{4,5},{5,4},{6,7},{7,6},{8,9},{9,8},{10,11... | collective-permute-start | bytes 1572872 | tf_op jit(solution)/shard_map/ppermute | solution.py:38
  66.0 7.8 %collective-permute-start.12 = (f32[64,512]{1,0:T(8,128)S(1)}, f32[64,512]{1,0:T(8,128)S(1)}, u32[]{:S(2)}, u32[]{:S(2)}) collective-permute-start(f32[64,512]{1,0:T(8,128)S(1)} %get-tuple-element.53), channel_id=1, source_target_pairs={{0,2},{1,3},{2,4},{3,5},{4,6},{5,7},{6,0},{7,1},{8,10},{9,11},{10,... | collective-permute-start | bytes 393224 | tf_op jit(solution)/shard_map/ppermute | solution.py:47
  67.5 8.5 %collective-permute-start.13 = (f32[64,512]{1,0:T(8,128)S(1)}, f32[64,512]{1,0:T(8,128)S(1)}, u32[]{:S(2)}, u32[]{:S(2)}) collective-permute-start(f32[64,512]{1,0:T(8,128)S(1)} %get-tuple-element.54), channel_id=1, source_target_pairs={{0,4},{1,5},{2,6},{3,7},{4,0},{5,1},{6,2},{7,3},{8,12},{9,13},{10,... | collective-permute-start | bytes 393224 | tf_op jit(solution)/shard_map/ppermute | solution.py:47
  69.9 6.1 %collective-permute-start.14 = (f32[64,512]{1,0:T(8,128)S(1)}, f32[64,512]{1,0:T(8,128)S(1)}, u32[]{:S(2)}, u32[]{:S(2)}) collective-permute-start(f32[64,512]{1,0:T(8,128)S(1)} %get-tuple-element.55), channel_id=1, source_target_pairs={{0,6},{1,7},{2,0},{3,1},{4,2},{5,3},{6,4},{7,5},{8,14},{9,15},{10,... | collective-permute-start | bytes 393224 | tf_op jit(solution)/shard_map/ppermute | solution.py:47
  76.1 16.3 %collective-permute-start.17 = (f32[152,512]{1,0:T(8,128)S(1)}, f32[152,512]{1,0:T(8,128)S(1)}, u32[]{:S(2)}, u32[]{:S(2)}) collective-permute-start(f32[152,512]{1,0:T(8,128)S(1)} %message.2.first_ref), channel_id=1, source_target_pairs={{0,8},{1,9},{2,10},{3,11},{4,12},{5,13},{6,14},{7,15},{8,0},{9,1},... | collective-permute-start | bytes 933896 | tf_op jit(solution)/shard_map/ppermute | solution.py:42
  78.8 5.3 %collective-permute-start.18 = (f32[64,512]{1,0:T(8,128)S(1)}, f32[64,512]{1,0:T(8,128)S(1)}, u32[]{:S(2)}, u32[]{:S(2)}) collective-permute-start(f32[64,512]{1,0:T(8,128)S(1)} %get-tuple-element.58), channel_id=1, source_target_pairs={{0,2},{1,3},{2,4},{3,5},{4,6},{5,7},{6,0},{7,1},{8,10},{9,11},{10,... | collective-permute-start | bytes 393224 | tf_op jit(solution)/shard_map/ppermute | solution.py:47
  79.8 7.1 %collective-permute-start.19 = (f32[64,512]{1,0:T(8,128)S(1)}, f32[64,512]{1,0:T(8,128)S(1)}, u32[]{:S(2)}, u32[]{:S(2)}) collective-permute-start(f32[64,512]{1,0:T(8,128)S(1)} %get-tuple-element.59), channel_id=1, source_target_pairs={{0,4},{1,5},{2,6},{3,7},{4,0},{5,1},{6,2},{7,3},{8,12},{9,13},{10,... | collective-permute-start | bytes 393224 | tf_op jit(solution)/shard_map/ppermute | solution.py:47
  82.0 4.9 %collective-permute-start.20 = (f32[64,512]{1,0:T(8,128)S(1)}, f32[64,512]{1,0:T(8,128)S(1)}, u32[]{:S(2)}, u32[]{:S(2)}) collective-permute-start(f32[64,512]{1,0:T(8,128)S(1)} %get-tuple-element.60), channel_id=1, source_target_pairs={{0,6},{1,7},{2,0},{3,1},{4,2},{5,3},{6,4},{7,5},{8,14},{9,15},{10,... | collective-permute-start | bytes 393224 | tf_op jit(solution)/shard_map/ppermute | solution.py:47
  86.9 5.4 %collective-permute-start.21 = (f32[64,512]{1,0:T(8,128)S(1)}, f32[64,512]{1,0:T(8,128)S(1)}, u32[]{:S(2)}, u32[]{:S(2)}) collective-permute-start(f32[64,512]{1,0:T(8,128)S(1)} %message.3.second_ref), channel_id=1, source_target_pairs={{0,8},{1,9},{2,10},{3,11},{4,12},{5,13},{6,14},{7,15},{8,0},{9,1},... | collective-permute-start | bytes 393224 | tf_op jit(solution)/shard_map/ppermute | solution.py:42
  93.3 9.0 %collective-permute-start.25 = (f32[64,512]{1,0:T(8,128)S(1)}, f32[64,512]{1,0:T(8,128)S(1)}, u32[]{:S(2)}, u32[]{:S(2)}) collective-permute-start(f32[64,512]{1,0:T(8,128)S(1)} %get-tuple-element.62), channel_id=1, source_target_pairs={{0,16},{16,32},{32,48},{48,64},{64,80},{80,96},{96,112},{112,128},... | collective-permute-start | bytes 393224 | tf_op jit(solution)/shard_map/ppermute | solution.py:34
  93.4 8.9 %collective-permute-start.26 = (f32[64,512]{1,0:T(8,128)S(1)}, f32[64,512]{1,0:T(8,128)S(1)}, u32[]{:S(2)}, u32[]{:S(2)}) collective-permute-start(f32[64,512]{1,0:T(8,128)S(1)} %get-tuple-element.63), channel_id=1, source_target_pairs={{0,240},{16,0},{32,16},{48,32},{64,48},{80,64},{96,80},{112,96},{1... | collective-permute-start | bytes 393224 | tf_op jit(solution)/shard_map/ppermute | solution.py:34
  97.4 12.4 %collective-permute-start.22 = (f32[192,512]{1,0:T(8,128)S(1)}, f32[192,512]{1,0:T(8,128)S(1)}, u32[]{:S(2)}, u32[]{:S(2)}) collective-permute-start(f32[192,512]{1,0:T(8,128)S(1)} %get-tuple-element.61.refs_0_), channel_id=1, source_target_pairs={{0,2},{1,3},{2,4},{3,5},{4,6},{5,7},{6,0},{7,1},{8,10},{9,11},{10,... | collective-permute-start | bytes 1179656 | tf_op jit(solution)/shard_map/ppermute | solution.py:47
  99.9 14.5 %collective-permute-start.23 = (f32[192,512]{1,0:T(8,128)S(1)}, f32[192,512]{1,0:T(8,128)S(1)}, u32[]{:S(2)}, u32[]{:S(2)}) collective-permute-start(f32[192,512]{1,0:T(8,128)S(1)} %get-tuple-element.61.refs_0_), channel_id=1, source_target_pairs={{0,4},{1,5},{2,6},{3,7},{4,0},{5,1},{6,2},{7,3},{8,12},{9,13},{10,... | collective-permute-start | bytes 1179656 | tf_op jit(solution)/shard_map/ppermute | solution.py:47
  100.9 15.5 %collective-permute-start.24 = (f32[192,512]{1,0:T(8,128)S(1)}, f32[192,512]{1,0:T(8,128)S(1)}, u32[]{:S(2)}, u32[]{:S(2)}) collective-permute-start(f32[192,512]{1,0:T(8,128)S(1)} %get-tuple-element.61.refs_0_), channel_id=1, source_target_pairs={{0,6},{1,7},{2,0},{3,1},{4,2},{5,3},{6,4},{7,5},{8,14},{9,15},{10,... | collective-permute-start | bytes 1179656 | tf_op jit(solution)/shard_map/ppermute | solution.py:47
  102.4 25.6 %copy-start.4 = (f32[1024,512]{1,0:T(8,128)S(1)}, f32[1024,512]{1,0:T(8,128)}, u32[]{:S(2)}) copy-start(f32[1024,512]{1,0:T(8,128)} %refs_2_.1) | copy-start | bytes 6291460
  102.4 7.4 %collective-permute-start.27 = (f32[128,512]{1,0:T(8,128)S(1)}, f32[128,512]{1,0:T(8,128)S(1)}, u32[]{:S(2)}, u32[]{:S(2)}) collective-permute-start(f32[128,512]{1,0:T(8,128)S(1)} %get-tuple-element.67), channel_id=1, source_target_pairs={{0,16},{16,32},{32,48},{48,64},{64,80},{80,96},{96,112},{112,128},... | collective-permute-start | bytes 786440 | tf_op jit(solution)/shard_map/ppermute | solution.py:34
  102.5 7.3 %collective-permute-start.28 = (f32[128,512]{1,0:T(8,128)S(1)}, f32[128,512]{1,0:T(8,128)S(1)}, u32[]{:S(2)}, u32[]{:S(2)}) collective-permute-start(f32[128,512]{1,0:T(8,128)S(1)} %get-tuple-element.67), channel_id=1, source_target_pairs={{0,240},{16,0},{32,16},{48,32},{64,48},{80,64},{96,80},{112,96},{1... | collective-permute-start | bytes 786440 | tf_op jit(solution)/shard_map/ppermute | solution.py:34
  116.6 9.9 %collective-permute-start.29 = (f32[4,192,512]{2,1,0:T(8,128)S(1)}, f32[4,192,512]{2,1,0:T(8,128)S(1)}, u32[]{:S(2)}, u32[]{:S(2)}) collective-permute-start(f32[4,192,512]{2,1,0:T(8,128)S(1)} %pack.2.mine_ref), channel_id=1, source_target_pairs={{0,1},{1,0},{2,3},{3,2},{4,5},{5,4},{6,7},{7,6},{8,9},{9,8},{10,11... | collective-permute-start | bytes 4718600 | tf_op jit(solution)/shard_map/ppermute | solution.py:38
  119.6 26.8 %collective-permute-start.33 = (f32[512,512]{1,0:T(8,128)S(1)}, f32[512,512]{1,0:T(8,128)S(1)}, u32[]{:S(2)}, u32[]{:S(2)}) collective-permute-start(f32[512,512]{1,0:T(8,128)S(1)} %get-tuple-element.73), channel_id=1, source_target_pairs={{0,16},{16,32},{32,48},{48,64},{64,80},{80,96},{96,112},{112,128},... | collective-permute-start | bytes 3145736 | tf_op jit(solution)/shard_map/ppermute | solution.py:34
  119.6 26.8 %collective-permute-start.34 = (f32[512,512]{1,0:T(8,128)S(1)}, f32[512,512]{1,0:T(8,128)S(1)}, u32[]{:S(2)}, u32[]{:S(2)}) collective-permute-start(f32[512,512]{1,0:T(8,128)S(1)} %get-tuple-element.73), channel_id=1, source_target_pairs={{0,240},{16,0},{32,16},{48,32},{64,48},{80,64},{96,80},{112,96},{1... | collective-permute-start | bytes 3145736 | tf_op jit(solution)/shard_map/ppermute | solution.py:34
  123.2 13.8 %collective-permute-start.30 = (f32[128,512]{1,0:T(8,128)S(1)}, f32[128,512]{1,0:T(8,128)S(1)}, u32[]{:S(2)}, u32[]{:S(2)}) collective-permute-start(f32[128,512]{1,0:T(8,128)S(1)} %get-tuple-element.66.refs_4_.refs_0_), channel_id=1, source_target_pairs={{0,2},{1,3},{2,4},{3,5},{4,6},{5,7},{6,0},{7,1},{8,10},{9,11},{10,... | collective-permute-start | bytes 786440 | tf_op jit(solution)/shard_map/ppermute | solution.py:47
  124.9 13.0 %collective-permute-start.31 = (f32[128,512]{1,0:T(8,128)S(1)}, f32[128,512]{1,0:T(8,128)S(1)}, u32[]{:S(2)}, u32[]{:S(2)}) collective-permute-start(f32[128,512]{1,0:T(8,128)S(1)} %get-tuple-element.66.refs_4_.refs_0_), channel_id=1, source_target_pairs={{0,4},{1,5},{2,6},{3,7},{4,0},{5,1},{6,2},{7,3},{8,12},{9,13},{10,... | collective-permute-start | bytes 786440 | tf_op jit(solution)/shard_map/ppermute | solution.py:47
  126.5 11.4 %collective-permute-start.32 = (f32[128,512]{1,0:T(8,128)S(1)}, f32[128,512]{1,0:T(8,128)S(1)}, u32[]{:S(2)}, u32[]{:S(2)}) collective-permute-start(f32[128,512]{1,0:T(8,128)S(1)} %get-tuple-element.66.refs_4_.refs_0_), channel_id=1, source_target_pairs={{0,6},{1,7},{2,0},{3,1},{4,2},{5,3},{6,4},{7,5},{8,14},{9,15},{10,... | collective-permute-start | bytes 786440 | tf_op jit(solution)/shard_map/ppermute | solution.py:47
  146.5 4.4 %collective-permute-start.35 = (f32[4,128,512]{2,1,0:T(8,128)S(1)}, f32[4,128,512]{2,1,0:T(8,128)S(1)}, u32[]{:S(2)}, u32[]{:S(2)}) collective-permute-start(f32[4,128,512]{2,1,0:T(8,128)S(1)} %pack.3.refs_0_.mine_ref), channel_id=1, source_target_pairs={{0,1},{1,0},{2,3},{3,2},{4,5},{5,4},{6,7},{7,6},{8,9},{9,8},{10,11... | collective-permute-start | bytes 3145736 | tf_op jit(solution)/shard_map/ppermute | solution.py:38

commit v7 on v5

--- a/solution.py
+++ b/solution.py
@@ -419,8 +419,52 @@
     ]
 
 
+def presplit_kernel(b_ref, prev_ref, next_ref, a_ref, f_ref, pf_ref, nf_ref, *refs):
+    bs_ref, a_out_ref = refs[-2:]
+    width = a_ref.shape[1]
+    for kind, (ref, facts_ref) in enumerate(
+        ((b_ref, f_ref), (prev_ref, pf_ref), (next_ref, nf_ref))
+    ):
+        high, low = split((ref[...] - facts_ref[2:3, :]) * facts_ref[3:4, :])
+        bs_ref[:, 2 * kind * width : (2 * kind + 1) * width] = high
+        bs_ref[:, (2 * kind + 1) * width : (2 * kind + 2) * width] = low
+    high, low = split((a_ref[...] - f_ref[0:1, :]) * f_ref[1:2, :])
+    a_out_ref[:, 0:width] = high
+    a_out_ref[:, width:] = low
+
+
+def presplit(b, prev_b, next_b, a, facts, wait_for):
+    rows, width = a.shape
+    tile = 256
+    spec = pl.BlockSpec((tile, width), lambda i: (i, 0))
+    whole = pl.BlockSpec((8, width), lambda i: (0, 0))
+    return call(
+        presplit_kernel,
+        mib=16,
+        grid=(rows // tile,),
+        in_specs=[spec] * 4 + [whole] * 3 + [any_spec] * len(wait_for),
+        out_specs=[
+            pl.BlockSpec((tile, 6 * width), lambda i: (i, 0)),
+            pl.BlockSpec((tile, 2 * width), lambda i: (i, 0)),
+        ],
+        out_shape=[
+            jax.ShapeDtypeStruct((rows, 6 * width), bf16),
+            jax.ShapeDtypeStruct((rows, 2 * width), bf16),
+        ],
+        name="presplit",
+    )(b, prev_b, next_b, a, *facts, *wait_for)
+
+
+def repeated(parts, width):
+    blocks = []
+    for first in range(0, parts.shape[1], 2 * width):
+        high = parts[:, first : first + width]
+        blocks += [high, high, parts[:, first + width : first + 2 * width]]
+    return jnp.concatenate(blocks, axis=1)
+
+
 def finish_a_kernel(at_ref, mine_ref, other_ref, *refs):
-    facts, (a_ref, *b_refs) = refs[:3], refs[3:7]
+    facts, (a_ref, parts_ref) = refs[:3], refs[3:5]
     out_ref, ready_ref, corr_ref, pen_ref, vec_ref = refs[-5:]
 
     @pl.when(pl.program_id(0) == 0)
@@ -432,16 +476,13 @@
         vec_ref[0:1, :] = mm(left, pen_ref[...])[5:6]
         vec_ref[1:2, :] = cross
 
-    norms = [
-        thrice((b_ref[...] - ref[2:3, :]) * ref[3:4, :]) for b_ref, ref in zip(b_refs, facts)
-    ]
-    grad = mm(jnp.concatenate(norms, axis=1), pen_ref[...])
+    grad = mm(repeated(parts_ref[...], a_ref.shape[1]), pen_ref[...])
     inverse = facts[0][1:2, :]
     normed = (a_ref[...] - facts[0][0:1, :]) * inverse
     out_ref[...] = (grad - vec_ref[0:1, :] - normed * vec_ref[1:2, :]) * inverse
 
 
-def finish_a(at, mine, other, facts, a, b, prev_b, next_b):
+def finish_a(at, mine, other, facts, a, parts):
     rows, width = a.shape
     tile = 256
     spec = pl.BlockSpec((tile, width), lambda i: (i, 0))
@@ -451,15 +492,17 @@
         finish_a_kernel,
         mib=40,
         grid=(rows // tile,),
-        in_specs=[smem_spec, slots, slots] + [whole] * 3 + [spec] * 4,
+        in_specs=[smem_spec, slots, slots]
+        + [whole] * 3
+        + [spec, pl.BlockSpec((tile, 6 * width), lambda i: (i, 0))],
         out_specs=[spec, whole],
         out_shape=[shape(rows, width), shape(8, width)],
         scratch_shapes=scratch_for(3, width),
         name="finish_a",
-    )(at, mine, other, *facts, a, b, prev_b, next_b)
-
-
-def own_b_kernel(at_ref, mine_ref, other_ref, facts_ref, a_ref, *refs):
+    )(at, mine, other, *facts, a, parts)
+
+
+def own_b_kernel(at_ref, mine_ref, other_ref, facts_ref, parts_ref, *refs):
     out_ref, sums_ref, corr_ref, pen_ref, _ = refs[-5:]
 
     @pl.when(pl.program_id(0) == 0)
@@ -469,12 +512,11 @@
         sums_ref[0:1, :] = mm(thrice(facts_ref[...]), pen_ref[...])[4:5]
         sums_ref[1:2, :] = cross
 
-    norm_a = (a_ref[...] - facts_ref[0:1, :]) * facts_ref[1:2, :]
-    out_ref[...] = mm(thrice(norm_a), pen_ref[...])
-
-
-def own_b(at, mine, other, facts, a, wait_for):
-    rows, width = a.shape
+    out_ref[...] = mm(repeated(parts_ref[...], out_ref.shape[1]), pen_ref[...])
+
+
+def own_b(at, mine, other, facts, parts, wait_for):
+    rows, width = parts.shape[0], parts.shape[1] // 2
     tile = 256
     spec = pl.BlockSpec((tile, width), lambda i: (i, 0))
     whole = pl.BlockSpec((8, width), lambda i: (0, 0))
@@ -483,16 +525,18 @@
         own_b_kernel,
         mib=24,
         grid=(rows // tile,),
-        in_specs=[smem_spec, slots, slots, whole, spec] + [any_spec] * len(wait_for),
+        in_specs=[smem_spec, slots, slots, whole]
+        + [pl.BlockSpec((tile, 2 * width), lambda i: (i, 0))]
+        + [any_spec] * len(wait_for),
         out_specs=[spec, whole],
         out_shape=[shape(rows, width), shape(8, width)],
         scratch_shapes=scratch_for(1, width),
         name="own_b",
-    )(at, mine, other, facts, a, *wait_for)
+    )(at, mine, other, facts, parts, *wait_for)
 
 
 def finish_b_kernel(bounds, at_ref, mine_ref, other_ref, f_ref, pf_ref, nf_ref, *refs):
-    sums_ref, part_ref, b_ref, *halos = refs[:9]
+    sums_ref, part_ref, b_ref, *halos = refs[:15]
     out_ref, corr_ref, pen_ref, vec_ref = refs[-4:]
     step = pl.program_id(0)
 
@@ -504,11 +548,15 @@
         vec_ref[1:2, :] = sums_ref[1:2, :] + cross
 
     def current(parts):
-        rest = jnp.where(step < bounds[2], parts[1][...], parts[2][...])
-        return jnp.where(step < bounds[1], parts[0][...], rest)
-
-    prev = current(halos[:3]) * pf_ref[6:7, :] + pf_ref[7:8, :]
-    next_ = current(halos[3:]) * nf_ref[6:7, :] + nf_ref[7:8, :]
+        blocks = []
+        for i in (0, 1):
+            at = 2 * step + i
+            rest = jnp.where(at < bounds[2], parts[3 * i + 1][...], parts[3 * i + 2][...])
+            blocks.append(jnp.where(at < bounds[1], parts[3 * i][...], rest))
+        return jnp.concatenate(blocks, axis=0)
+
+    prev = current(halos[:6]) * pf_ref[6:7, :] + pf_ref[7:8, :]
+    next_ = current(halos[6:]) * nf_ref[6:7, :] + nf_ref[7:8, :]
     both = jnp.concatenate([thrice(prev), thrice(next_)], axis=1)
     grad = part_ref[...] + mm(both, pen_ref[...])
     normed = (b_ref[...] - f_ref[2:3, :]) * f_ref[3:4, :]
@@ -517,10 +565,15 @@
 
 def finish_b(at, mine, other, facts, sums, part, b, halos):
     rows, width = b.shape
-    tile = 128
-    _, bounds, maps = halo_cuts(rows, tile)
+    block = 128
+    tile = 2 * block
+    _, bounds, maps = halo_cuts(rows, block)
     spec = pl.BlockSpec((tile, width), lambda i: (i, 0))
-    parts = [pl.BlockSpec((tile, width), part) for part in maps]
+    parts = [
+        pl.BlockSpec((block, width), lambda i, half=half, part=part: part(2 * i + half))
+        for half in (0, 1)
+        for part in maps
+    ]
     whole = pl.BlockSpec((8, width), lambda i: (0, 0))
     slots = pl.BlockSpec(mine.shape, lambda i: (0, 0, 0))
     return call(
@@ -532,7 +585,7 @@
         out_shape=shape(rows, width),
         scratch_shapes=scratch_for(2, width),
         name="finish_b",
-    )(at, mine, other, *facts, sums, part, b, *halos)
+    )(at, mine, other, *facts, sums, part, b, *halos[:3] * 2, *halos[3:] * 2)
 
 
 def per_device(view_a, view_b):
@@ -568,11 +621,12 @@
     prev_low = across(a_low, 1)
     next_low = across(a_low, -1)
     end_slots = [ends] + [to_x(ends, shift) for shift in (1, 2, 3)]
-    mine = pack(trio_slots, [ends, prev_mid, next_mid])
+    b_parts, a_parts = presplit(view_b, prev_raw, next_raw, view_a, facts, [ends])
+    mine = pack(trio_slots, [a_parts, prev_mid, next_mid])
     other = to_core(mine)
-    grad_a, ready = finish_a(at, mine, other, facts, view_a, view_b, prev_raw, next_raw)
+    grad_a, ready = finish_a(at, mine, other, facts, view_a, b_parts)
     ends = pack(end_slots, [ready, prev_low, next_low])
-    part_b, sums = own_b(at, mine, other, facts[0], view_a, [ends])
+    part_b, sums = own_b(at, mine, other, facts[0], a_parts, [ends])
     halos = [prev_top, prev_mid, prev_low, next_top, next_mid, next_low]
     grad_b = finish_b(at, ends, to_core(ends), facts, sums, part_b, view_b, halos)
     return (grad_a, grad_b)

time: 153 us -> 152 us (level)
  waiting for transfers between devices: 56.4 us -> 53.2 us
  Pallas kernels: 33.6 us -> 35.9 us
    ppermute x10, waiting for transfers between devices: 25.9 us -> 22.1 us  [across(): lax.ppermute(block, 'grp', [(i, (i + shift) % count) for i in range(count)])]
    pallas_call x0 -> x1, Pallas kernels: none -> 3.75 us  [presplit(): call(presplit_kernel, mib=16, grid=(rows // tile,), in_specs=[spec] * 4 +...]
  transfers between devices with their start and end apart: 32 -> 32, of which waited for: 16 -> 15; matrix products, arithmetic and copies ran while one was open for 0% -> 0% of each run, Pallas kernels for 16% -> 18%
where the time goes in v7:
time: 152 us; the launch traced here: 151 us
  starting transfers between devices  56.6 us (37%)
  waiting for transfers between devices  53.2 us (35%)
  Pallas kernels  35.9 us (24%)
  local copies, waits for them, and re-layouts  4.78 us (3%)
    ppermute x15, starting transfers between devices, to_x(): return lax.ppermute(block, 'row', pairs)  22.8 us
    ppermute x10, waiting for transfers between devices, across(): lax.ppermute(block, 'grp', [(i, (i + shift) % count) for i in range(count)])  22.1 us
    ppermute x10, starting transfers between devices, across(): lax.ppermute(block, 'grp', [(i, (i + shift) % count) for i in range(count)])  22.1 us
    ppermute x15, waiting for transfers between devices, to_x(): return lax.ppermute(block, 'row', pairs)  17.2 us
    ppermute x1, waiting for transfers between devices, to_y(): return lax.ppermute(block, 'row', [(i, i ^ 8) for i in range(16)])  9.32 us
    ppermute x6, starting transfers between devices, to_core(): return lax.ppermute(block, 'row', [(i, i ^ 1) for i in range(16)])  8.99 us
    pallas_call x1, Pallas kernels, finish_a(): call(finish_a_kernel, mib=40, grid=(rows // tile,), in_specs=[smem_spec,...  8.52 us
    pallas_call x1, Pallas kernels, finish_b(): call(functools.partial(finish_b_kernel, bounds), mib=24, grid=(rows // ti...  6.75 us
  transfers between devices with their start and end apart: 32, of which 15 were waited for; matrix products, arithmetic and copies ran while one was open for 0% of the time, Pallas kernels for 18%

profile of v7, /device:TPU:1, one launch (start us, length us, event | category | flops | bytes accessed | tf_op | source)
XLA Modules:
  0.0 151.4 jit_solution(14614893647732891583)
XLA Ops:
  0.6 2.5 %collective-permute-start.8 = (f32[1024,512]{1,0:T(8,128)}, f32[1024,512]{1,0:T(8,128)}, u32[]{:S(2)}, u32[]{:S(2)}) collective-permute-start(f32[1024,512]{1,0:T(8,128)} %refs_2_.1), channel_id=1, source_target_pairs={{0,16},{16,32},{32,48},{48,64},{64,80},{80,96},{96,112},{112,128},... | collective-permute-start | bytes 6291464 | tf_op jit(solution)/shard_map/ppermute | solution.py:34
  3.2 5.0 %collective-permute-start.9 = (f32[1024,512]{1,0:T(8,128)}, f32[1024,512]{1,0:T(8,128)}, u32[]{:S(2)}, u32[]{:S(2)}) collective-permute-start(f32[1024,512]{1,0:T(8,128)} %refs_2_.1), channel_id=1, source_target_pairs={{0,240},{16,0},{32,16},{48,32},{64,48},{80,64},{96,80},{112,96},{1... | collective-permute-start | bytes 6291464 | tf_op jit(solution)/shard_map/ppermute | solution.py:34
  8.2 1.6 %copy-done = f32[1024,512]{1,0:T(8,128)S(1)} copy-done((f32[1024,512]{1,0:T(8,128)S(1)}, f32[1024,512]{1,0:T(8,128)}, u32[]{:S(2)}) %copy-start) | copy-done | bytes 2097176
  9.8 1.6 %copy-done.2 = f32[1024,512]{1,0:T(8,128)S(1)} copy-done((f32[1024,512]{1,0:T(8,128)S(1)}, f32[1024,512]{1,0:T(8,128)}, u32[]{:S(2)}) %copy-start.2) | copy-done | bytes 2097176
  12.0 1.0 collective-permute-start
  13.1 0.8 collective-permute-done
  13.9 1.2 collective-permute-start.1
  15.1 2.5 %collective-permute-start.2 = (f32[8,512]{1,0:T(8,128)S(1)}, f32[8,512]{1,0:T(8,128)S(1)}, u32[]{:S(2)}, u32[]{:S(2)}) collective-permute-start(f32[8,512]{1,0:T(8,128)S(1)} %add.3.refs_0_), channel_id=1, source_target_pairs={{0,4},{1,5},{2,6},{3,7},{4,0},{5,1},{6,2},{7,3},{8,12},{9,13},{10,... | collective-permute-start | bytes 49160 | tf_op jit(solution)/shard_map/ppermute | solution.py:47
  17.6 1.2 collective-permute-start.3
  18.8 0.8 collective-permute-done.2.refs_2_
  19.6 0.9 collective-permute-done.3.refs_3_
  20.6 1.6 %copy-done.3 = f32[1024,512]{1,0:T(8,128)S(1)} copy-done((f32[1024,512]{1,0:T(8,128)S(1)}, f32[1024,512]{1,0:T(8,128)}, u32[]{:S(2)}) %copy-start.3) | copy-done | bytes 2097176
  22.2 5.4 %own_corr.1 = (f32[640,512]{1,0:T(8,128)S(1)}, f32[128,512]{1,0:T(8,128)S(1)}, f32[256,512]{1,0:T(8,128)S(1)}, f32[8,512]{1,0:T(8,128)S(1)}, f32[4,64,512]{2,1,0:T(8,128)S(1)}, /*index=5*/f32[4,64,512]{2,1,0:T(8,128)S(1)}) custom-call(s32[2]{0:T(128)S(1)} %pad_add_fusion.at_ref, f32[1024,512]{1,0:T(8,128)S(1)} %copy-done.1, f32[1024,512]{1,0:T(8,128)S(1)} %copy-done.3, ...), custom_call_target="tpu_custom_call" | custom-call | flops 1 | bytes 1 | tf_op jit(solution)/shard_map/own_corr/pallas_call | solution.py:159
  27.6 1.7 %collective-permute-start.4 = (f32[4,64,512]{2,1,0:T(8,128)S(1)}, f32[4,64,512]{2,1,0:T(8,128)S(1)}, u32[]{:S(2)}, u32[]{:S(2)}) collective-permute-start(f32[4,64,512]{2,1,0:T(8,128)S(1)} %get-tuple-element.37), channel_id=1, source_target_pairs={{0,1},{1,0},{2,3},{3,2},{4,5},{5,4},{6,7},{7,6},{8,9},{9,8},{10,11... | collective-permute-start | bytes 1572872 | tf_op jit(solution)/shard_map/ppermute | solution.py:38
  29.3 1.5 %collective-permute-done.4.refs_0_ = f32[4,64,512]{2,1,0:T(8,128)S(1)} collective-permute-done((f32[4,64,512]{2,1,0:T(8,128)S(1)}, f32[4,64,512]{2,1,0:T(8,128)S(1)}, u32[]{:S(2)}, u32[]{:S(2)}) %collective-permute-start.4) | collective-permute-done | bytes 524320 | tf_op jit(solution)/shard_map/ppermute | solution.py:38
  31.0 3.5 %collective-permute-start.6 = (f32[64,512]{1,0:T(8,128)S(1)}, f32[64,512]{1,0:T(8,128)S(1)}, u32[]{:S(2)}, u32[]{:S(2)}) collective-permute-start(f32[64,512]{1,0:T(8,128)S(1)} %get-tuple-element.40), channel_id=1, source_target_pairs={{0,4},{1,5},{2,6},{3,7},{4,0},{5,1},{6,2},{7,3},{8,12},{9,13},{10,... | collective-permute-start | bytes 393224 | tf_op jit(solution)/shard_map/ppermute | solution.py:47
  34.6 2.5 %collective-permute-done.5.refs_1_ = f32[64,512]{1,0:T(8,128)S(1)} collective-permute-done((f32[64,512]{1,0:T(8,128)S(1)}, f32[64,512]{1,0:T(8,128)S(1)}, u32[]{:S(2)}, u32[]{:S(2)}) %collective-permute-start.5) | collective-permute-done | bytes 131104 | tf_op jit(solution)/shard_map/ppermute | solution.py:47
  37.0 3.7 %collective-permute-done.6.refs_2_ = f32[64,512]{1,0:T(8,128)S(1)} collective-permute-done((f32[64,512]{1,0:T(8,128)S(1)}, f32[64,512]{1,0:T(8,128)S(1)}, u32[]{:S(2)}, u32[]{:S(2)}) %collective-permute-start.6) | collective-permute-done | bytes 131104 | tf_op jit(solution)/shard_map/ppermute | solution.py:47
  40.9 3.6 %collective-permute-start.16 = (f32[648,512]{1,0:T(8,128)S(1)}, f32[648,512]{1,0:T(8,128)S(1)}, u32[]{:S(2)}, u32[]{:S(2)}) collective-permute-start(f32[648,512]{1,0:T(8,128)S(1)} %get-tuple-element.52), channel_id=1, source_target_pairs={{0,240},{16,0},{32,16},{48,32},{64,48},{80,64},{96,80},{112,96},{1... | collective-permute-start | bytes 3981320 | tf_op jit(solution)/shard_map/ppermute | solution.py:34
  44.5 9.3 %collective-permute-done.8.prev_ref = f32[1024,512]{1,0:T(8,128)} collective-permute-done((f32[1024,512]{1,0:T(8,128)}, f32[1024,512]{1,0:T(8,128)}, u32[]{:S(2)}, u32[]{:S(2)}) %collective-permute-start.8) | collective-permute-done | bytes 2097184 | tf_op jit(solution)/shard_map/ppermute | solution.py:34
  53.8 5.9 %side_corr.1 = (f32[4,128,512]{2,1,0:T(8,128)S(1)}, f32[2,128,512]{2,1,0:T(8,128)S(1)}, f32[2,128,512]{2,1,0:T(8,128)S(1)}) custom-call(s32[2]{0:T(128)S(1)} %pad_add_fusion.at_ref, f32[1024,512]{1,0:T(8,128)S(1)} %copy-done.1, f32[1024,512]{1,0:T(8,128)} %collective-permute-done.8.prev_ref, f32[1024,512]{1,0:T(8,128)} %collective-permute-done.9.next_ref, ...), custom_call_target="tpu_custom_call" | custom-call | flops 1 | bytes 1 | tf_op jit(solution)/shard_map/side_corr/pallas_call | solution.py:200
  59.7 2.1 %collective-permute-start.10 = (f32[2,128,512]{2,1,0:T(8,128)S(1)}, f32[2,128,512]{2,1,0:T(8,128)S(1)}, u32[]{:S(2)}, u32[]{:S(2)}) collective-permute-start(f32[2,128,512]{2,1,0:T(8,128)S(1)} %get-tuple-element.46), channel_id=1, source_target_pairs={{0,1},{1,0},{2,3},{3,2},{4,5},{5,4},{6,7},{7,6},{8,9},{9,8},{10,11... | collective-permute-start | bytes 1572872 | tf_op jit(solution)/shard_map/ppermute | solution.py:38
  61.9 1.4 collective-permute-done.10.refs_0_
  64.2 1.5 collective-permute-start.12
  65.7 2.5 %collective-permute-start.13 = (f32[128,512]{1,0:T(8,128)S(1)}, f32[128,512]{1,0:T(8,128)S(1)}, u32[]{:S(2)}, u32[]{:S(2)}) collective-permute-start(f32[128,512]{1,0:T(8,128)S(1)} %get-tuple-element.50), channel_id=1, source_target_pairs={{0,4},{1,5},{2,6},{3,7},{4,0},{5,1},{6,2},{7,3},{8,12},{9,13},{10,... | collective-permute-start | bytes 786440 | tf_op jit(solution)/shard_map/ppermute | solution.py:47
  68.1 1.2 collective-permute-start.14
  69.3 12.8 %collective-permute-done.15.refs_5_.refs_3_.refs_6_ = f32[648,512]{1,0:T(8,128)S(1)} collective-permute-done((f32[648,512]{1,0:T(8,128)S(1)}, f32[648,512]{1,0:T(8,128)S(1)}, u32[]{:S(2)}, u32[]{:S(2)}) %collective-permute-start.15) | collective-permute-done | bytes 1327136 | tf_op jit(solution)/shard_map/ppermute | solution.py:34
  82.2 2.7 %collective-permute-start.17 = (f32[216,512]{1,0:T(8,128)S(1)}, f32[216,512]{1,0:T(8,128)S(1)}, u32[]{:S(2)}, u32[]{:S(2)}) collective-permute-start(f32[216,512]{1,0:T(8,128)S(1)} %message.1.mine_ref), channel_id=1, source_target_pairs={{0,8},{1,9},{2,10},{3,11},{4,12},{5,13},{6,14},{7,15},{8,0},{9,1},... | collective-permute-start | bytes 1327112 | tf_op jit(solution)/shard_map/ppermute | solution.py:42
  84.9 9.3 %collective-permute-done.17.got_ref = f32[216,512]{1,0:T(8,128)S(1)} collective-permute-done((f32[216,512]{1,0:T(8,128)S(1)}, f32[216,512]{1,0:T(8,128)S(1)}, u32[]{:S(2)}, u32[]{:S(2)}) %collective-permute-start.17) | collective-permute-done | bytes 442400 | tf_op jit(solution)/shard_map/ppermute | solution.py:42
  94.3 1.0 merge.1
  95.3 3.6 %collective-permute-start.22 = (f32[64,512]{1,0:T(8,128)S(1)}, f32[64,512]{1,0:T(8,128)S(1)}, u32[]{:S(2)}, u32[]{:S(2)}) collective-permute-start(f32[64,512]{1,0:T(8,128)S(1)} %get-tuple-element.58), channel_id=1, source_target_pairs={{0,240},{16,0},{32,16},{48,32},{64,48},{80,64},{96,80},{112,96},{1... | collective-permute-start | bytes 393224 | tf_op jit(solution)/shard_map/ppermute | solution.py:34
  98.9 1.2 collective-permute-start.18
  100.1 2.5 %collective-permute-start.19 = (f32[192,512]{1,0:T(8,128)S(1)}, f32[192,512]{1,0:T(8,128)S(1)}, u32[]{:S(2)}, u32[]{:S(2)}) collective-permute-start(f32[192,512]{1,0:T(8,128)S(1)} %get-tuple-element.53.refs_0_), channel_id=1, source_target_pairs={{0,4},{1,5},{2,6},{3,7},{4,0},{5,1},{6,2},{7,3},{8,12},{9,13},{10,... | collective-permute-start | bytes 1179656 | tf_op jit(solution)/shard_map/ppermute | solution.py:47
  102.6 1.2 collective-permute-start.20
  103.8 3.6 %collective-permute-start.24 = (f32[128,512]{1,0:T(8,128)S(1)}, f32[128,512]{1,0:T(8,128)S(1)}, u32[]{:S(2)}, u32[]{:S(2)}) collective-permute-start(f32[128,512]{1,0:T(8,128)S(1)} %get-tuple-element.63), channel_id=1, source_target_pairs={{0,240},{16,0},{32,16},{48,32},{64,48},{80,64},{96,80},{112,96},{1... | collective-permute-start | bytes 786440 | tf_op jit(solution)/shard_map/ppermute | solution.py:34
  107.4 3.8 %presplit.1 = (bf16[1024,3072]{1,0:T(8,128)(2,1)S(1)}, bf16[1024,1024]{1,0:T(8,128)(2,1)S(1)}) custom-call(f32[1024,512]{1,0:T(8,128)S(1)} %copy-done.4, f32[1024,512]{1,0:T(8,128)} %collective-permute-done.8.prev_ref, f32[1024,512]{1,0:T(8,128)} %collective-permute-done.9.next_ref, f32[1024,512]{1,0:T(8,128)S(1)} %copy-done.1, ...), custom_call_target="tpu_custom_call" | custom-call | flops 1 | bytes 1 | tf_op jit(solution)/shard_map/presplit/pallas_call | solution.py:441
  111.2 6.2 %collective-permute-done.19.refs_2_ = f32[192,512]{1,0:T(8,128)S(1)} collective-permute-done((f32[192,512]{1,0:T(8,128)S(1)}, f32[192,512]{1,0:T(8,128)S(1)}, u32[]{:S(2)}, u32[]{:S(2)}) %collective-permute-start.19) | collective-permute-done | bytes 393248 | tf_op jit(solution)/shard_map/ppermute | solution.py:47
  117.4 1.4 collective-permute-done.20.refs_3_
  118.9 2.3 %collective-permute-start.25 = (f32[4,192,512]{2,1,0:T(8,128)S(1)}, f32[4,192,512]{2,1,0:T(8,128)S(1)}, u32[]{:S(2)}, u32[]{:S(2)}) collective-permute-start(f32[4,192,512]{2,1,0:T(8,128)S(1)} %pack.2.mine_ref), channel_id=1, source_target_pairs={{0,1},{1,0},{2,3},{3,2},{4,5},{5,4},{6,7},{7,6},{8,9},{9,8},{10,11... | collective-permute-start | bytes 4718600 | tf_op jit(solution)/shard_map/ppermute | solution.py:38
  121.3 3.6 %collective-permute-start.30 = (f32[256,512]{1,0:T(8,128)S(1)}, f32[256,512]{1,0:T(8,128)S(1)}, u32[]{:S(2)}, u32[]{:S(2)}) collective-permute-start(f32[256,512]{1,0:T(8,128)S(1)} %get-tuple-element.67), channel_id=1, source_target_pairs={{0,240},{16,0},{32,16},{48,32},{64,48},{80,64},{96,80},{112,96},{1... | collective-permute-start | bytes 1572872 | tf_op jit(solution)/shard_map/ppermute | solution.py:34
  124.8 1.1 collective-permute-start.26
  125.9 2.1 %collective-permute-start.27 = (f32[128,512]{1,0:T(8,128)S(1)}, f32[128,512]{1,0:T(8,128)S(1)}, u32[]{:S(2)}, u32[]{:S(2)}) collective-permute-start(f32[128,512]{1,0:T(8,128)S(1)} %get-tuple-element.61.refs_0_), channel_id=1, source_target_pairs={{0,4},{1,5},{2,6},{3,7},{4,0},{5,1},{6,2},{7,3},{8,12},{9,13},{10,... | collective-permute-start | bytes 786440 | tf_op jit(solution)/shard_map/ppermute | solution.py:47
  128.0 1.3 collective-permute-start.28
  129.3 8.5 %finish_a.1 = (f32[1024,512]{1,0:T(8,128)}, f32[8,512]{1,0:T(8,128)S(1)}) custom-call(s32[2]{0:T(128)S(1)} %pad_add_fusion.at_ref, f32[4,192,512]{2,1,0:T(8,128)S(1)} %pack.2.mine_ref, f32[4,192,512]{2,1,0:T(8,128)S(1)} %collective-permute-done.25.other_ref, f32[8,512]{1,0:T(8,128)S(1)} %get-tuple-element.54.f_ref.refs_0_.facts_ref, ...), custom_call_target="tpu_custom_call" | custom-call | flops 1 | bytes 1 | tf_op jit(solution)/shard_map/finish_a/pallas_call | solution.py:491
  137.8 1.6 %collective-permute-done.27.refs_2_ = f32[128,512]{1,0:T(8,128)S(1)} collective-permute-done((f32[128,512]{1,0:T(8,128)S(1)}, f32[128,512]{1,0:T(8,128)S(1)}, u32[]{:S(2)}, u32[]{:S(2)}) %collective-permute-start.27) | collective-permute-done | bytes 262176 | tf_op jit(solution)/shard_map/ppermute | solution.py:47
  139.5 1.6 %collective-permute-start.31 = (f32[4,128,512]{2,1,0:T(8,128)S(1)}, f32[4,128,512]{2,1,0:T(8,128)S(1)}, u32[]{:S(2)}, u32[]{:S(2)}) collective-permute-start(f32[4,128,512]{2,1,0:T(8,128)S(1)} %pack.3.refs_0_.mine_ref), channel_id=1, source_target_pairs={{0,1},{1,0},{2,3},{3,2},{4,5},{5,4},{6,7},{7,6},{8,9},{9,8},{10,11... | collective-permute-start | bytes 3145736 | tf_op jit(solution)/shard_map/ppermute | solution.py:38
  141.2 3.5 %own_b.1 = (f32[1024,512]{1,0:T(8,128)S(1)}, f32[8,512]{1,0:T(8,128)S(1)}) custom-call(s32[2]{0:T(128)S(1)} %pad_add_fusion.at_ref, f32[4,192,512]{2,1,0:T(8,128)S(1)} %pack.2.mine_ref, f32[4,192,512]{2,1,0:T(8,128)S(1)} %collective-permute-done.25.other_ref, f32[8,512]{1,0:T(8,128)S(1)} %get-tuple-element.54.f_ref.refs_0_.facts_ref, ...), custom_call_target="tpu_custom_call" | custom-call | flops 1 | bytes 1 | tf_op jit(solution)/shard_map/own_b/pallas_call | solution.py:524
  144.7 6.8 %finish_b.1 = f32[1024,512]{1,0:T(8,128)} custom-call(s32[2]{0:T(128)S(1)} %pad_add_fusion.at_ref, f32[4,128,512]{2,1,0:T(8,128)S(1)} %pack.3.refs_0_.mine_ref, f32[4,128,512]{2,1,0:T(8,128)S(1)} %collective-permute-done.31.other_ref, f32[8,512]{1,0:T(8,128)S(1)} %get-tuple-element.54.f_ref.refs_0_.facts_ref, f32[8,512]{1,0:T(8,128)S(1)} %get-tuple-element.55.pf_ref.refs_1_, ...), custom_call_target="tpu_custom_call" | custom-call | flops 1 | bytes 1 | tf_op jit(solution)/shard_map/finish_b/pallas_call | solution.py:579
  (43 shorter events, 2.6 us)
Async XLA Ops:
  0.6 53.2 %collective-permute-start.8 = (f32[1024,512]{1,0:T(8,128)}, f32[1024,512]{1,0:T(8,128)}, u32[]{:S(2)}, u32[]{:S(2)}) collective-permute-start(f32[1024,512]{1,0:T(8,128)} %refs_2_.1), channel_id=1, source_target_pairs={{0,16},{16,32},{32,48},{48,64},{64,80},{80,96},{96,112},{112,128},... | collective-permute-start | bytes 6291464 | tf_op jit(solution)/shard_map/ppermute | solution.py:34
  3.2 50.6 %collective-permute-start.9 = (f32[1024,512]{1,0:T(8,128)}, f32[1024,512]{1,0:T(8,128)}, u32[]{:S(2)}, u32[]{:S(2)}) collective-permute-start(f32[1024,512]{1,0:T(8,128)} %refs_2_.1), channel_id=1, source_target_pairs={{0,240},{16,0},{32,16},{48,32},{64,48},{80,64},{96,80},{112,96},{1... | collective-permute-start | bytes 6291464 | tf_op jit(solution)/shard_map/ppermute | solution.py:34
  8.2 1.6 %copy-start = (f32[1024,512]{1,0:T(8,128)S(1)}, f32[1024,512]{1,0:T(8,128)}, u32[]{:S(2)}) copy-start(f32[1024,512]{1,0:T(8,128)} %refs_3_.1) | copy-start | bytes 6291460
  9.8 1.6 %copy-start.2 = (f32[1024,512]{1,0:T(8,128)S(1)}, f32[1024,512]{1,0:T(8,128)}, u32[]{:S(2)}) copy-start(f32[1024,512]{1,0:T(8,128)} %refs_2_.1) | copy-start | bytes 6291460
  11.4 9.2 %copy-start.1 = (f32[1024,512]{1,0:T(8,128)S(1)}, f32[1024,512]{1,0:T(8,128)}, u32[]{:S(2)}) copy-start(f32[1024,512]{1,0:T(8,128)} %refs_3_.1) | copy-start | bytes 6291460
  12.0 1.9 %collective-permute-start = (f32[8,512]{1,0:T(8,128)S(1)}, f32[8,512]{1,0:T(8,128)S(1)}, u32[]{:S(2)}, u32[]{:S(2)}) collective-permute-start(f32[8,512]{1,0:T(8,128)S(1)} %sums.1), channel_id=1, source_target_pairs={{0,1},{1,0},{2,3},{3,2},{4,5},{5,4},{6,7},{7,6},{8,9},{9,8},{10,11... | collective-permute-start | bytes 49160 | tf_op jit(solution)/shard_map/ppermute | solution.py:38
  13.9 4.9 %collective-permute-start.1 = (f32[8,512]{1,0:T(8,128)S(1)}, f32[8,512]{1,0:T(8,128)S(1)}, u32[]{:S(2)}, u32[]{:S(2)}) collective-permute-start(f32[8,512]{1,0:T(8,128)S(1)} %add.3.refs_0_), channel_id=1, source_target_pairs={{0,2},{1,3},{2,4},{3,5},{4,6},{5,7},{6,0},{7,1},{8,10},{9,11},{10,... | collective-permute-start | bytes 49160 | tf_op jit(solution)/shard_map/ppermute | solution.py:47
  15.1 4.5 %collective-permute-start.2 = (f32[8,512]{1,0:T(8,128)S(1)}, f32[8,512]{1,0:T(8,128)S(1)}, u32[]{:S(2)}, u32[]{:S(2)}) collective-permute-start(f32[8,512]{1,0:T(8,128)S(1)} %add.3.refs_0_), channel_id=1, source_target_pairs={{0,4},{1,5},{2,6},{3,7},{4,0},{5,1},{6,2},{7,3},{8,12},{9,13},{10,... | collective-permute-start | bytes 49160 | tf_op jit(solution)/shard_map/ppermute | solution.py:47
  17.6 3.0 %collective-permute-start.3 = (f32[8,512]{1,0:T(8,128)S(1)}, f32[8,512]{1,0:T(8,128)S(1)}, u32[]{:S(2)}, u32[]{:S(2)}) collective-permute-start(f32[8,512]{1,0:T(8,128)S(1)} %add.3.refs_0_), channel_id=1, source_target_pairs={{0,6},{1,7},{2,0},{3,1},{4,2},{5,3},{6,4},{7,5},{8,14},{9,15},{10,... | collective-permute-start | bytes 49160 | tf_op jit(solution)/shard_map/ppermute | solution.py:47
  20.6 1.6 %copy-start.3 = (f32[1024,512]{1,0:T(8,128)S(1)}, f32[1024,512]{1,0:T(8,128)}, u32[]{:S(2)}) copy-start(f32[1024,512]{1,0:T(8,128)} %refs_2_.1) | copy-start | bytes 6291460
  27.6 3.3 %collective-permute-start.4 = (f32[4,64,512]{2,1,0:T(8,128)S(1)}, f32[4,64,512]{2,1,0:T(8,128)S(1)}, u32[]{:S(2)}, u32[]{:S(2)}) collective-permute-start(f32[4,64,512]{2,1,0:T(8,128)S(1)} %get-tuple-element.37), channel_id=1, source_target_pairs={{0,1},{1,0},{2,3},{3,2},{4,5},{5,4},{6,7},{7,6},{8,9},{9,8},{10,11... | collective-permute-start | bytes 1572872 | tf_op jit(solution)/shard_map/ppermute | solution.py:38
  30.9 6.1 %collective-permute-start.5 = (f32[64,512]{1,0:T(8,128)S(1)}, f32[64,512]{1,0:T(8,128)S(1)}, u32[]{:S(2)}, u32[]{:S(2)}) collective-permute-start(f32[64,512]{1,0:T(8,128)S(1)} %get-tuple-element.39), channel_id=1, source_target_pairs={{0,2},{1,3},{2,4},{3,5},{4,6},{5,7},{6,0},{7,1},{8,10},{9,11},{10,... | collective-permute-start | bytes 393224 | tf_op jit(solution)/shard_map/ppermute | solution.py:47
  31.0 9.7 %collective-permute-start.6 = (f32[64,512]{1,0:T(8,128)S(1)}, f32[64,512]{1,0:T(8,128)S(1)}, u32[]{:S(2)}, u32[]{:S(2)}) collective-permute-start(f32[64,512]{1,0:T(8,128)S(1)} %get-tuple-element.40), channel_id=1, source_target_pairs={{0,4},{1,5},{2,6},{3,7},{4,0},{5,1},{6,2},{7,3},{8,12},{9,13},{10,... | collective-permute-start | bytes 393224 | tf_op jit(solution)/shard_map/ppermute | solution.py:47
  34.6 6.2 %collective-permute-start.7 = (f32[64,512]{1,0:T(8,128)S(1)}, f32[64,512]{1,0:T(8,128)S(1)}, u32[]{:S(2)}, u32[]{:S(2)}) collective-permute-start(f32[64,512]{1,0:T(8,128)S(1)} %get-tuple-element.41), channel_id=1, source_target_pairs={{0,6},{1,7},{2,0},{3,1},{4,2},{5,3},{6,4},{7,5},{8,14},{9,15},{10,... | collective-permute-start | bytes 393224 | tf_op jit(solution)/shard_map/ppermute | solution.py:47
  40.8 41.3 %collective-permute-start.15 = (f32[648,512]{1,0:T(8,128)S(1)}, f32[648,512]{1,0:T(8,128)S(1)}, u32[]{:S(2)}, u32[]{:S(2)}) collective-permute-start(f32[648,512]{1,0:T(8,128)S(1)} %get-tuple-element.52), channel_id=1, source_target_pairs={{0,16},{16,32},{32,48},{48,64},{64,80},{80,96},{96,112},{112,128},... | collective-permute-start | bytes 3981320 | tf_op jit(solution)/shard_map/ppermute | solution.py:34
  40.9 41.2 %collective-permute-start.16 = (f32[648,512]{1,0:T(8,128)S(1)}, f32[648,512]{1,0:T(8,128)S(1)}, u32[]{:S(2)}, u32[]{:S(2)}) collective-permute-start(f32[648,512]{1,0:T(8,128)S(1)} %get-tuple-element.52), channel_id=1, source_target_pairs={{0,240},{16,0},{32,16},{48,32},{64,48},{80,64},{96,80},{112,96},{1... | collective-permute-start | bytes 3981320 | tf_op jit(solution)/shard_map/ppermute | solution.py:34
  59.7 3.7 %collective-permute-start.10 = (f32[2,128,512]{2,1,0:T(8,128)S(1)}, f32[2,128,512]{2,1,0:T(8,128)S(1)}, u32[]{:S(2)}, u32[]{:S(2)}) collective-permute-start(f32[2,128,512]{2,1,0:T(8,128)S(1)} %get-tuple-element.46), channel_id=1, source_target_pairs={{0,1},{1,0},{2,3},{3,2},{4,5},{5,4},{6,7},{7,6},{8,9},{9,8},{10,11... | collective-permute-start | bytes 1572872 | tf_op jit(solution)/shard_map/ppermute | solution.py:38
  61.8 2.3 %collective-permute-start.11 = (f32[2,128,512]{2,1,0:T(8,128)S(1)}, f32[2,128,512]{2,1,0:T(8,128)S(1)}, u32[]{:S(2)}, u32[]{:S(2)}) collective-permute-start(f32[2,128,512]{2,1,0:T(8,128)S(1)} %get-tuple-element.47), channel_id=1, source_target_pairs={{0,1},{1,0},{2,3},{3,2},{4,5},{5,4},{6,7},{7,6},{8,9},{9,8},{10,11... | collective-permute-start | bytes 1572872 | tf_op jit(solution)/shard_map/ppermute | solution.py:38
  64.2 17.9 %collective-permute-start.12 = (f32[128,512]{1,0:T(8,128)S(1)}, f32[128,512]{1,0:T(8,128)S(1)}, u32[]{:S(2)}, u32[]{:S(2)}) collective-permute-start(f32[128,512]{1,0:T(8,128)S(1)} %get-tuple-element.49), channel_id=1, source_target_pairs={{0,2},{1,3},{2,4},{3,5},{4,6},{5,7},{6,0},{7,1},{8,10},{9,11},{10,... | collective-permute-start | bytes 786440 | tf_op jit(solution)/shard_map/ppermute | solution.py:47
  65.7 16.4 %collective-permute-start.13 = (f32[128,512]{1,0:T(8,128)S(1)}, f32[128,512]{1,0:T(8,128)S(1)}, u32[]{:S(2)}, u32[]{:S(2)}) collective-permute-start(f32[128,512]{1,0:T(8,128)S(1)} %get-tuple-element.50), channel_id=1, source_target_pairs={{0,4},{1,5},{2,6},{3,7},{4,0},{5,1},{6,2},{7,3},{8,12},{9,13},{10,... | collective-permute-start | bytes 786440 | tf_op jit(solution)/shard_map/ppermute | solution.py:47
  68.1 14.0 %collective-permute-start.14 = (f32[128,512]{1,0:T(8,128)S(1)}, f32[128,512]{1,0:T(8,128)S(1)}, u32[]{:S(2)}, u32[]{:S(2)}) collective-permute-start(f32[128,512]{1,0:T(8,128)S(1)} %get-tuple-element.51), channel_id=1, source_target_pairs={{0,6},{1,7},{2,0},{3,1},{4,2},{5,3},{6,4},{7,5},{8,14},{9,15},{10,... | collective-permute-start | bytes 786440 | tf_op jit(solution)/shard_map/ppermute | solution.py:47
  82.2 25.2 %copy-start.4 = (f32[1024,512]{1,0:T(8,128)S(1)}, f32[1024,512]{1,0:T(8,128)}, u32[]{:S(2)}) copy-start(f32[1024,512]{1,0:T(8,128)} %refs_2_.1) | copy-start | bytes 6291460
  82.2 12.0 %collective-permute-start.17 = (f32[216,512]{1,0:T(8,128)S(1)}, f32[216,512]{1,0:T(8,128)S(1)}, u32[]{:S(2)}, u32[]{:S(2)}) collective-permute-start(f32[216,512]{1,0:T(8,128)S(1)} %message.1.mine_ref), channel_id=1, source_target_pairs={{0,8},{1,9},{2,10},{3,11},{4,12},{5,13},{6,14},{7,15},{8,0},{9,1},... | collective-permute-start | bytes 1327112 | tf_op jit(solution)/shard_map/ppermute | solution.py:42
  95.2 8.5 %collective-permute-start.21 = (f32[64,512]{1,0:T(8,128)S(1)}, f32[64,512]{1,0:T(8,128)S(1)}, u32[]{:S(2)}, u32[]{:S(2)}) collective-permute-start(f32[64,512]{1,0:T(8,128)S(1)} %get-tuple-element.57), channel_id=1, source_target_pairs={{0,16},{16,32},{32,48},{48,64},{64,80},{80,96},{96,112},{112,128},... | collective-permute-start | bytes 393224 | tf_op jit(solution)/shard_map/ppermute | solution.py:34
  95.3 8.4 %collective-permute-start.22 = (f32[64,512]{1,0:T(8,128)S(1)}, f32[64,512]{1,0:T(8,128)S(1)}, u32[]{:S(2)}, u32[]{:S(2)}) collective-permute-start(f32[64,512]{1,0:T(8,128)S(1)} %get-tuple-element.58), channel_id=1, source_target_pairs={{0,240},{16,0},{32,16},{48,32},{64,48},{80,64},{96,80},{112,96},{1... | collective-permute-start | bytes 393224 | tf_op jit(solution)/shard_map/ppermute | solution.py:34
  98.9 12.3 %collective-permute-start.18 = (f32[192,512]{1,0:T(8,128)S(1)}, f32[192,512]{1,0:T(8,128)S(1)}, u32[]{:S(2)}, u32[]{:S(2)}) collective-permute-start(f32[192,512]{1,0:T(8,128)S(1)} %get-tuple-element.53.refs_0_), channel_id=1, source_target_pairs={{0,2},{1,3},{2,4},{3,5},{4,6},{5,7},{6,0},{7,1},{8,10},{9,11},{10,... | collective-permute-start | bytes 1179656 | tf_op jit(solution)/shard_map/ppermute | solution.py:47
  100.1 17.3 %collective-permute-start.19 = (f32[192,512]{1,0:T(8,128)S(1)}, f32[192,512]{1,0:T(8,128)S(1)}, u32[]{:S(2)}, u32[]{:S(2)}) collective-permute-start(f32[192,512]{1,0:T(8,128)S(1)} %get-tuple-element.53.refs_0_), channel_id=1, source_target_pairs={{0,4},{1,5},{2,6},{3,7},{4,0},{5,1},{6,2},{7,3},{8,12},{9,13},{10,... | collective-permute-start | bytes 1179656 | tf_op jit(solution)/shard_map/ppermute | solution.py:47
  102.6 16.3 %collective-permute-start.20 = (f32[192,512]{1,0:T(8,128)S(1)}, f32[192,512]{1,0:T(8,128)S(1)}, u32[]{:S(2)}, u32[]{:S(2)}) collective-permute-start(f32[192,512]{1,0:T(8,128)S(1)} %get-tuple-element.53.refs_0_), channel_id=1, source_target_pairs={{0,6},{1,7},{2,0},{3,1},{4,2},{5,3},{6,4},{7,5},{8,14},{9,15},{10,... | collective-permute-start | bytes 1179656 | tf_op jit(solution)/shard_map/ppermute | solution.py:47
  103.7 7.4 %collective-permute-start.23 = (f32[128,512]{1,0:T(8,128)S(1)}, f32[128,512]{1,0:T(8,128)S(1)}, u32[]{:S(2)}, u32[]{:S(2)}) collective-permute-start(f32[128,512]{1,0:T(8,128)S(1)} %get-tuple-element.63), channel_id=1, source_target_pairs={{0,16},{16,32},{32,48},{48,64},{64,80},{80,96},{96,112},{112,128},... | collective-permute-start | bytes 786440 | tf_op jit(solution)/shard_map/ppermute | solution.py:34
  103.8 7.3 %collective-permute-start.24 = (f32[128,512]{1,0:T(8,128)S(1)}, f32[128,512]{1,0:T(8,128)S(1)}, u32[]{:S(2)}, u32[]{:S(2)}) collective-permute-start(f32[128,512]{1,0:T(8,128)S(1)} %get-tuple-element.63), channel_id=1, source_target_pairs={{0,240},{16,0},{32,16},{48,32},{64,48},{80,64},{96,80},{112,96},{1... | collective-permute-start | bytes 786440 | tf_op jit(solution)/shard_map/ppermute | solution.py:34
  118.9 9.1 %collective-permute-start.25 = (f32[4,192,512]{2,1,0:T(8,128)S(1)}, f32[4,192,512]{2,1,0:T(8,128)S(1)}, u32[]{:S(2)}, u32[]{:S(2)}) collective-permute-start(f32[4,192,512]{2,1,0:T(8,128)S(1)} %pack.2.mine_ref), channel_id=1, source_target_pairs={{0,1},{1,0},{2,3},{3,2},{4,5},{5,4},{6,7},{7,6},{8,9},{9,8},{10,11... | collective-permute-start | bytes 4718600 | tf_op jit(solution)/shard_map/ppermute | solution.py:38
  121.2 18.2 %collective-permute-start.29 = (f32[256,512]{1,0:T(8,128)S(1)}, f32[256,512]{1,0:T(8,128)S(1)}, u32[]{:S(2)}, u32[]{:S(2)}) collective-permute-start(f32[256,512]{1,0:T(8,128)S(1)} %get-tuple-element.67), channel_id=1, source_target_pairs={{0,16},{16,32},{32,48},{48,64},{64,80},{80,96},{96,112},{112,128},... | collective-permute-start | bytes 1572872 | tf_op jit(solution)/shard_map/ppermute | solution.py:34
  121.3 18.2 %collective-permute-start.30 = (f32[256,512]{1,0:T(8,128)S(1)}, f32[256,512]{1,0:T(8,128)S(1)}, u32[]{:S(2)}, u32[]{:S(2)}) collective-permute-start(f32[256,512]{1,0:T(8,128)S(1)} %get-tuple-element.67), channel_id=1, source_target_pairs={{0,240},{16,0},{32,16},{48,32},{64,48},{80,64},{96,80},{112,96},{1... | collective-permute-start | bytes 1572872 | tf_op jit(solution)/shard_map/ppermute | solution.py:34
  124.8 13.0 %collective-permute-start.26 = (f32[128,512]{1,0:T(8,128)S(1)}, f32[128,512]{1,0:T(8,128)S(1)}, u32[]{:S(2)}, u32[]{:S(2)}) collective-permute-start(f32[128,512]{1,0:T(8,128)S(1)} %get-tuple-element.61.refs_0_), channel_id=1, source_target_pairs={{0,2},{1,3},{2,4},{3,5},{4,6},{5,7},{6,0},{7,1},{8,10},{9,11},{10,... | collective-permute-start | bytes 786440 | tf_op jit(solution)/shard_map/ppermute | solution.py:47
  125.9 13.5 %collective-permute-start.27 = (f32[128,512]{1,0:T(8,128)S(1)}, f32[128,512]{1,0:T(8,128)S(1)}, u32[]{:S(2)}, u32[]{:S(2)}) collective-permute-start(f32[128,512]{1,0:T(8,128)S(1)} %get-tuple-element.61.refs_0_), channel_id=1, source_target_pairs={{0,4},{1,5},{2,6},{3,7},{4,0},{5,1},{6,2},{7,3},{8,12},{9,13},{10,... | collective-permute-start | bytes 786440 | tf_op jit(solution)/shard_map/ppermute | solution.py:47
  128.0 11.4 %collective-permute-start.28 = (f32[128,512]{1,0:T(8,128)S(1)}, f32[128,512]{1,0:T(8,128)S(1)}, u32[]{:S(2)}, u32[]{:S(2)}) collective-permute-start(f32[128,512]{1,0:T(8,128)S(1)} %get-tuple-element.61.refs_0_), channel_id=1, source_target_pairs={{0,6},{1,7},{2,0},{3,1},{4,2},{5,3},{6,4},{7,5},{8,14},{9,15},{10,... | collective-permute-start | bytes 786440 | tf_op jit(solution)/shard_map/ppermute | solution.py:47
  139.5 5.1 %collective-permute-start.31 = (f32[4,128,512]{2,1,0:T(8,128)S(1)}, f32[4,128,512]{2,1,0:T(8,128)S(1)}, u32[]{:S(2)}, u32[]{:S(2)}) collective-permute-start(f32[4,128,512]{2,1,0:T(8,128)S(1)} %pack.3.refs_0_.mine_ref), channel_id=1, source_target_pairs={{0,1},{1,0},{2,3},{3,2},{4,5},{5,4},{6,7},{7,6},{8,9},{9,8},{10,11... | collective-permute-start | bytes 3145736 | tf_op jit(solution)/shard_map/ppermute | solution.py:38

commit v8 on v7

--- a/solution.py
+++ b/solution.py
@@ -56,8 +56,7 @@
     return lax.dot_general(a, b, (((1,), (0,)), ((), ())), preferred_element_type=f32)
 
 
-def gram(a, b):
-    a_high, a_low = split(a.T)
+def gram(a_high, a_low, b):
     b_high, b_low = split(b)
     return mm(
         jnp.concatenate([a_high, a_high, a_low], axis=1),
@@ -94,19 +93,20 @@
     )(a, b)
 
 
-def put_slots(at_ref, acc, keep_ref, sends, first, rows):
+def put_slots(at_ref, acc, keep_ref, send_ref):
     core, x = at_ref[0], at_ref[1]
+    rows = keep_ref.shape[1]
     for slot in range(4):
         chunk = (x + slot) & 3
         mine = pl.multiple_of((core * 4 + chunk) * rows, rows)
         theirs = pl.multiple_of(((1 - core) * 4 + chunk) * rows, rows)
-        keep_ref[slot, first : first + rows, :] = acc[pl.ds(mine, rows), :]
-        each = 4 // len(sends)
-        sends[slot // each][slot % each, first : first + rows, :] = acc[pl.ds(theirs, rows), :]
+        keep_ref[slot] = acc[pl.ds(mine, rows), :]
+        send_ref[slot] = acc[pl.ds(theirs, rows), :]
 
 
 def own_corr_kernel(half_rows, steps, bounds, at_ref, a_ref, b_ref, *refs):
-    parts, halos, (facts_ref, keep_ref, send_ref, acc_ref) = refs[:4], refs[4:7], refs[7:]
+    parts, halos, refs = refs[:4], refs[4:7], refs[7:]
+    facts_ref, keep_ref, send_ref, high_ref, low_ref, acc_ref = refs
     step = pl.program_id(0)
 
     @pl.when(step == 0)
@@ -131,11 +131,13 @@
         def _(ref=ref):
             ref[...] = norm_a
 
-    acc_ref[...] += gram(norm_a, norm_b)
+    a_parts = split(norm_a.T)
+    high_ref[...], low_ref[...] = a_parts
+    acc_ref[...] += gram(*a_parts, norm_b)
 
     @pl.when(step == steps - 1)
     def _():
-        put_slots(at_ref, acc_ref, keep_ref, [send_ref], 0, keep_ref.shape[1])
+        put_slots(at_ref, acc_ref, keep_ref, send_ref)
 
 
 def halo_cuts(rows, tile):
@@ -160,70 +162,88 @@
         functools.partial(own_corr_kernel, half_rows, rows // tile, bounds),
         grid=(rows // tile,),
         in_specs=[smem_spec, spec, spec] + [whole] * 4,
-        out_specs=[pl.BlockSpec((tile, width), part) for part in maps] + [whole, slots, slots],
+        out_specs=[pl.BlockSpec((tile, width), part) for part in maps] + [whole, slots, slots]
+        + [pl.BlockSpec((width, tile), lambda i: (0, i))] * 2,
         out_shape=[shape(size, width) for size in sizes]
         + [shape(8, width)]
-        + [shape(4, width // 8, width)] * 2,
+        + [shape(4, width // 8, width)] * 2
+        + [jax.ShapeDtypeStruct((width, rows), bf16)] * 2,
         scratch_shapes=[pltpu.VMEM((width, width), f32)],
         mib=16,
         name="own_corr",
     )(at, a, b, *parts)
 
 
-def side_corr_kernel(steps, at_ref, a_ref, prev_ref, next_ref, f_ref, *refs):
-    keep_ref, *sends, left_ref, right_ref = refs[-5:]
+def side_corr_kernel(steps, at_ref, high_ref, low_ref, b_ref, *refs):
+    keep_ref, send_ref, acc_ref = refs[-3:]
     step = pl.program_id(0)
 
     @pl.when(step == 0)
     def _():
-        left_ref[...] = jnp.zeros_like(left_ref)
-        right_ref[...] = jnp.zeros_like(right_ref)
-
-    norm_a = (a_ref[...] - f_ref[0:1, :]) * f_ref[1:2, :]
-    for acc_ref, b_ref in ((left_ref, prev_ref), (right_ref, next_ref)):
-        acc_ref[...] += gram(norm_a, b_ref[...])
+        acc_ref[...] = gram(high_ref[...], low_ref[...], b_ref[...])
+
+    @pl.when(step > 0)
+    def _():
+        acc_ref[...] += gram(high_ref[...], low_ref[...], b_ref[...])
 
     @pl.when(step == steps - 1)
     def _():
-        rows = keep_ref.shape[1] // 2
-        put_slots(at_ref, left_ref, keep_ref, sends, 0, rows)
-        put_slots(at_ref, right_ref, keep_ref, sends, rows, rows)
-
-
-def side_corr(at, a, prev_b, next_b, facts, wait_for):
-    rows, width = a.shape
-    steps = 4
-    spec = pl.BlockSpec((rows // steps, width), lambda i: (i, 0))
-    whole = pl.BlockSpec((8, width), lambda i: (0, 0))
-    slots = pl.BlockSpec((4, width // 4, width), lambda i: (0, 0, 0))
-    pair = pl.BlockSpec((2, width // 4, width), lambda i: (0, 0, 0))
+        put_slots(at_ref, acc_ref, keep_ref, send_ref)
+
+
+def side_corr(at, a_high, a_low, b, wait_for):
+    rows, width = b.shape
+    tile = rows
+    steps = rows // tile
+    spec = pl.BlockSpec((tile, width), lambda i: (i, 0))
+    lanes = pl.BlockSpec((width, tile), lambda i: (0, i))
+    slots = pl.BlockSpec((4, width // 8, width), lambda i: (0, 0, 0))
     return call(
         functools.partial(side_corr_kernel, steps),
         grid=(steps,),
-        in_specs=[smem_spec, spec, spec, spec, whole] + [any_spec] * len(wait_for),
-        out_specs=[slots, pair, pair],
-        out_shape=[shape(4, width // 4, width)] + [shape(2, width // 4, width)] * 2,
-        scratch_shapes=[pltpu.VMEM((width, width), f32)] * 2,
+        in_specs=[smem_spec, lanes, lanes, spec] + [any_spec] * len(wait_for),
+        out_specs=[slots, slots],
+        out_shape=[shape(4, width // 8, width)] * 2,
+        scratch_shapes=[pltpu.VMEM((width, width), f32)],
         mib=24,
         name="side_corr",
-    )(at, a, prev_b, next_b, facts, *wait_for)
-
-
-def fan_kernel(keep_ref, *refs):
-    gots, outs = refs[:-4], refs[-4:]
-    each = 4 // len(gots)
+    )(at, a_high, a_low, b, *wait_for)
+
+
+def fan_kernel(count, *refs):
+    keeps, gots, outs = refs[:count], refs[count : 2 * count], refs[2 * count :]
+    for i in range(count):
+        for slot in range(4):
+            outs[4 * i + slot][...] = keeps[i][slot] + gots[i][slot]
+
+
+def fan(keeps, gots):
+    count = len(keeps)
+    return call(
+        functools.partial(fan_kernel, count),
+        in_specs=[vmem_spec] * (2 * count),
+        out_specs=[vmem_spec] * (4 * count),
+        out_shape=[shape(*keep.shape[1:]) for keep in keeps for _ in range(4)],
+        name="fan",
+    )(*keeps, *gots)
+
+
+def joined_fan_kernel(left_ref, right_ref, got_left_ref, got_right_ref, *outs):
+    rows = left_ref.shape[1]
     for slot in range(4):
-        outs[slot][...] = keep_ref[slot] + gots[slot // each][slot % each]
-
-
-def fan(keep, *gots):
-    return call(
-        fan_kernel,
-        in_specs=[vmem_spec] * (1 + len(gots)),
+        outs[slot][0:rows, :] = left_ref[slot] + got_left_ref[slot]
+        outs[slot][rows:, :] = right_ref[slot] + got_right_ref[slot]
+
+
+def joined_fan(keeps, gots):
+    rows, width = keeps[0].shape[1:]
+    return call(
+        joined_fan_kernel,
+        in_specs=[vmem_spec] * 4,
         out_specs=[vmem_spec] * 4,
-        out_shape=[shape(*keep.shape[1:])] * 4,
-        name="fan",
-    )(keep, *gots)
+        out_shape=[shape(2 * rows, width)] * 4,
+        name="joined_fan",
+    )(*keeps, *gots)
 
 
 def own_sum_kernel(*refs):
@@ -600,15 +620,18 @@
     sums = sums + to_core(sums)
     parts = [sums] + [to_x(sums, shift) for shift in (1, 2, 3)]
 
-    a_top, a_mid, a_low, half_facts, keep, send = own_corr(at, view_a, view_b, parts, half_rows)
-    slots = fan(keep, to_core(send))
+    a_top, a_mid, a_low, half_facts, keep, send, a_high_t, a_low_t = own_corr(
+        at, view_a, view_b, parts, half_rows
+    )
+    slots = fan([keep], [to_core(send)])
     own_parts = [slots[0]] + [to_x(slots[shift], shift) for shift in (1, 2, 3)]
     own, a_top = own_sum(own_parts, a_top, half_facts)
     prev_top = across(a_top, 1)
     next_top = across(a_top, -1)
 
-    keep, *sends = side_corr(at, view_a, prev_raw, next_raw, half_facts, [own])
-    slots = fan(keep, *[to_core(send) for send in sends])
+    left_keep, left_send = side_corr(at, a_high_t, a_low_t, prev_raw, [own])
+    right_keep, right_send = side_corr(at, a_high_t, a_low_t, next_raw, [own])
+    slots = joined_fan([left_keep, right_keep], [to_core(left_send), to_core(right_send)])
     side_parts = [slots[0]] + [to_x(slots[shift], shift) for shift in (1, 2, 3)]
     mine = message(own, side_parts, half_facts, prev_top, next_top)
     left, right, trio, *facts = merge(at, mine, to_y(mine), half_rows)

time: 152 us -> 154 us (1.013)
  starting transfers between devices: 56.6 us -> 58.9 us
  waiting for transfers between devices: 53.2 us -> 51.4 us
  Pallas kernels: 35.9 us -> 37.6 us
    ppermute x6, starting transfers between devices: 8.99 us -> 11.3 us  [to_core(): return lax.ppermute(block, 'row', [(i, i ^ 1) for i in range(16)])]
    pallas_call x1 -> x2, Pallas kernels: 5.88 us -> 6.95 us  [side_corr(): call(functools.partial(side_corr_kernel, steps), grid=(steps,), in_specs=...]
  transfers between devices with their start and end apart: 32 -> 32, of which waited for: 15 -> 14; matrix products, arithmetic and copies ran while one was open for 0% -> 0% of each run, Pallas kernels for 18% -> 19%
where the time goes in v8:
time: 154 us
  starting transfers between devices  58.9 us (38%)
  waiting for transfers between devices  51.4 us (33%)
  Pallas kernels  37.6 us (24%)
  local copies, waits for them, and re-layouts  4.85 us (3%)
    ppermute x15, starting transfers between devices, to_x(): return lax.ppermute(block, 'row', pairs)  22.6 us
    ppermute x10, starting transfers between devices, across(): lax.ppermute(block, 'grp', [(i, (i + shift) % count) for i in range(count)])  22.4 us
    ppermute x10, waiting for transfers between devices, across(): lax.ppermute(block, 'grp', [(i, (i + shift) % count) for i in range(count)])  22.2 us
    ppermute x15, waiting for transfers between devices, to_x(): return lax.ppermute(block, 'row', pairs)  16.6 us
    ppermute x6, starting transfers between devices, to_core(): return lax.ppermute(block, 'row', [(i, i ^ 1) for i in range(16)])  11.3 us
    ppermute x1, waiting for transfers between devices, to_y(): return lax.ppermute(block, 'row', [(i, i ^ 8) for i in range(16)])  8.68 us
    pallas_call x1, Pallas kernels, finish_a(): call(finish_a_kernel, mib=40, grid=(rows // tile,), in_specs=[smem_spec,...  8.52 us
    pallas_call x2, Pallas kernels, side_corr(): call(functools.partial(side_corr_kernel, steps), grid=(steps,), in_specs=...  6.95 us
  transfers between devices with their start and end apart: 32, of which 14 were waited for; matrix products, arithmetic and copies ran while one was open for 0% of the time, Pallas kernels for 19%

profile of v8, /device:TPU:1, one launch (start us, length us, event | category | flops | bytes accessed | tf_op | source)
XLA Modules:
  0.0 153.7 jit_solution(15156789851124394555)
XLA Ops:
  0.6 7.5 %collective-permute-start.9 = (f32[1024,512]{1,0:T(8,128)}, f32[1024,512]{1,0:T(8,128)}, u32[]{:S(2)}, u32[]{:S(2)}) collective-permute-start(f32[1024,512]{1,0:T(8,128)} %refs_2_.1), channel_id=1, source_target_pairs={{0,240},{16,0},{32,16},{48,32},{64,48},{80,64},{96,80},{112,96},{1... | collective-permute-start | bytes 6291464 | tf_op jit(solution)/shard_map/ppermute | solution.py:34
  8.1 1.7 %copy-done = f32[1024,512]{1,0:T(8,128)S(1)} copy-done((f32[1024,512]{1,0:T(8,128)S(1)}, f32[1024,512]{1,0:T(8,128)}, u32[]{:S(2)}) %copy-start) | copy-done | bytes 2097176
  9.8 1.6 %copy-done.2 = f32[1024,512]{1,0:T(8,128)S(1)} copy-done((f32[1024,512]{1,0:T(8,128)S(1)}, f32[1024,512]{1,0:T(8,128)}, u32[]{:S(2)}) %copy-start.2) | copy-done | bytes 2097176
  12.0 1.0 collective-permute-start
  13.0 0.8 collective-permute-done
  13.9 1.2 collective-permute-start.1
  15.1 2.5 %collective-permute-start.2 = (f32[8,512]{1,0:T(8,128)S(1)}, f32[8,512]{1,0:T(8,128)S(1)}, u32[]{:S(2)}, u32[]{:S(2)}) collective-permute-start(f32[8,512]{1,0:T(8,128)S(1)} %add.3.refs_0_), channel_id=1, source_target_pairs={{0,4},{1,5},{2,6},{3,7},{4,0},{5,1},{6,2},{7,3},{8,12},{9,13},{10,... | collective-permute-start | bytes 49160 | tf_op jit(solution)/shard_map/ppermute | solution.py:47
  17.5 1.2 collective-permute-start.3
  19.6 0.9 collective-permute-done.3.refs_3_
  20.5 1.6 %copy-done.3 = f32[1024,512]{1,0:T(8,128)S(1)} copy-done((f32[1024,512]{1,0:T(8,128)S(1)}, f32[1024,512]{1,0:T(8,128)}, u32[]{:S(2)}) %copy-start.3) | copy-done | bytes 2097176
  22.1 6.1 %own_corr.1 = (f32[640,512]{1,0:T(8,128)S(1)}, f32[128,512]{1,0:T(8,128)S(1)}, f32[256,512]{1,0:T(8,128)S(1)}, f32[8,512]{1,0:T(8,128)S(1)}, f32[4,64,512]{2,1,0...) custom-call(s32[2]{0:T(128)S(1)} %pad_add_fusion.at_ref, ...), custom_call_target="tpu_custom_call" | custom-call | flops 1 | bytes 1 | tf_op jit(solution)/shard_map/own_corr/pallas_call | solution.py:161
  28.2 1.7 %collective-permute-start.4 = (f32[4,64,512]{2,1,0:T(8,128)S(1)}, f32[4,64,512]{2,1,0:T(8,128)S(1)}, u32[]{:S(2)}, u32[]{:S(2)}) collective-permute-start(f32[4,64,512]{2,1,0:T(8,128)S(1)} %get-tuple-element.40), channel_id=1, source_target_pairs={{0,1},{1,0},{2,3},{3,2},{4,5},{5,4},{6,7},{7,6},{8,9},{9,8},{10,11... | collective-permute-start | bytes 1572872 | tf_op jit(solution)/shard_map/ppermute | solution.py:38
  29.9 1.5 collective-permute-done.4.refs_1_
  31.6 3.5 %collective-permute-start.6 = (f32[64,512]{1,0:T(8,128)S(1)}, f32[64,512]{1,0:T(8,128)S(1)}, u32[]{:S(2)}, u32[]{:S(2)}) collective-permute-start(f32[64,512]{1,0:T(8,128)S(1)} %get-tuple-element.43), channel_id=1, source_target_pairs={{0,4},{1,5},{2,6},{3,7},{4,0},{5,1},{6,2},{7,3},{8,12},{9,13},{10,... | collective-permute-start | bytes 393224 | tf_op jit(solution)/shard_map/ppermute | solution.py:47
  35.2 2.5 %collective-permute-done.5.refs_1_ = f32[64,512]{1,0:T(8,128)S(1)} collective-permute-done((f32[64,512]{1,0:T(8,128)S(1)}, f32[64,512]{1,0:T(8,128)S(1)}, u32[]{:S(2)}, u32[]{:S(2)}) %collective-permute-start.5) | collective-permute-done | bytes 131104 | tf_op jit(solution)/shard_map/ppermute | solution.py:47
  37.6 3.7 %collective-permute-done.6.refs_2_ = f32[64,512]{1,0:T(8,128)S(1)} collective-permute-done((f32[64,512]{1,0:T(8,128)S(1)}, f32[64,512]{1,0:T(8,128)S(1)}, u32[]{:S(2)}, u32[]{:S(2)}) %collective-permute-start.6) | collective-permute-done | bytes 131104 | tf_op jit(solution)/shard_map/ppermute | solution.py:47
  41.5 3.9 %collective-permute-start.16 = (f32[648,512]{1,0:T(8,128)S(1)}, f32[648,512]{1,0:T(8,128)S(1)}, u32[]{:S(2)}, u32[]{:S(2)}) collective-permute-start(f32[648,512]{1,0:T(8,128)S(1)} %get-tuple-element.58), channel_id=1, source_target_pairs={{0,240},{16,0},{32,16},{48,32},{64,48},{80,64},{96,80},{112,96},{1... | collective-permute-start | bytes 3981320 | tf_op jit(solution)/shard_map/ppermute | solution.py:34
  45.4 7.3 %collective-permute-done.9.b_ref.next_ref = f32[1024,512]{1,0:T(8,128)} collective-permute-done((f32[1024,512]{1,0:T(8,128)}, f32[1024,512]{1,0:T(8,128)}, u32[]{:S(2)}, u32[]{:S(2)}) %collective-permute-start.9) | collective-permute-done | bytes 2097184 | tf_op jit(solution)/shard_map/ppermute | solution.py:34
  52.7 3.5 %side_corr.3 = (f32[4,64,512]{2,1,0:T(8,128)S(1)}, f32[4,64,512]{2,1,0:T(8,128)S(1)}) custom-call(s32[2]{0:T(128)S(1)} %pad_add_fusion.at_ref, bf16[512,1024]{1,0:T(8,128)(2,1)S(1)} %get-tuple-element.48.high_ref, bf16[512,1024]{1,0:T(8,128)(2,1)S(1)} %get-tuple-element.49.low_ref, f32[1024,512]{1,0:T(8,128)} %collective-permute-done.9.b_ref.next_ref, ...), custom_call_target="tpu_custom_call" | custom-call | flops 1 | bytes 1 | tf_op jit(solution)/shard_map/side_corr/pallas_call | solution.py:201
  56.2 3.0 %collective-permute-start.11 = (f32[4,64,512]{2,1,0:T(8,128)S(1)}, f32[4,64,512]{2,1,0:T(8,128)S(1)}, u32[]{:S(2)}, u32[]{:S(2)}) collective-permute-start(f32[4,64,512]{2,1,0:T(8,128)S(1)} %get-tuple-element.53), channel_id=1, source_target_pairs={{0,1},{1,0},{2,3},{3,2},{4,5},{5,4},{6,7},{7,6},{8,9},{9,8},{10,11... | collective-permute-start | bytes 1572872 | tf_op jit(solution)/shard_map/ppermute | solution.py:38
  59.2 3.5 %side_corr.2 = (f32[4,64,512]{2,1,0:T(8,128)S(1)}, f32[4,64,512]{2,1,0:T(8,128)S(1)}) custom-call(s32[2]{0:T(128)S(1)} %pad_add_fusion.at_ref, bf16[512,1024]{1,0:T(8,128)(2,1)S(1)} %get-tuple-element.48.high_ref, bf16[512,1024]{1,0:T(8,128)(2,1)S(1)} %get-tuple-element.49.low_ref, f32[1024,512]{1,0:T(8,128)} %collective-permute-done.8.b_ref.prev_ref, ...), custom_call_target="tpu_custom_call" | custom-call | flops 1 | bytes 1 | tf_op jit(solution)/shard_map/side_corr/pallas_call | solution.py:201
  62.7 1.0 collective-permute-start.10
  63.6 1.5 collective-permute-done.10.got_left_ref
  65.3 1.3 collective-permute-start.12
  66.6 2.4 %collective-permute-start.13 = (f32[128,512]{1,0:T(8,128)S(1)}, f32[128,512]{1,0:T(8,128)S(1)}, u32[]{:S(2)}, u32[]{:S(2)}) collective-permute-start(f32[128,512]{1,0:T(8,128)S(1)} %get-tuple-element.56), channel_id=1, source_target_pairs={{0,4},{1,5},{2,6},{3,7},{4,0},{5,1},{6,2},{7,3},{8,12},{9,13},{10,... | collective-permute-start | bytes 786440 | tf_op jit(solution)/shard_map/ppermute | solution.py:47
  69.0 1.1 collective-permute-start.14
  70.2 14.9 %collective-permute-done.15.refs_5_.refs_3_.refs_6_ = f32[648,512]{1,0:T(8,128)S(1)} collective-permute-done((f32[648,512]{1,0:T(8,128)S(1)}, f32[648,512]{1,0:T(8,128)S(1)}, u32[]{:S(2)}, u32[]{:S(2)}) %collective-permute-start.15) | collective-permute-done | bytes 1327136 | tf_op jit(solution)/shard_map/ppermute | solution.py:34
  85.2 2.7 %collective-permute-start.17 = (f32[216,512]{1,0:T(8,128)S(1)}, f32[216,512]{1,0:T(8,128)S(1)}, u32[]{:S(2)}, u32[]{:S(2)}) collective-permute-start(f32[216,512]{1,0:T(8,128)S(1)} %message.1.mine_ref), channel_id=1, source_target_pairs={{0,8},{1,9},{2,10},{3,11},{4,12},{5,13},{6,14},{7,15},{8,0},{9,1},... | collective-permute-start | bytes 1327112 | tf_op jit(solution)/shard_map/ppermute | solution.py:42
  87.9 8.7 %collective-permute-done.17.got_ref = f32[216,512]{1,0:T(8,128)S(1)} collective-permute-done((f32[216,512]{1,0:T(8,128)S(1)}, f32[216,512]{1,0:T(8,128)S(1)}, u32[]{:S(2)}, u32[]{:S(2)}) %collective-permute-start.17) | collective-permute-done | bytes 442400 | tf_op jit(solution)/shard_map/ppermute | solution.py:42
  96.6 1.0 merge.1
  97.6 3.6 %collective-permute-start.22 = (f32[64,512]{1,0:T(8,128)S(1)}, f32[64,512]{1,0:T(8,128)S(1)}, u32[]{:S(2)}, u32[]{:S(2)}) collective-permute-start(f32[64,512]{1,0:T(8,128)S(1)} %get-tuple-element.64), channel_id=1, source_target_pairs={{0,240},{16,0},{32,16},{48,32},{64,48},{80,64},{96,80},{112,96},{1... | collective-permute-start | bytes 393224 | tf_op jit(solution)/shard_map/ppermute | solution.py:34
  101.2 1.2 collective-permute-start.18
  102.4 2.5 %collective-permute-start.19 = (f32[192,512]{1,0:T(8,128)S(1)}, f32[192,512]{1,0:T(8,128)S(1)}, u32[]{:S(2)}, u32[]{:S(2)}) collective-permute-start(f32[192,512]{1,0:T(8,128)S(1)} %get-tuple-element.59.refs_0_), channel_id=1, source_target_pairs={{0,4},{1,5},{2,6},{3,7},{4,0},{5,1},{6,2},{7,3},{8,12},{9,13},{10,... | collective-permute-start | bytes 1179656 | tf_op jit(solution)/shard_map/ppermute | solution.py:47
  104.9 1.2 collective-permute-start.20
  106.1 3.6 %collective-permute-start.24 = (f32[128,512]{1,0:T(8,128)S(1)}, f32[128,512]{1,0:T(8,128)S(1)}, u32[]{:S(2)}, u32[]{:S(2)}) collective-permute-start(f32[128,512]{1,0:T(8,128)S(1)} %get-tuple-element.69), channel_id=1, source_target_pairs={{0,240},{16,0},{32,16},{48,32},{64,48},{80,64},{96,80},{112,96},{1... | collective-permute-start | bytes 786440 | tf_op jit(solution)/shard_map/ppermute | solution.py:34
  109.7 3.7 %presplit.1 = (bf16[1024,3072]{1,0:T(8,128)(2,1)S(1)}, bf16[1024,1024]{1,0:T(8,128)(2,1)S(1)}) custom-call(f32[1024,512]{1,0:T(8,128)S(1)} %copy-done.1, f32[1024,512]{1,0:T(8,128)} %collective-permute-done.8.b_ref.prev_ref, f32[1024,512]{1,0:T(8,128)} %collective-permute-done.9.b_ref.next_ref, f32[1024,512]{1,0:T(8,128)S(1)} %copy-done.4, ...), custom_call_target="tpu_custom_call" | custom-call | flops 1 | bytes 1 | tf_op jit(solution)/shard_map/presplit/pallas_call | solution.py:461
  113.5 5.6 %collective-permute-done.19.refs_2_ = f32[192,512]{1,0:T(8,128)S(1)} collective-permute-done((f32[192,512]{1,0:T(8,128)S(1)}, f32[192,512]{1,0:T(8,128)S(1)}, u32[]{:S(2)}, u32[]{:S(2)}) %collective-permute-start.19) | collective-permute-done | bytes 393248 | tf_op jit(solution)/shard_map/ppermute | solution.py:47
  119.1 1.4 collective-permute-done.20.refs_3_
  120.6 2.9 %collective-permute-start.25 = (f32[4,192,512]{2,1,0:T(8,128)S(1)}, f32[4,192,512]{2,1,0:T(8,128)S(1)}, u32[]{:S(2)}, u32[]{:S(2)}) collective-permute-start(f32[4,192,512]{2,1,0:T(8,128)S(1)} %pack.2.mine_ref), channel_id=1, source_target_pairs={{0,1},{1,0},{2,3},{3,2},{4,5},{5,4},{6,7},{7,6},{8,9},{9,8},{10,11... | collective-permute-start | bytes 4718600 | tf_op jit(solution)/shard_map/ppermute | solution.py:38
  123.5 3.6 %collective-permute-start.30 = (f32[256,512]{1,0:T(8,128)S(1)}, f32[256,512]{1,0:T(8,128)S(1)}, u32[]{:S(2)}, u32[]{:S(2)}) collective-permute-start(f32[256,512]{1,0:T(8,128)S(1)} %get-tuple-element.73), channel_id=1, source_target_pairs={{0,240},{16,0},{32,16},{48,32},{64,48},{80,64},{96,80},{112,96},{1... | collective-permute-start | bytes 1572872 | tf_op jit(solution)/shard_map/ppermute | solution.py:34
  127.1 1.1 collective-permute-start.26
  128.2 2.1 %collective-permute-start.27 = (f32[128,512]{1,0:T(8,128)S(1)}, f32[128,512]{1,0:T(8,128)S(1)}, u32[]{:S(2)}, u32[]{:S(2)}) collective-permute-start(f32[128,512]{1,0:T(8,128)S(1)} %get-tuple-element.67.refs_0_), channel_id=1, source_target_pairs={{0,4},{1,5},{2,6},{3,7},{4,0},{5,1},{6,2},{7,3},{8,12},{9,13},{10,... | collective-permute-start | bytes 786440 | tf_op jit(solution)/shard_map/ppermute | solution.py:47
  130.3 1.3 collective-permute-start.28
  131.6 8.5 %finish_a.1 = (f32[1024,512]{1,0:T(8,128)}, f32[8,512]{1,0:T(8,128)S(1)}) custom-call(s32[2]{0:T(128)S(1)} %pad_add_fusion.at_ref, f32[4,192,512]{2,1,0:T(8,128)S(1)} %pack.2.mine_ref, f32[4,192,512]{2,1,0:T(8,128)S(1)} %collective-permute-done.25.other_ref, f32[8,512]{1,0:T(8,128)S(1)} %get-tuple-element.60.f_ref.refs_0_.facts_ref, ...), custom_call_target="tpu_custom_call" | custom-call | flops 1 | bytes 1 | tf_op jit(solution)/shard_map/finish_a/pallas_call | solution.py:511
  140.1 1.6 %collective-permute-done.27.refs_2_ = f32[128,512]{1,0:T(8,128)S(1)} collective-permute-done((f32[128,512]{1,0:T(8,128)S(1)}, f32[128,512]{1,0:T(8,128)S(1)}, u32[]{:S(2)}, u32[]{:S(2)}) %collective-permute-start.27) | collective-permute-done | bytes 262176 | tf_op jit(solution)/shard_map/ppermute | solution.py:47
  141.8 1.6 %collective-permute-start.31 = (f32[4,128,512]{2,1,0:T(8,128)S(1)}, f32[4,128,512]{2,1,0:T(8,128)S(1)}, u32[]{:S(2)}, u32[]{:S(2)}) collective-permute-start(f32[4,128,512]{2,1,0:T(8,128)S(1)} %pack.3.refs_0_.mine_ref), channel_id=1, source_target_pairs={{0,1},{1,0},{2,3},{3,2},{4,5},{5,4},{6,7},{7,6},{8,9},{9,8},{10,11... | collective-permute-start | bytes 3145736 | tf_op jit(solution)/shard_map/ppermute | solution.py:38
  143.5 3.5 %own_b.1 = (f32[1024,512]{1,0:T(8,128)S(1)}, f32[8,512]{1,0:T(8,128)S(1)}) custom-call(s32[2]{0:T(128)S(1)} %pad_add_fusion.at_ref, f32[4,192,512]{2,1,0:T(8,128)S(1)} %pack.2.mine_ref, f32[4,192,512]{2,1,0:T(8,128)S(1)} %collective-permute-done.25.other_ref, f32[8,512]{1,0:T(8,128)S(1)} %get-tuple-element.60.f_ref.refs_0_.facts_ref, ...), custom_call_target="tpu_custom_call" | custom-call | flops 1 | bytes 1 | tf_op jit(solution)/shard_map/own_b/pallas_call | solution.py:544
  146.9 6.7 %finish_b.1 = f32[1024,512]{1,0:T(8,128)} custom-call(s32[2]{0:T(128)S(1)} %pad_add_fusion.at_ref, f32[4,128,512]{2,1,0:T(8,128)S(1)} %pack.3.refs_0_.mine_ref, f32[4,128,512]{2,1,0:T(8,128)S(1)} %collective-permute-done.31.other_ref, f32[8,512]{1,0:T(8,128)S(1)} %get-tuple-element.60.f_ref.refs_0_.facts_ref, f32[8,512]{1,0:T(8,128)S(1)} %get-tuple-element.61.pf_ref.refs_1_, ...), custom_call_target="tpu_custom_call" | custom-call | flops 1 | bytes 1 | tf_op jit(solution)/shard_map/finish_b/pallas_call | solution.py:599
  (44 shorter events, 2.5 us)
Async XLA Ops:
  0.6 52.1 %collective-permute-start.9 = (f32[1024,512]{1,0:T(8,128)}, f32[1024,512]{1,0:T(8,128)}, u32[]{:S(2)}, u32[]{:S(2)}) collective-permute-start(f32[1024,512]{1,0:T(8,128)} %refs_2_.1), channel_id=1, source_target_pairs={{0,240},{16,0},{32,16},{48,32},{64,48},{80,64},{96,80},{112,96},{1... | collective-permute-start | bytes 6291464 | tf_op jit(solution)/shard_map/ppermute | solution.py:34
  8.1 51.1 %collective-permute-start.8 = (f32[1024,512]{1,0:T(8,128)}, f32[1024,512]{1,0:T(8,128)}, u32[]{:S(2)}, u32[]{:S(2)}) collective-permute-start(f32[1024,512]{1,0:T(8,128)} %refs_2_.1), channel_id=1, source_target_pairs={{0,16},{16,32},{32,48},{48,64},{64,80},{80,96},{96,112},{112,128},... | collective-permute-start | bytes 6291464 | tf_op jit(solution)/shard_map/ppermute | solution.py:34
  8.1 1.7 %copy-start = (f32[1024,512]{1,0:T(8,128)S(1)}, f32[1024,512]{1,0:T(8,128)}, u32[]{:S(2)}) copy-start(f32[1024,512]{1,0:T(8,128)} %refs_2_.1) | copy-start | bytes 6291460
  9.8 1.6 %copy-start.2 = (f32[1024,512]{1,0:T(8,128)S(1)}, f32[1024,512]{1,0:T(8,128)}, u32[]{:S(2)}) copy-start(f32[1024,512]{1,0:T(8,128)} %refs_3_.1) | copy-start | bytes 6291460
  11.4 9.2 %copy-start.1 = (f32[1024,512]{1,0:T(8,128)S(1)}, f32[1024,512]{1,0:T(8,128)}, u32[]{:S(2)}) copy-start(f32[1024,512]{1,0:T(8,128)} %refs_2_.1) | copy-start | bytes 6291460
  12.0 1.9 %collective-permute-start = (f32[8,512]{1,0:T(8,128)S(1)}, f32[8,512]{1,0:T(8,128)S(1)}, u32[]{:S(2)}, u32[]{:S(2)}) collective-permute-start(f32[8,512]{1,0:T(8,128)S(1)} %sums.1), channel_id=1, source_target_pairs={{0,1},{1,0},{2,3},{3,2},{4,5},{5,4},{6,7},{7,6},{8,9},{9,8},{10,11... | collective-permute-start | bytes 49160 | tf_op jit(solution)/shard_map/ppermute | solution.py:38
  13.9 4.9 %collective-permute-start.1 = (f32[8,512]{1,0:T(8,128)S(1)}, f32[8,512]{1,0:T(8,128)S(1)}, u32[]{:S(2)}, u32[]{:S(2)}) collective-permute-start(f32[8,512]{1,0:T(8,128)S(1)} %add.3.refs_0_), channel_id=1, source_target_pairs={{0,2},{1,3},{2,4},{3,5},{4,6},{5,7},{6,0},{7,1},{8,10},{9,11},{10,... | collective-permute-start | bytes 49160 | tf_op jit(solution)/shard_map/ppermute | solution.py:47
  15.1 4.5 %collective-permute-start.2 = (f32[8,512]{1,0:T(8,128)S(1)}, f32[8,512]{1,0:T(8,128)S(1)}, u32[]{:S(2)}, u32[]{:S(2)}) collective-permute-start(f32[8,512]{1,0:T(8,128)S(1)} %add.3.refs_0_), channel_id=1, source_target_pairs={{0,4},{1,5},{2,6},{3,7},{4,0},{5,1},{6,2},{7,3},{8,12},{9,13},{10,... | collective-permute-start | bytes 49160 | tf_op jit(solution)/shard_map/ppermute | solution.py:47
  17.5 3.0 %collective-permute-start.3 = (f32[8,512]{1,0:T(8,128)S(1)}, f32[8,512]{1,0:T(8,128)S(1)}, u32[]{:S(2)}, u32[]{:S(2)}) collective-permute-start(f32[8,512]{1,0:T(8,128)S(1)} %add.3.refs_0_), channel_id=1, source_target_pairs={{0,6},{1,7},{2,0},{3,1},{4,2},{5,3},{6,4},{7,5},{8,14},{9,15},{10,... | collective-permute-start | bytes 49160 | tf_op jit(solution)/shard_map/ppermute | solution.py:47
  20.5 1.6 %copy-start.3 = (f32[1024,512]{1,0:T(8,128)S(1)}, f32[1024,512]{1,0:T(8,128)}, u32[]{:S(2)}) copy-start(f32[1024,512]{1,0:T(8,128)} %refs_3_.1) | copy-start | bytes 6291460
  28.2 3.3 %collective-permute-start.4 = (f32[4,64,512]{2,1,0:T(8,128)S(1)}, f32[4,64,512]{2,1,0:T(8,128)S(1)}, u32[]{:S(2)}, u32[]{:S(2)}) collective-permute-start(f32[4,64,512]{2,1,0:T(8,128)S(1)} %get-tuple-element.40), channel_id=1, source_target_pairs={{0,1},{1,0},{2,3},{3,2},{4,5},{5,4},{6,7},{7,6},{8,9},{9,8},{10,11... | collective-permute-start | bytes 1572872 | tf_op jit(solution)/shard_map/ppermute | solution.py:38
  31.5 6.1 %collective-permute-start.5 = (f32[64,512]{1,0:T(8,128)S(1)}, f32[64,512]{1,0:T(8,128)S(1)}, u32[]{:S(2)}, u32[]{:S(2)}) collective-permute-start(f32[64,512]{1,0:T(8,128)S(1)} %get-tuple-element.42), channel_id=1, source_target_pairs={{0,2},{1,3},{2,4},{3,5},{4,6},{5,7},{6,0},{7,1},{8,10},{9,11},{10,... | collective-permute-start | bytes 393224 | tf_op jit(solution)/shard_map/ppermute | solution.py:47
  31.6 9.7 %collective-permute-start.6 = (f32[64,512]{1,0:T(8,128)S(1)}, f32[64,512]{1,0:T(8,128)S(1)}, u32[]{:S(2)}, u32[]{:S(2)}) collective-permute-start(f32[64,512]{1,0:T(8,128)S(1)} %get-tuple-element.43), channel_id=1, source_target_pairs={{0,4},{1,5},{2,6},{3,7},{4,0},{5,1},{6,2},{7,3},{8,12},{9,13},{10,... | collective-permute-start | bytes 393224 | tf_op jit(solution)/shard_map/ppermute | solution.py:47
  35.2 6.2 %collective-permute-start.7 = (f32[64,512]{1,0:T(8,128)S(1)}, f32[64,512]{1,0:T(8,128)S(1)}, u32[]{:S(2)}, u32[]{:S(2)}) collective-permute-start(f32[64,512]{1,0:T(8,128)S(1)} %get-tuple-element.44), channel_id=1, source_target_pairs={{0,6},{1,7},{2,0},{3,1},{4,2},{5,3},{6,4},{7,5},{8,14},{9,15},{10,... | collective-permute-start | bytes 393224 | tf_op jit(solution)/shard_map/ppermute | solution.py:47
  41.4 43.6 %collective-permute-start.15 = (f32[648,512]{1,0:T(8,128)S(1)}, f32[648,512]{1,0:T(8,128)S(1)}, u32[]{:S(2)}, u32[]{:S(2)}) collective-permute-start(f32[648,512]{1,0:T(8,128)S(1)} %get-tuple-element.58), channel_id=1, source_target_pairs={{0,16},{16,32},{32,48},{48,64},{64,80},{80,96},{96,112},{112,128},... | collective-permute-start | bytes 3981320 | tf_op jit(solution)/shard_map/ppermute | solution.py:34
  41.5 43.5 %collective-permute-start.16 = (f32[648,512]{1,0:T(8,128)S(1)}, f32[648,512]{1,0:T(8,128)S(1)}, u32[]{:S(2)}, u32[]{:S(2)}) collective-permute-start(f32[648,512]{1,0:T(8,128)S(1)} %get-tuple-element.58), channel_id=1, source_target_pairs={{0,240},{16,0},{32,16},{48,32},{64,48},{80,64},{96,80},{112,96},{1... | collective-permute-start | bytes 3981320 | tf_op jit(solution)/shard_map/ppermute | solution.py:34
  56.2 7.4 %collective-permute-start.11 = (f32[4,64,512]{2,1,0:T(8,128)S(1)}, f32[4,64,512]{2,1,0:T(8,128)S(1)}, u32[]{:S(2)}, u32[]{:S(2)}) collective-permute-start(f32[4,64,512]{2,1,0:T(8,128)S(1)} %get-tuple-element.53), channel_id=1, source_target_pairs={{0,1},{1,0},{2,3},{3,2},{4,5},{5,4},{6,7},{7,6},{8,9},{9,8},{10,11... | collective-permute-start | bytes 1572872 | tf_op jit(solution)/shard_map/ppermute | solution.py:38
  62.7 2.5 %collective-permute-start.10 = (f32[4,64,512]{2,1,0:T(8,128)S(1)}, f32[4,64,512]{2,1,0:T(8,128)S(1)}, u32[]{:S(2)}, u32[]{:S(2)}) collective-permute-start(f32[4,64,512]{2,1,0:T(8,128)S(1)} %get-tuple-element.52), channel_id=1, source_target_pairs={{0,1},{1,0},{2,3},{3,2},{4,5},{5,4},{6,7},{7,6},{8,9},{9,8},{10,11... | collective-permute-start | bytes 1572872 | tf_op jit(solution)/shard_map/ppermute | solution.py:38
  65.3 19.8 %collective-permute-start.12 = (f32[128,512]{1,0:T(8,128)S(1)}, f32[128,512]{1,0:T(8,128)S(1)}, u32[]{:S(2)}, u32[]{:S(2)}) collective-permute-start(f32[128,512]{1,0:T(8,128)S(1)} %get-tuple-element.55), channel_id=1, source_target_pairs={{0,2},{1,3},{2,4},{3,5},{4,6},{5,7},{6,0},{7,1},{8,10},{9,11},{10,... | collective-permute-start | bytes 786440 | tf_op jit(solution)/shard_map/ppermute | solution.py:47
  66.6 18.5 %collective-permute-start.13 = (f32[128,512]{1,0:T(8,128)S(1)}, f32[128,512]{1,0:T(8,128)S(1)}, u32[]{:S(2)}, u32[]{:S(2)}) collective-permute-start(f32[128,512]{1,0:T(8,128)S(1)} %get-tuple-element.56), channel_id=1, source_target_pairs={{0,4},{1,5},{2,6},{3,7},{4,0},{5,1},{6,2},{7,3},{8,12},{9,13},{10,... | collective-permute-start | bytes 786440 | tf_op jit(solution)/shard_map/ppermute | solution.py:47
  69.0 16.1 %collective-permute-start.14 = (f32[128,512]{1,0:T(8,128)S(1)}, f32[128,512]{1,0:T(8,128)S(1)}, u32[]{:S(2)}, u32[]{:S(2)}) collective-permute-start(f32[128,512]{1,0:T(8,128)S(1)} %get-tuple-element.57), channel_id=1, source_target_pairs={{0,6},{1,7},{2,0},{3,1},{4,2},{5,3},{6,4},{7,5},{8,14},{9,15},{10,... | collective-permute-start | bytes 786440 | tf_op jit(solution)/shard_map/ppermute | solution.py:47
  85.1 24.6 %copy-start.4 = (f32[1024,512]{1,0:T(8,128)S(1)}, f32[1024,512]{1,0:T(8,128)}, u32[]{:S(2)}) copy-start(f32[1024,512]{1,0:T(8,128)} %refs_3_.1) | copy-start | bytes 6291460
  85.2 11.4 %collective-permute-start.17 = (f32[216,512]{1,0:T(8,128)S(1)}, f32[216,512]{1,0:T(8,128)S(1)}, u32[]{:S(2)}, u32[]{:S(2)}) collective-permute-start(f32[216,512]{1,0:T(8,128)S(1)} %message.1.mine_ref), channel_id=1, source_target_pairs={{0,8},{1,9},{2,10},{3,11},{4,12},{5,13},{6,14},{7,15},{8,0},{9,1},... | collective-permute-start | bytes 1327112 | tf_op jit(solution)/shard_map/ppermute | solution.py:42
  97.5 8.5 %collective-permute-start.21 = (f32[64,512]{1,0:T(8,128)S(1)}, f32[64,512]{1,0:T(8,128)S(1)}, u32[]{:S(2)}, u32[]{:S(2)}) collective-permute-start(f32[64,512]{1,0:T(8,128)S(1)} %get-tuple-element.63), channel_id=1, source_target_pairs={{0,16},{16,32},{32,48},{48,64},{64,80},{80,96},{96,112},{112,128},... | collective-permute-start | bytes 393224 | tf_op jit(solution)/shard_map/ppermute | solution.py:34
  97.6 8.4 %collective-permute-start.22 = (f32[64,512]{1,0:T(8,128)S(1)}, f32[64,512]{1,0:T(8,128)S(1)}, u32[]{:S(2)}, u32[]{:S(2)}) collective-permute-start(f32[64,512]{1,0:T(8,128)S(1)} %get-tuple-element.64), channel_id=1, source_target_pairs={{0,240},{16,0},{32,16},{48,32},{64,48},{80,64},{96,80},{112,96},{1... | collective-permute-start | bytes 393224 | tf_op jit(solution)/shard_map/ppermute | solution.py:34
  101.2 12.3 %collective-permute-start.18 = (f32[192,512]{1,0:T(8,128)S(1)}, f32[192,512]{1,0:T(8,128)S(1)}, u32[]{:S(2)}, u32[]{:S(2)}) collective-permute-start(f32[192,512]{1,0:T(8,128)S(1)} %get-tuple-element.59.refs_0_), channel_id=1, source_target_pairs={{0,2},{1,3},{2,4},{3,5},{4,6},{5,7},{6,0},{7,1},{8,10},{9,11},{10,... | collective-permute-start | bytes 1179656 | tf_op jit(solution)/shard_map/ppermute | solution.py:47
  102.4 16.7 %collective-permute-start.19 = (f32[192,512]{1,0:T(8,128)S(1)}, f32[192,512]{1,0:T(8,128)S(1)}, u32[]{:S(2)}, u32[]{:S(2)}) collective-permute-start(f32[192,512]{1,0:T(8,128)S(1)} %get-tuple-element.59.refs_0_), channel_id=1, source_target_pairs={{0,4},{1,5},{2,6},{3,7},{4,0},{5,1},{6,2},{7,3},{8,12},{9,13},{10,... | collective-permute-start | bytes 1179656 | tf_op jit(solution)/shard_map/ppermute | solution.py:47
  104.9 15.6 %collective-permute-start.20 = (f32[192,512]{1,0:T(8,128)S(1)}, f32[192,512]{1,0:T(8,128)S(1)}, u32[]{:S(2)}, u32[]{:S(2)}) collective-permute-start(f32[192,512]{1,0:T(8,128)S(1)} %get-tuple-element.59.refs_0_), channel_id=1, source_target_pairs={{0,6},{1,7},{2,0},{3,1},{4,2},{5,3},{6,4},{7,5},{8,14},{9,15},{10,... | collective-permute-start | bytes 1179656 | tf_op jit(solution)/shard_map/ppermute | solution.py:47
  106.0 7.4 %collective-permute-start.23 = (f32[128,512]{1,0:T(8,128)S(1)}, f32[128,512]{1,0:T(8,128)S(1)}, u32[]{:S(2)}, u32[]{:S(2)}) collective-permute-start(f32[128,512]{1,0:T(8,128)S(1)} %get-tuple-element.69), channel_id=1, source_target_pairs={{0,16},{16,32},{32,48},{48,64},{64,80},{80,96},{96,112},{112,128},... | collective-permute-start | bytes 786440 | tf_op jit(solution)/shard_map/ppermute | solution.py:34
  106.1 7.3 %collective-permute-start.24 = (f32[128,512]{1,0:T(8,128)S(1)}, f32[128,512]{1,0:T(8,128)S(1)}, u32[]{:S(2)}, u32[]{:S(2)}) collective-permute-start(f32[128,512]{1,0:T(8,128)S(1)} %get-tuple-element.69), channel_id=1, source_target_pairs={{0,240},{16,0},{32,16},{48,32},{64,48},{80,64},{96,80},{112,96},{1... | collective-permute-start | bytes 786440 | tf_op jit(solution)/shard_map/ppermute | solution.py:34
  120.6 9.7 %collective-permute-start.25 = (f32[4,192,512]{2,1,0:T(8,128)S(1)}, f32[4,192,512]{2,1,0:T(8,128)S(1)}, u32[]{:S(2)}, u32[]{:S(2)}) collective-permute-start(f32[4,192,512]{2,1,0:T(8,128)S(1)} %pack.2.mine_ref), channel_id=1, source_target_pairs={{0,1},{1,0},{2,3},{3,2},{4,5},{5,4},{6,7},{7,6},{8,9},{9,8},{10,11... | collective-permute-start | bytes 4718600 | tf_op jit(solution)/shard_map/ppermute | solution.py:38
  123.5 18.2 %collective-permute-start.29 = (f32[256,512]{1,0:T(8,128)S(1)}, f32[256,512]{1,0:T(8,128)S(1)}, u32[]{:S(2)}, u32[]{:S(2)}) collective-permute-start(f32[256,512]{1,0:T(8,128)S(1)} %get-tuple-element.73), channel_id=1, source_target_pairs={{0,16},{16,32},{32,48},{48,64},{64,80},{80,96},{96,112},{112,128},... | collective-permute-start | bytes 1572872 | tf_op jit(solution)/shard_map/ppermute | solution.py:34
  123.5 18.2 %collective-permute-start.30 = (f32[256,512]{1,0:T(8,128)S(1)}, f32[256,512]{1,0:T(8,128)S(1)}, u32[]{:S(2)}, u32[]{:S(2)}) collective-permute-start(f32[256,512]{1,0:T(8,128)S(1)} %get-tuple-element.73), channel_id=1, source_target_pairs={{0,240},{16,0},{32,16},{48,32},{64,48},{80,64},{96,80},{112,96},{1... | collective-permute-start | bytes 1572872 | tf_op jit(solution)/shard_map/ppermute | solution.py:34
  127.1 13.0 %collective-permute-start.26 = (f32[128,512]{1,0:T(8,128)S(1)}, f32[128,512]{1,0:T(8,128)S(1)}, u32[]{:S(2)}, u32[]{:S(2)}) collective-permute-start(f32[128,512]{1,0:T(8,128)S(1)} %get-tuple-element.67.refs_0_), channel_id=1, source_target_pairs={{0,2},{1,3},{2,4},{3,5},{4,6},{5,7},{6,0},{7,1},{8,10},{9,11},{10,... | collective-permute-start | bytes 786440 | tf_op jit(solution)/shard_map/ppermute | solution.py:47
  128.2 13.5 %collective-permute-start.27 = (f32[128,512]{1,0:T(8,128)S(1)}, f32[128,512]{1,0:T(8,128)S(1)}, u32[]{:S(2)}, u32[]{:S(2)}) collective-permute-start(f32[128,512]{1,0:T(8,128)S(1)} %get-tuple-element.67.refs_0_), channel_id=1, source_target_pairs={{0,4},{1,5},{2,6},{3,7},{4,0},{5,1},{6,2},{7,3},{8,12},{9,13},{10,... | collective-permute-start | bytes 786440 | tf_op jit(solution)/shard_map/ppermute | solution.py:47
  130.3 11.4 %collective-permute-start.28 = (f32[128,512]{1,0:T(8,128)S(1)}, f32[128,512]{1,0:T(8,128)S(1)}, u32[]{:S(2)}, u32[]{:S(2)}) collective-permute-start(f32[128,512]{1,0:T(8,128)S(1)} %get-tuple-element.67.refs_0_), channel_id=1, source_target_pairs={{0,6},{1,7},{2,0},{3,1},{4,2},{5,3},{6,4},{7,5},{8,14},{9,15},{10,... | collective-permute-start | bytes 786440 | tf_op jit(solution)/shard_map/ppermute | solution.py:47
  141.8 5.1 %collective-permute-start.31 = (f32[4,128,512]{2,1,0:T(8,128)S(1)}, f32[4,128,512]{2,1,0:T(8,128)S(1)}, u32[]{:S(2)}, u32[]{:S(2)}) collective-permute-start(f32[4,128,512]{2,1,0:T(8,128)S(1)} %pack.3.refs_0_.mine_ref), channel_id=1, source_target_pairs={{0,1},{1,0},{2,3},{3,2},{4,5},{5,4},{6,7},{7,6},{8,9},{9,8},{10,11... | collective-permute-start | bytes 3145736 | tf_op jit(solution)/shard_map/ppermute | solution.py:38

commit v9 on v7

--- a/solution.py
+++ b/solution.py
@@ -115,7 +115,7 @@
         total = total / half_rows
         for view in (0, 1):
             mean, square = total[2 * view : 2 * view + 1], total[2 * view + 1 : 2 * view + 2]
-            scale = jnp.sqrt(square - mean * mean + epsilon)
+            scale = jnp.sqrt(jnp.maximum(square - mean * mean, 0.0) + epsilon)
             facts_ref[2 * view : 2 * view + 1, :] = mean
             facts_ref[2 * view + 1 : 2 * view + 2, :] = 1.0 / scale
             facts_ref[4 + view : 5 + view, :] = square
@@ -484,7 +484,7 @@
 
 def finish_a(at, mine, other, facts, a, parts):
     rows, width = a.shape
-    tile = 256
+    tile = 512
     spec = pl.BlockSpec((tile, width), lambda i: (i, 0))
     whole = pl.BlockSpec((8, width), lambda i: (0, 0))
     slots = pl.BlockSpec(mine.shape, lambda i: (0, 0, 0))
@@ -517,7 +517,7 @@
 
 def own_b(at, mine, other, facts, parts, wait_for):
     rows, width = parts.shape[0], parts.shape[1] // 2
-    tile = 256
+    tile = 512
     spec = pl.BlockSpec((tile, width), lambda i: (i, 0))
     whole = pl.BlockSpec((8, width), lambda i: (0, 0))
     slots = pl.BlockSpec(mine.shape, lambda i: (0, 0, 0))

time: 152 us -> 151 us (level)
  no operation moved by 1% of the time
where the time goes in v9:
time: 151 us
  starting transfers between devices  56.6 us (37%)
  waiting for transfers between devices  53.5 us (35%)
  Pallas kernels  35.3 us (23%)
  local copies, waits for them, and re-layouts  4.78 us (3%)
    ppermute x15, starting transfers between devices, to_x(): return lax.ppermute(block, 'row', pairs)  22.8 us
    ppermute x10, waiting for transfers between devices, across(): lax.ppermute(block, 'grp', [(i, (i + shift) % count) for i in range(count)])  22.1 us
    ppermute x10, starting transfers between devices, across(): lax.ppermute(block, 'grp', [(i, (i + shift) % count) for i in range(count)])  22.1 us
    ppermute x15, waiting for transfers between devices, to_x(): return lax.ppermute(block, 'row', pairs)  17.5 us
    ppermute x1, waiting for transfers between devices, to_y(): return lax.ppermute(block, 'row', [(i, i ^ 8) for i in range(16)])  9.32 us
    ppermute x6, starting transfers between devices, to_core(): return lax.ppermute(block, 'row', [(i, i ^ 1) for i in range(16)])  8.99 us
    pallas_call x1, Pallas kernels, finish_a(): call(finish_a_kernel, mib=40, grid=(rows // tile,), in_specs=[smem_spec,...  8.24 us
    pallas_call x1, Pallas kernels, finish_b(): call(functools.partial(finish_b_kernel, bounds), mib=24, grid=(rows // ti...  6.75 us
  transfers between devices with their start and end apart: 32, of which 15 were waited for; matrix products, arithmetic and copies ran while one was open for 0% of the time, Pallas kernels for 18%

profile of v9, /device:TPU:1, one launch (start us, length us, event | category | flops | bytes accessed | tf_op | source)
XLA Modules:
  0.0 151.0 jit_solution(6965253538628833178)
XLA Ops:
  0.6 2.5 %collective-permute-start.8 = (f32[1024,512]{1,0:T(8,128)}, f32[1024,512]{1,0:T(8,128)}, u32[]{:S(2)}, u32[]{:S(2)}) collective-permute-start(f32[1024,512]{1,0:T(8,128)} %refs_2_.1), channel_id=1, source_target_pairs={{0,16},{16,32},{32,48},{48,64},{64,80},{80,96},{96,112},{112,128},... | collective-permute-start | bytes 6291464 | tf_op jit(solution)/shard_map/ppermute | solution.py:34
  3.2 5.0 %collective-permute-start.9 = (f32[1024,512]{1,0:T(8,128)}, f32[1024,512]{1,0:T(8,128)}, u32[]{:S(2)}, u32[]{:S(2)}) collective-permute-start(f32[1024,512]{1,0:T(8,128)} %refs_2_.1), channel_id=1, source_target_pairs={{0,240},{16,0},{32,16},{48,32},{64,48},{80,64},{96,80},{112,96},{1... | collective-permute-start | bytes 6291464 | tf_op jit(solution)/shard_map/ppermute | solution.py:34
  8.2 1.6 %copy-done = f32[1024,512]{1,0:T(8,128)S(1)} copy-done((f32[1024,512]{1,0:T(8,128)S(1)}, f32[1024,512]{1,0:T(8,128)}, u32[]{:S(2)}) %copy-start) | copy-done | bytes 2097176
  9.8 1.6 %copy-done.2 = f32[1024,512]{1,0:T(8,128)S(1)} copy-done((f32[1024,512]{1,0:T(8,128)S(1)}, f32[1024,512]{1,0:T(8,128)}, u32[]{:S(2)}) %copy-start.2) | copy-done | bytes 2097176
  12.0 1.0 collective-permute-start
  13.1 0.8 collective-permute-done
  13.9 1.2 collective-permute-start.1
  15.1 2.5 %collective-permute-start.2 = (f32[8,512]{1,0:T(8,128)S(1)}, f32[8,512]{1,0:T(8,128)S(1)}, u32[]{:S(2)}, u32[]{:S(2)}) collective-permute-start(f32[8,512]{1,0:T(8,128)S(1)} %add.3.refs_0_), channel_id=1, source_target_pairs={{0,4},{1,5},{2,6},{3,7},{4,0},{5,1},{6,2},{7,3},{8,12},{9,13},{10,... | collective-permute-start | bytes 49160 | tf_op jit(solution)/shard_map/ppermute | solution.py:47
  17.6 1.2 collective-permute-start.3
  18.8 0.8 collective-permute-done.2.refs_2_
  19.6 0.9 collective-permute-done.3.refs_3_
  20.6 1.6 %copy-done.3 = f32[1024,512]{1,0:T(8,128)S(1)} copy-done((f32[1024,512]{1,0:T(8,128)S(1)}, f32[1024,512]{1,0:T(8,128)}, u32[]{:S(2)}) %copy-start.3) | copy-done | bytes 2097176
  22.2 5.4 %own_corr.1 = (f32[640,512]{1,0:T(8,128)S(1)}, f32[128,512]{1,0:T(8,128)S(1)}, f32[256,512]{1,0:T(8,128)S(1)}, f32[8,512]{1,0:T(8,128)S(1)}, f32[4,64,512]{2,1,0:T(8,128)S(1)}, /*index=5*/f32[4,64,512]{2,1,0:T(8,128)S(1)}) custom-call(s32[2]{0:T(128)S(1)} %pad_add_fusion.at_ref, f32[1024,512]{1,0:T(8,128)S(1)} %copy-done.1, f32[1024,512]{1,0:T(8,128)S(1)} %copy-done.3, ...), custom_call_target="tpu_custom_call" | custom-call | flops 1 | bytes 1 | tf_op jit(solution)/shard_map/own_corr/pallas_call | solution.py:159
  27.6 1.7 %collective-permute-start.4 = (f32[4,64,512]{2,1,0:T(8,128)S(1)}, f32[4,64,512]{2,1,0:T(8,128)S(1)}, u32[]{:S(2)}, u32[]{:S(2)}) collective-permute-start(f32[4,64,512]{2,1,0:T(8,128)S(1)} %get-tuple-element.37), channel_id=1, source_target_pairs={{0,1},{1,0},{2,3},{3,2},{4,5},{5,4},{6,7},{7,6},{8,9},{9,8},{10,11... | collective-permute-start | bytes 1572872 | tf_op jit(solution)/shard_map/ppermute | solution.py:38
  29.3 1.5 %collective-permute-done.4.refs_0_ = f32[4,64,512]{2,1,0:T(8,128)S(1)} collective-permute-done((f32[4,64,512]{2,1,0:T(8,128)S(1)}, f32[4,64,512]{2,1,0:T(8,128)S(1)}, u32[]{:S(2)}, u32[]{:S(2)}) %collective-permute-start.4) | collective-permute-done | bytes 524320 | tf_op jit(solution)/shard_map/ppermute | solution.py:38
  31.0 3.5 %collective-permute-start.6 = (f32[64,512]{1,0:T(8,128)S(1)}, f32[64,512]{1,0:T(8,128)S(1)}, u32[]{:S(2)}, u32[]{:S(2)}) collective-permute-start(f32[64,512]{1,0:T(8,128)S(1)} %get-tuple-element.40), channel_id=1, source_target_pairs={{0,4},{1,5},{2,6},{3,7},{4,0},{5,1},{6,2},{7,3},{8,12},{9,13},{10,... | collective-permute-start | bytes 393224 | tf_op jit(solution)/shard_map/ppermute | solution.py:47
  34.6 2.5 %collective-permute-done.5.refs_1_ = f32[64,512]{1,0:T(8,128)S(1)} collective-permute-done((f32[64,512]{1,0:T(8,128)S(1)}, f32[64,512]{1,0:T(8,128)S(1)}, u32[]{:S(2)}, u32[]{:S(2)}) %collective-permute-start.5) | collective-permute-done | bytes 131104 | tf_op jit(solution)/shard_map/ppermute | solution.py:47
  37.0 3.7 %collective-permute-done.6.refs_2_ = f32[64,512]{1,0:T(8,128)S(1)} collective-permute-done((f32[64,512]{1,0:T(8,128)S(1)}, f32[64,512]{1,0:T(8,128)S(1)}, u32[]{:S(2)}, u32[]{:S(2)}) %collective-permute-start.6) | collective-permute-done | bytes 131104 | tf_op jit(solution)/shard_map/ppermute | solution.py:47
  40.9 3.6 %collective-permute-start.16 = (f32[648,512]{1,0:T(8,128)S(1)}, f32[648,512]{1,0:T(8,128)S(1)}, u32[]{:S(2)}, u32[]{:S(2)}) collective-permute-start(f32[648,512]{1,0:T(8,128)S(1)} %get-tuple-element.52), channel_id=1, source_target_pairs={{0,240},{16,0},{32,16},{48,32},{64,48},{80,64},{96,80},{112,96},{1... | collective-permute-start | bytes 3981320 | tf_op jit(solution)/shard_map/ppermute | solution.py:34
  44.5 9.3 %collective-permute-done.8.prev_ref = f32[1024,512]{1,0:T(8,128)} collective-permute-done((f32[1024,512]{1,0:T(8,128)}, f32[1024,512]{1,0:T(8,128)}, u32[]{:S(2)}, u32[]{:S(2)}) %collective-permute-start.8) | collective-permute-done | bytes 2097184 | tf_op jit(solution)/shard_map/ppermute | solution.py:34
  53.8 5.9 %side_corr.1 = (f32[4,128,512]{2,1,0:T(8,128)S(1)}, f32[2,128,512]{2,1,0:T(8,128)S(1)}, f32[2,128,512]{2,1,0:T(8,128)S(1)}) custom-call(s32[2]{0:T(128)S(1)} %pad_add_fusion.at_ref, f32[1024,512]{1,0:T(8,128)S(1)} %copy-done.1, f32[1024,512]{1,0:T(8,128)} %collective-permute-done.8.prev_ref, f32[1024,512]{1,0:T(8,128)} %collective-permute-done.9.next_ref, ...), custom_call_target="tpu_custom_call" | custom-call | flops 1 | bytes 1 | tf_op jit(solution)/shard_map/side_corr/pallas_call | solution.py:200
  59.7 2.1 %collective-permute-start.10 = (f32[2,128,512]{2,1,0:T(8,128)S(1)}, f32[2,128,512]{2,1,0:T(8,128)S(1)}, u32[]{:S(2)}, u32[]{:S(2)}) collective-permute-start(f32[2,128,512]{2,1,0:T(8,128)S(1)} %get-tuple-element.46), channel_id=1, source_target_pairs={{0,1},{1,0},{2,3},{3,2},{4,5},{5,4},{6,7},{7,6},{8,9},{9,8},{10,11... | collective-permute-start | bytes 1572872 | tf_op jit(solution)/shard_map/ppermute | solution.py:38
  61.9 1.4 collective-permute-done.10.refs_0_
  64.2 1.5 collective-permute-start.12
  65.7 2.5 %collective-permute-start.13 = (f32[128,512]{1,0:T(8,128)S(1)}, f32[128,512]{1,0:T(8,128)S(1)}, u32[]{:S(2)}, u32[]{:S(2)}) collective-permute-start(f32[128,512]{1,0:T(8,128)S(1)} %get-tuple-element.50), channel_id=1, source_target_pairs={{0,4},{1,5},{2,6},{3,7},{4,0},{5,1},{6,2},{7,3},{8,12},{9,13},{10,... | collective-permute-start | bytes 786440 | tf_op jit(solution)/shard_map/ppermute | solution.py:47
  68.1 1.2 collective-permute-start.14
  69.3 12.8 %collective-permute-done.15.refs_5_.refs_3_.refs_6_ = f32[648,512]{1,0:T(8,128)S(1)} collective-permute-done((f32[648,512]{1,0:T(8,128)S(1)}, f32[648,512]{1,0:T(8,128)S(1)}, u32[]{:S(2)}, u32[]{:S(2)}) %collective-permute-start.15) | collective-permute-done | bytes 1327136 | tf_op jit(solution)/shard_map/ppermute | solution.py:34
  82.2 2.7 %collective-permute-start.17 = (f32[216,512]{1,0:T(8,128)S(1)}, f32[216,512]{1,0:T(8,128)S(1)}, u32[]{:S(2)}, u32[]{:S(2)}) collective-permute-start(f32[216,512]{1,0:T(8,128)S(1)} %message.1.mine_ref), channel_id=1, source_target_pairs={{0,8},{1,9},{2,10},{3,11},{4,12},{5,13},{6,14},{7,15},{8,0},{9,1},... | collective-permute-start | bytes 1327112 | tf_op jit(solution)/shard_map/ppermute | solution.py:42
  84.9 9.3 %collective-permute-done.17.got_ref = f32[216,512]{1,0:T(8,128)S(1)} collective-permute-done((f32[216,512]{1,0:T(8,128)S(1)}, f32[216,512]{1,0:T(8,128)S(1)}, u32[]{:S(2)}, u32[]{:S(2)}) %collective-permute-start.17) | collective-permute-done | bytes 442400 | tf_op jit(solution)/shard_map/ppermute | solution.py:42
  94.3 1.0 merge.1
  95.3 3.6 %collective-permute-start.22 = (f32[64,512]{1,0:T(8,128)S(1)}, f32[64,512]{1,0:T(8,128)S(1)}, u32[]{:S(2)}, u32[]{:S(2)}) collective-permute-start(f32[64,512]{1,0:T(8,128)S(1)} %get-tuple-element.58), channel_id=1, source_target_pairs={{0,240},{16,0},{32,16},{48,32},{64,48},{80,64},{96,80},{112,96},{1... | collective-permute-start | bytes 393224 | tf_op jit(solution)/shard_map/ppermute | solution.py:34
  98.9 1.2 collective-permute-start.18
  100.1 2.5 %collective-permute-start.19 = (f32[192,512]{1,0:T(8,128)S(1)}, f32[192,512]{1,0:T(8,128)S(1)}, u32[]{:S(2)}, u32[]{:S(2)}) collective-permute-start(f32[192,512]{1,0:T(8,128)S(1)} %get-tuple-element.53.refs_0_), channel_id=1, source_target_pairs={{0,4},{1,5},{2,6},{3,7},{4,0},{5,1},{6,2},{7,3},{8,12},{9,13},{10,... | collective-permute-start | bytes 1179656 | tf_op jit(solution)/shard_map/ppermute | solution.py:47
  102.6 1.2 collective-permute-start.20
  103.8 3.6 %collective-permute-start.24 = (f32[128,512]{1,0:T(8,128)S(1)}, f32[128,512]{1,0:T(8,128)S(1)}, u32[]{:S(2)}, u32[]{:S(2)}) collective-permute-start(f32[128,512]{1,0:T(8,128)S(1)} %get-tuple-element.63), channel_id=1, source_target_pairs={{0,240},{16,0},{32,16},{48,32},{64,48},{80,64},{96,80},{112,96},{1... | collective-permute-start | bytes 786440 | tf_op jit(solution)/shard_map/ppermute | solution.py:34
  107.4 3.8 %presplit.1 = (bf16[1024,3072]{1,0:T(8,128)(2,1)S(1)}, bf16[1024,1024]{1,0:T(8,128)(2,1)S(1)}) custom-call(f32[1024,512]{1,0:T(8,128)S(1)} %copy-done.4, f32[1024,512]{1,0:T(8,128)} %collective-permute-done.8.prev_ref, f32[1024,512]{1,0:T(8,128)} %collective-permute-done.9.next_ref, f32[1024,512]{1,0:T(8,128)S(1)} %copy-done.1, ...), custom_call_target="tpu_custom_call" | custom-call | flops 1 | bytes 1 | tf_op jit(solution)/shard_map/presplit/pallas_call | solution.py:441
  111.2 6.2 %collective-permute-done.19.refs_2_ = f32[192,512]{1,0:T(8,128)S(1)} collective-permute-done((f32[192,512]{1,0:T(8,128)S(1)}, f32[192,512]{1,0:T(8,128)S(1)}, u32[]{:S(2)}, u32[]{:S(2)}) %collective-permute-start.19) | collective-permute-done | bytes 393248 | tf_op jit(solution)/shard_map/ppermute | solution.py:47
  117.4 1.4 collective-permute-done.20.refs_3_
  118.9 2.3 %collective-permute-start.25 = (f32[4,192,512]{2,1,0:T(8,128)S(1)}, f32[4,192,512]{2,1,0:T(8,128)S(1)}, u32[]{:S(2)}, u32[]{:S(2)}) collective-permute-start(f32[4,192,512]{2,1,0:T(8,128)S(1)} %pack.2.mine_ref), channel_id=1, source_target_pairs={{0,1},{1,0},{2,3},{3,2},{4,5},{5,4},{6,7},{7,6},{8,9},{9,8},{10,11... | collective-permute-start | bytes 4718600 | tf_op jit(solution)/shard_map/ppermute | solution.py:38
  121.3 3.6 %collective-permute-start.30 = (f32[256,512]{1,0:T(8,128)S(1)}, f32[256,512]{1,0:T(8,128)S(1)}, u32[]{:S(2)}, u32[]{:S(2)}) collective-permute-start(f32[256,512]{1,0:T(8,128)S(1)} %get-tuple-element.67), channel_id=1, source_target_pairs={{0,240},{16,0},{32,16},{48,32},{64,48},{80,64},{96,80},{112,96},{1... | collective-permute-start | bytes 1572872 | tf_op jit(solution)/shard_map/ppermute | solution.py:34
  124.8 1.1 collective-permute-start.26
  125.9 2.1 %collective-permute-start.27 = (f32[128,512]{1,0:T(8,128)S(1)}, f32[128,512]{1,0:T(8,128)S(1)}, u32[]{:S(2)}, u32[]{:S(2)}) collective-permute-start(f32[128,512]{1,0:T(8,128)S(1)} %get-tuple-element.61.refs_0_), channel_id=1, source_target_pairs={{0,4},{1,5},{2,6},{3,7},{4,0},{5,1},{6,2},{7,3},{8,12},{9,13},{10,... | collective-permute-start | bytes 786440 | tf_op jit(solution)/shard_map/ppermute | solution.py:47
  128.0 1.3 collective-permute-start.28
  129.3 8.2 %finish_a.1 = (f32[1024,512]{1,0:T(8,128)}, f32[8,512]{1,0:T(8,128)S(1)}) custom-call(s32[2]{0:T(128)S(1)} %pad_add_fusion.at_ref, f32[4,192,512]{2,1,0:T(8,128)S(1)} %pack.2.mine_ref, f32[4,192,512]{2,1,0:T(8,128)S(1)} %collective-permute-done.25.other_ref, f32[8,512]{1,0:T(8,128)S(1)} %get-tuple-element.54.f_ref.refs_0_.facts_ref, ...), custom_call_target="tpu_custom_call" | custom-call | flops 1 | bytes 1 | tf_op jit(solution)/shard_map/finish_a/pallas_call | solution.py:491
  137.5 1.8 %collective-permute-done.27.refs_2_ = f32[128,512]{1,0:T(8,128)S(1)} collective-permute-done((f32[128,512]{1,0:T(8,128)S(1)}, f32[128,512]{1,0:T(8,128)S(1)}, u32[]{:S(2)}, u32[]{:S(2)}) %collective-permute-start.27) | collective-permute-done | bytes 262176 | tf_op jit(solution)/shard_map/ppermute | solution.py:47
  139.5 1.6 %collective-permute-start.31 = (f32[4,128,512]{2,1,0:T(8,128)S(1)}, f32[4,128,512]{2,1,0:T(8,128)S(1)}, u32[]{:S(2)}, u32[]{:S(2)}) collective-permute-start(f32[4,128,512]{2,1,0:T(8,128)S(1)} %pack.3.refs_0_.mine_ref), channel_id=1, source_target_pairs={{0,1},{1,0},{2,3},{3,2},{4,5},{5,4},{6,7},{7,6},{8,9},{9,8},{10,11... | collective-permute-start | bytes 3145736 | tf_op jit(solution)/shard_map/ppermute | solution.py:38
  141.2 3.1 %own_b.1 = (f32[1024,512]{1,0:T(8,128)S(1)}, f32[8,512]{1,0:T(8,128)S(1)}) custom-call(s32[2]{0:T(128)S(1)} %pad_add_fusion.at_ref, f32[4,192,512]{2,1,0:T(8,128)S(1)} %pack.2.mine_ref, f32[4,192,512]{2,1,0:T(8,128)S(1)} %collective-permute-done.25.other_ref, f32[8,512]{1,0:T(8,128)S(1)} %get-tuple-element.54.f_ref.refs_0_.facts_ref, ...), custom_call_target="tpu_custom_call" | custom-call | flops 1 | bytes 1 | tf_op jit(solution)/shard_map/own_b/pallas_call | solution.py:524
  144.3 6.7 %finish_b.1 = f32[1024,512]{1,0:T(8,128)} custom-call(s32[2]{0:T(128)S(1)} %pad_add_fusion.at_ref, f32[4,128,512]{2,1,0:T(8,128)S(1)} %pack.3.refs_0_.mine_ref, f32[4,128,512]{2,1,0:T(8,128)S(1)} %collective-permute-done.31.other_ref, f32[8,512]{1,0:T(8,128)S(1)} %get-tuple-element.54.f_ref.refs_0_.facts_ref, f32[8,512]{1,0:T(8,128)S(1)} %get-tuple-element.55.pf_ref.refs_1_, ...), custom_call_target="tpu_custom_call" | custom-call | flops 1 | bytes 1 | tf_op jit(solution)/shard_map/finish_b/pallas_call | solution.py:579
  (43 shorter events, 2.6 us)
Async XLA Ops:
  0.6 53.2 %collective-permute-start.8 = (f32[1024,512]{1,0:T(8,128)}, f32[1024,512]{1,0:T(8,128)}, u32[]{:S(2)}, u32[]{:S(2)}) collective-permute-start(f32[1024,512]{1,0:T(8,128)} %refs_2_.1), channel_id=1, source_target_pairs={{0,16},{16,32},{32,48},{48,64},{64,80},{80,96},{96,112},{112,128},... | collective-permute-start | bytes 6291464 | tf_op jit(solution)/shard_map/ppermute | solution.py:34
  3.2 50.6 %collective-permute-start.9 = (f32[1024,512]{1,0:T(8,128)}, f32[1024,512]{1,0:T(8,128)}, u32[]{:S(2)}, u32[]{:S(2)}) collective-permute-start(f32[1024,512]{1,0:T(8,128)} %refs_2_.1), channel_id=1, source_target_pairs={{0,240},{16,0},{32,16},{48,32},{64,48},{80,64},{96,80},{112,96},{1... | collective-permute-start | bytes 6291464 | tf_op jit(solution)/shard_map/ppermute | solution.py:34
  8.2 1.6 %copy-start = (f32[1024,512]{1,0:T(8,128)S(1)}, f32[1024,512]{1,0:T(8,128)}, u32[]{:S(2)}) copy-start(f32[1024,512]{1,0:T(8,128)} %refs_3_.1) | copy-start | bytes 6291460
  9.8 1.6 %copy-start.2 = (f32[1024,512]{1,0:T(8,128)S(1)}, f32[1024,512]{1,0:T(8,128)}, u32[]{:S(2)}) copy-start(f32[1024,512]{1,0:T(8,128)} %refs_2_.1) | copy-start | bytes 6291460
  11.4 9.2 %copy-start.1 = (f32[1024,512]{1,0:T(8,128)S(1)}, f32[1024,512]{1,0:T(8,128)}, u32[]{:S(2)}) copy-start(f32[1024,512]{1,0:T(8,128)} %refs_3_.1) | copy-start | bytes 6291460
  12.0 1.9 %collective-permute-start = (f32[8,512]{1,0:T(8,128)S(1)}, f32[8,512]{1,0:T(8,128)S(1)}, u32[]{:S(2)}, u32[]{:S(2)}) collective-permute-start(f32[8,512]{1,0:T(8,128)S(1)} %sums.1), channel_id=1, source_target_pairs={{0,1},{1,0},{2,3},{3,2},{4,5},{5,4},{6,7},{7,6},{8,9},{9,8},{10,11... | collective-permute-start | bytes 49160 | tf_op jit(solution)/shard_map/ppermute | solution.py:38
  13.9 4.9 %collective-permute-start.1 = (f32[8,512]{1,0:T(8,128)S(1)}, f32[8,512]{1,0:T(8,128)S(1)}, u32[]{:S(2)}, u32[]{:S(2)}) collective-permute-start(f32[8,512]{1,0:T(8,128)S(1)} %add.3.refs_0_), channel_id=1, source_target_pairs={{0,2},{1,3},{2,4},{3,5},{4,6},{5,7},{6,0},{7,1},{8,10},{9,11},{10,... | collective-permute-start | bytes 49160 | tf_op jit(solution)/shard_map/ppermute | solution.py:47
  15.1 4.5 %collective-permute-start.2 = (f32[8,512]{1,0:T(8,128)S(1)}, f32[8,512]{1,0:T(8,128)S(1)}, u32[]{:S(2)}, u32[]{:S(2)}) collective-permute-start(f32[8,512]{1,0:T(8,128)S(1)} %add.3.refs_0_), channel_id=1, source_target_pairs={{0,4},{1,5},{2,6},{3,7},{4,0},{5,1},{6,2},{7,3},{8,12},{9,13},{10,... | collective-permute-start | bytes 49160 | tf_op jit(solution)/shard_map/ppermute | solution.py:47
  17.6 3.0 %collective-permute-start.3 = (f32[8,512]{1,0:T(8,128)S(1)}, f32[8,512]{1,0:T(8,128)S(1)}, u32[]{:S(2)}, u32[]{:S(2)}) collective-permute-start(f32[8,512]{1,0:T(8,128)S(1)} %add.3.refs_0_), channel_id=1, source_target_pairs={{0,6},{1,7},{2,0},{3,1},{4,2},{5,3},{6,4},{7,5},{8,14},{9,15},{10,... | collective-permute-start | bytes 49160 | tf_op jit(solution)/shard_map/ppermute | solution.py:47
  20.6 1.6 %copy-start.3 = (f32[1024,512]{1,0:T(8,128)S(1)}, f32[1024,512]{1,0:T(8,128)}, u32[]{:S(2)}) copy-start(f32[1024,512]{1,0:T(8,128)} %refs_2_.1) | copy-start | bytes 6291460
  27.6 3.3 %collective-permute-start.4 = (f32[4,64,512]{2,1,0:T(8,128)S(1)}, f32[4,64,512]{2,1,0:T(8,128)S(1)}, u32[]{:S(2)}, u32[]{:S(2)}) collective-permute-start(f32[4,64,512]{2,1,0:T(8,128)S(1)} %get-tuple-element.37), channel_id=1, source_target_pairs={{0,1},{1,0},{2,3},{3,2},{4,5},{5,4},{6,7},{7,6},{8,9},{9,8},{10,11... | collective-permute-start | bytes 1572872 | tf_op jit(solution)/shard_map/ppermute | solution.py:38
  30.9 6.1 %collective-permute-start.5 = (f32[64,512]{1,0:T(8,128)S(1)}, f32[64,512]{1,0:T(8,128)S(1)}, u32[]{:S(2)}, u32[]{:S(2)}) collective-permute-start(f32[64,512]{1,0:T(8,128)S(1)} %get-tuple-element.39), channel_id=1, source_target_pairs={{0,2},{1,3},{2,4},{3,5},{4,6},{5,7},{6,0},{7,1},{8,10},{9,11},{10,... | collective-permute-start | bytes 393224 | tf_op jit(solution)/shard_map/ppermute | solution.py:47
  31.0 9.7 %collective-permute-start.6 = (f32[64,512]{1,0:T(8,128)S(1)}, f32[64,512]{1,0:T(8,128)S(1)}, u32[]{:S(2)}, u32[]{:S(2)}) collective-permute-start(f32[64,512]{1,0:T(8,128)S(1)} %get-tuple-element.40), channel_id=1, source_target_pairs={{0,4},{1,5},{2,6},{3,7},{4,0},{5,1},{6,2},{7,3},{8,12},{9,13},{10,... | collective-permute-start | bytes 393224 | tf_op jit(solution)/shard_map/ppermute | solution.py:47
  34.6 6.2 %collective-permute-start.7 = (f32[64,512]{1,0:T(8,128)S(1)}, f32[64,512]{1,0:T(8,128)S(1)}, u32[]{:S(2)}, u32[]{:S(2)}) collective-permute-start(f32[64,512]{1,0:T(8,128)S(1)} %get-tuple-element.41), channel_id=1, source_target_pairs={{0,6},{1,7},{2,0},{3,1},{4,2},{5,3},{6,4},{7,5},{8,14},{9,15},{10,... | collective-permute-start | bytes 393224 | tf_op jit(solution)/shard_map/ppermute | solution.py:47
  40.9 41.3 %collective-permute-start.15 = (f32[648,512]{1,0:T(8,128)S(1)}, f32[648,512]{1,0:T(8,128)S(1)}, u32[]{:S(2)}, u32[]{:S(2)}) collective-permute-start(f32[648,512]{1,0:T(8,128)S(1)} %get-tuple-element.52), channel_id=1, source_target_pairs={{0,16},{16,32},{32,48},{48,64},{64,80},{80,96},{96,112},{112,128},... | collective-permute-start | bytes 3981320 | tf_op jit(solution)/shard_map/ppermute | solution.py:34
  40.9 41.2 %collective-permute-start.16 = (f32[648,512]{1,0:T(8,128)S(1)}, f32[648,512]{1,0:T(8,128)S(1)}, u32[]{:S(2)}, u32[]{:S(2)}) collective-permute-start(f32[648,512]{1,0:T(8,128)S(1)} %get-tuple-element.52), channel_id=1, source_target_pairs={{0,240},{16,0},{32,16},{48,32},{64,48},{80,64},{96,80},{112,96},{1... | collective-permute-start | bytes 3981320 | tf_op jit(solution)/shard_map/ppermute | solution.py:34
  59.7 3.7 %collective-permute-start.10 = (f32[2,128,512]{2,1,0:T(8,128)S(1)}, f32[2,128,512]{2,1,0:T(8,128)S(1)}, u32[]{:S(2)}, u32[]{:S(2)}) collective-permute-start(f32[2,128,512]{2,1,0:T(8,128)S(1)} %get-tuple-element.46), channel_id=1, source_target_pairs={{0,1},{1,0},{2,3},{3,2},{4,5},{5,4},{6,7},{7,6},{8,9},{9,8},{10,11... | collective-permute-start | bytes 1572872 | tf_op jit(solution)/shard_map/ppermute | solution.py:38
  61.8 2.3 %collective-permute-start.11 = (f32[2,128,512]{2,1,0:T(8,128)S(1)}, f32[2,128,512]{2,1,0:T(8,128)S(1)}, u32[]{:S(2)}, u32[]{:S(2)}) collective-permute-start(f32[2,128,512]{2,1,0:T(8,128)S(1)} %get-tuple-element.47), channel_id=1, source_target_pairs={{0,1},{1,0},{2,3},{3,2},{4,5},{5,4},{6,7},{7,6},{8,9},{9,8},{10,11... | collective-permute-start | bytes 1572872 | tf_op jit(solution)/shard_map/ppermute | solution.py:38
  64.2 17.9 %collective-permute-start.12 = (f32[128,512]{1,0:T(8,128)S(1)}, f32[128,512]{1,0:T(8,128)S(1)}, u32[]{:S(2)}, u32[]{:S(2)}) collective-permute-start(f32[128,512]{1,0:T(8,128)S(1)} %get-tuple-element.49), channel_id=1, source_target_pairs={{0,2},{1,3},{2,4},{3,5},{4,6},{5,7},{6,0},{7,1},{8,10},{9,11},{10,... | collective-permute-start | bytes 786440 | tf_op jit(solution)/shard_map/ppermute | solution.py:47
  65.7 16.4 %collective-permute-start.13 = (f32[128,512]{1,0:T(8,128)S(1)}, f32[128,512]{1,0:T(8,128)S(1)}, u32[]{:S(2)}, u32[]{:S(2)}) collective-permute-start(f32[128,512]{1,0:T(8,128)S(1)} %get-tuple-element.50), channel_id=1, source_target_pairs={{0,4},{1,5},{2,6},{3,7},{4,0},{5,1},{6,2},{7,3},{8,12},{9,13},{10,... | collective-permute-start | bytes 786440 | tf_op jit(solution)/shard_map/ppermute | solution.py:47
  68.1 14.0 %collective-permute-start.14 = (f32[128,512]{1,0:T(8,128)S(1)}, f32[128,512]{1,0:T(8,128)S(1)}, u32[]{:S(2)}, u32[]{:S(2)}) collective-permute-start(f32[128,512]{1,0:T(8,128)S(1)} %get-tuple-element.51), channel_id=1, source_target_pairs={{0,6},{1,7},{2,0},{3,1},{4,2},{5,3},{6,4},{7,5},{8,14},{9,15},{10,... | collective-permute-start | bytes 786440 | tf_op jit(solution)/shard_map/ppermute | solution.py:47
  82.2 25.2 %copy-start.4 = (f32[1024,512]{1,0:T(8,128)S(1)}, f32[1024,512]{1,0:T(8,128)}, u32[]{:S(2)}) copy-start(f32[1024,512]{1,0:T(8,128)} %refs_2_.1) | copy-start | bytes 6291460
  82.2 12.0 %collective-permute-start.17 = (f32[216,512]{1,0:T(8,128)S(1)}, f32[216,512]{1,0:T(8,128)S(1)}, u32[]{:S(2)}, u32[]{:S(2)}) collective-permute-start(f32[216,512]{1,0:T(8,128)S(1)} %message.1.mine_ref), channel_id=1, source_target_pairs={{0,8},{1,9},{2,10},{3,11},{4,12},{5,13},{6,14},{7,15},{8,0},{9,1},... | collective-permute-start | bytes 1327112 | tf_op jit(solution)/shard_map/ppermute | solution.py:42
  95.2 8.5 %collective-permute-start.21 = (f32[64,512]{1,0:T(8,128)S(1)}, f32[64,512]{1,0:T(8,128)S(1)}, u32[]{:S(2)}, u32[]{:S(2)}) collective-permute-start(f32[64,512]{1,0:T(8,128)S(1)} %get-tuple-element.57), channel_id=1, source_target_pairs={{0,16},{16,32},{32,48},{48,64},{64,80},{80,96},{96,112},{112,128},... | collective-permute-start | bytes 393224 | tf_op jit(solution)/shard_map/ppermute | solution.py:34
  95.3 8.4 %collective-permute-start.22 = (f32[64,512]{1,0:T(8,128)S(1)}, f32[64,512]{1,0:T(8,128)S(1)}, u32[]{:S(2)}, u32[]{:S(2)}) collective-permute-start(f32[64,512]{1,0:T(8,128)S(1)} %get-tuple-element.58), channel_id=1, source_target_pairs={{0,240},{16,0},{32,16},{48,32},{64,48},{80,64},{96,80},{112,96},{1... | collective-permute-start | bytes 393224 | tf_op jit(solution)/shard_map/ppermute | solution.py:34
  98.9 12.3 %collective-permute-start.18 = (f32[192,512]{1,0:T(8,128)S(1)}, f32[192,512]{1,0:T(8,128)S(1)}, u32[]{:S(2)}, u32[]{:S(2)}) collective-permute-start(f32[192,512]{1,0:T(8,128)S(1)} %get-tuple-element.53.refs_0_), channel_id=1, source_target_pairs={{0,2},{1,3},{2,4},{3,5},{4,6},{5,7},{6,0},{7,1},{8,10},{9,11},{10,... | collective-permute-start | bytes 1179656 | tf_op jit(solution)/shard_map/ppermute | solution.py:47
  100.1 17.3 %collective-permute-start.19 = (f32[192,512]{1,0:T(8,128)S(1)}, f32[192,512]{1,0:T(8,128)S(1)}, u32[]{:S(2)}, u32[]{:S(2)}) collective-permute-start(f32[192,512]{1,0:T(8,128)S(1)} %get-tuple-element.53.refs_0_), channel_id=1, source_target_pairs={{0,4},{1,5},{2,6},{3,7},{4,0},{5,1},{6,2},{7,3},{8,12},{9,13},{10,... | collective-permute-start | bytes 1179656 | tf_op jit(solution)/shard_map/ppermute | solution.py:47
  102.6 16.3 %collective-permute-start.20 = (f32[192,512]{1,0:T(8,128)S(1)}, f32[192,512]{1,0:T(8,128)S(1)}, u32[]{:S(2)}, u32[]{:S(2)}) collective-permute-start(f32[192,512]{1,0:T(8,128)S(1)} %get-tuple-element.53.refs_0_), channel_id=1, source_target_pairs={{0,6},{1,7},{2,0},{3,1},{4,2},{5,3},{6,4},{7,5},{8,14},{9,15},{10,... | collective-permute-start | bytes 1179656 | tf_op jit(solution)/shard_map/ppermute | solution.py:47
  103.7 7.4 %collective-permute-start.23 = (f32[128,512]{1,0:T(8,128)S(1)}, f32[128,512]{1,0:T(8,128)S(1)}, u32[]{:S(2)}, u32[]{:S(2)}) collective-permute-start(f32[128,512]{1,0:T(8,128)S(1)} %get-tuple-element.63), channel_id=1, source_target_pairs={{0,16},{16,32},{32,48},{48,64},{64,80},{80,96},{96,112},{112,128},... | collective-permute-start | bytes 786440 | tf_op jit(solution)/shard_map/ppermute | solution.py:34
  103.8 7.3 %collective-permute-start.24 = (f32[128,512]{1,0:T(8,128)S(1)}, f32[128,512]{1,0:T(8,128)S(1)}, u32[]{:S(2)}, u32[]{:S(2)}) collective-permute-start(f32[128,512]{1,0:T(8,128)S(1)} %get-tuple-element.63), channel_id=1, source_target_pairs={{0,240},{16,0},{32,16},{48,32},{64,48},{80,64},{96,80},{112,96},{1... | collective-permute-start | bytes 786440 | tf_op jit(solution)/shard_map/ppermute | solution.py:34
  118.9 9.1 %collective-permute-start.25 = (f32[4,192,512]{2,1,0:T(8,128)S(1)}, f32[4,192,512]{2,1,0:T(8,128)S(1)}, u32[]{:S(2)}, u32[]{:S(2)}) collective-permute-start(f32[4,192,512]{2,1,0:T(8,128)S(1)} %pack.2.mine_ref), channel_id=1, source_target_pairs={{0,1},{1,0},{2,3},{3,2},{4,5},{5,4},{6,7},{7,6},{8,9},{9,8},{10,11... | collective-permute-start | bytes 4718600 | tf_op jit(solution)/shard_map/ppermute | solution.py:38
  121.2 18.2 %collective-permute-start.29 = (f32[256,512]{1,0:T(8,128)S(1)}, f32[256,512]{1,0:T(8,128)S(1)}, u32[]{:S(2)}, u32[]{:S(2)}) collective-permute-start(f32[256,512]{1,0:T(8,128)S(1)} %get-tuple-element.67), channel_id=1, source_target_pairs={{0,16},{16,32},{32,48},{48,64},{64,80},{80,96},{96,112},{112,128},... | collective-permute-start | bytes 1572872 | tf_op jit(solution)/shard_map/ppermute | solution.py:34
  121.3 18.2 %collective-permute-start.30 = (f32[256,512]{1,0:T(8,128)S(1)}, f32[256,512]{1,0:T(8,128)S(1)}, u32[]{:S(2)}, u32[]{:S(2)}) collective-permute-start(f32[256,512]{1,0:T(8,128)S(1)} %get-tuple-element.67), channel_id=1, source_target_pairs={{0,240},{16,0},{32,16},{48,32},{64,48},{80,64},{96,80},{112,96},{1... | collective-permute-start | bytes 1572872 | tf_op jit(solution)/shard_map/ppermute | solution.py:34
  124.8 12.7 %collective-permute-start.26 = (f32[128,512]{1,0:T(8,128)S(1)}, f32[128,512]{1,0:T(8,128)S(1)}, u32[]{:S(2)}, u32[]{:S(2)}) collective-permute-start(f32[128,512]{1,0:T(8,128)S(1)} %get-tuple-element.61.refs_0_), channel_id=1, source_target_pairs={{0,2},{1,3},{2,4},{3,5},{4,6},{5,7},{6,0},{7,1},{8,10},{9,11},{10,... | collective-permute-start | bytes 786440 | tf_op jit(solution)/shard_map/ppermute | solution.py:47
  125.9 13.5 %collective-permute-start.27 = (f32[128,512]{1,0:T(8,128)S(1)}, f32[128,512]{1,0:T(8,128)S(1)}, u32[]{:S(2)}, u32[]{:S(2)}) collective-permute-start(f32[128,512]{1,0:T(8,128)S(1)} %get-tuple-element.61.refs_0_), channel_id=1, source_target_pairs={{0,4},{1,5},{2,6},{3,7},{4,0},{5,1},{6,2},{7,3},{8,12},{9,13},{10,... | collective-permute-start | bytes 786440 | tf_op jit(solution)/shard_map/ppermute | solution.py:47
  128.0 11.4 %collective-permute-start.28 = (f32[128,512]{1,0:T(8,128)S(1)}, f32[128,512]{1,0:T(8,128)S(1)}, u32[]{:S(2)}, u32[]{:S(2)}) collective-permute-start(f32[128,512]{1,0:T(8,128)S(1)} %get-tuple-element.61.refs_0_), channel_id=1, source_target_pairs={{0,6},{1,7},{2,0},{3,1},{4,2},{5,3},{6,4},{7,5},{8,14},{9,15},{10,... | collective-permute-start | bytes 786440 | tf_op jit(solution)/shard_map/ppermute | solution.py:47
  139.5 4.7 %collective-permute-start.31 = (f32[4,128,512]{2,1,0:T(8,128)S(1)}, f32[4,128,512]{2,1,0:T(8,128)S(1)}, u32[]{:S(2)}, u32[]{:S(2)}) collective-permute-start(f32[4,128,512]{2,1,0:T(8,128)S(1)} %pack.3.refs_0_.mine_ref), channel_id=1, source_target_pairs={{0,1},{1,0},{2,3},{3,2},{4,5},{5,4},{6,7},{7,6},{8,9},{9,8},{10,11... | collective-permute-start | bytes 3145736 | tf_op jit(solution)/shard_map/ppermute | solution.py:38

commit v10 on v9

--- a/solution.py
+++ b/solution.py
@@ -251,12 +251,15 @@
     last = first + side[0].shape[0]
     out_ref[0:first, :] = own_ref[...]
     out_ref[first:last, :] = side[0][...] + side[1][...] + side[2][...] + side[3][...]
-    for i, ref in enumerate(facts):
-        out_ref[last + 8 * i : last + 8 * i + 8, :] = ref[...]
+    out_ref[last : last + 8, :] = facts[0][...]
+    for i, ref in enumerate(facts[1:]):
+        for j, row in enumerate((0, 2, 4, 5)):
+            at = last + 8 + 4 * i + j
+            out_ref[at : at + 1, :] = ref[row : row + 1, :]
 
 
 def message(own, side, facts, prev_top, next_top):
-    rows = own.shape[0] + side[0].shape[0] + 24
+    rows = own.shape[0] + side[0].shape[0] + 16
     width = own.shape[1]
     below = pl.BlockSpec((8, width), lambda i: (top_rows // 8, 0))
     wholes = [pl.BlockSpec(block.shape, lambda i: (0, 0)) for block in (own, *side, facts)]
@@ -302,13 +305,20 @@
     return cols_ref[pl.ds(first, rows), :]
 
 
+def lengthened(short):
+    mean, square = short[0:2], short[2:4]
+    scale = jnp.sqrt(jnp.maximum(square - mean * mean, 0.0) + epsilon)
+    return jnp.concatenate([mean[0:1], mean[0:1], mean[1:2], mean[1:2], square, scale], axis=0)
+
+
 def merge_kernel(half_rows, at_ref, mine_ref, got_ref, *refs):
     left_ref, right_ref, trio_ref, *facts_refs, cols_ref = refs[-7:]
     rows = left_ref.shape[0]
-    facts = [
-        (mine_ref[first : first + 8, :], got_ref[first : first + 8, :])
-        for first in (3 * rows, 3 * rows + 8, 3 * rows + 16)
-    ]
+    first = 3 * rows
+    facts = [(mine_ref[first : first + 8, :], got_ref[first : first + 8, :])]
+    for first in (3 * rows + 8, 3 * rows + 12):
+        short = mine_ref[first : first + 4, :], got_ref[first : first + 4, :]
+        facts.append(tuple(lengthened(rows) for rows in short))
     full = [full_facts(*both) for both in facts]
     for ref, values in zip(facts_refs, full):
         for i in range(8):
@@ -334,7 +344,7 @@
 
 def merge(at, mine, got, half_rows):
     width = mine.shape[1]
-    rows = (mine.shape[0] - 24) // 3
+    rows = (mine.shape[0] - 16) // 3
     return call(
         functools.partial(merge_kernel, half_rows),
         in_specs=[smem_spec] + [vmem_spec] * 2,

time: 151 us -> 151 us (level)
  no operation moved by 1% of the time
where the time goes in v10:
time: 151 us
  starting transfers between devices  56.6 us (37%)
  waiting for transfers between devices  53.1 us (35%)
  Pallas kernels  35.3 us (23%)
  local copies, waits for them, and re-layouts  4.78 us (3%)
    ppermute x15, starting transfers between devices, to_x(): return lax.ppermute(block, 'row', pairs)  22.8 us
    ppermute x10, waiting for transfers between devices, across(): lax.ppermute(block, 'grp', [(i, (i + shift) % count) for i in range(count)])  22.1 us
    ppermute x10, starting transfers between devices, across(): lax.ppermute(block, 'grp', [(i, (i + shift) % count) for i in range(count)])  22.1 us
    ppermute x15, waiting for transfers between devices, to_x(): return lax.ppermute(block, 'row', pairs)  17.5 us
    ppermute x6, starting transfers between devices, to_core(): return lax.ppermute(block, 'row', [(i, i ^ 1) for i in range(16)])  8.99 us
    ppermute x1, waiting for transfers between devices, to_y(): return lax.ppermute(block, 'row', [(i, i ^ 8) for i in range(16)])  8.97 us
    pallas_call x1, Pallas kernels, finish_a(): call(finish_a_kernel, mib=40, grid=(rows // tile,), in_specs=[smem_spec,...  8.24 us
    pallas_call x1, Pallas kernels, finish_b(): call(functools.partial(finish_b_kernel, bounds), mib=24, grid=(rows // ti...  6.75 us
  transfers between devices with their start and end apart: 32, of which 15 were waited for; matrix products, arithmetic and copies ran while one was open for 0% of the time, Pallas kernels for 18%

profile of v10, /device:TPU:1, one launch (start us, length us, event | category | flops | bytes accessed | tf_op | source)
XLA Modules:
  0.0 150.7 jit_solution(9193604956110205812)
XLA Ops:
  0.6 2.5 %collective-permute-start.8 = (f32[1024,512]{1,0:T(8,128)}, f32[1024,512]{1,0:T(8,128)}, u32[]{:S(2)}, u32[]{:S(2)}) collective-permute-start(f32[1024,512]{1,0:T(8,128)} %refs_2_.1), channel_id=1, source_target_pairs={{0,16},{16,32},{32,48},{48,64},{64,80},{80,96},{96,112},{112,128},... | collective-permute-start | bytes 6291464 | tf_op jit(solution)/shard_map/ppermute | solution.py:34
  3.2 5.0 %collective-permute-start.9 = (f32[1024,512]{1,0:T(8,128)}, f32[1024,512]{1,0:T(8,128)}, u32[]{:S(2)}, u32[]{:S(2)}) collective-permute-start(f32[1024,512]{1,0:T(8,128)} %refs_2_.1), channel_id=1, source_target_pairs={{0,240},{16,0},{32,16},{48,32},{64,48},{80,64},{96,80},{112,96},{1... | collective-permute-start | bytes 6291464 | tf_op jit(solution)/shard_map/ppermute | solution.py:34
  8.2 1.6 %copy-done = f32[1024,512]{1,0:T(8,128)S(1)} copy-done((f32[1024,512]{1,0:T(8,128)S(1)}, f32[1024,512]{1,0:T(8,128)}, u32[]{:S(2)}) %copy-start) | copy-done | bytes 2097176
  9.8 1.6 %copy-done.2 = f32[1024,512]{1,0:T(8,128)S(1)} copy-done((f32[1024,512]{1,0:T(8,128)S(1)}, f32[1024,512]{1,0:T(8,128)}, u32[]{:S(2)}) %copy-start.2) | copy-done | bytes 2097176
  12.0 1.0 collective-permute-start
  13.1 0.8 collective-permute-done
  13.9 1.2 collective-permute-start.1
  15.1 2.5 %collective-permute-start.2 = (f32[8,512]{1,0:T(8,128)S(1)}, f32[8,512]{1,0:T(8,128)S(1)}, u32[]{:S(2)}, u32[]{:S(2)}) collective-permute-start(f32[8,512]{1,0:T(8,128)S(1)} %add.3.refs_0_), channel_id=1, source_target_pairs={{0,4},{1,5},{2,6},{3,7},{4,0},{5,1},{6,2},{7,3},{8,12},{9,13},{10,... | collective-permute-start | bytes 49160 | tf_op jit(solution)/shard_map/ppermute | solution.py:47
  17.6 1.2 collective-permute-start.3
  18.8 0.8 collective-permute-done.2.refs_2_
  19.6 0.9 collective-permute-done.3.refs_3_
  20.6 1.6 %copy-done.3 = f32[1024,512]{1,0:T(8,128)S(1)} copy-done((f32[1024,512]{1,0:T(8,128)S(1)}, f32[1024,512]{1,0:T(8,128)}, u32[]{:S(2)}) %copy-start.3) | copy-done | bytes 2097176
  22.2 5.4 %own_corr.1 = (f32[640,512]{1,0:T(8,128)S(1)}, f32[128,512]{1,0:T(8,128)S(1)}, f32[256,512]{1,0:T(8,128)S(1)}, f32[8,512]{1,0:T(8,128)S(1)}, f32[4,64,512]{2,1,0:T(8,128)S(1)}, /*index=5*/f32[4,64,512]{2,1,0:T(8,128)S(1)}) custom-call(s32[2]{0:T(128)S(1)} %pad_add_fusion.at_ref, f32[1024,512]{1,0:T(8,128)S(1)} %copy-done.1, f32[1024,512]{1,0:T(8,128)S(1)} %copy-done.3, ...), custom_call_target="tpu_custom_call" | custom-call | flops 1 | bytes 1 | tf_op jit(solution)/shard_map/own_corr/pallas_call | solution.py:159
  27.6 1.7 %collective-permute-start.4 = (f32[4,64,512]{2,1,0:T(8,128)S(1)}, f32[4,64,512]{2,1,0:T(8,128)S(1)}, u32[]{:S(2)}, u32[]{:S(2)}) collective-permute-start(f32[4,64,512]{2,1,0:T(8,128)S(1)} %get-tuple-element.37), channel_id=1, source_target_pairs={{0,1},{1,0},{2,3},{3,2},{4,5},{5,4},{6,7},{7,6},{8,9},{9,8},{10,11... | collective-permute-start | bytes 1572872 | tf_op jit(solution)/shard_map/ppermute | solution.py:38
  29.3 1.5 %collective-permute-done.4.refs_0_ = f32[4,64,512]{2,1,0:T(8,128)S(1)} collective-permute-done((f32[4,64,512]{2,1,0:T(8,128)S(1)}, f32[4,64,512]{2,1,0:T(8,128)S(1)}, u32[]{:S(2)}, u32[]{:S(2)}) %collective-permute-start.4) | collective-permute-done | bytes 524320 | tf_op jit(solution)/shard_map/ppermute | solution.py:38
  31.0 3.5 %collective-permute-start.6 = (f32[64,512]{1,0:T(8,128)S(1)}, f32[64,512]{1,0:T(8,128)S(1)}, u32[]{:S(2)}, u32[]{:S(2)}) collective-permute-start(f32[64,512]{1,0:T(8,128)S(1)} %get-tuple-element.40), channel_id=1, source_target_pairs={{0,4},{1,5},{2,6},{3,7},{4,0},{5,1},{6,2},{7,3},{8,12},{9,13},{10,... | collective-permute-start | bytes 393224 | tf_op jit(solution)/shard_map/ppermute | solution.py:47
  34.6 2.5 %collective-permute-done.5.refs_1_ = f32[64,512]{1,0:T(8,128)S(1)} collective-permute-done((f32[64,512]{1,0:T(8,128)S(1)}, f32[64,512]{1,0:T(8,128)S(1)}, u32[]{:S(2)}, u32[]{:S(2)}) %collective-permute-start.5) | collective-permute-done | bytes 131104 | tf_op jit(solution)/shard_map/ppermute | solution.py:47
  37.0 3.7 %collective-permute-done.6.refs_2_ = f32[64,512]{1,0:T(8,128)S(1)} collective-permute-done((f32[64,512]{1,0:T(8,128)S(1)}, f32[64,512]{1,0:T(8,128)S(1)}, u32[]{:S(2)}, u32[]{:S(2)}) %collective-permute-start.6) | collective-permute-done | bytes 131104 | tf_op jit(solution)/shard_map/ppermute | solution.py:47
  40.9 3.6 %collective-permute-start.16 = (f32[648,512]{1,0:T(8,128)S(1)}, f32[648,512]{1,0:T(8,128)S(1)}, u32[]{:S(2)}, u32[]{:S(2)}) collective-permute-start(f32[648,512]{1,0:T(8,128)S(1)} %get-tuple-element.52), channel_id=1, source_target_pairs={{0,240},{16,0},{32,16},{48,32},{64,48},{80,64},{96,80},{112,96},{1... | collective-permute-start | bytes 3981320 | tf_op jit(solution)/shard_map/ppermute | solution.py:34
  44.5 9.3 %collective-permute-done.8.prev_ref = f32[1024,512]{1,0:T(8,128)} collective-permute-done((f32[1024,512]{1,0:T(8,128)}, f32[1024,512]{1,0:T(8,128)}, u32[]{:S(2)}, u32[]{:S(2)}) %collective-permute-start.8) | collective-permute-done | bytes 2097184 | tf_op jit(solution)/shard_map/ppermute | solution.py:34
  53.8 5.9 %side_corr.1 = (f32[4,128,512]{2,1,0:T(8,128)S(1)}, f32[2,128,512]{2,1,0:T(8,128)S(1)}, f32[2,128,512]{2,1,0:T(8,128)S(1)}) custom-call(s32[2]{0:T(128)S(1)} %pad_add_fusion.at_ref, f32[1024,512]{1,0:T(8,128)S(1)} %copy-done.1, f32[1024,512]{1,0:T(8,128)} %collective-permute-done.8.prev_ref, f32[1024,512]{1,0:T(8,128)} %collective-permute-done.9.next_ref, ...), custom_call_target="tpu_custom_call" | custom-call | flops 1 | bytes 1 | tf_op jit(solution)/shard_map/side_corr/pallas_call | solution.py:200
  59.7 2.1 %collective-permute-start.10 = (f32[2,128,512]{2,1,0:T(8,128)S(1)}, f32[2,128,512]{2,1,0:T(8,128)S(1)}, u32[]{:S(2)}, u32[]{:S(2)}) collective-permute-start(f32[2,128,512]{2,1,0:T(8,128)S(1)} %get-tuple-element.46), channel_id=1, source_target_pairs={{0,1},{1,0},{2,3},{3,2},{4,5},{5,4},{6,7},{7,6},{8,9},{9,8},{10,11... | collective-permute-start | bytes 1572872 | tf_op jit(solution)/shard_map/ppermute | solution.py:38
  61.9 1.4 collective-permute-done.10.refs_0_
  64.2 1.5 collective-permute-start.12
  65.7 2.5 %collective-permute-start.13 = (f32[128,512]{1,0:T(8,128)S(1)}, f32[128,512]{1,0:T(8,128)S(1)}, u32[]{:S(2)}, u32[]{:S(2)}) collective-permute-start(f32[128,512]{1,0:T(8,128)S(1)} %get-tuple-element.50), channel_id=1, source_target_pairs={{0,4},{1,5},{2,6},{3,7},{4,0},{5,1},{6,2},{7,3},{8,12},{9,13},{10,... | collective-permute-start | bytes 786440 | tf_op jit(solution)/shard_map/ppermute | solution.py:47
  68.1 1.2 collective-permute-start.14
  69.3 12.8 %collective-permute-done.15.refs_5_.refs_3_.refs_6_ = f32[648,512]{1,0:T(8,128)S(1)} collective-permute-done((f32[648,512]{1,0:T(8,128)S(1)}, f32[648,512]{1,0:T(8,128)S(1)}, u32[]{:S(2)}, u32[]{:S(2)}) %collective-permute-start.15) | collective-permute-done | bytes 1327136 | tf_op jit(solution)/shard_map/ppermute | solution.py:34
  82.2 2.7 %collective-permute-start.17 = (f32[208,512]{1,0:T(8,128)S(1)}, f32[208,512]{1,0:T(8,128)S(1)}, u32[]{:S(2)}, u32[]{:S(2)}) collective-permute-start(f32[208,512]{1,0:T(8,128)S(1)} %message.1.mine_ref), channel_id=1, source_target_pairs={{0,8},{1,9},{2,10},{3,11},{4,12},{5,13},{6,14},{7,15},{8,0},{9,1},... | collective-permute-start | bytes 1277960 | tf_op jit(solution)/shard_map/ppermute | solution.py:42
  84.9 9.0 %collective-permute-done.17.got_ref = f32[208,512]{1,0:T(8,128)S(1)} collective-permute-done((f32[208,512]{1,0:T(8,128)S(1)}, f32[208,512]{1,0:T(8,128)S(1)}, u32[]{:S(2)}, u32[]{:S(2)}) %collective-permute-start.17) | collective-permute-done | bytes 426016 | tf_op jit(solution)/shard_map/ppermute | solution.py:42
  93.9 1.0 merge.1
  95.0 3.6 %collective-permute-start.22 = (f32[64,512]{1,0:T(8,128)S(1)}, f32[64,512]{1,0:T(8,128)S(1)}, u32[]{:S(2)}, u32[]{:S(2)}) collective-permute-start(f32[64,512]{1,0:T(8,128)S(1)} %get-tuple-element.58), channel_id=1, source_target_pairs={{0,240},{16,0},{32,16},{48,32},{64,48},{80,64},{96,80},{112,96},{1... | collective-permute-start | bytes 393224 | tf_op jit(solution)/shard_map/ppermute | solution.py:34
  98.6 1.2 collective-permute-start.18
  99.8 2.5 %collective-permute-start.19 = (f32[192,512]{1,0:T(8,128)S(1)}, f32[192,512]{1,0:T(8,128)S(1)}, u32[]{:S(2)}, u32[]{:S(2)}) collective-permute-start(f32[192,512]{1,0:T(8,128)S(1)} %get-tuple-element.53.refs_0_), channel_id=1, source_target_pairs={{0,4},{1,5},{2,6},{3,7},{4,0},{5,1},{6,2},{7,3},{8,12},{9,13},{10,... | collective-permute-start | bytes 1179656 | tf_op jit(solution)/shard_map/ppermute | solution.py:47
  102.2 1.2 collective-permute-start.20
  103.5 3.6 %collective-permute-start.24 = (f32[128,512]{1,0:T(8,128)S(1)}, f32[128,512]{1,0:T(8,128)S(1)}, u32[]{:S(2)}, u32[]{:S(2)}) collective-permute-start(f32[128,512]{1,0:T(8,128)S(1)} %get-tuple-element.63), channel_id=1, source_target_pairs={{0,240},{16,0},{32,16},{48,32},{64,48},{80,64},{96,80},{112,96},{1... | collective-permute-start | bytes 786440 | tf_op jit(solution)/shard_map/ppermute | solution.py:34
  107.1 3.8 %presplit.1 = (bf16[1024,3072]{1,0:T(8,128)(2,1)S(1)}, bf16[1024,1024]{1,0:T(8,128)(2,1)S(1)}) custom-call(f32[1024,512]{1,0:T(8,128)S(1)} %copy-done.4, f32[1024,512]{1,0:T(8,128)} %collective-permute-done.8.prev_ref, f32[1024,512]{1,0:T(8,128)} %collective-permute-done.9.next_ref, f32[1024,512]{1,0:T(8,128)S(1)} %copy-done.1, ...), custom_call_target="tpu_custom_call" | custom-call | flops 1 | bytes 1 | tf_op jit(solution)/shard_map/presplit/pallas_call | solution.py:451
  110.9 6.2 %collective-permute-done.19.refs_2_ = f32[192,512]{1,0:T(8,128)S(1)} collective-permute-done((f32[192,512]{1,0:T(8,128)S(1)}, f32[192,512]{1,0:T(8,128)S(1)}, u32[]{:S(2)}, u32[]{:S(2)}) %collective-permute-start.19) | collective-permute-done | bytes 393248 | tf_op jit(solution)/shard_map/ppermute | solution.py:47
  117.1 1.4 collective-permute-done.20.refs_3_
  118.6 2.3 %collective-permute-start.25 = (f32[4,192,512]{2,1,0:T(8,128)S(1)}, f32[4,192,512]{2,1,0:T(8,128)S(1)}, u32[]{:S(2)}, u32[]{:S(2)}) collective-permute-start(f32[4,192,512]{2,1,0:T(8,128)S(1)} %pack.2.mine_ref), channel_id=1, source_target_pairs={{0,1},{1,0},{2,3},{3,2},{4,5},{5,4},{6,7},{7,6},{8,9},{9,8},{10,11... | collective-permute-start | bytes 4718600 | tf_op jit(solution)/shard_map/ppermute | solution.py:38
  120.9 3.6 %collective-permute-start.30 = (f32[256,512]{1,0:T(8,128)S(1)}, f32[256,512]{1,0:T(8,128)S(1)}, u32[]{:S(2)}, u32[]{:S(2)}) collective-permute-start(f32[256,512]{1,0:T(8,128)S(1)} %get-tuple-element.67), channel_id=1, source_target_pairs={{0,240},{16,0},{32,16},{48,32},{64,48},{80,64},{96,80},{112,96},{1... | collective-permute-start | bytes 1572872 | tf_op jit(solution)/shard_map/ppermute | solution.py:34
  124.5 1.1 collective-permute-start.26
  125.6 2.1 %collective-permute-start.27 = (f32[128,512]{1,0:T(8,128)S(1)}, f32[128,512]{1,0:T(8,128)S(1)}, u32[]{:S(2)}, u32[]{:S(2)}) collective-permute-start(f32[128,512]{1,0:T(8,128)S(1)} %get-tuple-element.61.refs_0_), channel_id=1, source_target_pairs={{0,4},{1,5},{2,6},{3,7},{4,0},{5,1},{6,2},{7,3},{8,12},{9,13},{10,... | collective-permute-start | bytes 786440 | tf_op jit(solution)/shard_map/ppermute | solution.py:47
  127.7 1.3 collective-permute-start.28
  129.0 8.2 %finish_a.1 = (f32[1024,512]{1,0:T(8,128)}, f32[8,512]{1,0:T(8,128)S(1)}) custom-call(s32[2]{0:T(128)S(1)} %pad_add_fusion.at_ref, f32[4,192,512]{2,1,0:T(8,128)S(1)} %pack.2.mine_ref, f32[4,192,512]{2,1,0:T(8,128)S(1)} %collective-permute-done.25.other_ref, f32[8,512]{1,0:T(8,128)S(1)} %get-tuple-element.54.f_ref.refs_0_.facts_ref, ...), custom_call_target="tpu_custom_call" | custom-call | flops 1 | bytes 1 | tf_op jit(solution)/shard_map/finish_a/pallas_call | solution.py:501
  137.2 1.8 %collective-permute-done.27.refs_2_ = f32[128,512]{1,0:T(8,128)S(1)} collective-permute-done((f32[128,512]{1,0:T(8,128)S(1)}, f32[128,512]{1,0:T(8,128)S(1)}, u32[]{:S(2)}, u32[]{:S(2)}) %collective-permute-start.27) | collective-permute-done | bytes 262176 | tf_op jit(solution)/shard_map/ppermute | solution.py:47
  139.2 1.6 %collective-permute-start.31 = (f32[4,128,512]{2,1,0:T(8,128)S(1)}, f32[4,128,512]{2,1,0:T(8,128)S(1)}, u32[]{:S(2)}, u32[]{:S(2)}) collective-permute-start(f32[4,128,512]{2,1,0:T(8,128)S(1)} %pack.3.refs_0_.mine_ref), channel_id=1, source_target_pairs={{0,1},{1,0},{2,3},{3,2},{4,5},{5,4},{6,7},{7,6},{8,9},{9,8},{10,11... | collective-permute-start | bytes 3145736 | tf_op jit(solution)/shard_map/ppermute | solution.py:38
  140.9 3.1 %own_b.1 = (f32[1024,512]{1,0:T(8,128)S(1)}, f32[8,512]{1,0:T(8,128)S(1)}) custom-call(s32[2]{0:T(128)S(1)} %pad_add_fusion.at_ref, f32[4,192,512]{2,1,0:T(8,128)S(1)} %pack.2.mine_ref, f32[4,192,512]{2,1,0:T(8,128)S(1)} %collective-permute-done.25.other_ref, f32[8,512]{1,0:T(8,128)S(1)} %get-tuple-element.54.f_ref.refs_0_.facts_ref, ...), custom_call_target="tpu_custom_call" | custom-call | flops 1 | bytes 1 | tf_op jit(solution)/shard_map/own_b/pallas_call | solution.py:534
  144.0 6.7 %finish_b.1 = f32[1024,512]{1,0:T(8,128)} custom-call(s32[2]{0:T(128)S(1)} %pad_add_fusion.at_ref, f32[4,128,512]{2,1,0:T(8,128)S(1)} %pack.3.refs_0_.mine_ref, f32[4,128,512]{2,1,0:T(8,128)S(1)} %collective-permute-done.31.other_ref, f32[8,512]{1,0:T(8,128)S(1)} %get-tuple-element.54.f_ref.refs_0_.facts_ref, f32[8,512]{1,0:T(8,128)S(1)} %get-tuple-element.55.pf_ref.refs_1_, ...), custom_call_target="tpu_custom_call" | custom-call | flops 1 | bytes 1 | tf_op jit(solution)/shard_map/finish_b/pallas_call | solution.py:589
  (43 shorter events, 2.6 us)
Async XLA Ops:
  0.6 53.2 %collective-permute-start.8 = (f32[1024,512]{1,0:T(8,128)}, f32[1024,512]{1,0:T(8,128)}, u32[]{:S(2)}, u32[]{:S(2)}) collective-permute-start(f32[1024,512]{1,0:T(8,128)} %refs_2_.1), channel_id=1, source_target_pairs={{0,16},{16,32},{32,48},{48,64},{64,80},{80,96},{96,112},{112,128},... | collective-permute-start | bytes 6291464 | tf_op jit(solution)/shard_map/ppermute | solution.py:34
  3.2 50.6 %collective-permute-start.9 = (f32[1024,512]{1,0:T(8,128)}, f32[1024,512]{1,0:T(8,128)}, u32[]{:S(2)}, u32[]{:S(2)}) collective-permute-start(f32[1024,512]{1,0:T(8,128)} %refs_2_.1), channel_id=1, source_target_pairs={{0,240},{16,0},{32,16},{48,32},{64,48},{80,64},{96,80},{112,96},{1... | collective-permute-start | bytes 6291464 | tf_op jit(solution)/shard_map/ppermute | solution.py:34
  8.2 1.6 %copy-start = (f32[1024,512]{1,0:T(8,128)S(1)}, f32[1024,512]{1,0:T(8,128)}, u32[]{:S(2)}) copy-start(f32[1024,512]{1,0:T(8,128)} %refs_3_.1) | copy-start | bytes 6291460
  9.8 1.6 %copy-start.2 = (f32[1024,512]{1,0:T(8,128)S(1)}, f32[1024,512]{1,0:T(8,128)}, u32[]{:S(2)}) copy-start(f32[1024,512]{1,0:T(8,128)} %refs_2_.1) | copy-start | bytes 6291460
  11.4 9.2 %copy-start.1 = (f32[1024,512]{1,0:T(8,128)S(1)}, f32[1024,512]{1,0:T(8,128)}, u32[]{:S(2)}) copy-start(f32[1024,512]{1,0:T(8,128)} %refs_3_.1) | copy-start | bytes 6291460
  12.0 1.9 %collective-permute-start = (f32[8,512]{1,0:T(8,128)S(1)}, f32[8,512]{1,0:T(8,128)S(1)}, u32[]{:S(2)}, u32[]{:S(2)}) collective-permute-start(f32[8,512]{1,0:T(8,128)S(1)} %sums.1), channel_id=1, source_target_pairs={{0,1},{1,0},{2,3},{3,2},{4,5},{5,4},{6,7},{7,6},{8,9},{9,8},{10,11... | collective-permute-start | bytes 49160 | tf_op jit(solution)/shard_map/ppermute | solution.py:38
  13.9 4.9 %collective-permute-start.1 = (f32[8,512]{1,0:T(8,128)S(1)}, f32[8,512]{1,0:T(8,128)S(1)}, u32[]{:S(2)}, u32[]{:S(2)}) collective-permute-start(f32[8,512]{1,0:T(8,128)S(1)} %add.3.refs_0_), channel_id=1, source_target_pairs={{0,2},{1,3},{2,4},{3,5},{4,6},{5,7},{6,0},{7,1},{8,10},{9,11},{10,... | collective-permute-start | bytes 49160 | tf_op jit(solution)/shard_map/ppermute | solution.py:47
  15.1 4.5 %collective-permute-start.2 = (f32[8,512]{1,0:T(8,128)S(1)}, f32[8,512]{1,0:T(8,128)S(1)}, u32[]{:S(2)}, u32[]{:S(2)}) collective-permute-start(f32[8,512]{1,0:T(8,128)S(1)} %add.3.refs_0_), channel_id=1, source_target_pairs={{0,4},{1,5},{2,6},{3,7},{4,0},{5,1},{6,2},{7,3},{8,12},{9,13},{10,... | collective-permute-start | bytes 49160 | tf_op jit(solution)/shard_map/ppermute | solution.py:47
  17.6 3.0 %collective-permute-start.3 = (f32[8,512]{1,0:T(8,128)S(1)}, f32[8,512]{1,0:T(8,128)S(1)}, u32[]{:S(2)}, u32[]{:S(2)}) collective-permute-start(f32[8,512]{1,0:T(8,128)S(1)} %add.3.refs_0_), channel_id=1, source_target_pairs={{0,6},{1,7},{2,0},{3,1},{4,2},{5,3},{6,4},{7,5},{8,14},{9,15},{10,... | collective-permute-start | bytes 49160 | tf_op jit(solution)/shard_map/ppermute | solution.py:47
  20.6 1.6 %copy-start.3 = (f32[1024,512]{1,0:T(8,128)S(1)}, f32[1024,512]{1,0:T(8,128)}, u32[]{:S(2)}) copy-start(f32[1024,512]{1,0:T(8,128)} %refs_2_.1) | copy-start | bytes 6291460
  27.6 3.3 %collective-permute-start.4 = (f32[4,64,512]{2,1,0:T(8,128)S(1)}, f32[4,64,512]{2,1,0:T(8,128)S(1)}, u32[]{:S(2)}, u32[]{:S(2)}) collective-permute-start(f32[4,64,512]{2,1,0:T(8,128)S(1)} %get-tuple-element.37), channel_id=1, source_target_pairs={{0,1},{1,0},{2,3},{3,2},{4,5},{5,4},{6,7},{7,6},{8,9},{9,8},{10,11... | collective-permute-start | bytes 1572872 | tf_op jit(solution)/shard_map/ppermute | solution.py:38
  30.9 6.1 %collective-permute-start.5 = (f32[64,512]{1,0:T(8,128)S(1)}, f32[64,512]{1,0:T(8,128)S(1)}, u32[]{:S(2)}, u32[]{:S(2)}) collective-permute-start(f32[64,512]{1,0:T(8,128)S(1)} %get-tuple-element.39), channel_id=1, source_target_pairs={{0,2},{1,3},{2,4},{3,5},{4,6},{5,7},{6,0},{7,1},{8,10},{9,11},{10,... | collective-permute-start | bytes 393224 | tf_op jit(solution)/shard_map/ppermute | solution.py:47
  31.0 9.7 %collective-permute-start.6 = (f32[64,512]{1,0:T(8,128)S(1)}, f32[64,512]{1,0:T(8,128)S(1)}, u32[]{:S(2)}, u32[]{:S(2)}) collective-permute-start(f32[64,512]{1,0:T(8,128)S(1)} %get-tuple-element.40), channel_id=1, source_target_pairs={{0,4},{1,5},{2,6},{3,7},{4,0},{5,1},{6,2},{7,3},{8,12},{9,13},{10,... | collective-permute-start | bytes 393224 | tf_op jit(solution)/shard_map/ppermute | solution.py:47
  34.6 6.2 %collective-permute-start.7 = (f32[64,512]{1,0:T(8,128)S(1)}, f32[64,512]{1,0:T(8,128)S(1)}, u32[]{:S(2)}, u32[]{:S(2)}) collective-permute-start(f32[64,512]{1,0:T(8,128)S(1)} %get-tuple-element.41), channel_id=1, source_target_pairs={{0,6},{1,7},{2,0},{3,1},{4,2},{5,3},{6,4},{7,5},{8,14},{9,15},{10,... | collective-permute-start | bytes 393224 | tf_op jit(solution)/shard_map/ppermute | solution.py:47
  40.9 41.3 %collective-permute-start.15 = (f32[648,512]{1,0:T(8,128)S(1)}, f32[648,512]{1,0:T(8,128)S(1)}, u32[]{:S(2)}, u32[]{:S(2)}) collective-permute-start(f32[648,512]{1,0:T(8,128)S(1)} %get-tuple-element.52), channel_id=1, source_target_pairs={{0,16},{16,32},{32,48},{48,64},{64,80},{80,96},{96,112},{112,128},... | collective-permute-start | bytes 3981320 | tf_op jit(solution)/shard_map/ppermute | solution.py:34
  40.9 41.2 %collective-permute-start.16 = (f32[648,512]{1,0:T(8,128)S(1)}, f32[648,512]{1,0:T(8,128)S(1)}, u32[]{:S(2)}, u32[]{:S(2)}) collective-permute-start(f32[648,512]{1,0:T(8,128)S(1)} %get-tuple-element.52), channel_id=1, source_target_pairs={{0,240},{16,0},{32,16},{48,32},{64,48},{80,64},{96,80},{112,96},{1... | collective-permute-start | bytes 3981320 | tf_op jit(solution)/shard_map/ppermute | solution.py:34
  59.7 3.7 %collective-permute-start.10 = (f32[2,128,512]{2,1,0:T(8,128)S(1)}, f32[2,128,512]{2,1,0:T(8,128)S(1)}, u32[]{:S(2)}, u32[]{:S(2)}) collective-permute-start(f32[2,128,512]{2,1,0:T(8,128)S(1)} %get-tuple-element.46), channel_id=1, source_target_pairs={{0,1},{1,0},{2,3},{3,2},{4,5},{5,4},{6,7},{7,6},{8,9},{9,8},{10,11... | collective-permute-start | bytes 1572872 | tf_op jit(solution)/shard_map/ppermute | solution.py:38
  61.8 2.3 %collective-permute-start.11 = (f32[2,128,512]{2,1,0:T(8,128)S(1)}, f32[2,128,512]{2,1,0:T(8,128)S(1)}, u32[]{:S(2)}, u32[]{:S(2)}) collective-permute-start(f32[2,128,512]{2,1,0:T(8,128)S(1)} %get-tuple-element.47), channel_id=1, source_target_pairs={{0,1},{1,0},{2,3},{3,2},{4,5},{5,4},{6,7},{7,6},{8,9},{9,8},{10,11... | collective-permute-start | bytes 1572872 | tf_op jit(solution)/shard_map/ppermute | solution.py:38
  64.2 17.9 %collective-permute-start.12 = (f32[128,512]{1,0:T(8,128)S(1)}, f32[128,512]{1,0:T(8,128)S(1)}, u32[]{:S(2)}, u32[]{:S(2)}) collective-permute-start(f32[128,512]{1,0:T(8,128)S(1)} %get-tuple-element.49), channel_id=1, source_target_pairs={{0,2},{1,3},{2,4},{3,5},{4,6},{5,7},{6,0},{7,1},{8,10},{9,11},{10,... | collective-permute-start | bytes 786440 | tf_op jit(solution)/shard_map/ppermute | solution.py:47
  65.7 16.4 %collective-permute-start.13 = (f32[128,512]{1,0:T(8,128)S(1)}, f32[128,512]{1,0:T(8,128)S(1)}, u32[]{:S(2)}, u32[]{:S(2)}) collective-permute-start(f32[128,512]{1,0:T(8,128)S(1)} %get-tuple-element.50), channel_id=1, source_target_pairs={{0,4},{1,5},{2,6},{3,7},{4,0},{5,1},{6,2},{7,3},{8,12},{9,13},{10,... | collective-permute-start | bytes 786440 | tf_op jit(solution)/shard_map/ppermute | solution.py:47
  68.1 14.0 %collective-permute-start.14 = (f32[128,512]{1,0:T(8,128)S(1)}, f32[128,512]{1,0:T(8,128)S(1)}, u32[]{:S(2)}, u32[]{:S(2)}) collective-permute-start(f32[128,512]{1,0:T(8,128)S(1)} %get-tuple-element.51), channel_id=1, source_target_pairs={{0,6},{1,7},{2,0},{3,1},{4,2},{5,3},{6,4},{7,5},{8,14},{9,15},{10,... | collective-permute-start | bytes 786440 | tf_op jit(solution)/shard_map/ppermute | solution.py:47
  82.2 24.9 %copy-start.4 = (f32[1024,512]{1,0:T(8,128)S(1)}, f32[1024,512]{1,0:T(8,128)}, u32[]{:S(2)}) copy-start(f32[1024,512]{1,0:T(8,128)} %refs_2_.1) | copy-start | bytes 6291460
  82.2 11.7 %collective-permute-start.17 = (f32[208,512]{1,0:T(8,128)S(1)}, f32[208,512]{1,0:T(8,128)S(1)}, u32[]{:S(2)}, u32[]{:S(2)}) collective-permute-start(f32[208,512]{1,0:T(8,128)S(1)} %message.1.mine_ref), channel_id=1, source_target_pairs={{0,8},{1,9},{2,10},{3,11},{4,12},{5,13},{6,14},{7,15},{8,0},{9,1},... | collective-permute-start | bytes 1277960 | tf_op jit(solution)/shard_map/ppermute | solution.py:42
  94.9 8.5 %collective-permute-start.21 = (f32[64,512]{1,0:T(8,128)S(1)}, f32[64,512]{1,0:T(8,128)S(1)}, u32[]{:S(2)}, u32[]{:S(2)}) collective-permute-start(f32[64,512]{1,0:T(8,128)S(1)} %get-tuple-element.57), channel_id=1, source_target_pairs={{0,16},{16,32},{32,48},{48,64},{64,80},{80,96},{96,112},{112,128},... | collective-permute-start | bytes 393224 | tf_op jit(solution)/shard_map/ppermute | solution.py:34
  95.0 8.4 %collective-permute-start.22 = (f32[64,512]{1,0:T(8,128)S(1)}, f32[64,512]{1,0:T(8,128)S(1)}, u32[]{:S(2)}, u32[]{:S(2)}) collective-permute-start(f32[64,512]{1,0:T(8,128)S(1)} %get-tuple-element.58), channel_id=1, source_target_pairs={{0,240},{16,0},{32,16},{48,32},{64,48},{80,64},{96,80},{112,96},{1... | collective-permute-start | bytes 393224 | tf_op jit(solution)/shard_map/ppermute | solution.py:34
  98.6 12.3 %collective-permute-start.18 = (f32[192,512]{1,0:T(8,128)S(1)}, f32[192,512]{1,0:T(8,128)S(1)}, u32[]{:S(2)}, u32[]{:S(2)}) collective-permute-start(f32[192,512]{1,0:T(8,128)S(1)} %get-tuple-element.53.refs_0_), channel_id=1, source_target_pairs={{0,2},{1,3},{2,4},{3,5},{4,6},{5,7},{6,0},{7,1},{8,10},{9,11},{10,... | collective-permute-start | bytes 1179656 | tf_op jit(solution)/shard_map/ppermute | solution.py:47
  99.8 17.3 %collective-permute-start.19 = (f32[192,512]{1,0:T(8,128)S(1)}, f32[192,512]{1,0:T(8,128)S(1)}, u32[]{:S(2)}, u32[]{:S(2)}) collective-permute-start(f32[192,512]{1,0:T(8,128)S(1)} %get-tuple-element.53.refs_0_), channel_id=1, source_target_pairs={{0,4},{1,5},{2,6},{3,7},{4,0},{5,1},{6,2},{7,3},{8,12},{9,13},{10,... | collective-permute-start | bytes 1179656 | tf_op jit(solution)/shard_map/ppermute | solution.py:47
  102.2 16.3 %collective-permute-start.20 = (f32[192,512]{1,0:T(8,128)S(1)}, f32[192,512]{1,0:T(8,128)S(1)}, u32[]{:S(2)}, u32[]{:S(2)}) collective-permute-start(f32[192,512]{1,0:T(8,128)S(1)} %get-tuple-element.53.refs_0_), channel_id=1, source_target_pairs={{0,6},{1,7},{2,0},{3,1},{4,2},{5,3},{6,4},{7,5},{8,14},{9,15},{10,... | collective-permute-start | bytes 1179656 | tf_op jit(solution)/shard_map/ppermute | solution.py:47
  103.4 7.4 %collective-permute-start.23 = (f32[128,512]{1,0:T(8,128)S(1)}, f32[128,512]{1,0:T(8,128)S(1)}, u32[]{:S(2)}, u32[]{:S(2)}) collective-permute-start(f32[128,512]{1,0:T(8,128)S(1)} %get-tuple-element.63), channel_id=1, source_target_pairs={{0,16},{16,32},{32,48},{48,64},{64,80},{80,96},{96,112},{112,128},... | collective-permute-start | bytes 786440 | tf_op jit(solution)/shard_map/ppermute | solution.py:34
  103.5 7.3 %collective-permute-start.24 = (f32[128,512]{1,0:T(8,128)S(1)}, f32[128,512]{1,0:T(8,128)S(1)}, u32[]{:S(2)}, u32[]{:S(2)}) collective-permute-start(f32[128,512]{1,0:T(8,128)S(1)} %get-tuple-element.63), channel_id=1, source_target_pairs={{0,240},{16,0},{32,16},{48,32},{64,48},{80,64},{96,80},{112,96},{1... | collective-permute-start | bytes 786440 | tf_op jit(solution)/shard_map/ppermute | solution.py:34
  118.6 9.1 %collective-permute-start.25 = (f32[4,192,512]{2,1,0:T(8,128)S(1)}, f32[4,192,512]{2,1,0:T(8,128)S(1)}, u32[]{:S(2)}, u32[]{:S(2)}) collective-permute-start(f32[4,192,512]{2,1,0:T(8,128)S(1)} %pack.2.mine_ref), channel_id=1, source_target_pairs={{0,1},{1,0},{2,3},{3,2},{4,5},{5,4},{6,7},{7,6},{8,9},{9,8},{10,11... | collective-permute-start | bytes 4718600 | tf_op jit(solution)/shard_map/ppermute | solution.py:38
  120.9 18.2 %collective-permute-start.29 = (f32[256,512]{1,0:T(8,128)S(1)}, f32[256,512]{1,0:T(8,128)S(1)}, u32[]{:S(2)}, u32[]{:S(2)}) collective-permute-start(f32[256,512]{1,0:T(8,128)S(1)} %get-tuple-element.67), channel_id=1, source_target_pairs={{0,16},{16,32},{32,48},{48,64},{64,80},{80,96},{96,112},{112,128},... | collective-permute-start | bytes 1572872 | tf_op jit(solution)/shard_map/ppermute | solution.py:34
  120.9 18.2 %collective-permute-start.30 = (f32[256,512]{1,0:T(8,128)S(1)}, f32[256,512]{1,0:T(8,128)S(1)}, u32[]{:S(2)}, u32[]{:S(2)}) collective-permute-start(f32[256,512]{1,0:T(8,128)S(1)} %get-tuple-element.67), channel_id=1, source_target_pairs={{0,240},{16,0},{32,16},{48,32},{64,48},{80,64},{96,80},{112,96},{1... | collective-permute-start | bytes 1572872 | tf_op jit(solution)/shard_map/ppermute | solution.py:34
  124.5 12.7 %collective-permute-start.26 = (f32[128,512]{1,0:T(8,128)S(1)}, f32[128,512]{1,0:T(8,128)S(1)}, u32[]{:S(2)}, u32[]{:S(2)}) collective-permute-start(f32[128,512]{1,0:T(8,128)S(1)} %get-tuple-element.61.refs_0_), channel_id=1, source_target_pairs={{0,2},{1,3},{2,4},{3,5},{4,6},{5,7},{6,0},{7,1},{8,10},{9,11},{10,... | collective-permute-start | bytes 786440 | tf_op jit(solution)/shard_map/ppermute | solution.py:47
  125.6 13.5 %collective-permute-start.27 = (f32[128,512]{1,0:T(8,128)S(1)}, f32[128,512]{1,0:T(8,128)S(1)}, u32[]{:S(2)}, u32[]{:S(2)}) collective-permute-start(f32[128,512]{1,0:T(8,128)S(1)} %get-tuple-element.61.refs_0_), channel_id=1, source_target_pairs={{0,4},{1,5},{2,6},{3,7},{4,0},{5,1},{6,2},{7,3},{8,12},{9,13},{10,... | collective-permute-start | bytes 786440 | tf_op jit(solution)/shard_map/ppermute | solution.py:47
  127.7 11.4 %collective-permute-start.28 = (f32[128,512]{1,0:T(8,128)S(1)}, f32[128,512]{1,0:T(8,128)S(1)}, u32[]{:S(2)}, u32[]{:S(2)}) collective-permute-start(f32[128,512]{1,0:T(8,128)S(1)} %get-tuple-element.61.refs_0_), channel_id=1, source_target_pairs={{0,6},{1,7},{2,0},{3,1},{4,2},{5,3},{6,4},{7,5},{8,14},{9,15},{10,... | collective-permute-start | bytes 786440 | tf_op jit(solution)/shard_map/ppermute | solution.py:47
  139.2 4.7 %collective-permute-start.31 = (f32[4,128,512]{2,1,0:T(8,128)S(1)}, f32[4,128,512]{2,1,0:T(8,128)S(1)}, u32[]{:S(2)}, u32[]{:S(2)}) collective-permute-start(f32[4,128,512]{2,1,0:T(8,128)S(1)} %pack.3.refs_0_.mine_ref), channel_id=1, source_target_pairs={{0,1},{1,0},{2,3},{3,2},{4,5},{5,4},{6,7},{7,6},{8,9},{9,8},{10,11... | collective-permute-start | bytes 3145736 | tf_op jit(solution)/shard_map/ppermute | solution.py:38
